TPU v7x, 256 devices: a whole 4x4x8 slice. The times are simulated.
256 devices in a mesh: blk: 64 (over z, x_hi, y), par: 4 (over x_lo, core).
Axes of the slice: x: 4 (x_hi: 2, x_lo: 2; x = x_hi * 2 + x_lo), y: 4, z: 8, core: 2. Of those that a mesh axis runs over, the one named last changes fastest.
Arguments:
- log_derivs: float32 [16384, 4096], P('blk', 'par'), may hold values from -0.09375 to 0.09375
- energies: float32 [16384], P('blk'), may hold values from -6 to 6
Outputs:
- panel_tiles: float32 [16384, 256], P('blk')
- energies_next: float32 [16384], P('blk')
- diagonal_next: float32 [16384, 256], P(('blk', 'par'))
- neighbour_next: float32 [16384, 256], P(('blk', 'par'))
All inputs are finite; a program needn't handle non-finite values.
Results may differ from a plain program's by a relative error of at most 0.00011.
Values sent between devices are 32-bit elements; how exact they have to be, the bound alone decides.
No kernel may reach another device: no remote copies, remote signals or barrier semaphores. Data moves between devices by JAX's collectives and lax.ppermute only.
A program may use at most 64 MiB of HBM per device.

v0:
```python
import jax
import jax.numpy as jnp
from jax import lax
from jax.sharding import Mesh
from jax.sharding import PartitionSpec as P

BLK = ("blk_0", "blk_1", "blk_2")
BLK_PAR = ("blk_0", "blk_1", "blk_2", "par")


ridge_shift = 0.05


def from_root(value, axis, source):
    kept = jnp.where(lax.axis_index(axis) == source, value, 0).astype(value.dtype)
    return lax.psum(kept, axis)


def from_root_2(value, axes, root):
    value = jnp.where(lax.axis_index(axes) == root, value, jnp.zeros_like(value))
    for axis in axes:
        value = lax.psum(value, axis)
    return value


def passed_along(block, axis, distance):
    devices = range(lax.axis_size(axis))
    route = [((i - distance) % len(devices), i) for i in devices]
    return lax.ppermute(block, axis, route)


def from_everyone(value, axis):
    copies = jnp.broadcast_to(value, (lax.axis_size(axis), *value.shape))
    return lax.all_to_all(copies, axis, split_axis=0, concat_axis=0, tiled=True)


def taken_together(value, axis):
    return from_everyone(value, axis).sum(axis=0)


def in_one(arrays, axis):
    line, at, outs = (jnp.concatenate([a.reshape(-1) for a in arrays]), 0, [])
    subtotal = taken_together(line, axis)
    for a in arrays:
        outs.append(subtotal[at : at + a.size].reshape(a.shape))
        at += a.size
    return tuple(outs)


def kernel_tile(left_rows, right_rows):
    return jnp.dot(
        left_rows, right_rows.T, precision=lax.Precision.HIGHEST, preferred_element_type=jnp.float32
    )


def panel_solve(pivot_factor, cross_tile):
    return lax.linalg.triangular_solve(
        pivot_factor, cross_tile, left_side=False, lower=True, transpose_a=True
    )


def on_device(log_derivs, energies):
    block_size = log_derivs.shape[0]
    share_rows = block_size // lax.axis_size("par")
    row_start = lax.axis_index("par") * share_rows
    lead_rows = from_root(log_derivs, BLK, 0)
    lead_energy = from_root_2(energies, BLK, 0)
    prev_rows = passed_along(log_derivs, BLK, 1)
    cross_part = kernel_tile(log_derivs, lead_rows)
    self_part = kernel_tile(log_derivs, log_derivs)
    cycle_part = kernel_tile(log_derivs, prev_rows)
    pivot_part = kernel_tile(lead_rows, lead_rows)
    unit_full = jnp.eye(block_size, dtype=jnp.float32)
    cross_sum, self_sum, cycle_sum, pivot_sum = in_one(
        (cross_part, self_part, cycle_part, pivot_part), "par"
    )
    pivot_factor = jnp.linalg.cholesky(pivot_sum + ridge_shift * unit_full)
    panel_full = panel_solve(pivot_factor, cross_sum)
    panel_part = lax.dynamic_slice_in_dim(panel_full, row_start, share_rows, 0)
    self_rows = lax.dynamic_slice_in_dim(self_sum, row_start, share_rows, 0)
    cycle_rows = lax.dynamic_slice_in_dim(cycle_sum, row_start, share_rows, 0)
    panel_prev = passed_along(panel_full, BLK, 1)
    unit_rows = (
        lax.broadcasted_iota(jnp.int32, (share_rows, block_size), 0) + row_start
        == lax.broadcasted_iota(jnp.int32, (share_rows, block_size), 1)
    ).astype(jnp.float32)
    diagonal_next = self_rows + ridge_shift * unit_rows - kernel_tile(panel_part, panel_full)
    neighbour_next = cycle_rows - kernel_tile(panel_part, panel_prev)
    lead_solve = lax.linalg.triangular_solve(
        pivot_factor, lead_energy[:, None], left_side=True, lower=True
    )[:, 0]
    remainder = energies - jnp.dot(
        panel_full, lead_solve, precision=lax.Precision.HIGHEST, preferred_element_type=jnp.float32
    )
    energies_next = jnp.where(lax.axis_index(BLK) == 0, lead_solve, remainder)
    return (panel_full, energies_next, diagonal_next, neighbour_next)


def solution(mesh):
    torus = Mesh(
        mesh.devices.reshape(8, 2, 4, mesh.shape["par"]), ("blk_0", "blk_1", "blk_2", "par")
    )
    in_specs = (P(BLK, "par"), P(BLK))
    out_specs = (P(BLK, None), P(BLK), P(BLK_PAR, None), P(BLK_PAR, None))
    return jax.shard_map(
        on_device, mesh=torus, in_specs=in_specs, out_specs=out_specs, check_vma=False
    )
```

profile of v0, /device:TPU:1, one launch (start us, length us, event | category | flops | bytes accessed | tf_op | source)
XLA Modules:
  0.0 876.1 jit_solution(1223781947047268966)
XLA Ops:
  7.2 0.0 copy-start
  7.2 0.0 all-reduce.3.cloned.1.call-start
  7.2 2.5 broadcast_select_fusion
  9.7 0.0 all-reduce.3.cloned.1.call-update
  9.7 0.9 collective-permute-start
  10.6 0.0 copy-done
  10.6 1.0 convolution_bitcast_fusion.2
  11.6 0.8 copy.44
  12.5 659.4 %all-reduce.3.cloned.1.call-done = f32[256,1024]{1,0:T(8,128)} async-done(((f32[256,1024]{1,0:T(8,128)}), f32[256,1024]{1,0:T(8,128)}) %all-reduce.3.cloned.1.call-update) | async-done | bytes 1048592 | tf_op jit(solution)/shard_map/psum | solution.py:16
  671.9 2.3 convolution_bitcast_fusion.3
  674.3 0.9 copy.28
  675.1 1.1 copy.43
  676.3 1.0 convolution_bitcast_fusion
  677.3 0.1 copy.46
  677.4 0.0 collective-permute-done
  677.5 1.0 convolution_bitcast_fusion.1
  678.5 0.1 copy.45
  678.6 0.1 pad_maximum_fusion
  678.7 4.6 broadcast_in_dim.14
  683.3 49.0 %all-to-all-start = ((f32[4,1,262144]{2,1,0:T(1,128)}), f32[4,1,262144]{2,1,0:T(1,128)}, u32[]{:S(2)}, u32[]{:S(2)}) async-start(f32[4,1,262144]{2,1,0:T(1,128)} %broadcast_in_dim.14), calls=%async_computation | async-start | bytes 8388608 | tf_op jit(solution)/shard_map/all_to_all | solution.py:34
  732.3 0.0 copy-done.3
  732.3 11.0 %psum.29 = f32[256]{0:T(256)S(1)} all-reduce(f32[256]{0:T(256)S(1)} %broadcast_select_fusion.1), channel_id=1, replica_groups=mesh['blk_0'=8,'blk_1'=2,'blk_2'=4,'par'=4] {'blk_0'}, use_global_device_ids=true, to_apply=%region_6.7 | all-reduce | flops 256 | bytes 2048 | tf_op jit(solution)/shard_map/psum | solution.py:22
  743.3 34.6 %psum.30 = f32[256]{0:T(256)S(1)} all-reduce(f32[256]{0:T(256)S(1)} %psum.29), channel_id=1, replica_groups=mesh['blk_0'=8,'blk_1'=2,'blk_2'=4,'par'=4] {'blk_1'}, use_global_device_ids=true, to_apply=%region_7.8 | all-reduce | flops 256 | bytes 2048 | tf_op jit(solution)/shard_map/psum | solution.py:22
  777.9 6.7 psum.31
  784.6 0.0 all-to-all-done
  784.6 9.8 %reduce_sum.9 = f32[262144]{0:T(1024)S(1)} reduce(f32[4,1,262144]{2,1,0:T(1,128)} %all-to-all-done, f32[]{:T(128)} %constant.111.clone.1), dimensions={0,1}, to_apply=%region_1.2 | reduce | flops 786432 | bytes 5242884 | tf_op jit(solution)/shard_map/reduce_sum | solution.py:38
  794.4 0.1 fusion.22
  794.5 0.1 slice.109
  794.5 0.1 copy.30
  794.7 0.1 copy.31
  794.9 11.7 %cholesky.49 = f32[128,128]{1,0:T(8,128)S(1)} custom-call(f32[128,128]{1,0:T(8,128)S(1)} %cholesky.115), custom_call_target="Cholesky" | custom-call | tf_op jit(solution)/shard_map/jit(cholesky)/cholesky | solution.py:77
  806.7 9.8 %custom-call.16 = f32[1,128,128]{1,2,0:T(8,128)S(1)} custom-call(f32[1,128,128]{2,1,0:T(8,128)S(1)} %get-tuple-element.59), custom_call_target="InvertDiagBlocksLowerTriangular" | custom-call | tf_op jit(solution)/shard_map/jit(cholesky)/cholesky | solution.py:77
  816.5 0.2 fusion.6
  816.7 0.3 convolution_subtract_fusion.1
  817.0 11.7 %cholesky.103 = f32[128,128]{1,0:T(8,128)S(1)} custom-call(f32[128,128]{1,0:T(8,128)S(1)} %convolution_subtract_fusion.1), custom_call_target="Cholesky" | custom-call | tf_op jit(solution)/shard_map/jit(cholesky)/cholesky | solution.py:77
  828.7 0.1 copy.34
  828.8 0.1 copy.33
  828.9 0.1 copy.32
  829.0 0.6 compare_reduce_fusion
  831.1 0.1 triangular_solve.80
  831.1 4.2 while.1
  831.1 0.6 fusion.39
  831.7 1.4 dynamic-slice.7
  833.1 0.1 copy.48
  833.2 0.6 fusion.39
  833.8 1.4 dynamic-slice.7
  835.2 0.1 copy.48
  835.3 19.9 %custom-call.17 = f32[2,128,128]{1,2,0:T(8,128)S(1)} custom-call(f32[2,128,128]{2,1,0:T(8,128)S(1)} %get-tuple-element.11), custom_call_target="InvertDiagBlocksLowerTriangular" | custom-call | tf_op jit(solution)/shard_map/triangular_solve | solution.py:57
  855.3 0.1 slice.107
  855.3 0.3 fusion.4
  855.7 0.4 convolution_subtract_fusion
  856.0 0.3 fusion.9
  856.4 0.2 convolution_bitcast_fusion.6
  856.6 0.2 fusion.1
  856.7 0.2 convolution_bitcast_fusion.4
  856.9 0.2 fusion.20
  857.2 1.0 collective-permute-start.1
  858.2 0.6 subtract_select_fusion
  858.7 0.8 copy.36
  859.6 0.1 slice.113
  859.6 0.1 slice.111
  859.7 1.1 convolution_subtract_fusion.3
  860.8 7.4 collective-permute-done.1
  868.2 1.1 convolution_subtract_fusion.2
  (24 shorter events, 0.3 us)
Async XLA Ops:
  7.2 3.4 copy-start
  7.2 664.7 %all-reduce.3.cloned.1.call-start = ((), (), s32[]{:S(2)}) async-start(), calls=%async_computation.1 | async-start | bytes 2097152 | tf_op jit(solution)/shard_map/psum | solution.py:16
  9.7 667.7 %collective-permute-start = (f32[256,1024]{1,0:T(8,128)}, f32[256,1024]{1,0:T(8,128)S(1)}, u32[]{:S(2)}, u32[]{:S(2)}) collective-permute-start(f32[256,1024]{1,0:T(8,128)} %param.2), channel_id=1, source_target_pairs={{252,0},{0,4},{4,8},{8,12},{12,16},{16,20},{20,24},{24,28},{28,32}... | collective-permute-start | bytes 3145736 | tf_op jit(solution)/shard_map/ppermute | solution.py:29
  671.9 4.3 copy-start.1
  675.1 3.5 copy-start.2
  683.3 49.0 %copy-start.3 = (f32[256]{0:T(256)S(1)}, f32[256]{0:T(256)}, u32[]{:S(2)}) copy-start(f32[256]{0:T(256)} %param.3) | copy-start | bytes 3076
  683.3 101.2 %all-to-all-start = ((f32[4,1,262144]{2,1,0:T(1,128)}), f32[4,1,262144]{2,1,0:T(1,128)}, u32[]{:S(2)}, u32[]{:S(2)}) async-start(f32[4,1,262144]{2,1,0:T(1,128)} %broadcast_in_dim.14), calls=%async_computation | async-start | bytes 8388608 | tf_op jit(solution)/shard_map/all_to_all | solution.py:34
  857.2 11.0 %collective-permute-start.1 = (f32[256,256]{0,1:T(8,128)S(1)}, f32[256,256]{0,1:T(8,128)S(1)}, u32[]{:S(2)}, u32[]{:S(2)}) collective-permute-start(f32[256,256]{0,1:T(8,128)S(1)} %pad_maximum_fusion.1), channel_id=1, source_target_pairs={{252,0},{0,4},{4,8},{8,12},{12,16},{16,20},{20,24},{24,28},{28,32}... | collective-permute-start | bytes 786440 | tf_op jit(solution)/shard_map/ppermute | solution.py:29
Sparse Core Ops, SparseCore 0:
  10.6 661.2 all-reduce.2
where the time goes:
time: 881 us; the launch traced here: 876 us
  waiting for transfers between devices  667 us (76%)
  other arithmetic  66.9 us (8%)
  blocking collectives  52.2 us (6%)
  starting transfers between devices  50.9 us (6%)
  between operations  15.7 us (2%)
  local copies, waits for them, and re-layouts  13.7 us (2%)
  matrix products  9.81 us (1%)
    psum x1, waiting for transfers between devices, from_root(): return lax.psum(kept, axis)  659 us
    psum x3, blocking collectives, from_root_2(): value = lax.psum(value, axis)  52.2 us
    all_to_all x1, starting transfers between devices, from_everyone(): return lax.all_to_all(copies, axis, split_axis=0, concat_axis=0, tiled=True)  49 us
    another operation x6, other arithmetic, on_device(): pivot_factor = jnp.linalg.cholesky(pivot_sum + ridge_shift * unit_full)  33.9 us
    another operation x4, other arithmetic, panel_solve(): lax.linalg.triangular_solve(pivot_factor, cross_tile, left_side=False, lo...  20 us
  transfers between devices with their start and end apart: 4, of which 2 were waited for; matrix products, arithmetic and copies ran while one was open for 1% of the time, Pallas kernels for 0%

commit v1 on v0

v1 whole, which is shorter than its diff:
```python
import functools

import jax
import jax.numpy as jnp
from jax import lax
from jax.experimental import pallas as pl
from jax.experimental.pallas import tpu as pltpu
from jax.sharding import Mesh
from jax.sharding import PartitionSpec as P

BLK = ("z", "xh", "y")
PLANE = ("xh", "y")
PAR = ("xl", "core")
ALL = BLK + PAR
HIGHEST = lax.Precision.HIGHEST

ridge_shift = 0.05
CHUNK = 64


def dot(a, b, ca, cb):
    return lax.dot_general(
        a, b, (((ca,), (cb,)), ((), ())), precision=HIGHEST, preferred_element_type=jnp.float32
    )


def outer_tile(left_rows, right_rows):
    return dot(left_rows, right_rows, 1, 1)


def unit(rows, columns):
    return lax.broadcasted_iota(jnp.int32, (rows, columns), 0) == lax.broadcasted_iota(
        jnp.int32, (rows, columns), 1
    )


def triangle_inverse(tile):
    n = tile.shape[0]
    held = jnp.concatenate([tile, unit(n, n).astype(jnp.float32)], axis=1)
    rows = lax.broadcasted_iota(jnp.int32, held.shape, 0)
    for j in range(0, n, 2):
        low = (j // 8) * 8
        part, at = held[low:, :], rows[low:]
        first = jnp.broadcast_to(part[:, j : j + 1], part.shape)
        second = jnp.broadcast_to(part[:, j + 1 : j + 2], part.shape)
        row_a, row_b = held[j : j + 1, :], held[j + 1 : j + 2, :]
        k = j - low
        a, b, c = first[k : k + 1], first[k + 1 : k + 2], second[k + 1 : k + 2]
        over_a = 1.0 / a
        over_det = 1.0 / (a * c - b * b)
        t = b * over_a
        row_b = row_b - t * row_a
        update = first * over_a * row_a + (second - first * t) * (a * over_det) * row_b
        update = jnp.where(at > j + 1, update, 0.0)
        update = jnp.where(at == j + 1, jnp.broadcast_to(t * row_a, part.shape), update)
        part = part - update
        held = jnp.concatenate([held[:low], part], axis=0) if low else part
    pivots = jnp.sum(jnp.where(unit(n, 2 * n), held, 0.0), axis=1, keepdims=True)
    return held[:, n:] * (1.0 / jnp.sqrt(pivots))


def factor_inverse(tile_ref, inverse_ref):
    n = tile_ref.shape[0]
    inverse_ref[...] = jnp.zeros((n, n), jnp.float32)
    for r0 in range(0, n, CHUNK):
        r1 = r0 + CHUNK
        small = triangle_inverse(tile_ref[r0:r1, r0:r1])
        if r0:
            inverse_ref[r0:r1, :r0] = dot(small, inverse_ref[r0:r1, :r0], 1, 0)
        inverse_ref[r0:r1, r0:r1] = small
        if r1 < n:
            across = dot(small, tile_ref[r0:r1, r1:], 1, 0)
            tile_ref[r1:, r1:] = tile_ref[r1:, r1:] - dot(across, across, 0, 0)
            inverse_ref[r1:, :r1] = inverse_ref[r1:, :r1] - dot(
                across, inverse_ref[r0:r1, :r1], 0, 0
            )


def finish_kernel(
    at_ref, sums_ref, self_ref, cycle_ref, energy_ref, lead_ref,
    panel_ref, energies_ref, diagonal_ref, neighbour_ref, tile_ref, inverse_ref, prev_ref,
):
    n = tile_ref.shape[0]
    share = self_ref.shape[0]
    tile_ref[...] = sums_ref[2] + ridge_shift * unit(n, n).astype(jnp.float32)
    factor_inverse(tile_ref, inverse_ref)
    inverse = inverse_ref[...]
    panel = outer_tile(sums_ref[0], inverse)
    panel_ref[...] = panel
    prev_ref[...] = outer_tile(sums_ref[1], inverse)
    start = pl.multiple_of(at_ref[0] * share, share)
    own = panel_ref[pl.ds(start, share), :]
    shifted = (
        lax.broadcasted_iota(jnp.int32, (share, n), 0) + start
        == lax.broadcasted_iota(jnp.int32, (share, n), 1)
    ).astype(jnp.float32)
    diagonal_ref[...] = self_ref[...] + ridge_shift * shifted - outer_tile(own, panel)
    neighbour_ref[...] = cycle_ref[...] - outer_tile(own, prev_ref[...])
    lead = outer_tile(jnp.broadcast_to(lead_ref[...], (8, n)), inverse)
    remainder = energy_ref[...] - outer_tile(lead, panel)[:1]
    energies_ref[...] = jnp.where(at_ref[1] == 0, lead[:1], remainder)


def finish(at, sums, self_rows, cycle_rows, energies, lead_energy):
    n = sums.shape[-1]
    share = self_rows.shape[0]
    f32 = lambda *shape: jax.ShapeDtypeStruct(shape, jnp.float32)
    vmem = pl.BlockSpec(memory_space=pltpu.VMEM)
    return pl.pallas_call(
        finish_kernel,
        out_shape=(f32(n, n), f32(1, n), f32(share, n), f32(share, n)),
        in_specs=[pl.BlockSpec(memory_space=pltpu.SMEM)] + [vmem] * 5,
        out_specs=(vmem,) * 4,
        scratch_shapes=[pltpu.VMEM((n, n), jnp.float32)] * 3,
        name="finish",
    )(at, sums, self_rows, cycle_rows, energies, lead_energy)


def swapped(value, axis):
    return lax.ppermute(value, axis, [(0, 1), (1, 0)])


def passed_along(block, axis, distance):
    count = lax.axis_size(axis)
    return lax.ppermute(block, axis, [((i - distance) % count, i) for i in range(count)])


def sum_scattered(partials):
    k, n = partials.shape[0], partials.shape[-1]
    quarters = partials.reshape(k, 2, 2, n // 4, n)
    core, xl = lax.axis_index("core"), lax.axis_index("xl")
    pick = lambda a, i, d: lax.dynamic_index_in_dim(a, i, d, keepdims=False)
    halves = pick(quarters, core, 2) + swapped(pick(quarters, 1 - core, 2), "core")
    return pick(halves, xl, 1) + swapped(pick(halves, 1 - xl, 1), "xl")


def sum_everywhere(partials):
    k, n = partials.shape[0], partials.shape[-1]
    core = lax.axis_index("core")
    chip = partials + swapped(partials, "core")
    halves = chip.reshape(k, 2, n // 2, n)
    own = lax.dynamic_index_in_dim(halves, core, 1, keepdims=False)
    own = own + swapped(own, "xl")
    other = swapped(own, "core")
    upper = jnp.where(core == 0, own, other)
    lower = jnp.where(core == 0, other, own)
    return jnp.stack([upper, lower], axis=1).reshape(k, n, n)


def from_first(pieces, axis):
    count = lax.axis_size(axis)
    got = [lax.ppermute(pieces(k), axis, [(0, k)]) for k in range(1, count)]
    return jnp.where(lax.axis_index(axis) == 0, pieces(0), functools.reduce(jnp.add, got))


def broadcast_lead(rows):
    n = rows.shape[0]
    parts = lax.axis_size(PLANE)
    part = n // parts
    got = [
        lax.ppermute(rows[k * part : (k + 1) * part], BLK, [(0, k)]) for k in range(1, parts)
    ]
    piece = jnp.where(lax.axis_index(PLANE) == 0, rows[:part], functools.reduce(jnp.add, got))
    piece = from_first(lambda k: piece, "z")
    copies = jnp.broadcast_to(piece, (parts, *piece.shape))
    return lax.all_to_all(copies, PLANE, split_axis=0, concat_axis=0, tiled=True).reshape(rows.shape)


def on_device(log_derivs, energies):
    n = log_derivs.shape[0]
    width = log_derivs.shape[1]
    column = jnp.pad(energies[:, None], ((0, 0), (0, 127)))
    lead = broadcast_lead(jnp.concatenate([log_derivs, column], axis=1))
    lead_rows, lead_energy = lead[:, :width], lead[:, width].reshape(1, n)
    prev_rows = passed_along(log_derivs, BLK, 1)
    early = sum_scattered(
        jnp.stack([outer_tile(log_derivs, log_derivs), outer_tile(log_derivs, prev_rows)])
    )
    sums = sum_everywhere(
        jnp.stack(
            [
                outer_tile(log_derivs, lead_rows),
                outer_tile(prev_rows, lead_rows),
                outer_tile(lead_rows, lead_rows),
            ]
        )
    )
    at = jnp.stack([lax.axis_index(PAR), lax.axis_index(BLK)]).astype(jnp.int32)
    panel, energies_next, diagonal, neighbour = finish(
        at, sums, early[0], early[1], energies.reshape(1, n), lead_energy
    )
    return panel, energies_next.reshape(n), diagonal, neighbour


def solution(mesh):
    torus = Mesh(mesh.devices.reshape(8, 2, 4, 2, 2), ALL)
    in_specs = (P(BLK, PAR), P(BLK))
    out_specs = (P(BLK, None), P(BLK), P(ALL, None), P(ALL, None))
    return jax.shard_map(
        on_device, mesh=torus, in_specs=in_specs, out_specs=out_specs, check_vma=False
    )
```

time: 881 us -> 131 us (0.15)
  waiting for transfers between devices: 667 us -> 60.7 us
  other arithmetic: 66.9 us -> 3.33 us
  blocking collectives: 52.2 us -> 0 us
  Pallas kernels: 0 us -> 18.3 us
  between operations: 15.7 us -> 0.96 us
  starting transfers between devices: 50.9 us -> 38.8 us
  local copies, waits for them, and re-layouts: 13.7 us -> 3.43 us
    psum x1 -> x0, waiting for transfers between devices: 659 us -> none  [from_root(): return lax.psum(kept, axis)]
    another operation x11 -> x5, other arithmetic: 53.9 us -> 1.7 us  [the longest x2 1.01 us: sum_everywhere(): return jnp.stack([upper, lower], axis=1).reshape(k, n, n)]
    psum x3 -> x0, blocking collectives: 52.2 us -> none  [from_root_2(): value = lax.psum(value, axis)]
    all_to_all x1, starting transfers between devices: 49 us -> 5.11 us  [broadcast_lead(): lax.all_to_all(copies, PLANE, split_axis=0, concat_axis=0, tiled=True)]
    all_to_all x1, waiting for transfers between devices: 0.01 us -> 38.6 us  [broadcast_lead(): lax.all_to_all(copies, PLANE, split_axis=0, concat_axis=0, tiled=True)]
    ppermute x2 -> x20, starting transfers between devices: 1.89 us -> 33.7 us  [the longest x7 15.1 us: broadcast_lead(): lax.ppermute(rows[k * part:(k + 1) * part], BLK, [(0, k)])]
    pallas_call x0 -> x1, Pallas kernels: none -> 18.3 us  [finish(): pl.pallas_call(finish_kernel, out_shape=(f32(n, n), f32(1, n), f32(share,...]
    ppermute x2 -> x20, waiting for transfers between devices: 7.38 us -> 22.1 us  [the longest x5 9.21 us: swapped(): return lax.ppermute(value, axis, [(0, 1), (1, 0)])]
  transfers between devices with their start and end apart: 4 -> 21, of which waited for: 2 -> 11; matrix products, arithmetic and copies ran while one was open for 1% -> 5% of each run, Pallas kernels for 0% -> 0%
where the time goes in v1:
time: 131 us
  waiting for transfers between devices  60.7 us (46%)
  starting transfers between devices  38.8 us (30%)
  Pallas kernels  18.3 us (14%)
  matrix products  5.14 us (4%)
  local copies, waits for them, and re-layouts  3.43 us (3%)
  other arithmetic  3.33 us (3%)
    all_to_all x1, waiting for transfers between devices, broadcast_lead(): lax.all_to_all(copies, PLANE, split_axis=0, concat_axis=0, tiled=True)  38.6 us
    pallas_call x1, Pallas kernels, finish(): pl.pallas_call(finish_kernel, out_shape=(f32(n, n), f32(1, n), f32(share,...  18.3 us
    ppermute x7, starting transfers between devices, broadcast_lead(): lax.ppermute(rows[k * part:(k + 1) * part], BLK, [(0, k)])  15.1 us
    ppermute x5, waiting for transfers between devices, swapped(): return lax.ppermute(value, axis, [(0, 1), (1, 0)])  9.21 us
    ppermute x7, starting transfers between devices, from_first(): got = [lax.ppermute(pieces(k), axis, [(0, k)]) for k in range(1, count)]  9.09 us
    ppermute x5, starting transfers between devices, swapped(): return lax.ppermute(value, axis, [(0, 1), (1, 0)])  8.08 us
    ppermute x7, waiting for transfers between devices, from_first(): got = [lax.ppermute(pieces(k), axis, [(0, k)]) for k in range(1, count)]  7.47 us
    ppermute x7, waiting for transfers between devices, broadcast_lead(): lax.ppermute(rows[k * part:(k + 1) * part], BLK, [(0, k)])  5.43 us
  transfers between devices with their start and end apart: 21, of which 11 were waited for; matrix products, arithmetic and copies ran while one was open for 5% of the time, Pallas kernels for 0%

profile of v1, /device:TPU:1, one launch (start us, length us, event | category | flops | bytes accessed | tf_op | source)
XLA Modules:
  0.0 130.7 jit_solution(6145838001511079126)
XLA Ops:
  0.6 0.8 copy.18
  1.4 1.3 %select_maximum_fusion = f32[256,1152]{1,0:T(8,128)S(1)} fusion(f32[256,1]{1,0:T(8,128)S(1)} %copy.18, f32[256,1024]{1,0:T(8,128)} %param.2), kind=kLoop, calls=%fused_computation | loop fusion | flops 884736 | bytes 2229248 | tf_op jit(solution)/shard_map/concatenate | solution.py:173
  2.8 0.1 fusion.6
  2.8 5.6 %collective-permute-start.1 = (f32[32,1152]{1,0:T(8,128)S(1)}, f32[32,1152]{1,0:T(8,128)S(1)}, u32[]{:S(2)}, u32[]{:S(2)}) collective-permute-start(f32[32,1152]{1,0:T(8,128)S(1)} %get-tuple-element.12), channel_id=1, source_target_pairs={{0,8},{1,9},{2,10},{3,11}} | collective-permute-start | bytes 442376 | tf_op jit(solution)/shard_map/ppermute | solution.py:161
  8.5 3.0 %collective-permute-start.6 = (f32[32,1152]{1,0:T(8,128)S(1)}, f32[32,1152]{1,0:T(8,128)S(1)}, u32[]{:S(2)}, u32[]{:S(2)}) collective-permute-start(f32[32,1152]{1,0:T(8,128)S(1)} %get-tuple-element.13), channel_id=1, source_target_pairs={{0,28},{1,29},{2,30},{3,31}} | collective-permute-start | bytes 442376 | tf_op jit(solution)/shard_map/ppermute | solution.py:161
  11.5 1.3 collective-permute-start.5
  12.8 1.3 collective-permute-start.4
  14.1 1.3 collective-permute-start.3
  15.4 0.0 collective-permute-done.1
  15.4 1.3 collective-permute-start.2
  16.7 0.0 collective-permute-done.6
  16.7 1.3 collective-permute-start
  18.0 0.0 collective-permute-done.5
  18.0 2.3 %collective-permute-done.4 = f32[32,1152]{1,0:T(8,128)S(1)} collective-permute-done((f32[32,1152]{1,0:T(8,128)S(1)}, f32[32,1152]{1,0:T(8,128)S(1)}, u32[]{:S(2)}, u32[]{:S(2)}) %collective-permute-start.4) | collective-permute-done | bytes 147488 | tf_op jit(solution)/shard_map/ppermute | solution.py:161
  20.3 3.2 %collective-permute-done.3 = f32[32,1152]{1,0:T(8,128)S(1)} collective-permute-done((f32[32,1152]{1,0:T(8,128)S(1)}, f32[32,1152]{1,0:T(8,128)S(1)}, u32[]{:S(2)}, u32[]{:S(2)}) %collective-permute-start.3) | collective-permute-done | bytes 147488 | tf_op jit(solution)/shard_map/ppermute | solution.py:161
  23.4 0.0 collective-permute-done.2
  23.4 0.0 collective-permute-done
  23.4 0.1 slice_select_fusion
  23.5 1.3 collective-permute-start.13
  24.8 1.3 collective-permute-start.12
  26.1 1.3 collective-permute-start.11
  27.4 1.3 collective-permute-start.10
  28.7 1.3 collective-permute-start.9
  30.0 0.0 collective-permute-done.13
  30.1 1.3 collective-permute-start.8
  31.4 0.0 collective-permute-done.12
  31.4 1.3 collective-permute-start.7
  32.7 0.4 collective-permute-done.11
  33.1 0.0 collective-permute-done.10
  33.1 0.8 collective-permute-done.9
  33.8 3.2 %collective-permute-done.8 = f32[32,1152]{1,0:T(8,128)S(1)} collective-permute-done((f32[32,1152]{1,0:T(8,128)S(1)}, f32[32,1152]{1,0:T(8,128)S(1)}, u32[]{:S(2)}, u32[]{:S(2)}) %collective-permute-start.8) | collective-permute-done | bytes 147488 | tf_op jit(solution)/shard_map/ppermute | solution.py:152
  37.0 3.2 %collective-permute-done.7 = f32[32,1152]{1,0:T(8,128)S(1)} collective-permute-done((f32[32,1152]{1,0:T(8,128)S(1)}, f32[32,1152]{1,0:T(8,128)S(1)}, u32[]{:S(2)}, u32[]{:S(2)}) %collective-permute-start.7) | collective-permute-done | bytes 147488 | tf_op jit(solution)/shard_map/ppermute | solution.py:152
  40.1 0.1 add_select_fusion
  40.2 1.1 broadcast_in_dim.7
  41.3 0.0 copy-start
  41.3 5.1 %all-to-all-start = ((f32[8,32,1152]{2,1,0:T(8,128)}), f32[8,32,1152]{2,1,0:T(8,128)S(1)}, u32[]{:S(2)}, u32[]{:S(2)}) async-start(f32[8,32,1152]{2,1,0:T(8,128)} %broadcast_in_dim.7), calls=%async_computation | async-start | bytes 2359296 | tf_op jit(solution)/shard_map/all_to_all | solution.py:166
  46.4 0.0 copy-done
  46.4 1.5 %collective-permute-start.14 = (f32[256,1024]{1,0:T(8,128)S(1)}, f32[256,1024]{1,0:T(8,128)S(1)}, u32[]{:S(2)}, u32[]{:S(2)}) collective-permute-start(f32[256,1024]{1,0:T(8,128)S(1)} %copy-done), channel_id=1, source_target_pairs={{252,0},{0,4},{4,8},{8,12},{12,16},{16,20},{20,24},{24,28},{28,32}... | collective-permute-start | bytes 3145736 | tf_op jit(solution)/shard_map/ppermute | solution.py:125
  47.9 38.6 %all-to-all-done = f32[8,32,1152]{2,1,0:T(8,128)S(1)} async-done(((f32[8,32,1152]{2,1,0:T(8,128)}), f32[8,32,1152]{2,1,0:T(8,128)S(1)}, u32[]{:S(2)}, u32[]{:S(2)}) %all-to-all-start) | async-done | bytes 1179680 | tf_op jit(solution)/shard_map/all_to_all | solution.py:166
  86.5 1.0 convolution_bitcast_fusion
  87.6 1.0 convolution_bitcast_fusion.2
  88.6 0.0 collective-permute-done.14
  88.6 1.0 convolution_bitcast_fusion.1
  89.6 0.1 pad_maximum_fusion
  89.7 4.4 %collective-permute-start.15 = (f32[3,256,256]{2,1,0:T(8,128)S(1)}, f32[3,256,256]{2,1,0:T(8,128)S(1)}, u32[]{:S(2)}, u32[]{:S(2)}) collective-permute-start(f32[3,256,256]{2,1,0:T(8,128)S(1)} %pad_maximum_fusion), channel_id=1, source_target_pairs={{0,1},{1,0},{2,3},{3,2},{4,5},{5,4},{6,7},{7,6},{8,9},{9,8},{10,11... | collective-permute-start | bytes 2359304 | tf_op jit(solution)/shard_map/ppermute | solution.py:120
  94.2 0.6 pad_add_fusion.at_ref
  94.7 1.0 fusion.7
  95.8 1.0 fusion.8
  96.9 0.1 collective-permute-start.18
  97.0 0.0 collective-permute-done.15
  97.0 0.1 fusion.5
  97.2 0.5 collective-permute-start.16
  97.6 0.9 collective-permute-done.18
  98.6 0.5 collective-permute-start.19
  99.1 0.7 slice_reduce_fusion
  99.8 7.7 %collective-permute-done.16 = f32[3,128,256]{2,1,0:T(8,128)S(1)} collective-permute-done((f32[3,128,256]{2,1,0:T(8,128)S(1)}, f32[3,128,256]{2,1,0:T(8,128)S(1)}, u32[]{:S(2)}, u32[]{:S(2)}) %collective-permute-start.16) | collective-permute-done | bytes 393248 | tf_op jit(solution)/shard_map/ppermute | solution.py:120
  107.4 0.1 fusion.15
  107.5 2.6 %collective-permute-start.17 = (f32[3,128,256]{2,1,0:T(8,128)S(1)}, f32[3,128,256]{2,1,0:T(8,128)S(1)}, u32[]{:S(2)}, u32[]{:S(2)}) collective-permute-start(f32[3,128,256]{2,1,0:T(8,128)S(1)} %fusion.15), channel_id=1, source_target_pairs={{0,1},{1,0},{2,3},{3,2},{4,5},{5,4},{6,7},{7,6},{8,9},{9,8},{10,11... | collective-permute-start | bytes 1179656 | tf_op jit(solution)/shard_map/ppermute | solution.py:120
  110.0 0.2 collective-permute-done.19
  110.3 0.7 slice_bitcast_fusion
  110.9 0.5 collective-permute-done.17
  111.4 0.1 select_bitcast_fusion.1
  111.5 0.9 pad_maximum_fusion.1
  112.4 18.3 %finish.1 = (f32[256,256]{1,0:T(8,128)}, f32[1,256]{1,0:T(1,128)}, f32[64,256]{1,0:T(8,128)}, f32[64,256]{1,0:T(8,128)}) custom-call(s32[2]{0:T(128)} %pad_add_fusion.at_ref, f32[3,256,256]{2,1,0:T(8,128)} %bitcast.54, f32[64,256]{1,0:T(8,128)} %get-tuple-element.24.self_ref, f32[64,256]{1,0:T(8,128)} %get-tuple-element.23.cycle_ref, f32[1,256]{1,0:T(1,128)} %bitcast.61, ...), custom_call_target="tpu_custom_call" | custom-call | tf_op jit(solution)/shard_map/finish/pallas_call | solution.py:109
  (6 shorter events, 0.2 us)
Async XLA Ops:
  2.8 12.5 %collective-permute-start.1 = (f32[32,1152]{1,0:T(8,128)S(1)}, f32[32,1152]{1,0:T(8,128)S(1)}, u32[]{:S(2)}, u32[]{:S(2)}) collective-permute-start(f32[32,1152]{1,0:T(8,128)S(1)} %get-tuple-element.12), channel_id=1, source_target_pairs={{0,8},{1,9},{2,10},{3,11}} | collective-permute-start | bytes 442376 | tf_op jit(solution)/shard_map/ppermute | solution.py:161
  8.5 8.2 %collective-permute-start.6 = (f32[32,1152]{1,0:T(8,128)S(1)}, f32[32,1152]{1,0:T(8,128)S(1)}, u32[]{:S(2)}, u32[]{:S(2)}) collective-permute-start(f32[32,1152]{1,0:T(8,128)S(1)} %get-tuple-element.13), channel_id=1, source_target_pairs={{0,28},{1,29},{2,30},{3,31}} | collective-permute-start | bytes 442376 | tf_op jit(solution)/shard_map/ppermute | solution.py:161
  11.5 6.6 %collective-permute-start.5 = (f32[32,1152]{1,0:T(8,128)S(1)}, f32[32,1152]{1,0:T(8,128)S(1)}, u32[]{:S(2)}, u32[]{:S(2)}) collective-permute-start(f32[32,1152]{1,0:T(8,128)S(1)} %get-tuple-element.14), channel_id=1, source_target_pairs={{0,24},{1,25},{2,26},{3,27}} | collective-permute-start | bytes 442376 | tf_op jit(solution)/shard_map/ppermute | solution.py:161
  12.8 7.5 %collective-permute-start.4 = (f32[32,1152]{1,0:T(8,128)S(1)}, f32[32,1152]{1,0:T(8,128)S(1)}, u32[]{:S(2)}, u32[]{:S(2)}) collective-permute-start(f32[32,1152]{1,0:T(8,128)S(1)} %get-tuple-element.15), channel_id=1, source_target_pairs={{0,20},{1,21},{2,22},{3,23}} | collective-permute-start | bytes 442376 | tf_op jit(solution)/shard_map/ppermute | solution.py:161
  14.1 9.4 %collective-permute-start.3 = (f32[32,1152]{1,0:T(8,128)S(1)}, f32[32,1152]{1,0:T(8,128)S(1)}, u32[]{:S(2)}, u32[]{:S(2)}) collective-permute-start(f32[32,1152]{1,0:T(8,128)S(1)} %get-tuple-element.16), channel_id=1, source_target_pairs={{0,16},{1,17},{2,18},{3,19}} | collective-permute-start | bytes 442376 | tf_op jit(solution)/shard_map/ppermute | solution.py:161
  15.4 8.1 %collective-permute-start.2 = (f32[32,1152]{1,0:T(8,128)S(1)}, f32[32,1152]{1,0:T(8,128)S(1)}, u32[]{:S(2)}, u32[]{:S(2)}) collective-permute-start(f32[32,1152]{1,0:T(8,128)S(1)} %get-tuple-element.17), channel_id=1, source_target_pairs={{0,12},{1,13},{2,14},{3,15}} | collective-permute-start | bytes 442376 | tf_op jit(solution)/shard_map/ppermute | solution.py:161
  16.7 6.7 %collective-permute-start = (f32[32,1152]{1,0:T(8,128)S(1)}, f32[32,1152]{1,0:T(8,128)S(1)}, u32[]{:S(2)}, u32[]{:S(2)}) collective-permute-start(f32[32,1152]{1,0:T(8,128)S(1)} %get-tuple-element.18), channel_id=1, source_target_pairs={{0,4},{1,5},{2,6},{3,7}} | collective-permute-start | bytes 442376 | tf_op jit(solution)/shard_map/ppermute | solution.py:161
  23.5 6.5 %collective-permute-start.13 = (f32[32,1152]{1,0:T(8,128)S(1)}, f32[32,1152]{1,0:T(8,128)S(1)}, u32[]{:S(2)}, u32[]{:S(2)}) collective-permute-start(f32[32,1152]{1,0:T(8,128)S(1)} %slice_select_fusion), channel_id=1, source_target_pairs={{0,224},{1,225},{2,226},{3,227},{4,228},{5,229},{6,230},{7,231},{8... | collective-permute-start | bytes 442376 | tf_op jit(solution)/shard_map/ppermute | solution.py:152
  24.8 6.5 %collective-permute-start.12 = (f32[32,1152]{1,0:T(8,128)S(1)}, f32[32,1152]{1,0:T(8,128)S(1)}, u32[]{:S(2)}, u32[]{:S(2)}) collective-permute-start(f32[32,1152]{1,0:T(8,128)S(1)} %slice_select_fusion), channel_id=1, source_target_pairs={{0,192},{1,193},{2,194},{3,195},{4,196},{5,197},{6,198},{7,199},{8... | collective-permute-start | bytes 442376 | tf_op jit(solution)/shard_map/ppermute | solution.py:152
  26.1 6.9 %collective-permute-start.11 = (f32[32,1152]{1,0:T(8,128)S(1)}, f32[32,1152]{1,0:T(8,128)S(1)}, u32[]{:S(2)}, u32[]{:S(2)}) collective-permute-start(f32[32,1152]{1,0:T(8,128)S(1)} %slice_select_fusion), channel_id=1, source_target_pairs={{0,160},{1,161},{2,162},{3,163},{4,164},{5,165},{6,166},{7,167},{8... | collective-permute-start | bytes 442376 | tf_op jit(solution)/shard_map/ppermute | solution.py:152
  27.4 5.6 %collective-permute-start.10 = (f32[32,1152]{1,0:T(8,128)S(1)}, f32[32,1152]{1,0:T(8,128)S(1)}, u32[]{:S(2)}, u32[]{:S(2)}) collective-permute-start(f32[32,1152]{1,0:T(8,128)S(1)} %slice_select_fusion), channel_id=1, source_target_pairs={{0,128},{1,129},{2,130},{3,131},{4,132},{5,133},{6,134},{7,135},{8... | collective-permute-start | bytes 442376 | tf_op jit(solution)/shard_map/ppermute | solution.py:152
  28.7 5.1 %collective-permute-start.9 = (f32[32,1152]{1,0:T(8,128)S(1)}, f32[32,1152]{1,0:T(8,128)S(1)}, u32[]{:S(2)}, u32[]{:S(2)}) collective-permute-start(f32[32,1152]{1,0:T(8,128)S(1)} %slice_select_fusion), channel_id=1, source_target_pairs={{0,96},{1,97},{2,98},{3,99},{4,100},{5,101},{6,102},{7,103},{8,104... | collective-permute-start | bytes 442376 | tf_op jit(solution)/shard_map/ppermute | solution.py:152
  30.1 6.9 %collective-permute-start.8 = (f32[32,1152]{1,0:T(8,128)S(1)}, f32[32,1152]{1,0:T(8,128)S(1)}, u32[]{:S(2)}, u32[]{:S(2)}) collective-permute-start(f32[32,1152]{1,0:T(8,128)S(1)} %slice_select_fusion), channel_id=1, source_target_pairs={{0,64},{1,65},{2,66},{3,67},{4,68},{5,69},{6,70},{7,71},{8,72},{9,... | collective-permute-start | bytes 442376 | tf_op jit(solution)/shard_map/ppermute | solution.py:152
  31.4 8.8 %collective-permute-start.7 = (f32[32,1152]{1,0:T(8,128)S(1)}, f32[32,1152]{1,0:T(8,128)S(1)}, u32[]{:S(2)}, u32[]{:S(2)}) collective-permute-start(f32[32,1152]{1,0:T(8,128)S(1)} %slice_select_fusion), channel_id=1, source_target_pairs={{0,32},{1,33},{2,34},{3,35},{4,36},{5,37},{6,38},{7,39},{8,40},{9,... | collective-permute-start | bytes 442376 | tf_op jit(solution)/shard_map/ppermute | solution.py:152
  41.3 5.1 %copy-start = (f32[256,1024]{1,0:T(8,128)S(1)}, f32[256,1024]{1,0:T(8,128)}, u32[]{:S(2)}) copy-start(f32[256,1024]{1,0:T(8,128)} %param.2) | copy-start | bytes 3145732
  41.3 45.2 %all-to-all-start = ((f32[8,32,1152]{2,1,0:T(8,128)}), f32[8,32,1152]{2,1,0:T(8,128)S(1)}, u32[]{:S(2)}, u32[]{:S(2)}) async-start(f32[8,32,1152]{2,1,0:T(8,128)} %broadcast_in_dim.7), calls=%async_computation | async-start | bytes 2359296 | tf_op jit(solution)/shard_map/all_to_all | solution.py:166
  46.4 42.2 %collective-permute-start.14 = (f32[256,1024]{1,0:T(8,128)S(1)}, f32[256,1024]{1,0:T(8,128)S(1)}, u32[]{:S(2)}, u32[]{:S(2)}) collective-permute-start(f32[256,1024]{1,0:T(8,128)S(1)} %copy-done), channel_id=1, source_target_pairs={{252,0},{0,4},{4,8},{8,12},{12,16},{16,20},{20,24},{24,28},{28,32}... | collective-permute-start | bytes 3145736 | tf_op jit(solution)/shard_map/ppermute | solution.py:125
  89.7 7.3 %collective-permute-start.15 = (f32[3,256,256]{2,1,0:T(8,128)S(1)}, f32[3,256,256]{2,1,0:T(8,128)S(1)}, u32[]{:S(2)}, u32[]{:S(2)}) collective-permute-start(f32[3,256,256]{2,1,0:T(8,128)S(1)} %pad_maximum_fusion), channel_id=1, source_target_pairs={{0,1},{1,0},{2,3},{3,2},{4,5},{5,4},{6,7},{7,6},{8,9},{9,8},{10,11... | collective-permute-start | bytes 2359304 | tf_op jit(solution)/shard_map/ppermute | solution.py:120
  96.9 1.6 %collective-permute-start.18 = (f32[2,2,64,256]{3,2,0,1:T(8,128)S(1)}, f32[2,2,64,256]{3,2,0,1:T(8,128)S(1)}, u32[]{:S(2)}, u32[]{:S(2)}) collective-permute-start(f32[2,2,64,256]{3,2,0,1:T(8,128)S(1)} %bitcast.59), channel_id=1, source_target_pairs={{0,1},{1,0},{2,3},{3,2},{4,5},{5,4},{6,7},{7,6},{8,9},{9,8},{10,11... | collective-permute-start | bytes 786440 | tf_op jit(solution)/shard_map/ppermute | solution.py:120
  97.2 10.3 %collective-permute-start.16 = (f32[3,128,256]{2,1,0:T(8,128)S(1)}, f32[3,128,256]{2,1,0:T(8,128)S(1)}, u32[]{:S(2)}, u32[]{:S(2)}) collective-permute-start(f32[3,128,256]{2,1,0:T(8,128)S(1)} %dynamic-slice_bitcast_fusion), channel_id=1, source_target_pairs={{0,2},{2,0},{1,3},{3,1},{4,6},{6,4},{5,7},{7,5},{8,10},{10,8},{9,1... | collective-permute-start | bytes 1179656 | tf_op jit(solution)/shard_map/ppermute | solution.py:120
  98.6 11.7 %collective-permute-start.19 = (f32[2,64,256]{2,1,0:T(8,128)S(1)}, f32[2,64,256]{2,1,0:T(8,128)S(1)}, u32[]{:S(2)}, u32[]{:S(2)}) collective-permute-start(f32[2,64,256]{2,1,0:T(8,128)S(1)} %dynamic-slice_bitcast_fusion.1), channel_id=1, source_target_pairs={{0,2},{2,0},{1,3},{3,1},{4,6},{6,4},{5,7},{7,5},{8,10},{10,8},{9,1... | collective-permute-start | bytes 393224 | tf_op jit(solution)/shard_map/ppermute | solution.py:120
  107.5 3.9 %collective-permute-start.17 = (f32[3,128,256]{2,1,0:T(8,128)S(1)}, f32[3,128,256]{2,1,0:T(8,128)S(1)}, u32[]{:S(2)}, u32[]{:S(2)}) collective-permute-start(f32[3,128,256]{2,1,0:T(8,128)S(1)} %fusion.15), channel_id=1, source_target_pairs={{0,1},{1,0},{2,3},{3,2},{4,5},{5,4},{6,7},{7,6},{8,9},{9,8},{10,11... | collective-permute-start | bytes 1179656 | tf_op jit(solution)/shard_map/ppermute | solution.py:120

commit v2 on v1

v2 whole, which is shorter than its diff:
```python
import functools

import jax
import jax.numpy as jnp
from jax import lax
from jax.experimental import pallas as pl
from jax.experimental.pallas import tpu as pltpu
from jax.sharding import Mesh
from jax.sharding import PartitionSpec as P


BLK = ("z", "xh", "y")
PLANE = ("xh", "y")
PAR = ("xl", "core")
ALL = BLK + PAR
HIGHEST = lax.Precision.HIGHEST


ridge_shift = 0.05
CHUNK = 64


def dot(a, b, ca, cb):
    return lax.dot_general(
        a, b, (((ca,), (cb,)), ((), ())), precision=HIGHEST, preferred_element_type=jnp.float32
    )


def outer_tile(left_rows, right_rows):
    return dot(left_rows, right_rows, 1, 1)


def unit(rows, columns):
    return lax.broadcasted_iota(jnp.int32, (rows, columns), 0) == lax.broadcasted_iota(
        jnp.int32, (rows, columns), 1
    )


def triangle_inverse(tile):
    n = tile.shape[0]
    held = jnp.concatenate([tile, unit(n, n).astype(jnp.float32)], axis=1)
    rows = lax.broadcasted_iota(jnp.int32, held.shape, 0)
    for j in range(0, n, 2):
        low = (j // 8) * 8
        part, at = held[low:, :], rows[low:]
        first = jnp.broadcast_to(part[:, j : j + 1], part.shape)
        second = jnp.broadcast_to(part[:, j + 1 : j + 2], part.shape)
        row_a, row_b = held[j : j + 1, :], held[j + 1 : j + 2, :]
        k = j - low
        a, b, c = first[k : k + 1], first[k + 1 : k + 2], second[k + 1 : k + 2]
        over_a = 1.0 / a
        over_det = 1.0 / (a * c - b * b)
        t = b * over_a
        row_b = row_b - t * row_a
        update = first * over_a * row_a + (second - first * t) * (a * over_det) * row_b
        update = jnp.where(at > j + 1, update, 0.0)
        update = jnp.where(at == j + 1, jnp.broadcast_to(t * row_a, part.shape), update)
        part = part - update
        held = jnp.concatenate([held[:low], part], axis=0) if low else part
    pivots = jnp.sum(jnp.where(unit(n, 2 * n), held, 0.0), axis=1, keepdims=True)
    return held[:, n:] * (1.0 / jnp.sqrt(pivots))


def eliminate(tile_ref, inverse_ref, first, last):
    n = tile_ref.shape[0]
    for r0 in range(first * CHUNK, last * CHUNK, CHUNK):
        r1 = r0 + CHUNK
        small = triangle_inverse(tile_ref[r0:r1, r0:r1])
        if r0:
            inverse_ref[r0:r1, :r0] = dot(small, inverse_ref[r0:r1, :r0], 1, 0)
        inverse_ref[r0:r1, r0:r1] = small
        if r1 < n:
            across = dot(small, tile_ref[r0:r1, r1:], 1, 0)
            tile_ref[r1:, r1:] = tile_ref[r1:, r1:] - dot(across, across, 0, 0)
            inverse_ref[r1:, :r1] = inverse_ref[r1:, :r1] - dot(
                across, inverse_ref[r0:r1, :r1], 0, 0
            )


def factor_first_kernel(sum_ref, tile_ref, inverse_ref):
    n = sum_ref.shape[0]
    tile_ref[...] = sum_ref[...] + ridge_shift * unit(n, n).astype(jnp.float32)
    inverse_ref[...] = jnp.zeros((n, n), jnp.float32)
    eliminate(tile_ref, inverse_ref, 0, n // CHUNK // 2)


def factor_second_kernel(at_ref, tile_in_ref, inverse_in_ref, energy_ref, packed_ref, tile_ref, inverse_ref):
    n = tile_ref.shape[0]
    share = n // 4
    tile_ref[...] = tile_in_ref[...]
    inverse_ref[...] = inverse_in_ref[...]
    eliminate(tile_ref, inverse_ref, n // CHUNK // 2, n // CHUNK)
    start = pl.multiple_of(at_ref[0] * share, share)
    packed_ref[:share, :] = inverse_ref[pl.ds(start, share), :]
    packed_ref[share:, :] = outer_tile(jnp.broadcast_to(energy_ref[...], (8, n)), inverse_ref[...])


VMEM = pl.BlockSpec(memory_space=pltpu.VMEM)
SMEM = pl.BlockSpec(memory_space=pltpu.SMEM)


def f32(*shape):
    return jax.ShapeDtypeStruct(shape, jnp.float32)


def cost(flops):
    return pl.CostEstimate(flops=flops, bytes_accessed=2**20, transcendentals=0)


def factor_first(total):
    n = total.shape[0]
    return pl.pallas_call(
        factor_first_kernel,
        out_shape=(f32(n, n), f32(n, n)),
        in_specs=[VMEM],
        out_specs=(VMEM,) * 2,
        name="factor_first",
        cost_estimate=cost(8 * 10**9),
    )(total)


def factor_second(at, tile, inverse, energies):
    n = tile.shape[0]
    return pl.pallas_call(
        factor_second_kernel,
        out_shape=f32(n // 4 + 8, n),
        in_specs=[SMEM] + [VMEM] * 3,
        out_specs=VMEM,
        scratch_shapes=[pltpu.VMEM((n, n), jnp.float32)] * 2,
        name="factor_second",
        cost_estimate=cost(8 * 10**9),
    )(at, tile, inverse, energies)


def cross_kernel(rows_ref, prev_ref, lead_ref, out_ref):
    out_ref[0] = outer_tile(rows_ref[...], lead_ref[...])
    out_ref[1] = outer_tile(prev_ref[...], lead_ref[...])


def cross(rows, prev_rows, lead_rows):
    n = rows.shape[0]
    return pl.pallas_call(
        cross_kernel,
        out_shape=f32(2, n, n),
        in_specs=[VMEM] * 3,
        out_specs=VMEM,
        name="cross",
        cost_estimate=cost(10**9),
    )(rows, prev_rows, lead_rows)


def finish_kernel(
    at_ref, own_ref, other_ref, self_ref, cycle_ref, energy_ref, a0_ref, a1_ref, b0_ref, b1_ref,
    panel_ref, energies_ref, diagonal_ref, neighbour_ref, sums_ref, inverse_ref, prev_ref,
):
    n = inverse_ref.shape[0]
    share, half = n // 4, n // 2
    par, core = at_ref[0], at_ref[2]
    for i, source in ((0, a0_ref), (2, a1_ref), (1, b0_ref), (3, b1_ref)):
        flip = jnp.bitwise_xor(par, i)
        inverse_ref[pl.ds(pl.multiple_of(flip * share, share), share), :] = source[:share, :]
    for i, source in ((0, own_ref), (1, other_ref)):
        start = pl.multiple_of(jnp.bitwise_xor(core, i) * half, half)
        sums_ref[0, pl.ds(start, half), :] = source[0]
        sums_ref[1, pl.ds(start, half), :] = source[1]
    inverse = inverse_ref[...]
    panel = outer_tile(sums_ref[0], inverse)
    panel_ref[...] = panel
    prev_ref[...] = outer_tile(sums_ref[1], inverse)
    start = pl.multiple_of(par * share, share)
    own = panel_ref[pl.ds(start, share), :]
    shifted = (
        lax.broadcasted_iota(jnp.int32, (share, n), 0) + start
        == lax.broadcasted_iota(jnp.int32, (share, n), 1)
    ).astype(jnp.float32)
    diagonal_ref[...] = (
        self_ref[pl.ds(start, share), :] + ridge_shift * shifted - outer_tile(own, panel)
    )
    neighbour_ref[...] = cycle_ref[...] - outer_tile(own, prev_ref[...])
    lead = a0_ref[share:, :]
    remainder = energy_ref[...] - outer_tile(lead, panel)[:1]
    energies_ref[...] = jnp.where(at_ref[1] == 0, lead[:1], remainder)


def finish(at, own, other, self_sum, cycle_rows, energies, parts):
    n = self_sum.shape[-1]
    share = n // 4
    return pl.pallas_call(
        finish_kernel,
        out_shape=(f32(n, n), f32(1, n), f32(share, n), f32(share, n)),
        in_specs=[SMEM] + [VMEM] * 9,
        out_specs=(VMEM,) * 4,
        scratch_shapes=[
            pltpu.VMEM((2, n, n), jnp.float32),
            pltpu.VMEM((n, n), jnp.float32),
            pltpu.VMEM((n, n), jnp.float32),
        ],
        name="finish",
        cost_estimate=cost(10**9),
    )(at, own, other, self_sum, cycle_rows, energies, *parts)


def swapped(value, axis):
    return lax.ppermute(value, axis, [(0, 1), (1, 0)])


def passed_along(block, axis, distance):
    count = lax.axis_size(axis)
    return lax.ppermute(block, axis, [((i - distance) % count, i) for i in range(count)])


def sum_scattered(partials):
    k, n = partials.shape[0], partials.shape[-1]
    quarters = partials.reshape(k, 2, 2, n // 4, n)
    core, xl = lax.axis_index("core"), lax.axis_index("xl")
    pick = lambda a, i, d: lax.dynamic_index_in_dim(a, i, d, keepdims=False)
    halves = pick(quarters, core, 2) + swapped(pick(quarters, 1 - core, 2), "core")
    return pick(halves, xl, 1) + swapped(pick(halves, 1 - xl, 1), "xl")


def sum_halves(partials):
    k, n = partials.shape[0], partials.shape[-1]
    core = lax.axis_index("core")
    chip = partials + swapped(partials, "core")
    halves = chip.reshape(k, 2, n // 2, n)
    own = lax.dynamic_index_in_dim(halves, core, 1, keepdims=False)
    own = own + swapped(own, "xl")
    return own, swapped(own, "core")


def total(values):
    return functools.reduce(jnp.add, values)


def scatter_lead(rows):
    parts = lax.axis_size(PLANE)
    part = rows.shape[0] // parts
    got = [lax.ppermute(rows[k * part : (k + 1) * part], BLK, [(0, k)]) for k in range(1, parts)]
    return jnp.where(lax.axis_index(PLANE) == 0, rows[:part], total(got))


def along_z(piece):
    got = [lax.ppermute(piece, "z", [(0, k)]) for k in range(1, lax.axis_size("z"))]
    return jnp.where(lax.axis_index("z") == 0, piece, total(got))


def over_plane(piece):
    parts = lax.axis_size(PLANE)
    copies = jnp.broadcast_to(piece, (parts, *piece.shape))
    return lax.all_to_all(copies, PLANE, split_axis=0, concat_axis=0, tiled=True)


def small_tree(value):
    z, xh, y = (lax.axis_index(a) for a in BLK)
    rounds = (
        ([[(0, 8 * k)] for k in (4, 2, 6)], z == 0),
        ([[(8 * k, 8 * k + d) for k in range(0, 8, 2)] for d in (4, 12, 8)], (z % 2 == 0) & (xh == 0)),
        ([[(4 * k, 4 * k + d) for k in range(16)] for d in (2, 1, 3)], y == 0),
    )
    for routes, holds in rounds:
        got = [lax.ppermute(value, BLK, route) for route in routes]
        value = jnp.where(holds, value, total(got))
    return value


def on_device(log_derivs, energies):
    n = log_derivs.shape[0]
    energy_row = energies.reshape(1, n)
    at = jnp.stack(
        [lax.axis_index(PAR), lax.axis_index(BLK), lax.axis_index("core")]
    ).astype(jnp.int32)
    piece = scatter_lead(log_derivs)
    prev_rows = passed_along(log_derivs, BLK, 1)
    own, other = sum_halves(outer_tile(log_derivs, log_derivs)[None])
    core = lax.axis_index("core")
    self_sum = jnp.concatenate(
        [jnp.where(core == 0, own[0], other[0]), jnp.where(core == 0, other[0], own[0])]
    )
    piece = along_z(piece)
    tile, inverse = factor_first(self_sum)
    lead_rows = over_plane(piece).reshape(log_derivs.shape)
    packed = factor_second(at, tile, inverse, energy_row)
    packed = small_tree(packed)
    across = swapped(packed, "xl")
    parts = (packed, across, swapped(packed, "core"), swapped(across, "core"))
    cycle_rows = sum_scattered(outer_tile(log_derivs, prev_rows)[None])[0]
    own, other = sum_halves(cross(log_derivs, prev_rows, lead_rows))
    panel, energies_next, diagonal, neighbour = finish(
        at, own, other, self_sum, cycle_rows, energy_row, parts
    )
    return panel, energies_next.reshape(n), diagonal, neighbour


def solution(mesh):
    torus = Mesh(mesh.devices.reshape(8, 2, 4, 2, 2), ALL)
    in_specs = (P(BLK, PAR), P(BLK))
    out_specs = (P(BLK, None), P(BLK), P(ALL, None), P(ALL, None))
    return jax.shard_map(
        on_device, mesh=torus, in_specs=in_specs, out_specs=out_specs, check_vma=False
    )
```

time: 131 us -> 113 us (0.86)
  waiting for transfers between devices: 60.7 us -> 14.5 us
  starting transfers between devices: 38.8 us -> 57.9 us
  Pallas kernels: 18.3 us -> 26.3 us
  local copies, waits for them, and re-layouts: 3.43 us -> 5.78 us
  matrix products: 5.14 us -> 3.28 us
    all_to_all x1, waiting for transfers between devices: 38.6 us -> 0.01 us  [over_plane(): lax.all_to_all(copies, PLANE, split_axis=0, concat_axis=0, tiled=True)]
    pallas_call x0 -> x3, Pallas kernels: none -> 23 us  [the longest x1 9.33 us: factor_first(): pl.pallas_call(factor_first_kernel, out_shape=(f32(n, n), f32(n, n)), in_...]
    pallas_call x1, Pallas kernels: 18.3 us -> 3.28 us  [finish(): pl.pallas_call(finish_kernel, out_shape=(f32(n, n), f32(1, n), f32(share,...]
    ppermute x14 -> x23, starting transfers between devices: 24.2 us -> 39 us  [the longest x7 15.7 us: scatter_lead(): lax.ppermute(rows[k * part:(k + 1) * part], BLK, [(0, k)])]
    ppermute x14 -> x23, waiting for transfers between devices: 12.9 us -> 7.47 us  [the longest x9 3.35 us: small_tree(): got = [lax.ppermute(value, BLK, route) for route in routes]]
    ppermute x5 -> x11, starting transfers between devices: 8.08 us -> 11.3 us  [swapped(): return lax.ppermute(value, axis, [(0, 1), (1, 0)])]
    unnamed x3 -> x22, local copies, waits for them, and re-layouts: 0.81 us -> 3.21 us
    all_to_all x1, starting transfers between devices: 5.11 us -> 7.43 us  [over_plane(): lax.all_to_all(copies, PLANE, split_axis=0, concat_axis=0, tiled=True)]
  transfers between devices with their start and end apart: 21 -> 36, of which waited for: 11 -> 10; matrix products, arithmetic and copies ran while one was open for 5% -> 7% of each run, Pallas kernels for 0% -> 21%
where the time goes in v2:
time: 113 us; the launch traced here: 112 us
  starting transfers between devices  57.9 us (51%)
  Pallas kernels  26.3 us (23%)
  waiting for transfers between devices  14.5 us (13%)
  local copies, waits for them, and re-layouts  5.78 us (5%)
  matrix products  3.28 us (3%)
  other arithmetic  3.25 us (3%)
  between operations  1.17 us (1%)
    ppermute x7, starting transfers between devices, scatter_lead(): lax.ppermute(rows[k * part:(k + 1) * part], BLK, [(0, k)])  15.7 us
    ppermute x9, starting transfers between devices, small_tree(): got = [lax.ppermute(value, BLK, route) for route in routes]  14.3 us
    ppermute x11, starting transfers between devices, swapped(): return lax.ppermute(value, axis, [(0, 1), (1, 0)])  11.3 us
    pallas_call x1, Pallas kernels, factor_first(): pl.pallas_call(factor_first_kernel, out_shape=(f32(n, n), f32(n, n)), in_...  9.33 us
    pallas_call x1, Pallas kernels, factor_second(): pl.pallas_call(factor_second_kernel, out_shape=f32(n // 4 + 8, n), in_spe...  9.08 us
    ppermute x7, starting transfers between devices, along_z(): lax.ppermute(piece, 'z', [(0, k)])  9.07 us
    all_to_all x1, starting transfers between devices, over_plane(): lax.all_to_all(copies, PLANE, split_axis=0, concat_axis=0, tiled=True)  7.43 us
    ppermute x11, waiting for transfers between devices, swapped(): return lax.ppermute(value, axis, [(0, 1), (1, 0)])  7.03 us
  transfers between devices with their start and end apart: 36, of which 10 were waited for; matrix products, arithmetic and copies ran while one was open for 7% of the time, Pallas kernels for 21%

profile of v2, /device:TPU:1, one launch (start us, length us, event | category | flops | bytes accessed | tf_op | source)
XLA Modules:
  0.0 112.2 jit_solution(10439787146689024862)
XLA Ops:
  0.6 1.4 %fusion.1 = (f32[32,1024]{1,0:T(8,128)S(1)}, f32[32,1024]{1,0:T(8,128)S(1)}, f32[32,1024]{1,0:T(8,128)S(1)}, f32[32,1024]{1,0:T(8,128)S(1)}, f32[32,1024]{1,0:T(...) fusion(f32[256,1024]{1,0:T(8,128)} %rows_ref.1), kind=kLoop, calls=%fused_computation.17 | loop fusion | bytes 1835008 | tf_op jit(solution)/shard_map/slice | solution.py:238
  2.0 7.9 %collective-permute-start.7 = (f32[32,1024]{1,0:T(8,128)S(1)}, f32[32,1024]{1,0:T(8,128)S(1)}, u32[]{:S(2)}, u32[]{:S(2)}) collective-permute-start(f32[32,1024]{1,0:T(8,128)S(1)} %get-tuple-element.17), channel_id=1, source_target_pairs={{0,28},{1,29},{2,30},{3,31}} | collective-permute-start | bytes 393224 | tf_op jit(solution)/shard_map/ppermute | solution.py:238
  10.0 1.3 %collective-permute-start.6 = (f32[32,1024]{1,0:T(8,128)S(1)}, f32[32,1024]{1,0:T(8,128)S(1)}, u32[]{:S(2)}, u32[]{:S(2)}) collective-permute-start(f32[32,1024]{1,0:T(8,128)S(1)} %get-tuple-element.18), channel_id=1, source_target_pairs={{0,24},{1,25},{2,26},{3,27}} | collective-permute-start | bytes 393224 | tf_op jit(solution)/shard_map/ppermute | solution.py:238
  11.3 1.3 %collective-permute-start.5 = (f32[32,1024]{1,0:T(8,128)S(1)}, f32[32,1024]{1,0:T(8,128)S(1)}, u32[]{:S(2)}, u32[]{:S(2)}) collective-permute-start(f32[32,1024]{1,0:T(8,128)S(1)} %get-tuple-element.19), channel_id=1, source_target_pairs={{0,20},{1,21},{2,22},{3,23}} | collective-permute-start | bytes 393224 | tf_op jit(solution)/shard_map/ppermute | solution.py:238
  12.6 1.3 %collective-permute-start.4 = (f32[32,1024]{1,0:T(8,128)S(1)}, f32[32,1024]{1,0:T(8,128)S(1)}, u32[]{:S(2)}, u32[]{:S(2)}) collective-permute-start(f32[32,1024]{1,0:T(8,128)S(1)} %get-tuple-element.20), channel_id=1, source_target_pairs={{0,16},{1,17},{2,18},{3,19}} | collective-permute-start | bytes 393224 | tf_op jit(solution)/shard_map/ppermute | solution.py:238
  13.9 1.3 %collective-permute-start.3 = (f32[32,1024]{1,0:T(8,128)S(1)}, f32[32,1024]{1,0:T(8,128)S(1)}, u32[]{:S(2)}, u32[]{:S(2)}) collective-permute-start(f32[32,1024]{1,0:T(8,128)S(1)} %get-tuple-element.21), channel_id=1, source_target_pairs={{0,12},{1,13},{2,14},{3,15}} | collective-permute-start | bytes 393224 | tf_op jit(solution)/shard_map/ppermute | solution.py:238
  15.2 1.3 %collective-permute-start.1 = (f32[32,1024]{1,0:T(8,128)S(1)}, f32[32,1024]{1,0:T(8,128)S(1)}, u32[]{:S(2)}, u32[]{:S(2)}) collective-permute-start(f32[32,1024]{1,0:T(8,128)S(1)} %get-tuple-element.22), channel_id=1, source_target_pairs={{0,4},{1,5},{2,6},{3,7}} | collective-permute-start | bytes 393224 | tf_op jit(solution)/shard_map/ppermute | solution.py:238
  16.5 1.3 %collective-permute-start.2 = (f32[32,1024]{1,0:T(8,128)S(1)}, f32[32,1024]{1,0:T(8,128)S(1)}, u32[]{:S(2)}, u32[]{:S(2)}) collective-permute-start(f32[32,1024]{1,0:T(8,128)S(1)} %get-tuple-element.16), channel_id=1, source_target_pairs={{0,8},{1,9},{2,10},{3,11}} | collective-permute-start | bytes 393224 | tf_op jit(solution)/shard_map/ppermute | solution.py:238
  17.8 1.0 convolution_bitcast_fusion
  18.9 1.5 %collective-permute-start.18 = (f32[1,256,256]{2,1,0:T(8,128)S(1)}, f32[1,256,256]{2,1,0:T(8,128)S(1)}, u32[]{:S(2)}, u32[]{:S(2)}) collective-permute-start(f32[1,256,256]{2,1,0:T(8,128)S(1)} %convolution_bitcast_fusion), channel_id=1, source_target_pairs={{0,1},{1,0},{2,3},{3,2},{4,5},{5,4},{6,7},{7,6},{8,9},{9,8},{10,11... | collective-permute-start | bytes 786440 | tf_op jit(solution)/shard_map/ppermute | solution.py:204
  20.4 0.1 collective-permute-done.4
  20.6 0.9 collective-permute-done.2
  21.5 1.3 %collective-permute-start.14 = (f32[32,1024]{1,0:T(8,128)S(1)}, f32[32,1024]{1,0:T(8,128)S(1)}, u32[]{:S(2)}, u32[]{:S(2)}) collective-permute-start(f32[32,1024]{1,0:T(8,128)S(1)} %add_select_fusion.1), channel_id=1, source_target_pairs={{0,224},{1,225},{2,226},{3,227},{4,228},{5,229},{6,230},{7,231},{8... | collective-permute-start | bytes 393224 | tf_op jit(solution)/shard_map/ppermute | solution.py:243
  22.8 1.3 %collective-permute-start.13 = (f32[32,1024]{1,0:T(8,128)S(1)}, f32[32,1024]{1,0:T(8,128)S(1)}, u32[]{:S(2)}, u32[]{:S(2)}) collective-permute-start(f32[32,1024]{1,0:T(8,128)S(1)} %add_select_fusion.1), channel_id=1, source_target_pairs={{0,192},{1,193},{2,194},{3,195},{4,196},{5,197},{6,198},{7,199},{8... | collective-permute-start | bytes 393224 | tf_op jit(solution)/shard_map/ppermute | solution.py:243
  24.2 0.4 collective-permute-start.19
  24.6 0.7 pad_add_fusion.at_ref
  25.3 1.3 %collective-permute-start.12 = (f32[32,1024]{1,0:T(8,128)S(1)}, f32[32,1024]{1,0:T(8,128)S(1)}, u32[]{:S(2)}, u32[]{:S(2)}) collective-permute-start(f32[32,1024]{1,0:T(8,128)S(1)} %add_select_fusion.1), channel_id=1, source_target_pairs={{0,160},{1,161},{2,162},{3,163},{4,164},{5,165},{6,166},{7,167},{8... | collective-permute-start | bytes 393224 | tf_op jit(solution)/shard_map/ppermute | solution.py:243
  26.6 1.3 %collective-permute-start.11 = (f32[32,1024]{1,0:T(8,128)S(1)}, f32[32,1024]{1,0:T(8,128)S(1)}, u32[]{:S(2)}, u32[]{:S(2)}) collective-permute-start(f32[32,1024]{1,0:T(8,128)S(1)} %add_select_fusion.1), channel_id=1, source_target_pairs={{0,128},{1,129},{2,130},{3,131},{4,132},{5,133},{6,134},{7,135},{8... | collective-permute-start | bytes 393224 | tf_op jit(solution)/shard_map/ppermute | solution.py:243
  27.9 1.3 %collective-permute-start.10 = (f32[32,1024]{1,0:T(8,128)S(1)}, f32[32,1024]{1,0:T(8,128)S(1)}, u32[]{:S(2)}, u32[]{:S(2)}) collective-permute-start(f32[32,1024]{1,0:T(8,128)S(1)} %add_select_fusion.1), channel_id=1, source_target_pairs={{0,96},{1,97},{2,98},{3,99},{4,100},{5,101},{6,102},{7,103},{8,104... | collective-permute-start | bytes 393224 | tf_op jit(solution)/shard_map/ppermute | solution.py:243
  29.2 1.3 %collective-permute-start.8 = (f32[32,1024]{1,0:T(8,128)S(1)}, f32[32,1024]{1,0:T(8,128)S(1)}, u32[]{:S(2)}, u32[]{:S(2)}) collective-permute-start(f32[32,1024]{1,0:T(8,128)S(1)} %add_select_fusion.1), channel_id=1, source_target_pairs={{0,32},{1,33},{2,34},{3,35},{4,36},{5,37},{6,38},{7,39},{8,40},{9,... | collective-permute-start | bytes 393224 | tf_op jit(solution)/shard_map/ppermute | solution.py:243
  30.5 1.3 %collective-permute-start.9 = (f32[32,1024]{1,0:T(8,128)S(1)}, f32[32,1024]{1,0:T(8,128)S(1)}, u32[]{:S(2)}, u32[]{:S(2)}) collective-permute-start(f32[32,1024]{1,0:T(8,128)S(1)} %add_select_fusion.1), channel_id=1, source_target_pairs={{0,64},{1,65},{2,66},{3,67},{4,68},{5,69},{6,70},{7,71},{8,72},{9,... | collective-permute-start | bytes 393224 | tf_op jit(solution)/shard_map/ppermute | solution.py:243
  31.8 0.1 collective-permute-start
  31.9 2.6 %collective-permute-start.20 = (f32[1,128,256]{2,1,0:T(8,128)S(1)}, f32[1,128,256]{2,1,0:T(8,128)S(1)}, u32[]{:S(2)}, u32[]{:S(2)}) collective-permute-start(f32[1,128,256]{2,1,0:T(8,128)S(1)} %fusion.7), channel_id=1, source_target_pairs={{0,1},{1,0},{2,3},{3,2},{4,5},{5,4},{6,7},{7,6},{8,9},{9,8},{10,11... | collective-permute-start | bytes 393224 | tf_op jit(solution)/shard_map/ppermute | solution.py:204
  34.5 0.2 collective-permute-done.8
  34.8 2.8 %collective-permute-done.9 = f32[32,1024]{1,0:T(8,128)S(1)} collective-permute-done((f32[32,1024]{1,0:T(8,128)S(1)}, f32[32,1024]{1,0:T(8,128)S(1)}, u32[]{:S(2)}, u32[]{:S(2)}) %collective-permute-start.9) | collective-permute-done | bytes 131104 | tf_op jit(solution)/shard_map/ppermute | solution.py:243
  37.6 1.1 broadcast_in_dim.6
  38.8 7.4 %all-to-all-start = ((f32[8,32,1024]{2,1,0:T(8,128)}), f32[8,32,1024]{2,1,0:T(8,128)S(1)}, u32[]{:S(2)}, u32[]{:S(2)}) async-start(f32[8,32,1024]{2,1,0:T(8,128)} %broadcast_in_dim.6), calls=%async_computation | async-start | bytes 2097152 | tf_op jit(solution)/shard_map/all_to_all | solution.py:250
  46.2 0.7 pad_maximum_fusion.sum_ref.self_ref
  46.9 9.3 %factor_first.1 = (f32[256,256]{1,0:T(8,128)}, f32[256,256]{1,0:T(8,128)}) custom-call(f32[256,256]{1,0:T(8,128)} %pad_maximum_fusion.sum_ref.self_ref), custom_call_target="tpu_custom_call" | custom-call | flops 8000000000 | bytes 1048576 | tf_op jit(solution)/shard_map/factor_first/pallas_call | solution.py:112
  56.3 9.1 %factor_second.1 = f32[72,256]{1,0:T(8,128)} custom-call(s32[3]{0:T(128)} %pad_add_fusion.at_ref, f32[256,256]{1,0:T(8,128)} %get-tuple-element.10.tile_in_ref, f32[256,256]{1,0:T(8,128)} %get-tuple-element.11.inverse_in_ref, f32[1,256]{1,0:T(1,128)} %bitcast.48), custom_call_target="tpu_custom_call" | custom-call | flops 8000000000 | bytes 1048576 | tf_op jit(solution)/shard_map/factor_second/pallas_call | solution.py:124
  65.4 1.3 %collective-permute-start.25 = (f32[72,256]{1,0:T(8,128)}, f32[72,256]{1,0:T(8,128)S(1)}, u32[]{:S(2)}, u32[]{:S(2)}) collective-permute-start(f32[72,256]{1,0:T(8,128)} %factor_second.1), channel_id=1, source_target_pairs={{0,192},{1,193},{2,194},{3,195}} | collective-permute-start | bytes 221192 | tf_op jit(solution)/shard_map/ppermute | solution.py:261
  66.6 1.3 %collective-permute-start.23 = (f32[72,256]{1,0:T(8,128)}, f32[72,256]{1,0:T(8,128)S(1)}, u32[]{:S(2)}, u32[]{:S(2)}) collective-permute-start(f32[72,256]{1,0:T(8,128)} %factor_second.1), channel_id=1, source_target_pairs={{0,128},{1,129},{2,130},{3,131}} | collective-permute-start | bytes 221192 | tf_op jit(solution)/shard_map/ppermute | solution.py:261
  67.9 3.8 %collective-permute-start.24 = (f32[72,256]{1,0:T(8,128)}, f32[72,256]{1,0:T(8,128)S(1)}, u32[]{:S(2)}, u32[]{:S(2)}) collective-permute-start(f32[72,256]{1,0:T(8,128)} %factor_second.1), channel_id=1, source_target_pairs={{0,64},{1,65},{2,66},{3,67}} | collective-permute-start | bytes 221192 | tf_op jit(solution)/shard_map/ppermute | solution.py:261
  71.7 1.7 %collective-permute-done.24 = f32[72,256]{1,0:T(8,128)S(1)} collective-permute-done((f32[72,256]{1,0:T(8,128)}, f32[72,256]{1,0:T(8,128)S(1)}, u32[]{:S(2)}, u32[]{:S(2)}) %collective-permute-start.24) | collective-permute-done | bytes 73760 | tf_op jit(solution)/shard_map/ppermute | solution.py:261
  73.4 0.9 add_select_fusion.4
  74.3 1.3 %collective-permute-start.28 = (f32[72,256]{1,0:T(8,128)S(1)}, f32[72,256]{1,0:T(8,128)S(1)}, u32[]{:S(2)}, u32[]{:S(2)}) collective-permute-start(f32[72,256]{1,0:T(8,128)S(1)} %add_select_fusion.4), channel_id=1, source_target_pairs={{0,32},{64,96},{128,160},{192,224},{1,33},{65,97},{129,161},{193,2... | collective-permute-start | bytes 221192 | tf_op jit(solution)/shard_map/ppermute | solution.py:261
  75.6 1.3 %collective-permute-start.26 = (f32[72,256]{1,0:T(8,128)S(1)}, f32[72,256]{1,0:T(8,128)S(1)}, u32[]{:S(2)}, u32[]{:S(2)}) collective-permute-start(f32[72,256]{1,0:T(8,128)S(1)} %add_select_fusion.4), channel_id=1, source_target_pairs={{0,16},{64,80},{128,144},{192,208},{1,17},{65,81},{129,145},{193,2... | collective-permute-start | bytes 221192 | tf_op jit(solution)/shard_map/ppermute | solution.py:261
  76.9 1.3 %collective-permute-start.27 = (f32[72,256]{1,0:T(8,128)S(1)}, f32[72,256]{1,0:T(8,128)S(1)}, u32[]{:S(2)}, u32[]{:S(2)}) collective-permute-start(f32[72,256]{1,0:T(8,128)S(1)} %add_select_fusion.4), channel_id=1, source_target_pairs={{0,48},{64,112},{128,176},{192,240},{1,49},{65,113},{129,177},{193... | collective-permute-start | bytes 221192 | tf_op jit(solution)/shard_map/ppermute | solution.py:261
  78.3 1.6 %collective-permute-done.27 = f32[72,256]{1,0:T(8,128)S(1)} collective-permute-done((f32[72,256]{1,0:T(8,128)S(1)}, f32[72,256]{1,0:T(8,128)S(1)}, u32[]{:S(2)}, u32[]{:S(2)}) %collective-permute-start.27) | collective-permute-done | bytes 73760 | tf_op jit(solution)/shard_map/ppermute | solution.py:261
  79.9 1.3 %collective-permute-start.31 = (f32[72,256]{1,0:T(8,128)S(1)}, f32[72,256]{1,0:T(8,128)S(1)}, u32[]{:S(2)}, u32[]{:S(2)}) collective-permute-start(f32[72,256]{1,0:T(8,128)S(1)} %add_select_fusion.3), channel_id=1, source_target_pairs={{0,12},{16,28},{32,44},{48,60},{64,76},{80,92},{96,108},{112,124},... | collective-permute-start | bytes 221192 | tf_op jit(solution)/shard_map/ppermute | solution.py:261
  81.2 1.3 %collective-permute-start.29 = (f32[72,256]{1,0:T(8,128)S(1)}, f32[72,256]{1,0:T(8,128)S(1)}, u32[]{:S(2)}, u32[]{:S(2)}) collective-permute-start(f32[72,256]{1,0:T(8,128)S(1)} %add_select_fusion.3), channel_id=1, source_target_pairs={{0,8},{16,24},{32,40},{48,56},{64,72},{80,88},{96,104},{112,120},{... | collective-permute-start | bytes 221192 | tf_op jit(solution)/shard_map/ppermute | solution.py:261
  82.5 1.5 %collective-permute-start.30 = (f32[72,256]{1,0:T(8,128)S(1)}, f32[72,256]{1,0:T(8,128)S(1)}, u32[]{:S(2)}, u32[]{:S(2)}) collective-permute-start(f32[72,256]{1,0:T(8,128)S(1)} %add_select_fusion.3), channel_id=1, source_target_pairs={{0,4},{16,20},{32,36},{48,52},{64,68},{80,84},{96,100},{112,116},{... | collective-permute-start | bytes 221192 | tf_op jit(solution)/shard_map/ppermute | solution.py:261
  84.1 1.0 copy-done.2
  85.0 0.3 copy-done.3
  85.4 4.6 %cross.1 = f32[2,256,256]{2,1,0:T(8,128)} custom-call(f32[256,1024]{1,0:T(8,128)} %rows_ref.1, f32[256,1024]{1,0:T(8,128)} %copy-done.2, f32[256,1024]{1,0:T(8,128)} %bitcast.47), custom_call_target="tpu_custom_call" | custom-call | flops 1000000000 | bytes 1048576 | tf_op jit(solution)/shard_map/cross/pallas_call | solution.py:142
  90.0 2.3 %collective-permute-start.15 = (f32[2,256,256]{2,1,0:T(8,128)}, f32[2,256,256]{2,1,0:T(8,128)S(1)}, u32[]{:S(2)}, u32[]{:S(2)}) collective-permute-start(f32[2,256,256]{2,1,0:T(8,128)} %cross.1), channel_id=1, source_target_pairs={{0,1},{1,0},{2,3},{3,2},{4,5},{5,4},{6,7},{7,6},{8,9},{9,8},{10,11... | collective-permute-start | bytes 1572872 | tf_op jit(solution)/shard_map/ppermute | solution.py:204
  92.3 2.3 %fusion.2 = f32[256,256]{1,0:T(8,128)S(1)} fusion(f32[256,1024]{1,0:T(8,128)S(1)} %copy-done.1, f32[256,1024]{1,0:T(8,128)} %copy-done.2), kind=kOutput, calls=%fused_computation.18 | convolution fusion | flops 805306368 | bytes 2359296 | tf_op jit(solution)/shard_map/dot_general | solution.py:24
  94.6 0.1 collective-permute-start.21
  94.8 0.3 collective-permute-start.32
  95.0 0.6 copy-done.4
  95.6 0.1 add.121
  95.7 0.8 collective-permute-start.16
  96.6 0.8 collective-permute-start.22
  97.4 6.7 %collective-permute-done.16 = f32[2,128,256]{2,1,0:T(8,128)S(1)} collective-permute-done((f32[2,128,256]{2,1,0:T(8,128)S(1)}, f32[2,128,256]{2,1,0:T(8,128)S(1)}, u32[]{:S(2)}, u32[]{:S(2)}) %collective-permute-start.16) | collective-permute-done | bytes 262176 | tf_op jit(solution)/shard_map/ppermute | solution.py:204
  104.2 2.0 %collective-permute-start.17 = (f32[2,128,256]{2,1,0:T(8,128)S(1)}, f32[2,128,256]{2,1,0:T(8,128)S(1)}, u32[]{:S(2)}, u32[]{:S(2)}) collective-permute-start(f32[2,128,256]{2,1,0:T(8,128)S(1)} %fusion.8.own_ref), channel_id=1, source_target_pairs={{0,1},{1,0},{2,3},{3,2},{4,5},{5,4},{6,7},{7,6},{8,9},{9,8},{10,11... | collective-permute-start | bytes 786440 | tf_op jit(solution)/shard_map/ppermute | solution.py:204
  106.1 0.1 collective-permute-start.33
  106.3 0.4 collective-permute-start.34
  106.7 0.6 fusion.cycle_ref
  107.3 0.1 collective-permute-done.33.b0_ref
  107.4 0.2 collective-permute-done.34.b1_ref
  107.6 0.5 copy-done.9
  108.0 0.2 copy-done.10
  108.2 0.7 copy-done.7
  108.9 3.3 %finish.1 = (f32[256,256]{1,0:T(8,128)}, f32[1,256]{1,0:T(1,128)}, f32[64,256]{1,0:T(8,128)}, f32[64,256]{1,0:T(8,128)}) custom-call(s32[3]{0:T(128)} %pad_add_fusion.at_ref, f32[2,128,256]{2,1,0:T(8,128)} %copy-done.5, f32[2,128,256]{2,1,0:T(8,128)} %copy-done.7, f32[256,256]{1,0:T(8,128)} %pad_maximum_fusion.sum_ref.self_ref, f32[64,256]{1,0:T(8,128)} %fusion.cycle_ref, ...), custom_call_target="tpu_custom_call" | custom-call | flops 1000000000 | bytes 1048576 | tf_op jit(solution)/shard_map/finish/pallas_call | solution.py:188
  (56 shorter events, 0.5 us)
Async XLA Ops:
  0.6 17.2 %copy-start = (f32[256,1024]{1,0:T(8,128)S(1)}, f32[256,1024]{1,0:T(8,128)}, u32[]{:S(2)}) copy-start(f32[256,1024]{1,0:T(8,128)} %rows_ref.1) | copy-start | bytes 3145732
  2.0 13.2 %collective-permute-start.7 = (f32[32,1024]{1,0:T(8,128)S(1)}, f32[32,1024]{1,0:T(8,128)S(1)}, u32[]{:S(2)}, u32[]{:S(2)}) collective-permute-start(f32[32,1024]{1,0:T(8,128)S(1)} %get-tuple-element.17), channel_id=1, source_target_pairs={{0,28},{1,29},{2,30},{3,31}} | collective-permute-start | bytes 393224 | tf_op jit(solution)/shard_map/ppermute | solution.py:238
  10.0 6.5 %collective-permute-start.6 = (f32[32,1024]{1,0:T(8,128)S(1)}, f32[32,1024]{1,0:T(8,128)S(1)}, u32[]{:S(2)}, u32[]{:S(2)}) collective-permute-start(f32[32,1024]{1,0:T(8,128)S(1)} %get-tuple-element.18), channel_id=1, source_target_pairs={{0,24},{1,25},{2,26},{3,27}} | collective-permute-start | bytes 393224 | tf_op jit(solution)/shard_map/ppermute | solution.py:238
  11.3 7.6 %collective-permute-start.5 = (f32[32,1024]{1,0:T(8,128)S(1)}, f32[32,1024]{1,0:T(8,128)S(1)}, u32[]{:S(2)}, u32[]{:S(2)}) collective-permute-start(f32[32,1024]{1,0:T(8,128)S(1)} %get-tuple-element.19), channel_id=1, source_target_pairs={{0,20},{1,21},{2,22},{3,23}} | collective-permute-start | bytes 393224 | tf_op jit(solution)/shard_map/ppermute | solution.py:238
  12.6 8.0 %collective-permute-start.4 = (f32[32,1024]{1,0:T(8,128)S(1)}, f32[32,1024]{1,0:T(8,128)S(1)}, u32[]{:S(2)}, u32[]{:S(2)}) collective-permute-start(f32[32,1024]{1,0:T(8,128)S(1)} %get-tuple-element.20), channel_id=1, source_target_pairs={{0,16},{1,17},{2,18},{3,19}} | collective-permute-start | bytes 393224 | tf_op jit(solution)/shard_map/ppermute | solution.py:238
  13.9 6.7 %collective-permute-start.3 = (f32[32,1024]{1,0:T(8,128)S(1)}, f32[32,1024]{1,0:T(8,128)S(1)}, u32[]{:S(2)}, u32[]{:S(2)}) collective-permute-start(f32[32,1024]{1,0:T(8,128)S(1)} %get-tuple-element.21), channel_id=1, source_target_pairs={{0,12},{1,13},{2,14},{3,15}} | collective-permute-start | bytes 393224 | tf_op jit(solution)/shard_map/ppermute | solution.py:238
  15.2 5.4 %collective-permute-start.1 = (f32[32,1024]{1,0:T(8,128)S(1)}, f32[32,1024]{1,0:T(8,128)S(1)}, u32[]{:S(2)}, u32[]{:S(2)}) collective-permute-start(f32[32,1024]{1,0:T(8,128)S(1)} %get-tuple-element.22), channel_id=1, source_target_pairs={{0,4},{1,5},{2,6},{3,7}} | collective-permute-start | bytes 393224 | tf_op jit(solution)/shard_map/ppermute | solution.py:238
  16.5 5.0 %collective-permute-start.2 = (f32[32,1024]{1,0:T(8,128)S(1)}, f32[32,1024]{1,0:T(8,128)S(1)}, u32[]{:S(2)}, u32[]{:S(2)}) collective-permute-start(f32[32,1024]{1,0:T(8,128)S(1)} %get-tuple-element.16), channel_id=1, source_target_pairs={{0,8},{1,9},{2,10},{3,11}} | collective-permute-start | bytes 393224 | tf_op jit(solution)/shard_map/ppermute | solution.py:238
  18.9 5.3 %collective-permute-start.18 = (f32[1,256,256]{2,1,0:T(8,128)S(1)}, f32[1,256,256]{2,1,0:T(8,128)S(1)}, u32[]{:S(2)}, u32[]{:S(2)}) collective-permute-start(f32[1,256,256]{2,1,0:T(8,128)S(1)} %convolution_bitcast_fusion), channel_id=1, source_target_pairs={{0,1},{1,0},{2,3},{3,2},{4,5},{5,4},{6,7},{7,6},{8,9},{9,8},{10,11... | collective-permute-start | bytes 786440 | tf_op jit(solution)/shard_map/ppermute | solution.py:204
  21.5 6.3 %collective-permute-start.14 = (f32[32,1024]{1,0:T(8,128)S(1)}, f32[32,1024]{1,0:T(8,128)S(1)}, u32[]{:S(2)}, u32[]{:S(2)}) collective-permute-start(f32[32,1024]{1,0:T(8,128)S(1)} %add_select_fusion.1), channel_id=1, source_target_pairs={{0,224},{1,225},{2,226},{3,227},{4,228},{5,229},{6,230},{7,231},{8... | collective-permute-start | bytes 393224 | tf_op jit(solution)/shard_map/ppermute | solution.py:243
  22.8 6.4 %collective-permute-start.13 = (f32[32,1024]{1,0:T(8,128)S(1)}, f32[32,1024]{1,0:T(8,128)S(1)}, u32[]{:S(2)}, u32[]{:S(2)}) collective-permute-start(f32[32,1024]{1,0:T(8,128)S(1)} %add_select_fusion.1), channel_id=1, source_target_pairs={{0,192},{1,193},{2,194},{3,195},{4,196},{5,197},{6,198},{7,199},{8... | collective-permute-start | bytes 393224 | tf_op jit(solution)/shard_map/ppermute | solution.py:243
  24.2 6.3 %collective-permute-start.19 = (f32[1,128,256]{2,1,0:T(8,128)S(1)}, f32[1,128,256]{2,1,0:T(8,128)S(1)}, u32[]{:S(2)}, u32[]{:S(2)}) collective-permute-start(f32[1,128,256]{2,1,0:T(8,128)S(1)} %dynamic-slice_bitcast_fusion.2), channel_id=1, source_target_pairs={{0,2},{2,0},{1,3},{3,1},{4,6},{6,4},{5,7},{7,5},{8,10},{10,8},{9,1... | collective-permute-start | bytes 393224 | tf_op jit(solution)/shard_map/ppermute | solution.py:204
  25.3 6.6 %collective-permute-start.12 = (f32[32,1024]{1,0:T(8,128)S(1)}, f32[32,1024]{1,0:T(8,128)S(1)}, u32[]{:S(2)}, u32[]{:S(2)}) collective-permute-start(f32[32,1024]{1,0:T(8,128)S(1)} %add_select_fusion.1), channel_id=1, source_target_pairs={{0,160},{1,161},{2,162},{3,163},{4,164},{5,165},{6,166},{7,167},{8... | collective-permute-start | bytes 393224 | tf_op jit(solution)/shard_map/ppermute | solution.py:243
  26.6 5.4 %collective-permute-start.11 = (f32[32,1024]{1,0:T(8,128)S(1)}, f32[32,1024]{1,0:T(8,128)S(1)}, u32[]{:S(2)}, u32[]{:S(2)}) collective-permute-start(f32[32,1024]{1,0:T(8,128)S(1)} %add_select_fusion.1), channel_id=1, source_target_pairs={{0,128},{1,129},{2,130},{3,131},{4,132},{5,133},{6,134},{7,135},{8... | collective-permute-start | bytes 393224 | tf_op jit(solution)/shard_map/ppermute | solution.py:243
  27.9 6.7 %collective-permute-start.10 = (f32[32,1024]{1,0:T(8,128)S(1)}, f32[32,1024]{1,0:T(8,128)S(1)}, u32[]{:S(2)}, u32[]{:S(2)}) collective-permute-start(f32[32,1024]{1,0:T(8,128)S(1)} %add_select_fusion.1), channel_id=1, source_target_pairs={{0,96},{1,97},{2,98},{3,99},{4,100},{5,101},{6,102},{7,103},{8,104... | collective-permute-start | bytes 393224 | tf_op jit(solution)/shard_map/ppermute | solution.py:243
  29.2 5.6 %collective-permute-start.8 = (f32[32,1024]{1,0:T(8,128)S(1)}, f32[32,1024]{1,0:T(8,128)S(1)}, u32[]{:S(2)}, u32[]{:S(2)}) collective-permute-start(f32[32,1024]{1,0:T(8,128)S(1)} %add_select_fusion.1), channel_id=1, source_target_pairs={{0,32},{1,33},{2,34},{3,35},{4,36},{5,37},{6,38},{7,39},{8,40},{9,... | collective-permute-start | bytes 393224 | tf_op jit(solution)/shard_map/ppermute | solution.py:243
  30.5 7.1 %collective-permute-start.9 = (f32[32,1024]{1,0:T(8,128)S(1)}, f32[32,1024]{1,0:T(8,128)S(1)}, u32[]{:S(2)}, u32[]{:S(2)}) collective-permute-start(f32[32,1024]{1,0:T(8,128)S(1)} %add_select_fusion.1), channel_id=1, source_target_pairs={{0,64},{1,65},{2,66},{3,67},{4,68},{5,69},{6,70},{7,71},{8,72},{9,... | collective-permute-start | bytes 393224 | tf_op jit(solution)/shard_map/ppermute | solution.py:243
  31.8 52.2 %collective-permute-start = (f32[256,1024]{1,0:T(8,128)S(1)}, f32[256,1024]{1,0:T(8,128)S(1)}, u32[]{:S(2)}, u32[]{:S(2)}) collective-permute-start(f32[256,1024]{1,0:T(8,128)S(1)} %copy-done), channel_id=1, source_target_pairs={{252,0},{0,4},{4,8},{8,12},{12,16},{16,20},{20,24},{24,28},{28,32}... | collective-permute-start | bytes 3145736 | tf_op jit(solution)/shard_map/ppermute | solution.py:209
  31.9 14.2 %collective-permute-start.20 = (f32[1,128,256]{2,1,0:T(8,128)S(1)}, f32[1,128,256]{2,1,0:T(8,128)S(1)}, u32[]{:S(2)}, u32[]{:S(2)}) collective-permute-start(f32[1,128,256]{2,1,0:T(8,128)S(1)} %fusion.7), channel_id=1, source_target_pairs={{0,1},{1,0},{2,3},{3,2},{4,5},{5,4},{6,7},{7,6},{8,9},{9,8},{10,11... | collective-permute-start | bytes 393224 | tf_op jit(solution)/shard_map/ppermute | solution.py:204
  38.8 45.3 %all-to-all-start = ((f32[8,32,1024]{2,1,0:T(8,128)}), f32[8,32,1024]{2,1,0:T(8,128)S(1)}, u32[]{:S(2)}, u32[]{:S(2)}) async-start(f32[8,32,1024]{2,1,0:T(8,128)} %broadcast_in_dim.6), calls=%async_computation | async-start | bytes 2097152 | tf_op jit(solution)/shard_map/all_to_all | solution.py:250
  65.4 6.4 %collective-permute-start.25 = (f32[72,256]{1,0:T(8,128)}, f32[72,256]{1,0:T(8,128)S(1)}, u32[]{:S(2)}, u32[]{:S(2)}) collective-permute-start(f32[72,256]{1,0:T(8,128)} %factor_second.1), channel_id=1, source_target_pairs={{0,192},{1,193},{2,194},{3,195}} | collective-permute-start | bytes 221192 | tf_op jit(solution)/shard_map/ppermute | solution.py:261
  66.6 5.1 %collective-permute-start.23 = (f32[72,256]{1,0:T(8,128)}, f32[72,256]{1,0:T(8,128)S(1)}, u32[]{:S(2)}, u32[]{:S(2)}) collective-permute-start(f32[72,256]{1,0:T(8,128)} %factor_second.1), channel_id=1, source_target_pairs={{0,128},{1,129},{2,130},{3,131}} | collective-permute-start | bytes 221192 | tf_op jit(solution)/shard_map/ppermute | solution.py:261
  67.9 5.5 %collective-permute-start.24 = (f32[72,256]{1,0:T(8,128)}, f32[72,256]{1,0:T(8,128)S(1)}, u32[]{:S(2)}, u32[]{:S(2)}) collective-permute-start(f32[72,256]{1,0:T(8,128)} %factor_second.1), channel_id=1, source_target_pairs={{0,64},{1,65},{2,66},{3,67}} | collective-permute-start | bytes 221192 | tf_op jit(solution)/shard_map/ppermute | solution.py:261
  74.3 3.9 %collective-permute-start.28 = (f32[72,256]{1,0:T(8,128)S(1)}, f32[72,256]{1,0:T(8,128)S(1)}, u32[]{:S(2)}, u32[]{:S(2)}) collective-permute-start(f32[72,256]{1,0:T(8,128)S(1)} %add_select_fusion.4), channel_id=1, source_target_pairs={{0,32},{64,96},{128,160},{192,224},{1,33},{65,97},{129,161},{193,2... | collective-permute-start | bytes 221192 | tf_op jit(solution)/shard_map/ppermute | solution.py:261
  75.6 2.7 %collective-permute-start.26 = (f32[72,256]{1,0:T(8,128)S(1)}, f32[72,256]{1,0:T(8,128)S(1)}, u32[]{:S(2)}, u32[]{:S(2)}) collective-permute-start(f32[72,256]{1,0:T(8,128)S(1)} %add_select_fusion.4), channel_id=1, source_target_pairs={{0,16},{64,80},{128,144},{192,208},{1,17},{65,81},{129,145},{193,2... | collective-permute-start | bytes 221192 | tf_op jit(solution)/shard_map/ppermute | solution.py:261
  76.9 3.0 %collective-permute-start.27 = (f32[72,256]{1,0:T(8,128)S(1)}, f32[72,256]{1,0:T(8,128)S(1)}, u32[]{:S(2)}, u32[]{:S(2)}) collective-permute-start(f32[72,256]{1,0:T(8,128)S(1)} %add_select_fusion.4), channel_id=1, source_target_pairs={{0,48},{64,112},{128,176},{192,240},{1,49},{65,113},{129,177},{193... | collective-permute-start | bytes 221192 | tf_op jit(solution)/shard_map/ppermute | solution.py:261
  79.9 14.8 %collective-permute-start.31 = (f32[72,256]{1,0:T(8,128)S(1)}, f32[72,256]{1,0:T(8,128)S(1)}, u32[]{:S(2)}, u32[]{:S(2)}) collective-permute-start(f32[72,256]{1,0:T(8,128)S(1)} %add_select_fusion.3), channel_id=1, source_target_pairs={{0,12},{16,28},{32,44},{48,60},{64,76},{80,92},{96,108},{112,124},... | collective-permute-start | bytes 221192 | tf_op jit(solution)/shard_map/ppermute | solution.py:261
  81.2 13.5 %collective-permute-start.29 = (f32[72,256]{1,0:T(8,128)S(1)}, f32[72,256]{1,0:T(8,128)S(1)}, u32[]{:S(2)}, u32[]{:S(2)}) collective-permute-start(f32[72,256]{1,0:T(8,128)S(1)} %add_select_fusion.3), channel_id=1, source_target_pairs={{0,8},{16,24},{32,40},{48,56},{64,72},{80,88},{96,104},{112,120},{... | collective-permute-start | bytes 221192 | tf_op jit(solution)/shard_map/ppermute | solution.py:261
  82.5 12.2 %collective-permute-start.30 = (f32[72,256]{1,0:T(8,128)S(1)}, f32[72,256]{1,0:T(8,128)S(1)}, u32[]{:S(2)}, u32[]{:S(2)}) collective-permute-start(f32[72,256]{1,0:T(8,128)S(1)} %add_select_fusion.3), channel_id=1, source_target_pairs={{0,4},{16,20},{32,36},{48,52},{64,68},{80,84},{96,100},{112,116},{... | collective-permute-start | bytes 221192 | tf_op jit(solution)/shard_map/ppermute | solution.py:261
  84.0 1.0 copy-start.2
  84.0 1.3 %copy-start.3 = (f32[8,32,1024]{2,1,0:T(8,128)}, f32[8,32,1024]{2,1,0:T(8,128)S(1)}, u32[]{:S(2)}) copy-start(f32[8,32,1024]{2,1,0:T(8,128)S(1)} %all-to-all-done) | copy-start | bytes 3145732
  85.4 6.9 %copy-start.1 = (f32[256,1024]{1,0:T(8,128)S(1)}, f32[256,1024]{1,0:T(8,128)}, u32[]{:S(2)}) copy-start(f32[256,1024]{1,0:T(8,128)} %rows_ref.1) | copy-start | bytes 3145732
  90.0 5.1 %collective-permute-start.15 = (f32[2,256,256]{2,1,0:T(8,128)}, f32[2,256,256]{2,1,0:T(8,128)S(1)}, u32[]{:S(2)}, u32[]{:S(2)}) collective-permute-start(f32[2,256,256]{2,1,0:T(8,128)} %cross.1), channel_id=1, source_target_pairs={{0,1},{1,0},{2,3},{3,2},{4,5},{5,4},{6,7},{7,6},{8,9},{9,8},{10,11... | collective-permute-start | bytes 1572872 | tf_op jit(solution)/shard_map/ppermute | solution.py:204
  94.6 1.0 copy-start.4
  94.6 1.9 %collective-permute-start.21 = (f32[1,2,64,256]{3,2,1,0:T(8,128)S(1)}, f32[1,2,64,256]{3,2,1,0:T(8,128)S(1)}, u32[]{:S(2)}, u32[]{:S(2)}) collective-permute-start(f32[1,2,64,256]{3,2,1,0:T(8,128)S(1)} %dynamic-slice_bitcast_fusion.1), channel_id=1, source_target_pairs={{0,1},{1,0},{2,3},{3,2},{4,5},{5,4},{6,7},{7,6},{8,9},{9,8},{10,11... | collective-permute-start | bytes 393224 | tf_op jit(solution)/shard_map/ppermute | solution.py:204
  94.8 11.4 %copy-start.6 = (f32[72,256]{1,0:T(8,128)}, f32[72,256]{1,0:T(8,128)S(1)}, u32[]{:S(2)}) copy-start(f32[72,256]{1,0:T(8,128)S(1)} %add_select_fusion.2.a0_ref) | copy-start | bytes 221188
  94.8 11.5 %collective-permute-start.32 = (f32[72,256]{1,0:T(8,128)S(1)}, f32[72,256]{1,0:T(8,128)S(1)}, u32[]{:S(2)}, u32[]{:S(2)}) collective-permute-start(f32[72,256]{1,0:T(8,128)S(1)} %add_select_fusion.2.a0_ref), channel_id=1, source_target_pairs={{0,2},{2,0},{1,3},{3,1},{4,6},{6,4},{5,7},{7,5},{8,10},{10,8},{9,1... | collective-permute-start | bytes 221192 | tf_op jit(solution)/shard_map/ppermute | solution.py:204
  95.7 8.4 %collective-permute-start.16 = (f32[2,128,256]{2,1,0:T(8,128)S(1)}, f32[2,128,256]{2,1,0:T(8,128)S(1)}, u32[]{:S(2)}, u32[]{:S(2)}) collective-permute-start(f32[2,128,256]{2,1,0:T(8,128)S(1)} %dynamic-slice_bitcast_fusion), channel_id=1, source_target_pairs={{0,2},{2,0},{1,3},{3,1},{4,6},{6,4},{5,7},{7,5},{8,10},{10,8},{9,1... | collective-permute-start | bytes 786440 | tf_op jit(solution)/shard_map/ppermute | solution.py:204
  96.6 10.1 %collective-permute-start.22 = (f32[1,64,256]{2,1,0:T(8,128)S(1)}, f32[1,64,256]{2,1,0:T(8,128)S(1)}, u32[]{:S(2)}, u32[]{:S(2)}) collective-permute-start(f32[1,64,256]{2,1,0:T(8,128)S(1)} %dynamic-slice_bitcast_fusion.3), channel_id=1, source_target_pairs={{0,2},{2,0},{1,3},{3,1},{4,6},{6,4},{5,7},{7,5},{8,10},{10,8},{9,1... | collective-permute-start | bytes 196616 | tf_op jit(solution)/shard_map/ppermute | solution.py:204
  104.2 3.4 %copy-start.5 = (f32[2,128,256]{2,1,0:T(8,128)}, f32[2,128,256]{2,1,0:T(8,128)S(1)}, u32[]{:S(2)}) copy-start(f32[2,128,256]{2,1,0:T(8,128)S(1)} %fusion.8.own_ref) | copy-start | bytes 786436
  104.2 3.4 %collective-permute-start.17 = (f32[2,128,256]{2,1,0:T(8,128)S(1)}, f32[2,128,256]{2,1,0:T(8,128)S(1)}, u32[]{:S(2)}, u32[]{:S(2)}) collective-permute-start(f32[2,128,256]{2,1,0:T(8,128)S(1)} %fusion.8.own_ref), channel_id=1, source_target_pairs={{0,1},{1,0},{2,3},{3,2},{4,5},{5,4},{6,7},{7,6},{8,9},{9,8},{10,11... | collective-permute-start | bytes 786440 | tf_op jit(solution)/shard_map/ppermute | solution.py:204
  106.1 1.3 %collective-permute-start.33 = (f32[72,256]{1,0:T(8,128)S(1)}, f32[72,256]{1,0:T(8,128)S(1)}, u32[]{:S(2)}, u32[]{:S(2)}) collective-permute-start(f32[72,256]{1,0:T(8,128)S(1)} %add_select_fusion.2.a0_ref), channel_id=1, source_target_pairs={{0,1},{1,0},{2,3},{3,2},{4,5},{5,4},{6,7},{7,6},{8,9},{9,8},{10,11... | collective-permute-start | bytes 221192 | tf_op jit(solution)/shard_map/ppermute | solution.py:204
  106.2 1.0 copy-start.8
  106.3 1.3 %collective-permute-start.34 = (f32[72,256]{1,0:T(8,128)S(1)}, f32[72,256]{1,0:T(8,128)S(1)}, u32[]{:S(2)}, u32[]{:S(2)}) collective-permute-start(f32[72,256]{1,0:T(8,128)S(1)} %collective-permute-done.32.a1_ref), channel_id=1, source_target_pairs={{0,1},{1,0},{2,3},{3,2},{4,5},{5,4},{6,7},{7,6},{8,9},{9,8},{10,11... | collective-permute-start | bytes 221192 | tf_op jit(solution)/shard_map/ppermute | solution.py:204
  107.4 0.6 copy-start.9
  107.6 0.6 copy-start.10
  108.2 0.7 copy-start.7

commit v3 on v2

--- a/solution.py
+++ b/solution.py
@@ -9,8 +9,9 @@
 from jax.sharding import PartitionSpec as P
 
 
-BLK = ("z", "xh", "y")
-PLANE = ("xh", "y")
+BLK = ("zh", "zl", "xh", "y")
+PLANE = ("zl", "y")
+STACK = ("zh", "xh")
 PAR = ("xl", "core")
 ALL = BLK + PAR
 HIGHEST = lax.Precision.HIGHEST
@@ -90,13 +91,19 @@
     tile_ref[...] = tile_in_ref[...]
     inverse_ref[...] = inverse_in_ref[...]
     eliminate(tile_ref, inverse_ref, n // CHUNK // 2, n // CHUNK)
-    start = pl.multiple_of(at_ref[0] * share, share)
-    packed_ref[:share, :] = inverse_ref[pl.ds(start, share), :]
-    packed_ref[share:, :] = outer_tile(jnp.broadcast_to(energy_ref[...], (8, n)), inverse_ref[...])
+    half = n // 2
+    start = pl.multiple_of(at_ref[2] * share, share)
+    packed_ref[:share, :] = inverse_ref[pl.ds(start, share), :half]
+    packed_ref[share:half, :] = inverse_ref[pl.ds(start + half, share), :half]
+    packed_ref[half : half + share, :] = inverse_ref[pl.ds(start + half, share), half:]
+    lead = outer_tile(jnp.broadcast_to(energy_ref[...], (8, n)), inverse_ref[...])
+    first = lax.broadcasted_iota(jnp.int32, (8, half), 0) == 0
+    packed_ref[half + share :, :] = jnp.where(first, lead[:, :half], lead[:, half:])
 
 
 VMEM = pl.BlockSpec(memory_space=pltpu.VMEM)
 SMEM = pl.BlockSpec(memory_space=pltpu.SMEM)
+GRANT = pltpu.CompilerParams(vmem_limit_bytes=16 * 2**20)
 
 
 def f32(*shape):
@@ -115,6 +122,7 @@
         in_specs=[VMEM],
         out_specs=(VMEM,) * 2,
         name="factor_first",
+        compiler_params=GRANT,
         cost_estimate=cost(8 * 10**9),
     )(total)
 
@@ -123,11 +131,12 @@
     n = tile.shape[0]
     return pl.pallas_call(
         factor_second_kernel,
-        out_shape=f32(n // 4 + 8, n),
+        out_shape=f32(3 * n // 4 + 8, n // 2),
         in_specs=[SMEM] + [VMEM] * 3,
         out_specs=VMEM,
         scratch_shapes=[pltpu.VMEM((n, n), jnp.float32)] * 2,
         name="factor_second",
+        compiler_params=GRANT,
         cost_estimate=cost(8 * 10**9),
     )(at, tile, inverse, energies)
 
@@ -145,20 +154,24 @@
         in_specs=[VMEM] * 3,
         out_specs=VMEM,
         name="cross",
+        compiler_params=GRANT,
         cost_estimate=cost(10**9),
     )(rows, prev_rows, lead_rows)
 
 
 def finish_kernel(
-    at_ref, own_ref, other_ref, self_ref, cycle_ref, energy_ref, a0_ref, a1_ref, b0_ref, b1_ref,
+    at_ref, own_ref, other_ref, self_ref, cycle_ref, energy_ref, mine_ref, twin_ref,
     panel_ref, energies_ref, diagonal_ref, neighbour_ref, sums_ref, inverse_ref, prev_ref,
 ):
     n = inverse_ref.shape[0]
     share, half = n // 4, n // 2
     par, core = at_ref[0], at_ref[2]
-    for i, source in ((0, a0_ref), (2, a1_ref), (1, b0_ref), (3, b1_ref)):
-        flip = jnp.bitwise_xor(par, i)
-        inverse_ref[pl.ds(pl.multiple_of(flip * share, share), share), :] = source[:share, :]
+    inverse_ref[:half, half:] = jnp.zeros((half, half), jnp.float32)
+    for i, source in ((0, mine_ref), (1, twin_ref)):
+        start = pl.multiple_of(jnp.bitwise_xor(core, i) * share, share)
+        inverse_ref[pl.ds(start, share), :half] = source[:share, :]
+        inverse_ref[pl.ds(start + half, share), :half] = source[share:half, :]
+        inverse_ref[pl.ds(start + half, share), half:] = source[half : half + share, :]
     for i, source in ((0, own_ref), (1, other_ref)):
         start = pl.multiple_of(jnp.bitwise_xor(core, i) * half, half)
         sums_ref[0, pl.ds(start, half), :] = source[0]
@@ -177,9 +190,10 @@
         self_ref[pl.ds(start, share), :] + ridge_shift * shifted - outer_tile(own, panel)
     )
     neighbour_ref[...] = cycle_ref[...] - outer_tile(own, prev_ref[...])
-    lead = a0_ref[share:, :]
-    remainder = energy_ref[...] - outer_tile(lead, panel)[:1]
-    energies_ref[...] = jnp.where(at_ref[1] == 0, lead[:1], remainder)
+    last = half + share
+    lead = jnp.concatenate([mine_ref[last : last + 1, :], mine_ref[last + 1 : last + 2, :]], axis=1)
+    remainder = energy_ref[...] - outer_tile(jnp.broadcast_to(lead, (8, n)), panel)[:1]
+    energies_ref[...] = jnp.where(at_ref[1] == 0, lead, remainder)
 
 
 def finish(at, own, other, self_sum, cycle_rows, energies, parts):
@@ -188,7 +202,7 @@
     return pl.pallas_call(
         finish_kernel,
         out_shape=(f32(n, n), f32(1, n), f32(share, n), f32(share, n)),
-        in_specs=[SMEM] + [VMEM] * 9,
+        in_specs=[SMEM] + [VMEM] * 7,
         out_specs=(VMEM,) * 4,
         scratch_shapes=[
             pltpu.VMEM((2, n, n), jnp.float32),
@@ -196,6 +210,7 @@
             pltpu.VMEM((n, n), jnp.float32),
         ],
         name="finish",
+        compiler_params=GRANT,
         cost_estimate=cost(10**9),
     )(at, own, other, self_sum, cycle_rows, energies, *parts)
 
@@ -228,6 +243,10 @@
     return own, swapped(own, "core")
 
 
+SCATTER_ORDER = (6, 2, 5, 7, 1, 3, 4)
+STACK_ORDER = (5, 4, 3, 7, 2, 6, 1)
+
+
 def total(values):
     return functools.reduce(jnp.add, values)
 
@@ -235,13 +254,16 @@
 def scatter_lead(rows):
     parts = lax.axis_size(PLANE)
     part = rows.shape[0] // parts
-    got = [lax.ppermute(rows[k * part : (k + 1) * part], BLK, [(0, k)]) for k in range(1, parts)]
+    got = [
+        lax.ppermute(rows[k * part : (k + 1) * part], BLK, [(0, k // 4 * 8 + k % 4)])
+        for k in SCATTER_ORDER
+    ]
     return jnp.where(lax.axis_index(PLANE) == 0, rows[:part], total(got))
 
 
-def along_z(piece):
-    got = [lax.ppermute(piece, "z", [(0, k)]) for k in range(1, lax.axis_size("z"))]
-    return jnp.where(lax.axis_index("z") == 0, piece, total(got))
+def along_stack(piece):
+    got = [lax.ppermute(piece, STACK, [(0, k)]) for k in STACK_ORDER]
+    return jnp.where(lax.axis_index(STACK) == 0, piece, total(got))
 
 
 def over_plane(piece):
@@ -251,7 +273,8 @@
 
 
 def small_tree(value):
-    z, xh, y = (lax.axis_index(a) for a in BLK)
+    zh, zl, xh, y = (lax.axis_index(a) for a in BLK)
+    z = zh * 2 + zl
     rounds = (
         ([[(0, 8 * k)] for k in (4, 2, 6)], z == 0),
         ([[(8 * k, 8 * k + d) for k in range(0, 8, 2)] for d in (4, 12, 8)], (z % 2 == 0) & (xh == 0)),
@@ -271,28 +294,29 @@
     ).astype(jnp.int32)
     piece = scatter_lead(log_derivs)
     prev_rows = passed_along(log_derivs, BLK, 1)
-    own, other = sum_halves(outer_tile(log_derivs, log_derivs)[None])
-    core = lax.axis_index("core")
+    self_part = outer_tile(log_derivs, log_derivs)[None]
+    own, other = sum_halves(self_part)
+    upper = lax.axis_index("core") == 0
     self_sum = jnp.concatenate(
-        [jnp.where(core == 0, own[0], other[0]), jnp.where(core == 0, other[0], own[0])]
-    )
-    piece = along_z(piece)
+        [jnp.where(upper, own[0], other[0]), jnp.where(upper, other[0], own[0])]
+    )
+    piece = along_stack(piece)
     tile, inverse = factor_first(self_sum)
     lead_rows = over_plane(piece).reshape(log_derivs.shape)
     packed = factor_second(at, tile, inverse, energy_row)
     packed = small_tree(packed)
-    across = swapped(packed, "xl")
-    parts = (packed, across, swapped(packed, "core"), swapped(across, "core"))
+    twin = swapped(packed, "core")
     cycle_rows = sum_scattered(outer_tile(log_derivs, prev_rows)[None])[0]
-    own, other = sum_halves(cross(log_derivs, prev_rows, lead_rows))
+    partials = cross(log_derivs, prev_rows, lead_rows)
+    own, other = sum_halves(partials)
     panel, energies_next, diagonal, neighbour = finish(
-        at, own, other, self_sum, cycle_rows, energy_row, parts
+        at, own, other, self_sum, cycle_rows, energy_row, (packed, twin)
     )
     return panel, energies_next.reshape(n), diagonal, neighbour
 
 
 def solution(mesh):
-    torus = Mesh(mesh.devices.reshape(8, 2, 4, 2, 2), ALL)
+    torus = Mesh(mesh.devices.reshape(4, 2, 2, 4, 2, 2), ALL)
     in_specs = (P(BLK, PAR), P(BLK))
     out_specs = (P(BLK, None), P(BLK), P(ALL, None), P(ALL, None))
     return jax.shard_map(

time: 113 us -> 108 us (0.956)
  starting transfers between devices: 57.9 us -> 66.5 us
  Pallas kernels: 26.3 us -> 20 us
  waiting for transfers between devices: 14.5 us -> 10.3 us
  local copies, waits for them, and re-layouts: 5.78 us -> 3.24 us
  matrix products: 3.28 us -> 2.07 us
    ppermute x9, starting transfers between devices: 14.3 us -> 21.1 us  [small_tree(): got = [lax.ppermute(value, BLK, route) for route in routes]]
    ppermute x11 -> x9, starting transfers between devices: 11.3 us -> 14.4 us  [swapped(): return lax.ppermute(value, axis, [(0, 1), (1, 0)])]
    pallas_call x1, Pallas kernels: 4.61 us -> 1.92 us  [cross(): pl.pallas_call(cross_kernel, out_shape=f32(2, n, n), in_specs=[VMEM] * 3,...]
    unnamed x22 -> x4, local copies, waits for them, and re-layouts: 3.21 us -> 0.68 us
    ppermute x9, waiting for transfers between devices: 3.35 us -> 1.03 us  [small_tree(): got = [lax.ppermute(value, BLK, route) for route in routes]]
    all_to_all x1, starting transfers between devices: 7.43 us -> 5.3 us  [over_plane(): lax.all_to_all(copies, PLANE, split_axis=0, concat_axis=0, tiled=True)]
    ppermute x14, waiting for transfers between devices: 4.13 us -> 2.16 us  [the longest x7 1.19 us: scatter_lead(): lax.ppermute(rows[k * part:(k + 1) * part], BLK, [(0, k // 4 * 8 + k % 4)])]
    ppermute x1, starting transfers between devices: 0.08 us -> 1.94 us  [passed_along(): lax.ppermute(block, axis, [((i - distance) % count, i) for i in range(cou...]
  transfers between devices with their start and end apart: 36 -> 34, of which waited for: 10 -> 5; matrix products, arithmetic and copies ran while one was open for 7% -> 6% of each run, Pallas kernels for 21% -> 16%
where the time goes in v3:
time: 108 us; the launch traced here: 106 us
  starting transfers between devices  66.5 us (62%)
  Pallas kernels  20 us (19%)
  waiting for transfers between devices  10.3 us (10%)
  local copies, waits for them, and re-layouts  3.24 us (3%)
  other arithmetic  3.18 us (3%)
  matrix products  2.07 us (2%)
    ppermute x9, starting transfers between devices, small_tree(): got = [lax.ppermute(value, BLK, route) for route in routes]  21.1 us
    ppermute x7, starting transfers between devices, scatter_lead(): lax.ppermute(rows[k * part:(k + 1) * part], BLK, [(0, k // 4 * 8 + k % 4)])  14.8 us
    ppermute x9, starting transfers between devices, swapped(): return lax.ppermute(value, axis, [(0, 1), (1, 0)])  14.4 us
    ppermute x7, starting transfers between devices, along_stack(): got = [lax.ppermute(piece, STACK, [(0, k)]) for k in STACK_ORDER]  9.07 us
    pallas_call x1, Pallas kernels, factor_second(): pl.pallas_call(factor_second_kernel, out_shape=f32(3 * n // 4 + 8, n // 2...  7.92 us
    pallas_call x1, Pallas kernels, factor_first(): pl.pallas_call(factor_first_kernel, out_shape=(f32(n, n), f32(n, n)), in_...  7.59 us
    ppermute x9, waiting for transfers between devices, swapped(): return lax.ppermute(value, axis, [(0, 1), (1, 0)])  7.06 us
    all_to_all x1, starting transfers between devices, over_plane(): lax.all_to_all(copies, PLANE, split_axis=0, concat_axis=0, tiled=True)  5.3 us
  transfers between devices with their start and end apart: 34, of which 5 were waited for; matrix products, arithmetic and copies ran while one was open for 6% of the time, Pallas kernels for 16%

profile of v3, /device:TPU:1, one launch (start us, length us, event | category | flops | bytes accessed | tf_op | source)
XLA Modules:
  0.0 106.3 jit_solution(9905746181614335421)
XLA Ops:
  0.6 1.4 %fusion.1 = (f32[32,1024]{1,0:T(8,128)S(1)}, f32[32,1024]{1,0:T(8,128)S(1)}, f32[32,1024]{1,0:T(8,128)S(1)}, f32[32,1024]{1,0:T(8,128)S(1)}, f32[32,1024]{1,0:T(...) fusion(f32[256,1024]{1,0:T(8,128)} %rows_ref.1), kind=kLoop, calls=%fused_computation.17 | loop fusion | bytes 1835008 | tf_op jit(solution)/shard_map/slice | solution.py:258
  2.0 7.0 %collective-permute-start.1 = (f32[32,1024]{1,0:T(8,128)S(1)}, f32[32,1024]{1,0:T(8,128)S(1)}, u32[]{:S(2)}, u32[]{:S(2)}) collective-permute-start(f32[32,1024]{1,0:T(8,128)S(1)} %get-tuple-element.22), channel_id=1, source_target_pairs={{0,40},{1,41},{2,42},{3,43}} | collective-permute-start | bytes 393224 | tf_op jit(solution)/shard_map/ppermute | solution.py:258
  9.0 1.3 %collective-permute-start.2 = (f32[32,1024]{1,0:T(8,128)S(1)}, f32[32,1024]{1,0:T(8,128)S(1)}, u32[]{:S(2)}, u32[]{:S(2)}) collective-permute-start(f32[32,1024]{1,0:T(8,128)S(1)} %get-tuple-element.16), channel_id=1, source_target_pairs={{0,8},{1,9},{2,10},{3,11}} | collective-permute-start | bytes 393224 | tf_op jit(solution)/shard_map/ppermute | solution.py:258
  10.3 1.3 %collective-permute-start.3 = (f32[32,1024]{1,0:T(8,128)S(1)}, f32[32,1024]{1,0:T(8,128)S(1)}, u32[]{:S(2)}, u32[]{:S(2)}) collective-permute-start(f32[32,1024]{1,0:T(8,128)S(1)} %get-tuple-element.21), channel_id=1, source_target_pairs={{0,36},{1,37},{2,38},{3,39}} | collective-permute-start | bytes 393224 | tf_op jit(solution)/shard_map/ppermute | solution.py:258
  11.7 1.3 %collective-permute-start.4 = (f32[32,1024]{1,0:T(8,128)S(1)}, f32[32,1024]{1,0:T(8,128)S(1)}, u32[]{:S(2)}, u32[]{:S(2)}) collective-permute-start(f32[32,1024]{1,0:T(8,128)S(1)} %get-tuple-element.20), channel_id=1, source_target_pairs={{0,44},{1,45},{2,46},{3,47}} | collective-permute-start | bytes 393224 | tf_op jit(solution)/shard_map/ppermute | solution.py:258
  13.0 1.3 %collective-permute-start.5 = (f32[32,1024]{1,0:T(8,128)S(1)}, f32[32,1024]{1,0:T(8,128)S(1)}, u32[]{:S(2)}, u32[]{:S(2)}) collective-permute-start(f32[32,1024]{1,0:T(8,128)S(1)} %get-tuple-element.19), channel_id=1, source_target_pairs={{0,4},{1,5},{2,6},{3,7}} | collective-permute-start | bytes 393224 | tf_op jit(solution)/shard_map/ppermute | solution.py:258
  14.3 0.0 collective-permute-done.1
  14.3 1.3 %collective-permute-start.6 = (f32[32,1024]{1,0:T(8,128)S(1)}, f32[32,1024]{1,0:T(8,128)S(1)}, u32[]{:S(2)}, u32[]{:S(2)}) collective-permute-start(f32[32,1024]{1,0:T(8,128)S(1)} %get-tuple-element.18), channel_id=1, source_target_pairs={{0,12},{1,13},{2,14},{3,15}} | collective-permute-start | bytes 393224 | tf_op jit(solution)/shard_map/ppermute | solution.py:258
  15.6 1.3 %collective-permute-start.7 = (f32[32,1024]{1,0:T(8,128)S(1)}, f32[32,1024]{1,0:T(8,128)S(1)}, u32[]{:S(2)}, u32[]{:S(2)}) collective-permute-start(f32[32,1024]{1,0:T(8,128)S(1)} %get-tuple-element.17), channel_id=1, source_target_pairs={{0,32},{1,33},{2,34},{3,35}} | collective-permute-start | bytes 393224 | tf_op jit(solution)/shard_map/ppermute | solution.py:258
  16.9 1.0 convolution_bitcast_fusion
  18.0 1.0 collective-permute-start.18
  19.0 0.0 collective-permute-done.4
  19.0 0.0 collective-permute-done.5
  19.0 0.0 collective-permute-done.6
  19.0 1.2 %collective-permute-done.7 = f32[32,1024]{1,0:T(8,128)S(1)} collective-permute-done((f32[32,1024]{1,0:T(8,128)S(1)}, f32[32,1024]{1,0:T(8,128)S(1)}, u32[]{:S(2)}, u32[]{:S(2)}) %collective-permute-start.7) | collective-permute-done | bytes 131104 | tf_op jit(solution)/shard_map/ppermute | solution.py:258
  20.2 0.1 add_select_fusion.1
  20.3 1.3 %collective-permute-start.10 = (f32[32,1024]{1,0:T(8,128)S(1)}, f32[32,1024]{1,0:T(8,128)S(1)}, u32[]{:S(2)}, u32[]{:S(2)}) collective-permute-start(f32[32,1024]{1,0:T(8,128)S(1)} %add_select_fusion.1), channel_id=1, source_target_pairs={{0,80},{1,81},{2,82},{3,83},{4,84},{5,85},{6,86},{7,87},{8,88},{9,... | collective-permute-start | bytes 393224 | tf_op jit(solution)/shard_map/ppermute | solution.py:265
  21.6 1.3 %collective-permute-start.11 = (f32[32,1024]{1,0:T(8,128)S(1)}, f32[32,1024]{1,0:T(8,128)S(1)}, u32[]{:S(2)}, u32[]{:S(2)}) collective-permute-start(f32[32,1024]{1,0:T(8,128)S(1)} %add_select_fusion.1), channel_id=1, source_target_pairs={{0,208},{1,209},{2,210},{3,211},{4,212},{5,213},{6,214},{7,215},{8... | collective-permute-start | bytes 393224 | tf_op jit(solution)/shard_map/ppermute | solution.py:265
  23.0 1.3 %collective-permute-start.19 = (f32[1,128,256]{2,1,0:T(8,128)S(1)}, f32[1,128,256]{2,1,0:T(8,128)S(1)}, u32[]{:S(2)}, u32[]{:S(2)}) collective-permute-start(f32[1,128,256]{2,1,0:T(8,128)S(1)} %dynamic-slice_bitcast_fusion.2), channel_id=1, source_target_pairs={{0,2},{2,0},{1,3},{3,1},{4,6},{6,4},{5,7},{7,5},{8,10},{10,8},{9,1... | collective-permute-start | bytes 393224 | tf_op jit(solution)/shard_map/ppermute | solution.py:219
  24.3 0.1 pad_add_fusion.at_ref
  24.3 1.3 %collective-permute-start.12 = (f32[32,1024]{1,0:T(8,128)S(1)}, f32[32,1024]{1,0:T(8,128)S(1)}, u32[]{:S(2)}, u32[]{:S(2)}) collective-permute-start(f32[32,1024]{1,0:T(8,128)S(1)} %add_select_fusion.1), channel_id=1, source_target_pairs={{0,64},{1,65},{2,66},{3,67},{4,68},{5,69},{6,70},{7,71},{8,72},{9,... | collective-permute-start | bytes 393224 | tf_op jit(solution)/shard_map/ppermute | solution.py:265
  25.6 1.3 %collective-permute-start.13 = (f32[32,1024]{1,0:T(8,128)S(1)}, f32[32,1024]{1,0:T(8,128)S(1)}, u32[]{:S(2)}, u32[]{:S(2)}) collective-permute-start(f32[32,1024]{1,0:T(8,128)S(1)} %add_select_fusion.1), channel_id=1, source_target_pairs={{0,192},{1,193},{2,194},{3,195},{4,196},{5,197},{6,198},{7,199},{8... | collective-permute-start | bytes 393224 | tf_op jit(solution)/shard_map/ppermute | solution.py:265
  26.9 1.3 %collective-permute-start.14 = (f32[32,1024]{1,0:T(8,128)S(1)}, f32[32,1024]{1,0:T(8,128)S(1)}, u32[]{:S(2)}, u32[]{:S(2)}) collective-permute-start(f32[32,1024]{1,0:T(8,128)S(1)} %add_select_fusion.1), channel_id=1, source_target_pairs={{0,16},{1,17},{2,18},{3,19},{4,20},{5,21},{6,22},{7,23},{8,24},{9,... | collective-permute-start | bytes 393224 | tf_op jit(solution)/shard_map/ppermute | solution.py:265
  28.2 0.0 collective-permute-done.11
  28.3 1.3 %collective-permute-start.8 = (f32[32,1024]{1,0:T(8,128)S(1)}, f32[32,1024]{1,0:T(8,128)S(1)}, u32[]{:S(2)}, u32[]{:S(2)}) collective-permute-start(f32[32,1024]{1,0:T(8,128)S(1)} %add_select_fusion.1), channel_id=1, source_target_pairs={{0,144},{1,145},{2,146},{3,147},{4,148},{5,149},{6,150},{7,151},{8... | collective-permute-start | bytes 393224 | tf_op jit(solution)/shard_map/ppermute | solution.py:265
  29.6 1.3 %collective-permute-start.9 = (f32[32,1024]{1,0:T(8,128)S(1)}, f32[32,1024]{1,0:T(8,128)S(1)}, u32[]{:S(2)}, u32[]{:S(2)}) collective-permute-start(f32[32,1024]{1,0:T(8,128)S(1)} %add_select_fusion.1), channel_id=1, source_target_pairs={{0,128},{1,129},{2,130},{3,131},{4,132},{5,133},{6,134},{7,135},{8... | collective-permute-start | bytes 393224 | tf_op jit(solution)/shard_map/ppermute | solution.py:265
  30.9 1.9 %collective-permute-start = (f32[256,1024]{1,0:T(8,128)S(1)}, f32[256,1024]{1,0:T(8,128)S(1)}, u32[]{:S(2)}, u32[]{:S(2)}) collective-permute-start(f32[256,1024]{1,0:T(8,128)S(1)} %copy-done), channel_id=1, source_target_pairs={{252,0},{0,4},{4,8},{8,12},{12,16},{16,20},{20,24},{24,28},{28,32}... | collective-permute-start | bytes 3145736 | tf_op jit(solution)/shard_map/ppermute | solution.py:224
  32.9 0.9 collective-permute-done.13
  33.8 4.0 %collective-permute-start.20 = (f32[1,128,256]{2,1,0:T(8,128)S(1)}, f32[1,128,256]{2,1,0:T(8,128)S(1)}, u32[]{:S(2)}, u32[]{:S(2)}) collective-permute-start(f32[1,128,256]{2,1,0:T(8,128)S(1)} %fusion.7), channel_id=1, source_target_pairs={{0,1},{1,0},{2,3},{3,2},{4,5},{5,4},{6,7},{7,6},{8,9},{9,8},{10,11... | collective-permute-start | bytes 393224 | tf_op jit(solution)/shard_map/ppermute | solution.py:219
  37.8 0.0 collective-permute-done.9
  37.8 0.1 add_select_fusion
  37.9 1.1 %broadcast_in_dim.6 = f32[8,32,1024]{2,1,0:T(8,128)} broadcast(f32[32,1024]{1,0:T(8,128)S(1)} %add_select_fusion), dimensions={1,2} | broadcast | bytes 1179648 | tf_op jit(solution)/shard_map/broadcast_in_dim | solution.py:271
  39.0 5.3 %all-to-all-start = ((f32[8,32,1024]{2,1,0:T(8,128)}), f32[8,32,1024]{2,1,0:T(8,128)S(1)}, u32[]{:S(2)}, u32[]{:S(2)}) async-start(f32[8,32,1024]{2,1,0:T(8,128)} %broadcast_in_dim.6), calls=%async_computation | async-start | bytes 2097152 | tf_op jit(solution)/shard_map/all_to_all | solution.py:272
  44.4 7.6 %factor_first.1 = (f32[256,256]{1,0:T(8,128)S(1)}, f32[256,256]{1,0:T(8,128)S(1)}) custom-call(f32[256,256]{1,0:T(8,128)S(1)} %pad_maximum_fusion.sum_ref.self_ref), custom_call_target="tpu_custom_call" | custom-call | flops 8000000000 | bytes 1048576 | tf_op jit(solution)/shard_map/factor_first/pallas_call | solution.py:119
  52.0 0.0 copy-start.1
  52.0 0.7 copy-done.1
  52.7 7.9 %factor_second.1 = f32[200,128]{1,0:T(8,128)S(1)} custom-call(s32[3]{0:T(128)S(1)} %pad_add_fusion.at_ref, f32[256,256]{1,0:T(8,128)S(1)} %get-tuple-element.10.tile_in_ref, f32[256,256]{1,0:T(8,128)S(1)} %get-tuple-element.11.inverse_in_ref, f32[1,256]{1,0:T(1,128)S(1)} %bitcast.42), custom_call_target="tpu_custom_call" | custom-call | flops 8000000000 | bytes 1048576 | tf_op jit(solution)/shard_map/factor_second/pallas_call | solution.py:132
  60.6 4.8 %collective-permute-start.23 = (f32[200,128]{1,0:T(8,128)S(1)}, f32[200,128]{1,0:T(8,128)}, u32[]{:S(2)}, u32[]{:S(2)}) collective-permute-start(f32[200,128]{1,0:T(8,128)S(1)} %factor_second.1), channel_id=1, source_target_pairs={{0,128},{1,129},{2,130},{3,131}} | collective-permute-start | bytes 307208 | tf_op jit(solution)/shard_map/ppermute | solution.py:284
  65.3 5.4 %collective-permute-start.24 = (f32[200,128]{1,0:T(8,128)S(1)}, f32[200,128]{1,0:T(8,128)}, u32[]{:S(2)}, u32[]{:S(2)}) collective-permute-start(f32[200,128]{1,0:T(8,128)S(1)} %factor_second.1), channel_id=1, source_target_pairs={{0,64},{1,65},{2,66},{3,67}} | collective-permute-start | bytes 307208 | tf_op jit(solution)/shard_map/ppermute | solution.py:284
  70.7 1.9 %collective-permute-start.25 = (f32[200,128]{1,0:T(8,128)S(1)}, f32[200,128]{1,0:T(8,128)}, u32[]{:S(2)}, u32[]{:S(2)}) collective-permute-start(f32[200,128]{1,0:T(8,128)S(1)} %factor_second.1), channel_id=1, source_target_pairs={{0,192},{1,193},{2,194},{3,195}} | collective-permute-start | bytes 307208 | tf_op jit(solution)/shard_map/ppermute | solution.py:284
  72.6 0.0 collective-permute-done.23
  72.6 0.0 collective-permute-done.24
  72.6 1.0 collective-permute-done.25
  73.6 1.7 %add_select_fusion.4 = f32[200,128]{1,0:T(8,128)} fusion(f32[200,128]{1,0:T(8,128)S(1)} %factor_second.1, f32[200,128]{1,0:T(8,128)} %collective-permute-done.25, f32[200,128]{1,0:T(8,128)} %collective-permute-done.23, f32[200,128]{1,0:T(8,128)} %collective-permute-done.24, pred[]{:T(512)S(6)} %eq.29), kind=kLoop, calls=%fused_computation.12 | loop fusion | flops 76800 | bytes 512001 | tf_op jit(solution)/shard_map/jit(_where)/select_n | solution.py:285
  75.3 1.3 %collective-permute-start.26 = (f32[200,128]{1,0:T(8,128)}, f32[200,128]{1,0:T(8,128)S(1)}, u32[]{:S(2)}, u32[]{:S(2)}) collective-permute-start(f32[200,128]{1,0:T(8,128)} %add_select_fusion.4), channel_id=1, source_target_pairs={{0,16},{64,80},{128,144},{192,208},{1,17},{65,81},{129,145},{193,2... | collective-permute-start | bytes 307208 | tf_op jit(solution)/shard_map/ppermute | solution.py:284
  76.6 1.9 %collective-permute-start.27 = (f32[200,128]{1,0:T(8,128)}, f32[200,128]{1,0:T(8,128)}, u32[]{:S(2)}, u32[]{:S(2)}) collective-permute-start(f32[200,128]{1,0:T(8,128)} %add_select_fusion.4), channel_id=1, source_target_pairs={{0,48},{64,112},{128,176},{192,240},{1,49},{65,113},{129,177},{193... | collective-permute-start | bytes 307208 | tf_op jit(solution)/shard_map/ppermute | solution.py:284
  78.5 1.9 %collective-permute-start.28 = (f32[200,128]{1,0:T(8,128)}, f32[200,128]{1,0:T(8,128)}, u32[]{:S(2)}, u32[]{:S(2)}) collective-permute-start(f32[200,128]{1,0:T(8,128)} %add_select_fusion.4), channel_id=1, source_target_pairs={{0,32},{64,96},{128,160},{192,224},{1,33},{65,97},{129,161},{193,2... | collective-permute-start | bytes 307208 | tf_op jit(solution)/shard_map/ppermute | solution.py:284
  80.5 1.9 %cross.1 = f32[2,256,256]{2,1,0:T(8,128)S(1)} custom-call(f32[256,1024]{1,0:T(8,128)S(1)} %copy-done, f32[256,1024]{1,0:T(8,128)S(1)} %collective-permute-done.prev_ref, f32[256,1024]{1,0:T(8,128)S(1)} %bitcast.41), custom_call_target="tpu_custom_call" | custom-call | flops 1000000000 | bytes 1048576 | tf_op jit(solution)/shard_map/cross/pallas_call | solution.py:151
  82.4 4.0 %collective-permute-start.15 = (f32[2,256,256]{2,1,0:T(8,128)S(1)}, f32[2,256,256]{2,1,0:T(8,128)S(1)}, u32[]{:S(2)}, u32[]{:S(2)}) collective-permute-start(f32[2,256,256]{2,1,0:T(8,128)S(1)} %cross.1), channel_id=1, source_target_pairs={{0,1},{1,0},{2,3},{3,2},{4,5},{5,4},{6,7},{7,6},{8,9},{9,8},{10,11... | collective-permute-start | bytes 1572872 | tf_op jit(solution)/shard_map/ppermute | solution.py:219
  86.4 1.0 fusion.2
  87.5 0.1 collective-permute-start.21
  87.6 0.0 collective-permute-done.26
  87.6 1.0 add_select_fusion.3
  88.6 1.3 %collective-permute-start.29 = (f32[200,128]{1,0:T(8,128)S(1)}, f32[200,128]{1,0:T(8,128)S(1)}, u32[]{:S(2)}, u32[]{:S(2)}) collective-permute-start(f32[200,128]{1,0:T(8,128)S(1)} %add_select_fusion.3), channel_id=1, source_target_pairs={{0,8},{16,24},{32,40},{48,56},{64,72},{80,88},{96,104},{112,120},{... | collective-permute-start | bytes 307208 | tf_op jit(solution)/shard_map/ppermute | solution.py:284
  89.9 1.3 %collective-permute-start.30 = (f32[200,128]{1,0:T(8,128)S(1)}, f32[200,128]{1,0:T(8,128)S(1)}, u32[]{:S(2)}, u32[]{:S(2)}) collective-permute-start(f32[200,128]{1,0:T(8,128)S(1)} %add_select_fusion.3), channel_id=1, source_target_pairs={{0,4},{16,20},{32,36},{48,52},{64,68},{80,84},{96,100},{112,116},{... | collective-permute-start | bytes 307208 | tf_op jit(solution)/shard_map/ppermute | solution.py:284
  91.2 1.3 %collective-permute-start.31 = (f32[200,128]{1,0:T(8,128)S(1)}, f32[200,128]{1,0:T(8,128)S(1)}, u32[]{:S(2)}, u32[]{:S(2)}) collective-permute-start(f32[200,128]{1,0:T(8,128)S(1)} %add_select_fusion.3), channel_id=1, source_target_pairs={{0,12},{16,28},{32,44},{48,60},{64,76},{80,92},{96,108},{112,124},... | collective-permute-start | bytes 307208 | tf_op jit(solution)/shard_map/ppermute | solution.py:284
  92.6 0.1 add.135
  92.7 0.6 collective-permute-start.16
  93.3 1.0 collective-permute-start.22
  94.4 5.8 %collective-permute-done.16 = f32[2,128,256]{2,1,0:T(8,128)S(1)} collective-permute-done((f32[2,128,256]{2,1,0:T(8,128)S(1)}, f32[2,128,256]{2,1,0:T(8,128)S(1)}, u32[]{:S(2)}, u32[]{:S(2)}) %collective-permute-start.16) | collective-permute-done | bytes 262176 | tf_op jit(solution)/shard_map/ppermute | solution.py:219
  100.2 2.1 %collective-permute-start.17 = (f32[2,128,256]{2,1,0:T(8,128)S(1)}, f32[2,128,256]{2,1,0:T(8,128)S(1)}, u32[]{:S(2)}, u32[]{:S(2)}) collective-permute-start(f32[2,128,256]{2,1,0:T(8,128)S(1)} %fusion.8.own_ref), channel_id=1, source_target_pairs={{0,1},{1,0},{2,3},{3,2},{4,5},{5,4},{6,7},{7,6},{8,9},{9,8},{10,11... | collective-permute-start | bytes 786440 | tf_op jit(solution)/shard_map/ppermute | solution.py:219
  102.4 0.1 collective-permute-start.32
  102.5 1.3 %collective-permute-done.32.twin_ref = f32[200,128]{1,0:T(8,128)S(1)} collective-permute-done((f32[200,128]{1,0:T(8,128)S(1)}, f32[200,128]{1,0:T(8,128)S(1)}, u32[]{:S(2)}, u32[]{:S(2)}) %collective-permute-start.32) | collective-permute-done | bytes 102432 | tf_op jit(solution)/shard_map/ppermute | solution.py:219
  103.8 2.6 %finish.1 = (f32[256,256]{1,0:T(8,128)}, f32[1,256]{1,0:T(1,128)}, f32[64,256]{1,0:T(8,128)}, f32[64,256]{1,0:T(8,128)}) custom-call(s32[3]{0:T(128)S(1)} %pad_add_fusion.at_ref, f32[2,128,256]{2,1,0:T(8,128)S(1)} %fusion.8.own_ref, f32[2,128,256]{2,1,0:T(8,128)S(1)} %collective-permute-done.17.other_ref, f32[256,256]{1,0:T(8,128)S(1)} %pad_maximum_fusion.sum_ref.self_ref, ...), custom_call_target="tpu_custom_call" | custom-call | flops 1000000000 | bytes 1048576 | tf_op jit(solution)/shard_map/finish/pallas_call | solution.py:202
  (34 shorter events, 0.3 us)
Async XLA Ops:
  0.6 16.3 %copy-start = (f32[256,1024]{1,0:T(8,128)S(1)}, f32[256,1024]{1,0:T(8,128)}, u32[]{:S(2)}) copy-start(f32[256,1024]{1,0:T(8,128)} %rows_ref.1) | copy-start | bytes 3145732
  2.0 12.2 %collective-permute-start.1 = (f32[32,1024]{1,0:T(8,128)S(1)}, f32[32,1024]{1,0:T(8,128)S(1)}, u32[]{:S(2)}, u32[]{:S(2)}) collective-permute-start(f32[32,1024]{1,0:T(8,128)S(1)} %get-tuple-element.22), channel_id=1, source_target_pairs={{0,40},{1,41},{2,42},{3,43}} | collective-permute-start | bytes 393224 | tf_op jit(solution)/shard_map/ppermute | solution.py:258
  9.0 6.5 %collective-permute-start.2 = (f32[32,1024]{1,0:T(8,128)S(1)}, f32[32,1024]{1,0:T(8,128)S(1)}, u32[]{:S(2)}, u32[]{:S(2)}) collective-permute-start(f32[32,1024]{1,0:T(8,128)S(1)} %get-tuple-element.16), channel_id=1, source_target_pairs={{0,8},{1,9},{2,10},{3,11}} | collective-permute-start | bytes 393224 | tf_op jit(solution)/shard_map/ppermute | solution.py:258
  10.3 7.6 %collective-permute-start.3 = (f32[32,1024]{1,0:T(8,128)S(1)}, f32[32,1024]{1,0:T(8,128)S(1)}, u32[]{:S(2)}, u32[]{:S(2)}) collective-permute-start(f32[32,1024]{1,0:T(8,128)S(1)} %get-tuple-element.21), channel_id=1, source_target_pairs={{0,36},{1,37},{2,38},{3,39}} | collective-permute-start | bytes 393224 | tf_op jit(solution)/shard_map/ppermute | solution.py:258
  11.7 7.3 %collective-permute-start.4 = (f32[32,1024]{1,0:T(8,128)S(1)}, f32[32,1024]{1,0:T(8,128)S(1)}, u32[]{:S(2)}, u32[]{:S(2)}) collective-permute-start(f32[32,1024]{1,0:T(8,128)S(1)} %get-tuple-element.20), channel_id=1, source_target_pairs={{0,44},{1,45},{2,46},{3,47}} | collective-permute-start | bytes 393224 | tf_op jit(solution)/shard_map/ppermute | solution.py:258
  13.0 6.0 %collective-permute-start.5 = (f32[32,1024]{1,0:T(8,128)S(1)}, f32[32,1024]{1,0:T(8,128)S(1)}, u32[]{:S(2)}, u32[]{:S(2)}) collective-permute-start(f32[32,1024]{1,0:T(8,128)S(1)} %get-tuple-element.19), channel_id=1, source_target_pairs={{0,4},{1,5},{2,6},{3,7}} | collective-permute-start | bytes 393224 | tf_op jit(solution)/shard_map/ppermute | solution.py:258
  14.3 4.7 %collective-permute-start.6 = (f32[32,1024]{1,0:T(8,128)S(1)}, f32[32,1024]{1,0:T(8,128)S(1)}, u32[]{:S(2)}, u32[]{:S(2)}) collective-permute-start(f32[32,1024]{1,0:T(8,128)S(1)} %get-tuple-element.18), channel_id=1, source_target_pairs={{0,12},{1,13},{2,14},{3,15}} | collective-permute-start | bytes 393224 | tf_op jit(solution)/shard_map/ppermute | solution.py:258
  15.6 4.6 %collective-permute-start.7 = (f32[32,1024]{1,0:T(8,128)S(1)}, f32[32,1024]{1,0:T(8,128)S(1)}, u32[]{:S(2)}, u32[]{:S(2)}) collective-permute-start(f32[32,1024]{1,0:T(8,128)S(1)} %get-tuple-element.17), channel_id=1, source_target_pairs={{0,32},{1,33},{2,34},{3,35}} | collective-permute-start | bytes 393224 | tf_op jit(solution)/shard_map/ppermute | solution.py:258
  18.0 4.9 %collective-permute-start.18 = (f32[1,256,256]{2,1,0:T(8,128)S(1)}, f32[1,256,256]{2,1,0:T(8,128)S(1)}, u32[]{:S(2)}, u32[]{:S(2)}) collective-permute-start(f32[1,256,256]{2,1,0:T(8,128)S(1)} %convolution_bitcast_fusion), channel_id=1, source_target_pairs={{0,1},{1,0},{2,3},{3,2},{4,5},{5,4},{6,7},{7,6},{8,9},{9,8},{10,11... | collective-permute-start | bytes 786440 | tf_op jit(solution)/shard_map/ppermute | solution.py:219
  20.3 6.7 %collective-permute-start.10 = (f32[32,1024]{1,0:T(8,128)S(1)}, f32[32,1024]{1,0:T(8,128)S(1)}, u32[]{:S(2)}, u32[]{:S(2)}) collective-permute-start(f32[32,1024]{1,0:T(8,128)S(1)} %add_select_fusion.1), channel_id=1, source_target_pairs={{0,80},{1,81},{2,82},{3,83},{4,84},{5,85},{6,86},{7,87},{8,88},{9,... | collective-permute-start | bytes 393224 | tf_op jit(solution)/shard_map/ppermute | solution.py:265
  21.6 6.7 %collective-permute-start.11 = (f32[32,1024]{1,0:T(8,128)S(1)}, f32[32,1024]{1,0:T(8,128)S(1)}, u32[]{:S(2)}, u32[]{:S(2)}) collective-permute-start(f32[32,1024]{1,0:T(8,128)S(1)} %add_select_fusion.1), channel_id=1, source_target_pairs={{0,208},{1,209},{2,210},{3,211},{4,212},{5,213},{6,214},{7,215},{8... | collective-permute-start | bytes 393224 | tf_op jit(solution)/shard_map/ppermute | solution.py:265
  23.0 6.6 %collective-permute-start.19 = (f32[1,128,256]{2,1,0:T(8,128)S(1)}, f32[1,128,256]{2,1,0:T(8,128)S(1)}, u32[]{:S(2)}, u32[]{:S(2)}) collective-permute-start(f32[1,128,256]{2,1,0:T(8,128)S(1)} %dynamic-slice_bitcast_fusion.2), channel_id=1, source_target_pairs={{0,2},{2,0},{1,3},{3,1},{4,6},{6,4},{5,7},{7,5},{8,10},{10,8},{9,1... | collective-permute-start | bytes 393224 | tf_op jit(solution)/shard_map/ppermute | solution.py:219
  24.3 6.6 %collective-permute-start.12 = (f32[32,1024]{1,0:T(8,128)S(1)}, f32[32,1024]{1,0:T(8,128)S(1)}, u32[]{:S(2)}, u32[]{:S(2)}) collective-permute-start(f32[32,1024]{1,0:T(8,128)S(1)} %add_select_fusion.1), channel_id=1, source_target_pairs={{0,64},{1,65},{2,66},{3,67},{4,68},{5,69},{6,70},{7,71},{8,72},{9,... | collective-permute-start | bytes 393224 | tf_op jit(solution)/shard_map/ppermute | solution.py:265
  25.6 8.2 %collective-permute-start.13 = (f32[32,1024]{1,0:T(8,128)S(1)}, f32[32,1024]{1,0:T(8,128)S(1)}, u32[]{:S(2)}, u32[]{:S(2)}) collective-permute-start(f32[32,1024]{1,0:T(8,128)S(1)} %add_select_fusion.1), channel_id=1, source_target_pairs={{0,192},{1,193},{2,194},{3,195},{4,196},{5,197},{6,198},{7,199},{8... | collective-permute-start | bytes 393224 | tf_op jit(solution)/shard_map/ppermute | solution.py:265
  26.9 10.9 %collective-permute-start.14 = (f32[32,1024]{1,0:T(8,128)S(1)}, f32[32,1024]{1,0:T(8,128)S(1)}, u32[]{:S(2)}, u32[]{:S(2)}) collective-permute-start(f32[32,1024]{1,0:T(8,128)S(1)} %add_select_fusion.1), channel_id=1, source_target_pairs={{0,16},{1,17},{2,18},{3,19},{4,20},{5,21},{6,22},{7,23},{8,24},{9,... | collective-permute-start | bytes 393224 | tf_op jit(solution)/shard_map/ppermute | solution.py:265
  28.3 9.6 %collective-permute-start.8 = (f32[32,1024]{1,0:T(8,128)S(1)}, f32[32,1024]{1,0:T(8,128)S(1)}, u32[]{:S(2)}, u32[]{:S(2)}) collective-permute-start(f32[32,1024]{1,0:T(8,128)S(1)} %add_select_fusion.1), channel_id=1, source_target_pairs={{0,144},{1,145},{2,146},{3,147},{4,148},{5,149},{6,150},{7,151},{8... | collective-permute-start | bytes 393224 | tf_op jit(solution)/shard_map/ppermute | solution.py:265
  29.6 8.3 %collective-permute-start.9 = (f32[32,1024]{1,0:T(8,128)S(1)}, f32[32,1024]{1,0:T(8,128)S(1)}, u32[]{:S(2)}, u32[]{:S(2)}) collective-permute-start(f32[32,1024]{1,0:T(8,128)S(1)} %add_select_fusion.1), channel_id=1, source_target_pairs={{0,128},{1,129},{2,130},{3,131},{4,132},{5,133},{6,134},{7,135},{8... | collective-permute-start | bytes 393224 | tf_op jit(solution)/shard_map/ppermute | solution.py:265
  30.9 49.5 %collective-permute-start = (f32[256,1024]{1,0:T(8,128)S(1)}, f32[256,1024]{1,0:T(8,128)S(1)}, u32[]{:S(2)}, u32[]{:S(2)}) collective-permute-start(f32[256,1024]{1,0:T(8,128)S(1)} %copy-done), channel_id=1, source_target_pairs={{252,0},{0,4},{4,8},{8,12},{12,16},{16,20},{20,24},{24,28},{28,32}... | collective-permute-start | bytes 3145736 | tf_op jit(solution)/shard_map/ppermute | solution.py:224
  33.8 10.5 %collective-permute-start.20 = (f32[1,128,256]{2,1,0:T(8,128)S(1)}, f32[1,128,256]{2,1,0:T(8,128)S(1)}, u32[]{:S(2)}, u32[]{:S(2)}) collective-permute-start(f32[1,128,256]{2,1,0:T(8,128)S(1)} %fusion.7), channel_id=1, source_target_pairs={{0,1},{1,0},{2,3},{3,2},{4,5},{5,4},{6,7},{7,6},{8,9},{9,8},{10,11... | collective-permute-start | bytes 393224 | tf_op jit(solution)/shard_map/ppermute | solution.py:219
  39.0 41.4 %all-to-all-start = ((f32[8,32,1024]{2,1,0:T(8,128)}), f32[8,32,1024]{2,1,0:T(8,128)S(1)}, u32[]{:S(2)}, u32[]{:S(2)}) async-start(f32[8,32,1024]{2,1,0:T(8,128)} %broadcast_in_dim.6), calls=%async_computation | async-start | bytes 2097152 | tf_op jit(solution)/shard_map/all_to_all | solution.py:272
  52.0 0.7 copy-start.1
  60.6 12.0 %collective-permute-start.23 = (f32[200,128]{1,0:T(8,128)S(1)}, f32[200,128]{1,0:T(8,128)}, u32[]{:S(2)}, u32[]{:S(2)}) collective-permute-start(f32[200,128]{1,0:T(8,128)S(1)} %factor_second.1), channel_id=1, source_target_pairs={{0,128},{1,129},{2,130},{3,131}} | collective-permute-start | bytes 307208 | tf_op jit(solution)/shard_map/ppermute | solution.py:284
  65.3 7.3 %collective-permute-start.24 = (f32[200,128]{1,0:T(8,128)S(1)}, f32[200,128]{1,0:T(8,128)}, u32[]{:S(2)}, u32[]{:S(2)}) collective-permute-start(f32[200,128]{1,0:T(8,128)S(1)} %factor_second.1), channel_id=1, source_target_pairs={{0,64},{1,65},{2,66},{3,67}} | collective-permute-start | bytes 307208 | tf_op jit(solution)/shard_map/ppermute | solution.py:284
  70.7 2.9 %collective-permute-start.25 = (f32[200,128]{1,0:T(8,128)S(1)}, f32[200,128]{1,0:T(8,128)}, u32[]{:S(2)}, u32[]{:S(2)}) collective-permute-start(f32[200,128]{1,0:T(8,128)S(1)} %factor_second.1), channel_id=1, source_target_pairs={{0,192},{1,193},{2,194},{3,195}} | collective-permute-start | bytes 307208 | tf_op jit(solution)/shard_map/ppermute | solution.py:284
  75.3 12.3 %collective-permute-start.26 = (f32[200,128]{1,0:T(8,128)}, f32[200,128]{1,0:T(8,128)S(1)}, u32[]{:S(2)}, u32[]{:S(2)}) collective-permute-start(f32[200,128]{1,0:T(8,128)} %add_select_fusion.4), channel_id=1, source_target_pairs={{0,16},{64,80},{128,144},{192,208},{1,17},{65,81},{129,145},{193,2... | collective-permute-start | bytes 307208 | tf_op jit(solution)/shard_map/ppermute | solution.py:284
  76.6 11.0 %collective-permute-start.27 = (f32[200,128]{1,0:T(8,128)}, f32[200,128]{1,0:T(8,128)}, u32[]{:S(2)}, u32[]{:S(2)}) collective-permute-start(f32[200,128]{1,0:T(8,128)} %add_select_fusion.4), channel_id=1, source_target_pairs={{0,48},{64,112},{128,176},{192,240},{1,49},{65,113},{129,177},{193... | collective-permute-start | bytes 307208 | tf_op jit(solution)/shard_map/ppermute | solution.py:284
  78.5 9.1 %collective-permute-start.28 = (f32[200,128]{1,0:T(8,128)}, f32[200,128]{1,0:T(8,128)}, u32[]{:S(2)}, u32[]{:S(2)}) collective-permute-start(f32[200,128]{1,0:T(8,128)} %add_select_fusion.4), channel_id=1, source_target_pairs={{0,32},{64,96},{128,160},{192,224},{1,33},{65,97},{129,161},{193,2... | collective-permute-start | bytes 307208 | tf_op jit(solution)/shard_map/ppermute | solution.py:284
  82.4 10.2 %collective-permute-start.15 = (f32[2,256,256]{2,1,0:T(8,128)S(1)}, f32[2,256,256]{2,1,0:T(8,128)S(1)}, u32[]{:S(2)}, u32[]{:S(2)}) collective-permute-start(f32[2,256,256]{2,1,0:T(8,128)S(1)} %cross.1), channel_id=1, source_target_pairs={{0,1},{1,0},{2,3},{3,2},{4,5},{5,4},{6,7},{7,6},{8,9},{9,8},{10,11... | collective-permute-start | bytes 1572872 | tf_op jit(solution)/shard_map/ppermute | solution.py:219
  87.5 5.8 %collective-permute-start.21 = (f32[1,2,64,256]{3,2,1,0:T(8,128)S(1)}, f32[1,2,64,256]{3,2,1,0:T(8,128)S(1)}, u32[]{:S(2)}, u32[]{:S(2)}) collective-permute-start(f32[1,2,64,256]{3,2,1,0:T(8,128)S(1)} %dynamic-slice_bitcast_fusion.1), channel_id=1, source_target_pairs={{0,1},{1,0},{2,3},{3,2},{4,5},{5,4},{6,7},{7,6},{8,9},{9,8},{10,11... | collective-permute-start | bytes 393224 | tf_op jit(solution)/shard_map/ppermute | solution.py:219
  88.6 13.7 %collective-permute-start.29 = (f32[200,128]{1,0:T(8,128)S(1)}, f32[200,128]{1,0:T(8,128)S(1)}, u32[]{:S(2)}, u32[]{:S(2)}) collective-permute-start(f32[200,128]{1,0:T(8,128)S(1)} %add_select_fusion.3), channel_id=1, source_target_pairs={{0,8},{16,24},{32,40},{48,56},{64,72},{80,88},{96,104},{112,120},{... | collective-permute-start | bytes 307208 | tf_op jit(solution)/shard_map/ppermute | solution.py:284
  89.9 12.4 %collective-permute-start.30 = (f32[200,128]{1,0:T(8,128)S(1)}, f32[200,128]{1,0:T(8,128)S(1)}, u32[]{:S(2)}, u32[]{:S(2)}) collective-permute-start(f32[200,128]{1,0:T(8,128)S(1)} %add_select_fusion.3), channel_id=1, source_target_pairs={{0,4},{16,20},{32,36},{48,52},{64,68},{80,84},{96,100},{112,116},{... | collective-permute-start | bytes 307208 | tf_op jit(solution)/shard_map/ppermute | solution.py:284
  91.2 11.1 %collective-permute-start.31 = (f32[200,128]{1,0:T(8,128)S(1)}, f32[200,128]{1,0:T(8,128)S(1)}, u32[]{:S(2)}, u32[]{:S(2)}) collective-permute-start(f32[200,128]{1,0:T(8,128)S(1)} %add_select_fusion.3), channel_id=1, source_target_pairs={{0,12},{16,28},{32,44},{48,60},{64,76},{80,92},{96,108},{112,124},... | collective-permute-start | bytes 307208 | tf_op jit(solution)/shard_map/ppermute | solution.py:284
  92.7 7.5 %collective-permute-start.16 = (f32[2,128,256]{2,1,0:T(8,128)S(1)}, f32[2,128,256]{2,1,0:T(8,128)S(1)}, u32[]{:S(2)}, u32[]{:S(2)}) collective-permute-start(f32[2,128,256]{2,1,0:T(8,128)S(1)} %dynamic-slice_bitcast_fusion), channel_id=1, source_target_pairs={{0,2},{2,0},{1,3},{3,1},{4,6},{6,4},{5,7},{7,5},{8,10},{10,8},{9,1... | collective-permute-start | bytes 786440 | tf_op jit(solution)/shard_map/ppermute | solution.py:219
  93.3 9.2 %collective-permute-start.22 = (f32[1,64,256]{2,1,0:T(8,128)S(1)}, f32[1,64,256]{2,1,0:T(8,128)S(1)}, u32[]{:S(2)}, u32[]{:S(2)}) collective-permute-start(f32[1,64,256]{2,1,0:T(8,128)S(1)} %dynamic-slice_bitcast_fusion.3), channel_id=1, source_target_pairs={{0,2},{2,0},{1,3},{3,1},{4,6},{6,4},{5,7},{7,5},{8,10},{10,8},{9,1... | collective-permute-start | bytes 196616 | tf_op jit(solution)/shard_map/ppermute | solution.py:219
  100.2 3.6 %collective-permute-start.17 = (f32[2,128,256]{2,1,0:T(8,128)S(1)}, f32[2,128,256]{2,1,0:T(8,128)S(1)}, u32[]{:S(2)}, u32[]{:S(2)}) collective-permute-start(f32[2,128,256]{2,1,0:T(8,128)S(1)} %fusion.8.own_ref), channel_id=1, source_target_pairs={{0,1},{1,0},{2,3},{3,2},{4,5},{5,4},{6,7},{7,6},{8,9},{9,8},{10,11... | collective-permute-start | bytes 786440 | tf_op jit(solution)/shard_map/ppermute | solution.py:219
  102.4 1.4 %collective-permute-start.32 = (f32[200,128]{1,0:T(8,128)S(1)}, f32[200,128]{1,0:T(8,128)S(1)}, u32[]{:S(2)}, u32[]{:S(2)}) collective-permute-start(f32[200,128]{1,0:T(8,128)S(1)} %add_select_fusion.2.mine_ref), channel_id=1, source_target_pairs={{0,1},{1,0},{2,3},{3,2},{4,5},{5,4},{6,7},{7,6},{8,9},{9,8},{10,11... | collective-permute-start | bytes 307208 | tf_op jit(solution)/shard_map/ppermute | solution.py:219

commit v4 on v3

--- a/solution.py
+++ b/solution.py
@@ -9,9 +9,8 @@
 from jax.sharding import PartitionSpec as P
 
 
-BLK = ("zh", "zl", "xh", "y")
-PLANE = ("zl", "y")
-STACK = ("zh", "xh")
+BLK = ("z", "xh", "y")
+PLANE = ("xh", "y")
 PAR = ("xl", "core")
 ALL = BLK + PAR
 HIGHEST = lax.Precision.HIGHEST
@@ -78,18 +77,18 @@
             )
 
 
-def factor_first_kernel(sum_ref, tile_ref, inverse_ref):
+def factor_first_kernel(sum_ref, state_ref):
     n = sum_ref.shape[0]
+    tile_ref, inverse_ref = state_ref.at[0], state_ref.at[1]
     tile_ref[...] = sum_ref[...] + ridge_shift * unit(n, n).astype(jnp.float32)
     inverse_ref[...] = jnp.zeros((n, n), jnp.float32)
     eliminate(tile_ref, inverse_ref, 0, n // CHUNK // 2)
 
 
-def factor_second_kernel(at_ref, tile_in_ref, inverse_in_ref, energy_ref, packed_ref, tile_ref, inverse_ref):
-    n = tile_ref.shape[0]
+def factor_second_kernel(at_ref, state_ref, energy_ref, packed_ref):
+    n = state_ref.shape[-1]
     share = n // 4
-    tile_ref[...] = tile_in_ref[...]
-    inverse_ref[...] = inverse_in_ref[...]
+    tile_ref, inverse_ref = state_ref.at[0], state_ref.at[1]
     eliminate(tile_ref, inverse_ref, n // CHUNK // 2, n // CHUNK)
     half = n // 2
     start = pl.multiple_of(at_ref[2] * share, share)
@@ -118,27 +117,32 @@
     n = total.shape[0]
     return pl.pallas_call(
         factor_first_kernel,
-        out_shape=(f32(n, n), f32(n, n)),
+        out_shape=f32(2, n, n),
         in_specs=[VMEM],
-        out_specs=(VMEM,) * 2,
+        out_specs=VMEM,
         name="factor_first",
         compiler_params=GRANT,
         cost_estimate=cost(8 * 10**9),
     )(total)
 
 
-def factor_second(at, tile, inverse, energies):
-    n = tile.shape[0]
+def factor_second(at, state, energies):
+    n = state.shape[-1]
+
+    def kernel(at_ref, state_in_ref, energy_ref, packed_ref, state_ref):
+        state_ref[...] = state_in_ref[...]
+        factor_second_kernel(at_ref, state_ref, energy_ref, packed_ref)
+
     return pl.pallas_call(
-        factor_second_kernel,
+        kernel,
         out_shape=f32(3 * n // 4 + 8, n // 2),
-        in_specs=[SMEM] + [VMEM] * 3,
+        in_specs=[SMEM] + [VMEM] * 2,
         out_specs=VMEM,
-        scratch_shapes=[pltpu.VMEM((n, n), jnp.float32)] * 2,
+        scratch_shapes=[pltpu.VMEM((2, n, n), jnp.float32)],
         name="factor_second",
         compiler_params=GRANT,
         cost_estimate=cost(8 * 10**9),
-    )(at, tile, inverse, energies)
+    )(at, state, energies)
 
 
 def cross_kernel(rows_ref, prev_ref, lead_ref, out_ref):
@@ -244,7 +248,7 @@
 
 
 SCATTER_ORDER = (6, 2, 5, 7, 1, 3, 4)
-STACK_ORDER = (5, 4, 3, 7, 2, 6, 1)
+STACK_ORDER = (4, 3, 5, 2, 6, 1, 7)
 
 
 def total(values):
@@ -255,15 +259,15 @@
     parts = lax.axis_size(PLANE)
     part = rows.shape[0] // parts
     got = [
-        lax.ppermute(rows[k * part : (k + 1) * part], BLK, [(0, k // 4 * 8 + k % 4)])
+        lax.ppermute(rows[k * part : (k + 1) * part], BLK, [(0, k)])
         for k in SCATTER_ORDER
     ]
     return jnp.where(lax.axis_index(PLANE) == 0, rows[:part], total(got))
 
 
-def along_stack(piece):
-    got = [lax.ppermute(piece, STACK, [(0, k)]) for k in STACK_ORDER]
-    return jnp.where(lax.axis_index(STACK) == 0, piece, total(got))
+def along_z(piece):
+    got = [lax.ppermute(piece, "z", [(0, k)]) for k in STACK_ORDER]
+    return jnp.where(lax.axis_index("z") == 0, piece, total(got))
 
 
 def over_plane(piece):
@@ -273,8 +277,7 @@
 
 
 def small_tree(value):
-    zh, zl, xh, y = (lax.axis_index(a) for a in BLK)
-    z = zh * 2 + zl
+    z, xh, y = (lax.axis_index(a) for a in BLK)
     rounds = (
         ([[(0, 8 * k)] for k in (4, 2, 6)], z == 0),
         ([[(8 * k, 8 * k + d) for k in range(0, 8, 2)] for d in (4, 12, 8)], (z % 2 == 0) & (xh == 0)),
@@ -300,10 +303,10 @@
     self_sum = jnp.concatenate(
         [jnp.where(upper, own[0], other[0]), jnp.where(upper, other[0], own[0])]
     )
-    piece = along_stack(piece)
-    tile, inverse = factor_first(self_sum)
+    piece = along_z(piece)
+    state = factor_first(self_sum)
     lead_rows = over_plane(piece).reshape(log_derivs.shape)
-    packed = factor_second(at, tile, inverse, energy_row)
+    packed = factor_second(at, state, energy_row)
     packed = small_tree(packed)
     twin = swapped(packed, "core")
     cycle_rows = sum_scattered(outer_tile(log_derivs, prev_rows)[None])[0]
@@ -316,7 +319,7 @@
 
 
 def solution(mesh):
-    torus = Mesh(mesh.devices.reshape(4, 2, 2, 4, 2, 2), ALL)
+    torus = Mesh(mesh.devices.reshape(8, 2, 4, 2, 2), ALL)
     in_specs = (P(BLK, PAR), P(BLK))
     out_specs = (P(BLK, None), P(BLK), P(ALL, None), P(ALL, None))
     return jax.shard_map(

time: 108 us -> 102 us (0.944)
  starting transfers between devices: 66.5 us -> 60.2 us
  waiting for transfers between devices: 10.3 us -> 11.6 us
    ppermute x9, starting transfers between devices: 14.4 us -> 10.8 us  [swapped(): return lax.ppermute(value, axis, [(0, 1), (1, 0)])]
    ppermute x9, starting transfers between devices: 21.1 us -> 18.4 us  [small_tree(): got = [lax.ppermute(value, BLK, route) for route in routes]]
    ppermute x1, starting transfers between devices: 1.94 us -> 0.08 us  [passed_along(): lax.ppermute(block, axis, [((i - distance) % count, i) for i in range(cou...]
    ppermute x14, waiting for transfers between devices: 2.16 us -> 3.48 us  [the longest x7 2.29 us: along_z(): got = [lax.ppermute(piece, 'z', [(0, k)]) for k in STACK_ORDER]]
    ppermute x14, starting transfers between devices: 23.9 us -> 25 us  [the longest x7 15.9 us: scatter_lead(): lax.ppermute(rows[k * part:(k + 1) * part], BLK, [(0, k)])]
  transfers between devices with their start and end apart: 34 -> 34, of which waited for: 5 -> 5; matrix products, arithmetic and copies ran while one was open for 6% -> 6% of each run, Pallas kernels for 16% -> 17%
where the time goes in v4:
time: 102 us; the launch traced here: 101 us
  starting transfers between devices  60.2 us (59%)
  Pallas kernels  20 us (20%)
  waiting for transfers between devices  11.6 us (11%)
  local copies, waits for them, and re-layouts  3.25 us (3%)
  other arithmetic  3.18 us (3%)
  matrix products  2.07 us (2%)
  between operations  1.07 us (1%)
    ppermute x9, starting transfers between devices, small_tree(): got = [lax.ppermute(value, BLK, route) for route in routes]  18.4 us
    ppermute x7, starting transfers between devices, scatter_lead(): lax.ppermute(rows[k * part:(k + 1) * part], BLK, [(0, k)])  15.9 us
    ppermute x9, starting transfers between devices, swapped(): return lax.ppermute(value, axis, [(0, 1), (1, 0)])  10.8 us
    ppermute x7, starting transfers between devices, along_z(): got = [lax.ppermute(piece, 'z', [(0, k)]) for k in STACK_ORDER]  9.07 us
    pallas_call x1, Pallas kernels, factor_second(): pl.pallas_call(kernel, out_shape=f32(3 * n // 4 + 8, n // 2), in_specs=[S...  7.92 us
    pallas_call x1, Pallas kernels, factor_first(): pl.pallas_call(factor_first_kernel, out_shape=f32(2, n, n), in_specs=[VME...  7.6 us
    ppermute x9, waiting for transfers between devices, swapped(): return lax.ppermute(value, axis, [(0, 1), (1, 0)])  7.06 us
    all_to_all x1, starting transfers between devices, over_plane(): lax.all_to_all(copies, PLANE, split_axis=0, concat_axis=0, tiled=True)  5.89 us
  transfers between devices with their start and end apart: 34, of which 5 were waited for; matrix products, arithmetic and copies ran while one was open for 6% of the time, Pallas kernels for 17%

profile of v4, /device:TPU:1, one launch (start us, length us, event | category | flops | bytes accessed | tf_op | source)
XLA Modules:
  0.0 101.3 jit_solution(14550185385857800045)
XLA Ops:
  0.6 1.4 %fusion.1 = (f32[32,1024]{1,0:T(8,128)S(1)}, f32[32,1024]{1,0:T(8,128)S(1)}, f32[32,1024]{1,0:T(8,128)S(1)}, f32[32,1024]{1,0:T(8,128)S(1)}, f32[32,1024]{1,0:T(...) fusion(f32[256,1024]{1,0:T(8,128)} %rows_ref.1), kind=kLoop, calls=%fused_computation.17 | loop fusion | bytes 1835008 | tf_op jit(solution)/shard_map/slice | solution.py:262
  2.0 8.1 %collective-permute-start.1 = (f32[32,1024]{1,0:T(8,128)S(1)}, f32[32,1024]{1,0:T(8,128)S(1)}, u32[]{:S(2)}, u32[]{:S(2)}) collective-permute-start(f32[32,1024]{1,0:T(8,128)S(1)} %get-tuple-element.18), channel_id=1, source_target_pairs={{0,24},{1,25},{2,26},{3,27}} | collective-permute-start | bytes 393224 | tf_op jit(solution)/shard_map/ppermute | solution.py:262
  10.1 1.3 %collective-permute-start.2 = (f32[32,1024]{1,0:T(8,128)S(1)}, f32[32,1024]{1,0:T(8,128)S(1)}, u32[]{:S(2)}, u32[]{:S(2)}) collective-permute-start(f32[32,1024]{1,0:T(8,128)S(1)} %get-tuple-element.12), channel_id=1, source_target_pairs={{0,8},{1,9},{2,10},{3,11}} | collective-permute-start | bytes 393224 | tf_op jit(solution)/shard_map/ppermute | solution.py:262
  11.5 1.3 %collective-permute-start.3 = (f32[32,1024]{1,0:T(8,128)S(1)}, f32[32,1024]{1,0:T(8,128)S(1)}, u32[]{:S(2)}, u32[]{:S(2)}) collective-permute-start(f32[32,1024]{1,0:T(8,128)S(1)} %get-tuple-element.17), channel_id=1, source_target_pairs={{0,20},{1,21},{2,22},{3,23}} | collective-permute-start | bytes 393224 | tf_op jit(solution)/shard_map/ppermute | solution.py:262
  12.8 1.3 %collective-permute-start.4 = (f32[32,1024]{1,0:T(8,128)S(1)}, f32[32,1024]{1,0:T(8,128)S(1)}, u32[]{:S(2)}, u32[]{:S(2)}) collective-permute-start(f32[32,1024]{1,0:T(8,128)S(1)} %get-tuple-element.16), channel_id=1, source_target_pairs={{0,28},{1,29},{2,30},{3,31}} | collective-permute-start | bytes 393224 | tf_op jit(solution)/shard_map/ppermute | solution.py:262
  14.1 1.3 %collective-permute-start.5 = (f32[32,1024]{1,0:T(8,128)S(1)}, f32[32,1024]{1,0:T(8,128)S(1)}, u32[]{:S(2)}, u32[]{:S(2)}) collective-permute-start(f32[32,1024]{1,0:T(8,128)S(1)} %get-tuple-element.15), channel_id=1, source_target_pairs={{0,4},{1,5},{2,6},{3,7}} | collective-permute-start | bytes 393224 | tf_op jit(solution)/shard_map/ppermute | solution.py:262
  15.4 0.0 collective-permute-done.1
  15.4 1.3 %collective-permute-start.6 = (f32[32,1024]{1,0:T(8,128)S(1)}, f32[32,1024]{1,0:T(8,128)S(1)}, u32[]{:S(2)}, u32[]{:S(2)}) collective-permute-start(f32[32,1024]{1,0:T(8,128)S(1)} %get-tuple-element.14), channel_id=1, source_target_pairs={{0,12},{1,13},{2,14},{3,15}} | collective-permute-start | bytes 393224 | tf_op jit(solution)/shard_map/ppermute | solution.py:262
  16.7 0.0 collective-permute-done.2
  16.7 1.3 %collective-permute-start.7 = (f32[32,1024]{1,0:T(8,128)S(1)}, f32[32,1024]{1,0:T(8,128)S(1)}, u32[]{:S(2)}, u32[]{:S(2)}) collective-permute-start(f32[32,1024]{1,0:T(8,128)S(1)} %get-tuple-element.13), channel_id=1, source_target_pairs={{0,16},{1,17},{2,18},{3,19}} | collective-permute-start | bytes 393224 | tf_op jit(solution)/shard_map/ppermute | solution.py:262
  18.0 1.0 %convolution_bitcast_fusion = f32[1,256,256]{2,1,0:T(8,128)S(1)} fusion(f32[256,1024]{1,0:T(8,128)S(1)} %copy-done), kind=kOutput, calls=%fused_computation | convolution fusion | flops 805306368 | bytes 1310720 | tf_op jit(solution)/shard_map/dot_general | solution.py:24
  19.0 0.0 collective-permute-done.3
  19.1 1.0 %collective-permute-start.18 = (f32[1,256,256]{2,1,0:T(8,128)S(1)}, f32[1,256,256]{2,1,0:T(8,128)S(1)}, u32[]{:S(2)}, u32[]{:S(2)}) collective-permute-start(f32[1,256,256]{2,1,0:T(8,128)S(1)} %convolution_bitcast_fusion), channel_id=1, source_target_pairs={{0,1},{1,0},{2,3},{3,2},{4,5},{5,4},{6,7},{7,6},{8,9},{9,8},{10,11... | collective-permute-start | bytes 786440 | tf_op jit(solution)/shard_map/ppermute | solution.py:223
  20.1 0.0 collective-permute-done.4
  20.1 1.2 %collective-permute-done.7 = f32[32,1024]{1,0:T(8,128)S(1)} collective-permute-done((f32[32,1024]{1,0:T(8,128)S(1)}, f32[32,1024]{1,0:T(8,128)S(1)}, u32[]{:S(2)}, u32[]{:S(2)}) %collective-permute-start.7) | collective-permute-done | bytes 131104 | tf_op jit(solution)/shard_map/ppermute | solution.py:262
  21.3 0.1 add_select_fusion.1
  21.4 1.3 %collective-permute-start.10 = (f32[32,1024]{1,0:T(8,128)S(1)}, f32[32,1024]{1,0:T(8,128)S(1)}, u32[]{:S(2)}, u32[]{:S(2)}) collective-permute-start(f32[32,1024]{1,0:T(8,128)S(1)} %add_select_fusion.1), channel_id=1, source_target_pairs={{0,160},{1,161},{2,162},{3,163},{4,164},{5,165},{6,166},{7,167},{8... | collective-permute-start | bytes 393224 | tf_op jit(solution)/shard_map/ppermute | solution.py:269
  22.7 1.3 %collective-permute-start.11 = (f32[32,1024]{1,0:T(8,128)S(1)}, f32[32,1024]{1,0:T(8,128)S(1)}, u32[]{:S(2)}, u32[]{:S(2)}) collective-permute-start(f32[32,1024]{1,0:T(8,128)S(1)} %add_select_fusion.1), channel_id=1, source_target_pairs={{0,64},{1,65},{2,66},{3,67},{4,68},{5,69},{6,70},{7,71},{8,72},{9,... | collective-permute-start | bytes 393224 | tf_op jit(solution)/shard_map/ppermute | solution.py:269
  24.1 0.4 collective-permute-start.19
  24.5 0.1 pad_add_fusion.at_ref
  24.5 1.3 %collective-permute-start.12 = (f32[32,1024]{1,0:T(8,128)S(1)}, f32[32,1024]{1,0:T(8,128)S(1)}, u32[]{:S(2)}, u32[]{:S(2)}) collective-permute-start(f32[32,1024]{1,0:T(8,128)S(1)} %add_select_fusion.1), channel_id=1, source_target_pairs={{0,192},{1,193},{2,194},{3,195},{4,196},{5,197},{6,198},{7,199},{8... | collective-permute-start | bytes 393224 | tf_op jit(solution)/shard_map/ppermute | solution.py:269
  25.8 1.3 %collective-permute-start.13 = (f32[32,1024]{1,0:T(8,128)S(1)}, f32[32,1024]{1,0:T(8,128)S(1)}, u32[]{:S(2)}, u32[]{:S(2)}) collective-permute-start(f32[32,1024]{1,0:T(8,128)S(1)} %add_select_fusion.1), channel_id=1, source_target_pairs={{0,32},{1,33},{2,34},{3,35},{4,36},{5,37},{6,38},{7,39},{8,40},{9,... | collective-permute-start | bytes 393224 | tf_op jit(solution)/shard_map/ppermute | solution.py:269
  27.1 0.0 collective-permute-done.10
  27.1 1.3 %collective-permute-start.14 = (f32[32,1024]{1,0:T(8,128)S(1)}, f32[32,1024]{1,0:T(8,128)S(1)}, u32[]{:S(2)}, u32[]{:S(2)}) collective-permute-start(f32[32,1024]{1,0:T(8,128)S(1)} %add_select_fusion.1), channel_id=1, source_target_pairs={{0,224},{1,225},{2,226},{3,227},{4,228},{5,229},{6,230},{7,231},{8... | collective-permute-start | bytes 393224 | tf_op jit(solution)/shard_map/ppermute | solution.py:269
  28.5 1.3 %collective-permute-start.8 = (f32[32,1024]{1,0:T(8,128)S(1)}, f32[32,1024]{1,0:T(8,128)S(1)}, u32[]{:S(2)}, u32[]{:S(2)}) collective-permute-start(f32[32,1024]{1,0:T(8,128)S(1)} %add_select_fusion.1), channel_id=1, source_target_pairs={{0,128},{1,129},{2,130},{3,131},{4,132},{5,133},{6,134},{7,135},{8... | collective-permute-start | bytes 393224 | tf_op jit(solution)/shard_map/ppermute | solution.py:269
  29.8 0.0 collective-permute-done.19
  29.8 1.3 %collective-permute-start.9 = (f32[32,1024]{1,0:T(8,128)S(1)}, f32[32,1024]{1,0:T(8,128)S(1)}, u32[]{:S(2)}, u32[]{:S(2)}) collective-permute-start(f32[32,1024]{1,0:T(8,128)S(1)} %add_select_fusion.1), channel_id=1, source_target_pairs={{0,96},{1,97},{2,98},{3,99},{4,100},{5,101},{6,102},{7,103},{8,104... | collective-permute-start | bytes 393224 | tf_op jit(solution)/shard_map/ppermute | solution.py:269
  31.1 0.0 collective-permute-done.12
  31.1 0.1 collective-permute-start
  31.2 1.3 %collective-permute-start.20 = (f32[1,128,256]{2,1,0:T(8,128)S(1)}, f32[1,128,256]{2,1,0:T(8,128)S(1)}, u32[]{:S(2)}, u32[]{:S(2)}) collective-permute-start(f32[1,128,256]{2,1,0:T(8,128)S(1)} %fusion.7), channel_id=1, source_target_pairs={{0,1},{1,0},{2,3},{3,2},{4,5},{5,4},{6,7},{7,6},{8,9},{9,8},{10,11... | collective-permute-start | bytes 393224 | tf_op jit(solution)/shard_map/ppermute | solution.py:223
  32.6 2.3 %collective-permute-done.9 = f32[32,1024]{1,0:T(8,128)S(1)} collective-permute-done((f32[32,1024]{1,0:T(8,128)S(1)}, f32[32,1024]{1,0:T(8,128)S(1)}, u32[]{:S(2)}, u32[]{:S(2)}) %collective-permute-start.9) | collective-permute-done | bytes 131104 | tf_op jit(solution)/shard_map/ppermute | solution.py:269
  34.8 0.1 add_select_fusion
  34.9 1.1 %broadcast_in_dim.6 = f32[8,32,1024]{2,1,0:T(8,128)} broadcast(f32[32,1024]{1,0:T(8,128)S(1)} %add_select_fusion), dimensions={1,2} | broadcast | bytes 1179648 | tf_op jit(solution)/shard_map/broadcast_in_dim | solution.py:275
  36.0 5.9 %all-to-all-start = ((f32[8,32,1024]{2,1,0:T(8,128)}), f32[8,32,1024]{2,1,0:T(8,128)S(1)}, u32[]{:S(2)}, u32[]{:S(2)}) async-start(f32[8,32,1024]{2,1,0:T(8,128)} %broadcast_in_dim.6), calls=%async_computation | async-start | bytes 2097152 | tf_op jit(solution)/shard_map/all_to_all | solution.py:276
  41.9 0.0 collective-permute-done.20
  42.0 7.6 %factor_first.1.state_in_ref = f32[2,256,256]{2,1,0:T(8,128)S(1)} custom-call(f32[256,256]{1,0:T(8,128)S(1)} %pad_maximum_fusion.sum_ref.self_ref), custom_call_target="tpu_custom_call" | custom-call | flops 8000000000 | bytes 1048576 | tf_op jit(solution)/shard_map/factor_first/pallas_call | solution.py:118
  49.6 0.0 copy-start.1
  49.6 0.7 copy-done.1
  50.2 7.9 %factor_second.1 = f32[200,128]{1,0:T(8,128)S(1)} custom-call(s32[3]{0:T(128)S(1)} %pad_add_fusion.at_ref, f32[2,256,256]{2,1,0:T(8,128)S(1)} %factor_first.1.state_in_ref, f32[1,256]{1,0:T(1,128)S(1)} %bitcast.42), custom_call_target="tpu_custom_call" | custom-call | flops 8000000000 | bytes 1048576 | tf_op jit(solution)/shard_map/factor_second/pallas_call | solution.py:136
  58.2 5.6 %collective-permute-start.23 = (f32[200,128]{1,0:T(8,128)S(1)}, f32[200,128]{1,0:T(8,128)}, u32[]{:S(2)}, u32[]{:S(2)}) collective-permute-start(f32[200,128]{1,0:T(8,128)S(1)} %factor_second.1), channel_id=1, source_target_pairs={{0,128},{1,129},{2,130},{3,131}} | collective-permute-start | bytes 307208 | tf_op jit(solution)/shard_map/ppermute | solution.py:287
  63.7 1.9 %collective-permute-start.24 = (f32[200,128]{1,0:T(8,128)S(1)}, f32[200,128]{1,0:T(8,128)}, u32[]{:S(2)}, u32[]{:S(2)}) collective-permute-start(f32[200,128]{1,0:T(8,128)S(1)} %factor_second.1), channel_id=1, source_target_pairs={{0,64},{1,65},{2,66},{3,67}} | collective-permute-start | bytes 307208 | tf_op jit(solution)/shard_map/ppermute | solution.py:287
  65.6 1.9 %collective-permute-start.25 = (f32[200,128]{1,0:T(8,128)S(1)}, f32[200,128]{1,0:T(8,128)}, u32[]{:S(2)}, u32[]{:S(2)}) collective-permute-start(f32[200,128]{1,0:T(8,128)S(1)} %factor_second.1), channel_id=1, source_target_pairs={{0,192},{1,193},{2,194},{3,195}} | collective-permute-start | bytes 307208 | tf_op jit(solution)/shard_map/ppermute | solution.py:287
  67.6 0.0 collective-permute-done.24
  67.6 1.0 %collective-permute-done.25 = f32[200,128]{1,0:T(8,128)} collective-permute-done((f32[200,128]{1,0:T(8,128)S(1)}, f32[200,128]{1,0:T(8,128)}, u32[]{:S(2)}, u32[]{:S(2)}) %collective-permute-start.25) | collective-permute-done | bytes 102432 | tf_op jit(solution)/shard_map/ppermute | solution.py:287
  68.6 1.7 %add_select_fusion.4 = f32[200,128]{1,0:T(8,128)} fusion(f32[200,128]{1,0:T(8,128)S(1)} %factor_second.1, f32[200,128]{1,0:T(8,128)} %collective-permute-done.25, f32[200,128]{1,0:T(8,128)} %collective-permute-done.23, f32[200,128]{1,0:T(8,128)} %collective-permute-done.24, pred[]{:T(512)S(6)} %eq.21), kind=kLoop, calls=%fused_computation.12 | loop fusion | flops 76800 | bytes 512001 | tf_op jit(solution)/shard_map/jit(_where)/select_n | solution.py:288
  70.3 1.3 %collective-permute-start.26 = (f32[200,128]{1,0:T(8,128)}, f32[200,128]{1,0:T(8,128)S(1)}, u32[]{:S(2)}, u32[]{:S(2)}) collective-permute-start(f32[200,128]{1,0:T(8,128)} %add_select_fusion.4), channel_id=1, source_target_pairs={{0,16},{64,80},{128,144},{192,208},{1,17},{65,81},{129,145},{193,2... | collective-permute-start | bytes 307208 | tf_op jit(solution)/shard_map/ppermute | solution.py:287
  71.5 1.9 %collective-permute-start.27 = (f32[200,128]{1,0:T(8,128)}, f32[200,128]{1,0:T(8,128)}, u32[]{:S(2)}, u32[]{:S(2)}) collective-permute-start(f32[200,128]{1,0:T(8,128)} %add_select_fusion.4), channel_id=1, source_target_pairs={{0,48},{64,112},{128,176},{192,240},{1,49},{65,113},{129,177},{193... | collective-permute-start | bytes 307208 | tf_op jit(solution)/shard_map/ppermute | solution.py:287
  73.5 1.9 %collective-permute-start.28 = (f32[200,128]{1,0:T(8,128)}, f32[200,128]{1,0:T(8,128)}, u32[]{:S(2)}, u32[]{:S(2)}) collective-permute-start(f32[200,128]{1,0:T(8,128)} %add_select_fusion.4), channel_id=1, source_target_pairs={{0,32},{64,96},{128,160},{192,224},{1,33},{65,97},{129,161},{193,2... | collective-permute-start | bytes 307208 | tf_op jit(solution)/shard_map/ppermute | solution.py:287
  75.4 1.9 %cross.1 = f32[2,256,256]{2,1,0:T(8,128)S(1)} custom-call(f32[256,1024]{1,0:T(8,128)S(1)} %copy-done, f32[256,1024]{1,0:T(8,128)S(1)} %collective-permute-done.prev_ref, f32[256,1024]{1,0:T(8,128)S(1)} %bitcast.41), custom_call_target="tpu_custom_call" | custom-call | flops 1000000000 | bytes 1048576 | tf_op jit(solution)/shard_map/cross/pallas_call | solution.py:155
  77.3 4.1 %collective-permute-start.15 = (f32[2,256,256]{2,1,0:T(8,128)S(1)}, f32[2,256,256]{2,1,0:T(8,128)S(1)}, u32[]{:S(2)}, u32[]{:S(2)}) collective-permute-start(f32[2,256,256]{2,1,0:T(8,128)S(1)} %cross.1), channel_id=1, source_target_pairs={{0,1},{1,0},{2,3},{3,2},{4,5},{5,4},{6,7},{7,6},{8,9},{9,8},{10,11... | collective-permute-start | bytes 1572872 | tf_op jit(solution)/shard_map/ppermute | solution.py:223
  81.4 1.0 %fusion.2 = f32[256,256]{1,0:T(8,128)S(1)} fusion(f32[256,1024]{1,0:T(8,128)S(1)} %copy-done, f32[256,1024]{1,0:T(8,128)S(1)} %collective-permute-done.prev_ref), kind=kOutput, calls=%fused_computation.18 | convolution fusion | flops 805306368 | bytes 2359296 | tf_op jit(solution)/shard_map/dot_general | solution.py:24
  82.5 0.1 collective-permute-start.21
  82.6 1.0 %add_select_fusion.3 = f32[200,128]{1,0:T(8,128)S(1)} fusion(f32[200,128]{1,0:T(8,128)} %add_select_fusion.4, f32[200,128]{1,0:T(8,128)} %collective-permute-done.28, f32[200,128]{1,0:T(8,128)S(1)} %collective-permute-done.26, f32[200,128]{1,0:T(8,128)} %collective-permute-done.27, pred[]{:T(512)S(6)} %and.14), kind=kLoop, calls=%fused_computation.11 | loop fusion | flops 76800 | bytes 512001 | tf_op jit(solution)/shard_map/jit(_where)/select_n | solution.py:288
  83.7 1.3 %collective-permute-start.29 = (f32[200,128]{1,0:T(8,128)S(1)}, f32[200,128]{1,0:T(8,128)S(1)}, u32[]{:S(2)}, u32[]{:S(2)}) collective-permute-start(f32[200,128]{1,0:T(8,128)S(1)} %add_select_fusion.3), channel_id=1, source_target_pairs={{0,8},{16,24},{32,40},{48,56},{64,72},{80,88},{96,104},{112,120},{... | collective-permute-start | bytes 307208 | tf_op jit(solution)/shard_map/ppermute | solution.py:287
  85.0 1.3 %collective-permute-start.30 = (f32[200,128]{1,0:T(8,128)S(1)}, f32[200,128]{1,0:T(8,128)S(1)}, u32[]{:S(2)}, u32[]{:S(2)}) collective-permute-start(f32[200,128]{1,0:T(8,128)S(1)} %add_select_fusion.3), channel_id=1, source_target_pairs={{0,4},{16,20},{32,36},{48,52},{64,68},{80,84},{96,100},{112,116},{... | collective-permute-start | bytes 307208 | tf_op jit(solution)/shard_map/ppermute | solution.py:287
  86.3 1.3 %collective-permute-start.31 = (f32[200,128]{1,0:T(8,128)S(1)}, f32[200,128]{1,0:T(8,128)S(1)}, u32[]{:S(2)}, u32[]{:S(2)}) collective-permute-start(f32[200,128]{1,0:T(8,128)S(1)} %add_select_fusion.3), channel_id=1, source_target_pairs={{0,12},{16,28},{32,44},{48,60},{64,76},{80,92},{96,108},{112,124},... | collective-permute-start | bytes 307208 | tf_op jit(solution)/shard_map/ppermute | solution.py:287
  87.6 0.1 add.121
  87.7 0.1 collective-permute-start.16
  87.8 1.5 %collective-permute-start.22 = (f32[1,64,256]{2,1,0:T(8,128)S(1)}, f32[1,64,256]{2,1,0:T(8,128)S(1)}, u32[]{:S(2)}, u32[]{:S(2)}) collective-permute-start(f32[1,64,256]{2,1,0:T(8,128)S(1)} %dynamic-slice_bitcast_fusion.3), channel_id=1, source_target_pairs={{0,2},{2,0},{1,3},{3,1},{4,6},{6,4},{5,7},{7,5},{8,10},{10,8},{9,1... | collective-permute-start | bytes 196616 | tf_op jit(solution)/shard_map/ppermute | solution.py:223
  89.4 5.8 %collective-permute-done.16 = f32[2,128,256]{2,1,0:T(8,128)S(1)} collective-permute-done((f32[2,128,256]{2,1,0:T(8,128)S(1)}, f32[2,128,256]{2,1,0:T(8,128)S(1)}, u32[]{:S(2)}, u32[]{:S(2)}) %collective-permute-start.16) | collective-permute-done | bytes 262176 | tf_op jit(solution)/shard_map/ppermute | solution.py:223
  95.2 2.1 %collective-permute-start.17 = (f32[2,128,256]{2,1,0:T(8,128)S(1)}, f32[2,128,256]{2,1,0:T(8,128)S(1)}, u32[]{:S(2)}, u32[]{:S(2)}) collective-permute-start(f32[2,128,256]{2,1,0:T(8,128)S(1)} %fusion.8.own_ref), channel_id=1, source_target_pairs={{0,1},{1,0},{2,3},{3,2},{4,5},{5,4},{6,7},{7,6},{8,9},{9,8},{10,11... | collective-permute-start | bytes 786440 | tf_op jit(solution)/shard_map/ppermute | solution.py:223
  97.4 0.1 collective-permute-start.32
  97.5 1.3 %collective-permute-done.32.twin_ref = f32[200,128]{1,0:T(8,128)S(1)} collective-permute-done((f32[200,128]{1,0:T(8,128)S(1)}, f32[200,128]{1,0:T(8,128)S(1)}, u32[]{:S(2)}, u32[]{:S(2)}) %collective-permute-start.32) | collective-permute-done | bytes 102432 | tf_op jit(solution)/shard_map/ppermute | solution.py:223
  98.8 2.5 %finish.1 = (f32[256,256]{1,0:T(8,128)}, f32[1,256]{1,0:T(1,128)}, f32[64,256]{1,0:T(8,128)}, f32[64,256]{1,0:T(8,128)}) custom-call(s32[3]{0:T(128)S(1)} %pad_add_fusion.at_ref, f32[2,128,256]{2,1,0:T(8,128)S(1)} %fusion.8.own_ref, f32[2,128,256]{2,1,0:T(8,128)S(1)} %collective-permute-done.17.other_ref, f32[256,256]{1,0:T(8,128)S(1)} %pad_maximum_fusion.sum_ref.self_ref, ...), custom_call_target="tpu_custom_call" | custom-call | flops 1000000000 | bytes 1048576 | tf_op jit(solution)/shard_map/finish/pallas_call | solution.py:206
  (34 shorter events, 0.3 us)
Async XLA Ops:
  0.6 17.4 %copy-start = (f32[256,1024]{1,0:T(8,128)S(1)}, f32[256,1024]{1,0:T(8,128)}, u32[]{:S(2)}) copy-start(f32[256,1024]{1,0:T(8,128)} %rows_ref.1) | copy-start | bytes 3145732
  2.0 13.3 %collective-permute-start.1 = (f32[32,1024]{1,0:T(8,128)S(1)}, f32[32,1024]{1,0:T(8,128)S(1)}, u32[]{:S(2)}, u32[]{:S(2)}) collective-permute-start(f32[32,1024]{1,0:T(8,128)S(1)} %get-tuple-element.18), channel_id=1, source_target_pairs={{0,24},{1,25},{2,26},{3,27}} | collective-permute-start | bytes 393224 | tf_op jit(solution)/shard_map/ppermute | solution.py:262
  10.1 6.5 %collective-permute-start.2 = (f32[32,1024]{1,0:T(8,128)S(1)}, f32[32,1024]{1,0:T(8,128)S(1)}, u32[]{:S(2)}, u32[]{:S(2)}) collective-permute-start(f32[32,1024]{1,0:T(8,128)S(1)} %get-tuple-element.12), channel_id=1, source_target_pairs={{0,8},{1,9},{2,10},{3,11}} | collective-permute-start | bytes 393224 | tf_op jit(solution)/shard_map/ppermute | solution.py:262
  11.5 7.6 %collective-permute-start.3 = (f32[32,1024]{1,0:T(8,128)S(1)}, f32[32,1024]{1,0:T(8,128)S(1)}, u32[]{:S(2)}, u32[]{:S(2)}) collective-permute-start(f32[32,1024]{1,0:T(8,128)S(1)} %get-tuple-element.17), channel_id=1, source_target_pairs={{0,20},{1,21},{2,22},{3,23}} | collective-permute-start | bytes 393224 | tf_op jit(solution)/shard_map/ppermute | solution.py:262
  12.8 7.3 %collective-permute-start.4 = (f32[32,1024]{1,0:T(8,128)S(1)}, f32[32,1024]{1,0:T(8,128)S(1)}, u32[]{:S(2)}, u32[]{:S(2)}) collective-permute-start(f32[32,1024]{1,0:T(8,128)S(1)} %get-tuple-element.16), channel_id=1, source_target_pairs={{0,28},{1,29},{2,30},{3,31}} | collective-permute-start | bytes 393224 | tf_op jit(solution)/shard_map/ppermute | solution.py:262
  14.1 6.0 %collective-permute-start.5 = (f32[32,1024]{1,0:T(8,128)S(1)}, f32[32,1024]{1,0:T(8,128)S(1)}, u32[]{:S(2)}, u32[]{:S(2)}) collective-permute-start(f32[32,1024]{1,0:T(8,128)S(1)} %get-tuple-element.15), channel_id=1, source_target_pairs={{0,4},{1,5},{2,6},{3,7}} | collective-permute-start | bytes 393224 | tf_op jit(solution)/shard_map/ppermute | solution.py:262
  15.4 4.7 %collective-permute-start.6 = (f32[32,1024]{1,0:T(8,128)S(1)}, f32[32,1024]{1,0:T(8,128)S(1)}, u32[]{:S(2)}, u32[]{:S(2)}) collective-permute-start(f32[32,1024]{1,0:T(8,128)S(1)} %get-tuple-element.14), channel_id=1, source_target_pairs={{0,12},{1,13},{2,14},{3,15}} | collective-permute-start | bytes 393224 | tf_op jit(solution)/shard_map/ppermute | solution.py:262
  16.7 4.6 %collective-permute-start.7 = (f32[32,1024]{1,0:T(8,128)S(1)}, f32[32,1024]{1,0:T(8,128)S(1)}, u32[]{:S(2)}, u32[]{:S(2)}) collective-permute-start(f32[32,1024]{1,0:T(8,128)S(1)} %get-tuple-element.13), channel_id=1, source_target_pairs={{0,16},{1,17},{2,18},{3,19}} | collective-permute-start | bytes 393224 | tf_op jit(solution)/shard_map/ppermute | solution.py:262
  19.1 4.9 %collective-permute-start.18 = (f32[1,256,256]{2,1,0:T(8,128)S(1)}, f32[1,256,256]{2,1,0:T(8,128)S(1)}, u32[]{:S(2)}, u32[]{:S(2)}) collective-permute-start(f32[1,256,256]{2,1,0:T(8,128)S(1)} %convolution_bitcast_fusion), channel_id=1, source_target_pairs={{0,1},{1,0},{2,3},{3,2},{4,5},{5,4},{6,7},{7,6},{8,9},{9,8},{10,11... | collective-permute-start | bytes 786440 | tf_op jit(solution)/shard_map/ppermute | solution.py:223
  21.4 5.8 %collective-permute-start.10 = (f32[32,1024]{1,0:T(8,128)S(1)}, f32[32,1024]{1,0:T(8,128)S(1)}, u32[]{:S(2)}, u32[]{:S(2)}) collective-permute-start(f32[32,1024]{1,0:T(8,128)S(1)} %add_select_fusion.1), channel_id=1, source_target_pairs={{0,160},{1,161},{2,162},{3,163},{4,164},{5,165},{6,166},{7,167},{8... | collective-permute-start | bytes 393224 | tf_op jit(solution)/shard_map/ppermute | solution.py:269
  22.7 5.8 %collective-permute-start.11 = (f32[32,1024]{1,0:T(8,128)S(1)}, f32[32,1024]{1,0:T(8,128)S(1)}, u32[]{:S(2)}, u32[]{:S(2)}) collective-permute-start(f32[32,1024]{1,0:T(8,128)S(1)} %add_select_fusion.1), channel_id=1, source_target_pairs={{0,64},{1,65},{2,66},{3,67},{4,68},{5,69},{6,70},{7,71},{8,72},{9,... | collective-permute-start | bytes 393224 | tf_op jit(solution)/shard_map/ppermute | solution.py:269
  24.1 5.7 %collective-permute-start.19 = (f32[1,128,256]{2,1,0:T(8,128)S(1)}, f32[1,128,256]{2,1,0:T(8,128)S(1)}, u32[]{:S(2)}, u32[]{:S(2)}) collective-permute-start(f32[1,128,256]{2,1,0:T(8,128)S(1)} %dynamic-slice_bitcast_fusion.2), channel_id=1, source_target_pairs={{0,2},{2,0},{1,3},{3,1},{4,6},{6,4},{5,7},{7,5},{8,10},{10,8},{9,1... | collective-permute-start | bytes 393224 | tf_op jit(solution)/shard_map/ppermute | solution.py:223
  24.5 6.6 %collective-permute-start.12 = (f32[32,1024]{1,0:T(8,128)S(1)}, f32[32,1024]{1,0:T(8,128)S(1)}, u32[]{:S(2)}, u32[]{:S(2)}) collective-permute-start(f32[32,1024]{1,0:T(8,128)S(1)} %add_select_fusion.1), channel_id=1, source_target_pairs={{0,192},{1,193},{2,194},{3,195},{4,196},{5,197},{6,198},{7,199},{8... | collective-permute-start | bytes 393224 | tf_op jit(solution)/shard_map/ppermute | solution.py:269
  25.8 5.4 %collective-permute-start.13 = (f32[32,1024]{1,0:T(8,128)S(1)}, f32[32,1024]{1,0:T(8,128)S(1)}, u32[]{:S(2)}, u32[]{:S(2)}) collective-permute-start(f32[32,1024]{1,0:T(8,128)S(1)} %add_select_fusion.1), channel_id=1, source_target_pairs={{0,32},{1,33},{2,34},{3,35},{4,36},{5,37},{6,38},{7,39},{8,40},{9,... | collective-permute-start | bytes 393224 | tf_op jit(solution)/shard_map/ppermute | solution.py:269
  27.1 5.4 %collective-permute-start.14 = (f32[32,1024]{1,0:T(8,128)S(1)}, f32[32,1024]{1,0:T(8,128)S(1)}, u32[]{:S(2)}, u32[]{:S(2)}) collective-permute-start(f32[32,1024]{1,0:T(8,128)S(1)} %add_select_fusion.1), channel_id=1, source_target_pairs={{0,224},{1,225},{2,226},{3,227},{4,228},{5,229},{6,230},{7,231},{8... | collective-permute-start | bytes 393224 | tf_op jit(solution)/shard_map/ppermute | solution.py:269
  28.5 4.1 %collective-permute-start.8 = (f32[32,1024]{1,0:T(8,128)S(1)}, f32[32,1024]{1,0:T(8,128)S(1)}, u32[]{:S(2)}, u32[]{:S(2)}) collective-permute-start(f32[32,1024]{1,0:T(8,128)S(1)} %add_select_fusion.1), channel_id=1, source_target_pairs={{0,128},{1,129},{2,130},{3,131},{4,132},{5,133},{6,134},{7,135},{8... | collective-permute-start | bytes 393224 | tf_op jit(solution)/shard_map/ppermute | solution.py:269
  29.8 5.1 %collective-permute-start.9 = (f32[32,1024]{1,0:T(8,128)S(1)}, f32[32,1024]{1,0:T(8,128)S(1)}, u32[]{:S(2)}, u32[]{:S(2)}) collective-permute-start(f32[32,1024]{1,0:T(8,128)S(1)} %add_select_fusion.1), channel_id=1, source_target_pairs={{0,96},{1,97},{2,98},{3,99},{4,100},{5,101},{6,102},{7,103},{8,104... | collective-permute-start | bytes 393224 | tf_op jit(solution)/shard_map/ppermute | solution.py:269
  31.1 44.3 %collective-permute-start = (f32[256,1024]{1,0:T(8,128)S(1)}, f32[256,1024]{1,0:T(8,128)S(1)}, u32[]{:S(2)}, u32[]{:S(2)}) collective-permute-start(f32[256,1024]{1,0:T(8,128)S(1)} %copy-done), channel_id=1, source_target_pairs={{252,0},{0,4},{4,8},{8,12},{12,16},{16,20},{20,24},{24,28},{28,32}... | collective-permute-start | bytes 3145736 | tf_op jit(solution)/shard_map/ppermute | solution.py:228
  31.2 10.7 %collective-permute-start.20 = (f32[1,128,256]{2,1,0:T(8,128)S(1)}, f32[1,128,256]{2,1,0:T(8,128)S(1)}, u32[]{:S(2)}, u32[]{:S(2)}) collective-permute-start(f32[1,128,256]{2,1,0:T(8,128)S(1)} %fusion.7), channel_id=1, source_target_pairs={{0,1},{1,0},{2,3},{3,2},{4,5},{5,4},{6,7},{7,6},{8,9},{9,8},{10,11... | collective-permute-start | bytes 393224 | tf_op jit(solution)/shard_map/ppermute | solution.py:223
  36.0 39.4 %all-to-all-start = ((f32[8,32,1024]{2,1,0:T(8,128)}), f32[8,32,1024]{2,1,0:T(8,128)S(1)}, u32[]{:S(2)}, u32[]{:S(2)}) async-start(f32[8,32,1024]{2,1,0:T(8,128)} %broadcast_in_dim.6), calls=%async_computation | async-start | bytes 2097152 | tf_op jit(solution)/shard_map/all_to_all | solution.py:276
  49.6 0.7 copy-start.1
  58.2 9.4 %collective-permute-start.23 = (f32[200,128]{1,0:T(8,128)S(1)}, f32[200,128]{1,0:T(8,128)}, u32[]{:S(2)}, u32[]{:S(2)}) collective-permute-start(f32[200,128]{1,0:T(8,128)S(1)} %factor_second.1), channel_id=1, source_target_pairs={{0,128},{1,129},{2,130},{3,131}} | collective-permute-start | bytes 307208 | tf_op jit(solution)/shard_map/ppermute | solution.py:287
  63.7 3.9 %collective-permute-start.24 = (f32[200,128]{1,0:T(8,128)S(1)}, f32[200,128]{1,0:T(8,128)}, u32[]{:S(2)}, u32[]{:S(2)}) collective-permute-start(f32[200,128]{1,0:T(8,128)S(1)} %factor_second.1), channel_id=1, source_target_pairs={{0,64},{1,65},{2,66},{3,67}} | collective-permute-start | bytes 307208 | tf_op jit(solution)/shard_map/ppermute | solution.py:287
  65.6 2.9 %collective-permute-start.25 = (f32[200,128]{1,0:T(8,128)S(1)}, f32[200,128]{1,0:T(8,128)}, u32[]{:S(2)}, u32[]{:S(2)}) collective-permute-start(f32[200,128]{1,0:T(8,128)S(1)} %factor_second.1), channel_id=1, source_target_pairs={{0,192},{1,193},{2,194},{3,195}} | collective-permute-start | bytes 307208 | tf_op jit(solution)/shard_map/ppermute | solution.py:287
  70.3 12.3 %collective-permute-start.26 = (f32[200,128]{1,0:T(8,128)}, f32[200,128]{1,0:T(8,128)S(1)}, u32[]{:S(2)}, u32[]{:S(2)}) collective-permute-start(f32[200,128]{1,0:T(8,128)} %add_select_fusion.4), channel_id=1, source_target_pairs={{0,16},{64,80},{128,144},{192,208},{1,17},{65,81},{129,145},{193,2... | collective-permute-start | bytes 307208 | tf_op jit(solution)/shard_map/ppermute | solution.py:287
  71.5 11.0 %collective-permute-start.27 = (f32[200,128]{1,0:T(8,128)}, f32[200,128]{1,0:T(8,128)}, u32[]{:S(2)}, u32[]{:S(2)}) collective-permute-start(f32[200,128]{1,0:T(8,128)} %add_select_fusion.4), channel_id=1, source_target_pairs={{0,48},{64,112},{128,176},{192,240},{1,49},{65,113},{129,177},{193... | collective-permute-start | bytes 307208 | tf_op jit(solution)/shard_map/ppermute | solution.py:287
  73.5 9.1 %collective-permute-start.28 = (f32[200,128]{1,0:T(8,128)}, f32[200,128]{1,0:T(8,128)}, u32[]{:S(2)}, u32[]{:S(2)}) collective-permute-start(f32[200,128]{1,0:T(8,128)} %add_select_fusion.4), channel_id=1, source_target_pairs={{0,32},{64,96},{128,160},{192,224},{1,33},{65,97},{129,161},{193,2... | collective-permute-start | bytes 307208 | tf_op jit(solution)/shard_map/ppermute | solution.py:287
  77.3 10.2 %collective-permute-start.15 = (f32[2,256,256]{2,1,0:T(8,128)S(1)}, f32[2,256,256]{2,1,0:T(8,128)S(1)}, u32[]{:S(2)}, u32[]{:S(2)}) collective-permute-start(f32[2,256,256]{2,1,0:T(8,128)S(1)} %cross.1), channel_id=1, source_target_pairs={{0,1},{1,0},{2,3},{3,2},{4,5},{5,4},{6,7},{7,6},{8,9},{9,8},{10,11... | collective-permute-start | bytes 1572872 | tf_op jit(solution)/shard_map/ppermute | solution.py:223
  82.5 5.3 %collective-permute-start.21 = (f32[1,2,64,256]{3,2,1,0:T(8,128)S(1)}, f32[1,2,64,256]{3,2,1,0:T(8,128)S(1)}, u32[]{:S(2)}, u32[]{:S(2)}) collective-permute-start(f32[1,2,64,256]{3,2,1,0:T(8,128)S(1)} %dynamic-slice_bitcast_fusion.1), channel_id=1, source_target_pairs={{0,1},{1,0},{2,3},{3,2},{4,5},{5,4},{6,7},{7,6},{8,9},{9,8},{10,11... | collective-permute-start | bytes 393224 | tf_op jit(solution)/shard_map/ppermute | solution.py:223
  83.7 13.7 %collective-permute-start.29 = (f32[200,128]{1,0:T(8,128)S(1)}, f32[200,128]{1,0:T(8,128)S(1)}, u32[]{:S(2)}, u32[]{:S(2)}) collective-permute-start(f32[200,128]{1,0:T(8,128)S(1)} %add_select_fusion.3), channel_id=1, source_target_pairs={{0,8},{16,24},{32,40},{48,56},{64,72},{80,88},{96,104},{112,120},{... | collective-permute-start | bytes 307208 | tf_op jit(solution)/shard_map/ppermute | solution.py:287
  85.0 12.4 %collective-permute-start.30 = (f32[200,128]{1,0:T(8,128)S(1)}, f32[200,128]{1,0:T(8,128)S(1)}, u32[]{:S(2)}, u32[]{:S(2)}) collective-permute-start(f32[200,128]{1,0:T(8,128)S(1)} %add_select_fusion.3), channel_id=1, source_target_pairs={{0,4},{16,20},{32,36},{48,52},{64,68},{80,84},{96,100},{112,116},{... | collective-permute-start | bytes 307208 | tf_op jit(solution)/shard_map/ppermute | solution.py:287
  86.3 11.1 %collective-permute-start.31 = (f32[200,128]{1,0:T(8,128)S(1)}, f32[200,128]{1,0:T(8,128)S(1)}, u32[]{:S(2)}, u32[]{:S(2)}) collective-permute-start(f32[200,128]{1,0:T(8,128)S(1)} %add_select_fusion.3), channel_id=1, source_target_pairs={{0,12},{16,28},{32,44},{48,60},{64,76},{80,92},{96,108},{112,124},... | collective-permute-start | bytes 307208 | tf_op jit(solution)/shard_map/ppermute | solution.py:287
  87.7 7.5 %collective-permute-start.16 = (f32[2,128,256]{2,1,0:T(8,128)S(1)}, f32[2,128,256]{2,1,0:T(8,128)S(1)}, u32[]{:S(2)}, u32[]{:S(2)}) collective-permute-start(f32[2,128,256]{2,1,0:T(8,128)S(1)} %dynamic-slice_bitcast_fusion), channel_id=1, source_target_pairs={{0,2},{2,0},{1,3},{3,1},{4,6},{6,4},{5,7},{7,5},{8,10},{10,8},{9,1... | collective-permute-start | bytes 786440 | tf_op jit(solution)/shard_map/ppermute | solution.py:223
  87.8 9.6 %collective-permute-start.22 = (f32[1,64,256]{2,1,0:T(8,128)S(1)}, f32[1,64,256]{2,1,0:T(8,128)S(1)}, u32[]{:S(2)}, u32[]{:S(2)}) collective-permute-start(f32[1,64,256]{2,1,0:T(8,128)S(1)} %dynamic-slice_bitcast_fusion.3), channel_id=1, source_target_pairs={{0,2},{2,0},{1,3},{3,1},{4,6},{6,4},{5,7},{7,5},{8,10},{10,8},{9,1... | collective-permute-start | bytes 196616 | tf_op jit(solution)/shard_map/ppermute | solution.py:223
  95.2 3.6 %collective-permute-start.17 = (f32[2,128,256]{2,1,0:T(8,128)S(1)}, f32[2,128,256]{2,1,0:T(8,128)S(1)}, u32[]{:S(2)}, u32[]{:S(2)}) collective-permute-start(f32[2,128,256]{2,1,0:T(8,128)S(1)} %fusion.8.own_ref), channel_id=1, source_target_pairs={{0,1},{1,0},{2,3},{3,2},{4,5},{5,4},{6,7},{7,6},{8,9},{9,8},{10,11... | collective-permute-start | bytes 786440 | tf_op jit(solution)/shard_map/ppermute | solution.py:223
  97.4 1.4 %collective-permute-start.32 = (f32[200,128]{1,0:T(8,128)S(1)}, f32[200,128]{1,0:T(8,128)S(1)}, u32[]{:S(2)}, u32[]{:S(2)}) collective-permute-start(f32[200,128]{1,0:T(8,128)S(1)} %add_select_fusion.2.mine_ref), channel_id=1, source_target_pairs={{0,1},{1,0},{2,3},{3,2},{4,5},{5,4},{6,7},{7,6},{8,9},{9,8},{10,11... | collective-permute-start | bytes 307208 | tf_op jit(solution)/shard_map/ppermute | solution.py:223

commit v5 on v4

--- a/solution.py
+++ b/solution.py
@@ -223,11 +223,6 @@
     return lax.ppermute(value, axis, [(0, 1), (1, 0)])
 
 
-def passed_along(block, axis, distance):
-    count = lax.axis_size(axis)
-    return lax.ppermute(block, axis, [((i - distance) % count, i) for i in range(count)])
-
-
 def sum_scattered(partials):
     k, n = partials.shape[0], partials.shape[-1]
     quarters = partials.reshape(k, 2, 2, n // 4, n)
@@ -295,8 +290,10 @@
     at = jnp.stack(
         [lax.axis_index(PAR), lax.axis_index(BLK), lax.axis_index("core")]
     ).astype(jnp.int32)
+    wrapped = lax.ppermute(log_derivs, BLK, [(b, (b + 1) % 64) for b in range(7, 64, 8)])
     piece = scatter_lead(log_derivs)
-    prev_rows = passed_along(log_derivs, BLK, 1)
+    near = lax.ppermute(log_derivs, BLK, [(b, b + 1) for b in range(64) if b % 8 != 7])
+    prev_rows = jnp.where(lax.axis_index(PLANE) == 0, wrapped, near)
     self_part = outer_tile(log_derivs, log_derivs)[None]
     own, other = sum_halves(self_part)
     upper = lax.axis_index("core") == 0

time: 102 us -> 103 us (level)
  starting transfers between devices: 60.2 us -> 62.3 us
  waiting for transfers between devices: 11.6 us -> 10.5 us
    ppermute x1 -> x2, starting transfers between devices: 0.08 us -> 3.56 us  [the longest x1 2.27 us: on_device(): lax.ppermute(log_derivs, BLK, [(b, b + 1) for b in range(64) if b % 8 != 7])]
    ppermute x7, waiting for transfers between devices: 2.29 us -> 0.02 us  [along_z(): got = [lax.ppermute(piece, 'z', [(0, k)]) for k in STACK_ORDER]]
    all_to_all x1, starting transfers between devices: 5.89 us -> 8.07 us  [over_plane(): lax.all_to_all(copies, PLANE, split_axis=0, concat_axis=0, tiled=True)]
    ppermute x7, starting transfers between devices: 15.9 us -> 13.8 us  [scatter_lead(): lax.ppermute(rows[k * part:(k + 1) * part], BLK, [(0, k)])]
    ppermute x9, starting transfers between devices: 18.4 us -> 16.4 us  [small_tree(): got = [lax.ppermute(value, BLK, route) for route in routes]]
    select_n x3, other arithmetic: 2.73 us -> 1.1 us  [small_tree(): value = jnp.where(holds, value, total(got))]
    select_n x0 -> x1, other arithmetic: none -> 1.37 us  [on_device(): prev_rows = jnp.where(lax.axis_index(PLANE) == 0, wrapped, near)]
  transfers between devices with their start and end apart: 34 -> 35, of which waited for: 5 -> 5; matrix products, arithmetic and copies ran while one was open for 6% -> 6% of each run, Pallas kernels for 17% -> 17%
where the time goes in v5:
time: 103 us; the launch traced here: 102 us
  starting transfers between devices  62.3 us (60%)
  Pallas kernels  19.9 us (19%)
  waiting for transfers between devices  10.5 us (10%)
  local copies, waits for them, and re-layouts  3.24 us (3%)
  other arithmetic  2.88 us (3%)
  matrix products  2.05 us (2%)
  between operations  1.13 us (1%)
    ppermute x9, starting transfers between devices, small_tree(): got = [lax.ppermute(value, BLK, route) for route in routes]  16.4 us
    ppermute x7, starting transfers between devices, scatter_lead(): lax.ppermute(rows[k * part:(k + 1) * part], BLK, [(0, k)])  13.8 us
    ppermute x9, starting transfers between devices, swapped(): return lax.ppermute(value, axis, [(0, 1), (1, 0)])  11.3 us
    ppermute x7, starting transfers between devices, along_z(): got = [lax.ppermute(piece, 'z', [(0, k)]) for k in STACK_ORDER]  9.07 us
    all_to_all x1, starting transfers between devices, over_plane(): lax.all_to_all(copies, PLANE, split_axis=0, concat_axis=0, tiled=True)  8.07 us
    pallas_call x1, Pallas kernels, factor_second(): pl.pallas_call(kernel, out_shape=f32(3 * n // 4 + 8, n // 2), in_specs=[S...  7.92 us
    pallas_call x1, Pallas kernels, factor_first(): pl.pallas_call(factor_first_kernel, out_shape=f32(2, n, n), in_specs=[VME...  7.59 us
    ppermute x9, waiting for transfers between devices, swapped(): return lax.ppermute(value, axis, [(0, 1), (1, 0)])  7.06 us
  transfers between devices with their start and end apart: 35, of which 5 were waited for; matrix products, arithmetic and copies ran while one was open for 6% of the time, Pallas kernels for 17%

profile of v5, /device:TPU:1, one launch (start us, length us, event | category | flops | bytes accessed | tf_op | source)
XLA Modules:
  0.0 102.0 jit_solution(17378603403701012288)
XLA Ops:
  0.6 1.4 %fusion.1 = (f32[32,1024]{1,0:T(8,128)S(1)}, f32[32,1024]{1,0:T(8,128)S(1)}, f32[32,1024]{1,0:T(8,128)S(1)}, f32[32,1024]{1,0:T(8,128)S(1)}, f32[32,1024]{1,0:T(...) fusion(f32[256,1024]{1,0:T(8,128)} %rows_ref.1), kind=kLoop, calls=%fused_computation.18 | loop fusion | bytes 1835008 | tf_op jit(solution)/shard_map/slice | solution.py:257
  2.0 5.5 %collective-permute-start.8 = (f32[32,1024]{1,0:T(8,128)S(1)}, f32[32,1024]{1,0:T(8,128)S(1)}, u32[]{:S(2)}, u32[]{:S(2)}) collective-permute-start(f32[32,1024]{1,0:T(8,128)S(1)} %get-tuple-element.13), channel_id=1, source_target_pairs={{0,16},{1,17},{2,18},{3,19}} | collective-permute-start | bytes 393224 | tf_op jit(solution)/shard_map/ppermute | solution.py:257
  7.5 1.3 %collective-permute-start.7 = (f32[32,1024]{1,0:T(8,128)S(1)}, f32[32,1024]{1,0:T(8,128)S(1)}, u32[]{:S(2)}, u32[]{:S(2)}) collective-permute-start(f32[32,1024]{1,0:T(8,128)S(1)} %get-tuple-element.14), channel_id=1, source_target_pairs={{0,12},{1,13},{2,14},{3,15}} | collective-permute-start | bytes 393224 | tf_op jit(solution)/shard_map/ppermute | solution.py:257
  8.8 1.3 %collective-permute-start.6 = (f32[32,1024]{1,0:T(8,128)S(1)}, f32[32,1024]{1,0:T(8,128)S(1)}, u32[]{:S(2)}, u32[]{:S(2)}) collective-permute-start(f32[32,1024]{1,0:T(8,128)S(1)} %get-tuple-element.15), channel_id=1, source_target_pairs={{0,4},{1,5},{2,6},{3,7}} | collective-permute-start | bytes 393224 | tf_op jit(solution)/shard_map/ppermute | solution.py:257
  10.1 1.9 %collective-permute-start.5 = (f32[32,1024]{1,0:T(8,128)S(1)}, f32[32,1024]{1,0:T(8,128)S(1)}, u32[]{:S(2)}, u32[]{:S(2)}) collective-permute-start(f32[32,1024]{1,0:T(8,128)S(1)} %get-tuple-element.16), channel_id=1, source_target_pairs={{0,28},{1,29},{2,30},{3,31}} | collective-permute-start | bytes 393224 | tf_op jit(solution)/shard_map/ppermute | solution.py:257
  12.0 1.3 %collective-permute-start.4 = (f32[32,1024]{1,0:T(8,128)S(1)}, f32[32,1024]{1,0:T(8,128)S(1)}, u32[]{:S(2)}, u32[]{:S(2)}) collective-permute-start(f32[32,1024]{1,0:T(8,128)S(1)} %get-tuple-element.17), channel_id=1, source_target_pairs={{0,20},{1,21},{2,22},{3,23}} | collective-permute-start | bytes 393224 | tf_op jit(solution)/shard_map/ppermute | solution.py:257
  13.3 0.0 collective-permute-done.8
  13.3 1.3 %collective-permute-start.2 = (f32[32,1024]{1,0:T(8,128)S(1)}, f32[32,1024]{1,0:T(8,128)S(1)}, u32[]{:S(2)}, u32[]{:S(2)}) collective-permute-start(f32[32,1024]{1,0:T(8,128)S(1)} %get-tuple-element.18), channel_id=1, source_target_pairs={{0,24},{1,25},{2,26},{3,27}} | collective-permute-start | bytes 393224 | tf_op jit(solution)/shard_map/ppermute | solution.py:257
  14.6 1.3 %collective-permute-start.3 = (f32[32,1024]{1,0:T(8,128)S(1)}, f32[32,1024]{1,0:T(8,128)S(1)}, u32[]{:S(2)}, u32[]{:S(2)}) collective-permute-start(f32[32,1024]{1,0:T(8,128)S(1)} %get-tuple-element.12), channel_id=1, source_target_pairs={{0,8},{1,9},{2,10},{3,11}} | collective-permute-start | bytes 393224 | tf_op jit(solution)/shard_map/ppermute | solution.py:257
  15.9 1.0 %convolution_bitcast_fusion = f32[1,256,256]{2,1,0:T(8,128)S(1)} fusion(f32[256,1024]{1,0:T(8,128)S(1)} %copy-done), kind=kOutput, calls=%fused_computation | convolution fusion | flops 805306368 | bytes 1310720 | tf_op jit(solution)/shard_map/dot_general | solution.py:24
  17.0 1.0 %collective-permute-start.19 = (f32[1,256,256]{2,1,0:T(8,128)S(1)}, f32[1,256,256]{2,1,0:T(8,128)S(1)}, u32[]{:S(2)}, u32[]{:S(2)}) collective-permute-start(f32[1,256,256]{2,1,0:T(8,128)S(1)} %convolution_bitcast_fusion), channel_id=1, source_target_pairs={{0,1},{1,0},{2,3},{3,2},{4,5},{5,4},{6,7},{7,6},{8,9},{9,8},{10,11... | collective-permute-start | bytes 786440 | tf_op jit(solution)/shard_map/ppermute | solution.py:223
  18.0 1.7 %collective-permute-done.2 = f32[32,1024]{1,0:T(8,128)S(1)} collective-permute-done((f32[32,1024]{1,0:T(8,128)S(1)}, f32[32,1024]{1,0:T(8,128)S(1)}, u32[]{:S(2)}, u32[]{:S(2)}) %collective-permute-start.2) | collective-permute-done | bytes 131104 | tf_op jit(solution)/shard_map/ppermute | solution.py:257
  19.8 0.0 collective-permute-done.3
  19.8 0.1 add_select_fusion.1
  19.8 1.3 %collective-permute-start.15 = (f32[32,1024]{1,0:T(8,128)S(1)}, f32[32,1024]{1,0:T(8,128)S(1)}, u32[]{:S(2)}, u32[]{:S(2)}) collective-permute-start(f32[32,1024]{1,0:T(8,128)S(1)} %add_select_fusion.1), channel_id=1, source_target_pairs={{0,224},{1,225},{2,226},{3,227},{4,228},{5,229},{6,230},{7,231},{8... | collective-permute-start | bytes 393224 | tf_op jit(solution)/shard_map/ppermute | solution.py:264
  21.1 1.3 %collective-permute-start.14 = (f32[32,1024]{1,0:T(8,128)S(1)}, f32[32,1024]{1,0:T(8,128)S(1)}, u32[]{:S(2)}, u32[]{:S(2)}) collective-permute-start(f32[32,1024]{1,0:T(8,128)S(1)} %add_select_fusion.1), channel_id=1, source_target_pairs={{0,32},{1,33},{2,34},{3,35},{4,36},{5,37},{6,38},{7,39},{8,40},{9,... | collective-permute-start | bytes 393224 | tf_op jit(solution)/shard_map/ppermute | solution.py:264
  22.4 0.0 collective-permute-done.19
  22.5 0.4 collective-permute-start.20
  22.9 0.1 pad_add_fusion.at_ref
  23.0 1.3 %collective-permute-start.13 = (f32[32,1024]{1,0:T(8,128)S(1)}, f32[32,1024]{1,0:T(8,128)S(1)}, u32[]{:S(2)}, u32[]{:S(2)}) collective-permute-start(f32[32,1024]{1,0:T(8,128)S(1)} %add_select_fusion.1), channel_id=1, source_target_pairs={{0,192},{1,193},{2,194},{3,195},{4,196},{5,197},{6,198},{7,199},{8... | collective-permute-start | bytes 393224 | tf_op jit(solution)/shard_map/ppermute | solution.py:264
  24.3 1.3 %collective-permute-start.12 = (f32[32,1024]{1,0:T(8,128)S(1)}, f32[32,1024]{1,0:T(8,128)S(1)}, u32[]{:S(2)}, u32[]{:S(2)}) collective-permute-start(f32[32,1024]{1,0:T(8,128)S(1)} %add_select_fusion.1), channel_id=1, source_target_pairs={{0,64},{1,65},{2,66},{3,67},{4,68},{5,69},{6,70},{7,71},{8,72},{9,... | collective-permute-start | bytes 393224 | tf_op jit(solution)/shard_map/ppermute | solution.py:264
  25.6 1.3 %collective-permute-start.11 = (f32[32,1024]{1,0:T(8,128)S(1)}, f32[32,1024]{1,0:T(8,128)S(1)}, u32[]{:S(2)}, u32[]{:S(2)}) collective-permute-start(f32[32,1024]{1,0:T(8,128)S(1)} %add_select_fusion.1), channel_id=1, source_target_pairs={{0,160},{1,161},{2,162},{3,163},{4,164},{5,165},{6,166},{7,167},{8... | collective-permute-start | bytes 393224 | tf_op jit(solution)/shard_map/ppermute | solution.py:264
  26.9 0.0 collective-permute-done.14
  26.9 1.3 %collective-permute-start.9 = (f32[32,1024]{1,0:T(8,128)S(1)}, f32[32,1024]{1,0:T(8,128)S(1)}, u32[]{:S(2)}, u32[]{:S(2)}) collective-permute-start(f32[32,1024]{1,0:T(8,128)S(1)} %add_select_fusion.1), channel_id=1, source_target_pairs={{0,128},{1,129},{2,130},{3,131},{4,132},{5,133},{6,134},{7,135},{8... | collective-permute-start | bytes 393224 | tf_op jit(solution)/shard_map/ppermute | solution.py:264
  28.2 1.3 %collective-permute-start.10 = (f32[32,1024]{1,0:T(8,128)S(1)}, f32[32,1024]{1,0:T(8,128)S(1)}, u32[]{:S(2)}, u32[]{:S(2)}) collective-permute-start(f32[32,1024]{1,0:T(8,128)S(1)} %add_select_fusion.1), channel_id=1, source_target_pairs={{0,96},{1,97},{2,98},{3,99},{4,100},{5,101},{6,102},{7,103},{8,104... | collective-permute-start | bytes 393224 | tf_op jit(solution)/shard_map/ppermute | solution.py:264
  29.6 1.3 %collective-permute-start = (f32[256,1024]{1,0:T(8,128)S(1)}, f32[256,1024]{1,0:T(8,128)}, u32[]{:S(2)}, u32[]{:S(2)}) collective-permute-start(f32[256,1024]{1,0:T(8,128)S(1)} %copy-done), channel_id=1, source_target_pairs={{28,32},{60,64},{92,96},{124,128},{156,160},{188,192},{220,224},{2... | collective-permute-start | bytes 3145736 | tf_op jit(solution)/shard_map/ppermute | solution.py:293
  30.9 0.0 collective-permute-done.12
  30.9 2.3 %collective-permute-start.1 = (f32[256,1024]{1,0:T(8,128)S(1)}, f32[256,1024]{1,0:T(8,128)}, u32[]{:S(2)}, u32[]{:S(2)}) collective-permute-start(f32[256,1024]{1,0:T(8,128)S(1)} %copy-done), channel_id=1, source_target_pairs={{0,4},{4,8},{8,12},{12,16},{16,20},{20,24},{24,28},{32,36},{36,40}... | collective-permute-start | bytes 3145736 | tf_op jit(solution)/shard_map/ppermute | solution.py:295
  33.2 0.0 collective-permute-done.11
  33.2 1.8 %collective-permute-start.21 = (f32[1,128,256]{2,1,0:T(8,128)S(1)}, f32[1,128,256]{2,1,0:T(8,128)S(1)}, u32[]{:S(2)}, u32[]{:S(2)}) collective-permute-start(f32[1,128,256]{2,1,0:T(8,128)S(1)} %fusion.7), channel_id=1, source_target_pairs={{0,1},{1,0},{2,3},{3,2},{4,5},{5,4},{6,7},{7,6},{8,9},{9,8},{10,11... | collective-permute-start | bytes 393224 | tf_op jit(solution)/shard_map/ppermute | solution.py:223
  35.0 0.0 collective-permute-done.9
  35.0 0.0 collective-permute-done.10
  35.0 0.1 add_select_fusion
  35.0 1.1 %broadcast_in_dim.6 = f32[8,32,1024]{2,1,0:T(8,128)} broadcast(f32[32,1024]{1,0:T(8,128)S(1)} %add_select_fusion), dimensions={1,2} | broadcast | bytes 1179648 | tf_op jit(solution)/shard_map/broadcast_in_dim | solution.py:270
  36.1 8.1 %all-to-all-start = ((f32[8,32,1024]{2,1,0:T(8,128)}), f32[8,32,1024]{2,1,0:T(8,128)S(1)}, u32[]{:S(2)}, u32[]{:S(2)}) async-start(f32[8,32,1024]{2,1,0:T(8,128)} %broadcast_in_dim.6), calls=%async_computation | async-start | bytes 2097152 | tf_op jit(solution)/shard_map/all_to_all | solution.py:271
  44.3 7.6 %factor_first.1.state_in_ref = f32[2,256,256]{2,1,0:T(8,128)S(1)} custom-call(f32[256,256]{1,0:T(8,128)S(1)} %pad_maximum_fusion.sum_ref.self_ref), custom_call_target="tpu_custom_call" | custom-call | flops 8000000000 | bytes 1048576 | tf_op jit(solution)/shard_map/factor_first/pallas_call | solution.py:118
  51.9 0.0 copy-start.1
  51.9 0.7 copy-done.1
  52.6 7.9 %factor_second.1 = f32[200,128]{1,0:T(8,128)S(1)} custom-call(s32[3]{0:T(128)S(1)} %pad_add_fusion.at_ref, f32[2,256,256]{2,1,0:T(8,128)S(1)} %factor_first.1.state_in_ref, f32[1,256]{1,0:T(1,128)S(1)} %bitcast.44), custom_call_target="tpu_custom_call" | custom-call | flops 8000000000 | bytes 1048576 | tf_op jit(solution)/shard_map/factor_second/pallas_call | solution.py:136
  60.5 4.2 %collective-permute-start.26 = (f32[200,128]{1,0:T(8,128)S(1)}, f32[200,128]{1,0:T(8,128)S(1)}, u32[]{:S(2)}, u32[]{:S(2)}) collective-permute-start(f32[200,128]{1,0:T(8,128)S(1)} %factor_second.1), channel_id=1, source_target_pairs={{0,192},{1,193},{2,194},{3,195}} | collective-permute-start | bytes 307208 | tf_op jit(solution)/shard_map/ppermute | solution.py:282
  64.7 1.3 %collective-permute-start.24 = (f32[200,128]{1,0:T(8,128)S(1)}, f32[200,128]{1,0:T(8,128)S(1)}, u32[]{:S(2)}, u32[]{:S(2)}) collective-permute-start(f32[200,128]{1,0:T(8,128)S(1)} %factor_second.1), channel_id=1, source_target_pairs={{0,128},{1,129},{2,130},{3,131}} | collective-permute-start | bytes 307208 | tf_op jit(solution)/shard_map/ppermute | solution.py:282
  66.0 1.3 %collective-permute-start.25 = (f32[200,128]{1,0:T(8,128)S(1)}, f32[200,128]{1,0:T(8,128)S(1)}, u32[]{:S(2)}, u32[]{:S(2)}) collective-permute-start(f32[200,128]{1,0:T(8,128)S(1)} %factor_second.1), channel_id=1, source_target_pairs={{0,64},{1,65},{2,66},{3,67}} | collective-permute-start | bytes 307208 | tf_op jit(solution)/shard_map/ppermute | solution.py:282
  67.3 0.3 collective-permute-done.24
  67.6 1.3 %collective-permute-done.25 = f32[200,128]{1,0:T(8,128)S(1)} collective-permute-done((f32[200,128]{1,0:T(8,128)S(1)}, f32[200,128]{1,0:T(8,128)S(1)}, u32[]{:S(2)}, u32[]{:S(2)}) %collective-permute-start.25) | collective-permute-done | bytes 102432 | tf_op jit(solution)/shard_map/ppermute | solution.py:282
  69.0 1.9 %collective-permute-start.29 = (f32[200,128]{1,0:T(8,128)S(1)}, f32[200,128]{1,0:T(8,128)}, u32[]{:S(2)}, u32[]{:S(2)}) collective-permute-start(f32[200,128]{1,0:T(8,128)S(1)} %add_select_fusion.4), channel_id=1, source_target_pairs={{0,32},{64,96},{128,160},{192,224},{1,33},{65,97},{129,161},{193,2... | collective-permute-start | bytes 307208 | tf_op jit(solution)/shard_map/ppermute | solution.py:282
  70.9 1.9 %collective-permute-start.27 = (f32[200,128]{1,0:T(8,128)S(1)}, f32[200,128]{1,0:T(8,128)}, u32[]{:S(2)}, u32[]{:S(2)}) collective-permute-start(f32[200,128]{1,0:T(8,128)S(1)} %add_select_fusion.4), channel_id=1, source_target_pairs={{0,16},{64,80},{128,144},{192,208},{1,17},{65,81},{129,145},{193,2... | collective-permute-start | bytes 307208 | tf_op jit(solution)/shard_map/ppermute | solution.py:282
  72.8 1.9 %collective-permute-start.28 = (f32[200,128]{1,0:T(8,128)S(1)}, f32[200,128]{1,0:T(8,128)}, u32[]{:S(2)}, u32[]{:S(2)}) collective-permute-start(f32[200,128]{1,0:T(8,128)S(1)} %add_select_fusion.4), channel_id=1, source_target_pairs={{0,48},{64,112},{128,176},{192,240},{1,49},{65,113},{129,177},{193... | collective-permute-start | bytes 307208 | tf_op jit(solution)/shard_map/ppermute | solution.py:282
  74.7 1.4 %broadcast_select_fusion.prev_ref = f32[256,1024]{1,0:T(8,128)S(1)} fusion(f32[256,1024]{1,0:T(8,128)} %collective-permute-done, f32[256,1024]{1,0:T(8,128)} %collective-permute-done.1, pred[]{:T(512)S(6)} %eq.22), kind=kLoop, calls=%fused_computation.1 | loop fusion | flops 262144 | bytes 3145729 | tf_op jit(solution)/shard_map/jit(_where)/select_n | solution.py:296
  76.1 1.9 %cross.1 = f32[2,256,256]{2,1,0:T(8,128)S(1)} custom-call(f32[256,1024]{1,0:T(8,128)S(1)} %copy-done, f32[256,1024]{1,0:T(8,128)S(1)} %broadcast_select_fusion.prev_ref, f32[256,1024]{1,0:T(8,128)S(1)} %bitcast.43), custom_call_target="tpu_custom_call" | custom-call | flops 1000000000 | bytes 1048576 | tf_op jit(solution)/shard_map/cross/pallas_call | solution.py:155
  78.0 4.1 %collective-permute-start.16 = (f32[2,256,256]{2,1,0:T(8,128)S(1)}, f32[2,256,256]{2,1,0:T(8,128)S(1)}, u32[]{:S(2)}, u32[]{:S(2)}) collective-permute-start(f32[2,256,256]{2,1,0:T(8,128)S(1)} %cross.1), channel_id=1, source_target_pairs={{0,1},{1,0},{2,3},{3,2},{4,5},{5,4},{6,7},{7,6},{8,9},{9,8},{10,11... | collective-permute-start | bytes 1572872 | tf_op jit(solution)/shard_map/ppermute | solution.py:223
  82.1 1.0 %fusion.2 = f32[256,256]{0,1:T(8,128)S(1)} fusion(f32[256,1024]{1,0:T(8,128)S(1)} %broadcast_select_fusion.prev_ref, f32[256,1024]{1,0:T(8,128)S(1)} %copy-done), kind=kOutput, calls=%fused_computation.19 | convolution fusion | flops 805306368 | bytes 2359296 | tf_op jit(solution)/shard_map/dot_general | solution.py:24
  83.2 0.1 collective-permute-start.22
  83.3 1.0 %add_select_fusion.3 = f32[200,128]{1,0:T(8,128)S(1)} fusion(f32[200,128]{1,0:T(8,128)S(1)} %add_select_fusion.4, f32[200,128]{1,0:T(8,128)} %collective-permute-done.29, f32[200,128]{1,0:T(8,128)} %collective-permute-done.27, f32[200,128]{1,0:T(8,128)} %collective-permute-done.28, pred[]{:T(512)S(6)} %and.14), kind=kLoop, calls=%fused_computation.12 | loop fusion | flops 76800 | bytes 512001 | tf_op jit(solution)/shard_map/jit(_where)/select_n | solution.py:283
  84.4 1.3 %collective-permute-start.32 = (f32[200,128]{1,0:T(8,128)S(1)}, f32[200,128]{1,0:T(8,128)S(1)}, u32[]{:S(2)}, u32[]{:S(2)}) collective-permute-start(f32[200,128]{1,0:T(8,128)S(1)} %add_select_fusion.3), channel_id=1, source_target_pairs={{0,12},{16,28},{32,44},{48,60},{64,76},{80,92},{96,108},{112,124},... | collective-permute-start | bytes 307208 | tf_op jit(solution)/shard_map/ppermute | solution.py:282
  85.7 1.3 %collective-permute-start.30 = (f32[200,128]{1,0:T(8,128)S(1)}, f32[200,128]{1,0:T(8,128)S(1)}, u32[]{:S(2)}, u32[]{:S(2)}) collective-permute-start(f32[200,128]{1,0:T(8,128)S(1)} %add_select_fusion.3), channel_id=1, source_target_pairs={{0,8},{16,24},{32,40},{48,56},{64,72},{80,88},{96,104},{112,120},{... | collective-permute-start | bytes 307208 | tf_op jit(solution)/shard_map/ppermute | solution.py:282
  87.0 1.3 %collective-permute-start.31 = (f32[200,128]{1,0:T(8,128)S(1)}, f32[200,128]{1,0:T(8,128)S(1)}, u32[]{:S(2)}, u32[]{:S(2)}) collective-permute-start(f32[200,128]{1,0:T(8,128)S(1)} %add_select_fusion.3), channel_id=1, source_target_pairs={{0,4},{16,20},{32,36},{48,52},{64,68},{80,84},{96,100},{112,116},{... | collective-permute-start | bytes 307208 | tf_op jit(solution)/shard_map/ppermute | solution.py:282
  88.3 0.1 add.122
  88.4 0.1 collective-permute-start.17
  88.6 1.5 %collective-permute-start.23 = (f32[1,64,256]{2,1,0:T(8,128)S(1)}, f32[1,64,256]{2,1,0:T(8,128)S(1)}, u32[]{:S(2)}, u32[]{:S(2)}) collective-permute-start(f32[1,64,256]{2,1,0:T(8,128)S(1)} %dynamic-slice_bitcast_fusion.3), channel_id=1, source_target_pairs={{0,2},{2,0},{1,3},{3,1},{4,6},{6,4},{5,7},{7,5},{8,10},{10,8},{9,1... | collective-permute-start | bytes 196616 | tf_op jit(solution)/shard_map/ppermute | solution.py:223
  90.1 5.8 %collective-permute-done.17 = f32[2,128,256]{2,1,0:T(8,128)S(1)} collective-permute-done((f32[2,128,256]{2,1,0:T(8,128)S(1)}, f32[2,128,256]{2,1,0:T(8,128)S(1)}, u32[]{:S(2)}, u32[]{:S(2)}) %collective-permute-start.17) | collective-permute-done | bytes 262176 | tf_op jit(solution)/shard_map/ppermute | solution.py:223
  95.9 2.1 %collective-permute-start.18 = (f32[2,128,256]{2,1,0:T(8,128)S(1)}, f32[2,128,256]{2,1,0:T(8,128)S(1)}, u32[]{:S(2)}, u32[]{:S(2)}) collective-permute-start(f32[2,128,256]{2,1,0:T(8,128)S(1)} %fusion.8.own_ref), channel_id=1, source_target_pairs={{0,1},{1,0},{2,3},{3,2},{4,5},{5,4},{6,7},{7,6},{8,9},{9,8},{10,11... | collective-permute-start | bytes 786440 | tf_op jit(solution)/shard_map/ppermute | solution.py:223
  98.1 0.1 collective-permute-start.33
  98.2 1.3 %collective-permute-done.33.twin_ref = f32[200,128]{1,0:T(8,128)S(1)} collective-permute-done((f32[200,128]{1,0:T(8,128)S(1)}, f32[200,128]{1,0:T(8,128)S(1)}, u32[]{:S(2)}, u32[]{:S(2)}) %collective-permute-start.33) | collective-permute-done | bytes 102432 | tf_op jit(solution)/shard_map/ppermute | solution.py:223
  99.5 2.5 %finish.1 = (f32[256,256]{1,0:T(8,128)}, f32[1,256]{1,0:T(1,128)}, f32[64,256]{1,0:T(8,128)}, f32[64,256]{1,0:T(8,128)}) custom-call(s32[3]{0:T(128)S(1)} %pad_add_fusion.at_ref, f32[2,128,256]{2,1,0:T(8,128)S(1)} %fusion.8.own_ref, f32[2,128,256]{2,1,0:T(8,128)S(1)} %collective-permute-done.18.other_ref, f32[256,256]{1,0:T(8,128)S(1)} %pad_maximum_fusion.sum_ref.self_ref, ...), custom_call_target="tpu_custom_call" | custom-call | flops 1000000000 | bytes 1048576 | tf_op jit(solution)/shard_map/finish/pallas_call | solution.py:206
  (37 shorter events, 0.4 us)
Async XLA Ops:
  0.6 15.3 %copy-start = (f32[256,1024]{1,0:T(8,128)S(1)}, f32[256,1024]{1,0:T(8,128)}, u32[]{:S(2)}) copy-start(f32[256,1024]{1,0:T(8,128)} %rows_ref.1) | copy-start | bytes 3145732
  2.0 11.3 %collective-permute-start.8 = (f32[32,1024]{1,0:T(8,128)S(1)}, f32[32,1024]{1,0:T(8,128)S(1)}, u32[]{:S(2)}, u32[]{:S(2)}) collective-permute-start(f32[32,1024]{1,0:T(8,128)S(1)} %get-tuple-element.13), channel_id=1, source_target_pairs={{0,16},{1,17},{2,18},{3,19}} | collective-permute-start | bytes 393224 | tf_op jit(solution)/shard_map/ppermute | solution.py:257
  7.5 7.1 %collective-permute-start.7 = (f32[32,1024]{1,0:T(8,128)S(1)}, f32[32,1024]{1,0:T(8,128)S(1)}, u32[]{:S(2)}, u32[]{:S(2)}) collective-permute-start(f32[32,1024]{1,0:T(8,128)S(1)} %get-tuple-element.14), channel_id=1, source_target_pairs={{0,12},{1,13},{2,14},{3,15}} | collective-permute-start | bytes 393224 | tf_op jit(solution)/shard_map/ppermute | solution.py:257
  8.8 8.2 %collective-permute-start.6 = (f32[32,1024]{1,0:T(8,128)S(1)}, f32[32,1024]{1,0:T(8,128)S(1)}, u32[]{:S(2)}, u32[]{:S(2)}) collective-permute-start(f32[32,1024]{1,0:T(8,128)S(1)} %get-tuple-element.15), channel_id=1, source_target_pairs={{0,4},{1,5},{2,6},{3,7}} | collective-permute-start | bytes 393224 | tf_op jit(solution)/shard_map/ppermute | solution.py:257
  10.1 7.9 %collective-permute-start.5 = (f32[32,1024]{1,0:T(8,128)S(1)}, f32[32,1024]{1,0:T(8,128)S(1)}, u32[]{:S(2)}, u32[]{:S(2)}) collective-permute-start(f32[32,1024]{1,0:T(8,128)S(1)} %get-tuple-element.16), channel_id=1, source_target_pairs={{0,28},{1,29},{2,30},{3,31}} | collective-permute-start | bytes 393224 | tf_op jit(solution)/shard_map/ppermute | solution.py:257
  12.0 6.0 %collective-permute-start.4 = (f32[32,1024]{1,0:T(8,128)S(1)}, f32[32,1024]{1,0:T(8,128)S(1)}, u32[]{:S(2)}, u32[]{:S(2)}) collective-permute-start(f32[32,1024]{1,0:T(8,128)S(1)} %get-tuple-element.17), channel_id=1, source_target_pairs={{0,20},{1,21},{2,22},{3,23}} | collective-permute-start | bytes 393224 | tf_op jit(solution)/shard_map/ppermute | solution.py:257
  13.3 6.5 %collective-permute-start.2 = (f32[32,1024]{1,0:T(8,128)S(1)}, f32[32,1024]{1,0:T(8,128)S(1)}, u32[]{:S(2)}, u32[]{:S(2)}) collective-permute-start(f32[32,1024]{1,0:T(8,128)S(1)} %get-tuple-element.18), channel_id=1, source_target_pairs={{0,24},{1,25},{2,26},{3,27}} | collective-permute-start | bytes 393224 | tf_op jit(solution)/shard_map/ppermute | solution.py:257
  14.6 5.1 %collective-permute-start.3 = (f32[32,1024]{1,0:T(8,128)S(1)}, f32[32,1024]{1,0:T(8,128)S(1)}, u32[]{:S(2)}, u32[]{:S(2)}) collective-permute-start(f32[32,1024]{1,0:T(8,128)S(1)} %get-tuple-element.12), channel_id=1, source_target_pairs={{0,8},{1,9},{2,10},{3,11}} | collective-permute-start | bytes 393224 | tf_op jit(solution)/shard_map/ppermute | solution.py:257
  17.0 5.5 %collective-permute-start.19 = (f32[1,256,256]{2,1,0:T(8,128)S(1)}, f32[1,256,256]{2,1,0:T(8,128)S(1)}, u32[]{:S(2)}, u32[]{:S(2)}) collective-permute-start(f32[1,256,256]{2,1,0:T(8,128)S(1)} %convolution_bitcast_fusion), channel_id=1, source_target_pairs={{0,1},{1,0},{2,3},{3,2},{4,5},{5,4},{6,7},{7,6},{8,9},{9,8},{10,11... | collective-permute-start | bytes 786440 | tf_op jit(solution)/shard_map/ppermute | solution.py:223
  19.8 5.8 %collective-permute-start.15 = (f32[32,1024]{1,0:T(8,128)S(1)}, f32[32,1024]{1,0:T(8,128)S(1)}, u32[]{:S(2)}, u32[]{:S(2)}) collective-permute-start(f32[32,1024]{1,0:T(8,128)S(1)} %add_select_fusion.1), channel_id=1, source_target_pairs={{0,224},{1,225},{2,226},{3,227},{4,228},{5,229},{6,230},{7,231},{8... | collective-permute-start | bytes 393224 | tf_op jit(solution)/shard_map/ppermute | solution.py:264
  21.1 5.8 %collective-permute-start.14 = (f32[32,1024]{1,0:T(8,128)S(1)}, f32[32,1024]{1,0:T(8,128)S(1)}, u32[]{:S(2)}, u32[]{:S(2)}) collective-permute-start(f32[32,1024]{1,0:T(8,128)S(1)} %add_select_fusion.1), channel_id=1, source_target_pairs={{0,32},{1,33},{2,34},{3,35},{4,36},{5,37},{6,38},{7,39},{8,40},{9,... | collective-permute-start | bytes 393224 | tf_op jit(solution)/shard_map/ppermute | solution.py:264
  22.5 5.7 %collective-permute-start.20 = (f32[1,128,256]{2,1,0:T(8,128)S(1)}, f32[1,128,256]{2,1,0:T(8,128)S(1)}, u32[]{:S(2)}, u32[]{:S(2)}) collective-permute-start(f32[1,128,256]{2,1,0:T(8,128)S(1)} %dynamic-slice_bitcast_fusion.2), channel_id=1, source_target_pairs={{0,2},{2,0},{1,3},{3,1},{4,6},{6,4},{5,7},{7,5},{8,10},{10,8},{9,1... | collective-permute-start | bytes 393224 | tf_op jit(solution)/shard_map/ppermute | solution.py:223
  23.0 6.6 %collective-permute-start.13 = (f32[32,1024]{1,0:T(8,128)S(1)}, f32[32,1024]{1,0:T(8,128)S(1)}, u32[]{:S(2)}, u32[]{:S(2)}) collective-permute-start(f32[32,1024]{1,0:T(8,128)S(1)} %add_select_fusion.1), channel_id=1, source_target_pairs={{0,192},{1,193},{2,194},{3,195},{4,196},{5,197},{6,198},{7,199},{8... | collective-permute-start | bytes 393224 | tf_op jit(solution)/shard_map/ppermute | solution.py:264
  24.3 6.6 %collective-permute-start.12 = (f32[32,1024]{1,0:T(8,128)S(1)}, f32[32,1024]{1,0:T(8,128)S(1)}, u32[]{:S(2)}, u32[]{:S(2)}) collective-permute-start(f32[32,1024]{1,0:T(8,128)S(1)} %add_select_fusion.1), channel_id=1, source_target_pairs={{0,64},{1,65},{2,66},{3,67},{4,68},{5,69},{6,70},{7,71},{8,72},{9,... | collective-permute-start | bytes 393224 | tf_op jit(solution)/shard_map/ppermute | solution.py:264
  25.6 7.6 %collective-permute-start.11 = (f32[32,1024]{1,0:T(8,128)S(1)}, f32[32,1024]{1,0:T(8,128)S(1)}, u32[]{:S(2)}, u32[]{:S(2)}) collective-permute-start(f32[32,1024]{1,0:T(8,128)S(1)} %add_select_fusion.1), channel_id=1, source_target_pairs={{0,160},{1,161},{2,162},{3,163},{4,164},{5,165},{6,166},{7,167},{8... | collective-permute-start | bytes 393224 | tf_op jit(solution)/shard_map/ppermute | solution.py:264
  26.9 8.1 %collective-permute-start.9 = (f32[32,1024]{1,0:T(8,128)S(1)}, f32[32,1024]{1,0:T(8,128)S(1)}, u32[]{:S(2)}, u32[]{:S(2)}) collective-permute-start(f32[32,1024]{1,0:T(8,128)S(1)} %add_select_fusion.1), channel_id=1, source_target_pairs={{0,128},{1,129},{2,130},{3,131},{4,132},{5,133},{6,134},{7,135},{8... | collective-permute-start | bytes 393224 | tf_op jit(solution)/shard_map/ppermute | solution.py:264
  28.2 6.7 %collective-permute-start.10 = (f32[32,1024]{1,0:T(8,128)S(1)}, f32[32,1024]{1,0:T(8,128)S(1)}, u32[]{:S(2)}, u32[]{:S(2)}) collective-permute-start(f32[32,1024]{1,0:T(8,128)S(1)} %add_select_fusion.1), channel_id=1, source_target_pairs={{0,96},{1,97},{2,98},{3,99},{4,100},{5,101},{6,102},{7,103},{8,104... | collective-permute-start | bytes 393224 | tf_op jit(solution)/shard_map/ppermute | solution.py:264
  29.6 45.2 %collective-permute-start = (f32[256,1024]{1,0:T(8,128)S(1)}, f32[256,1024]{1,0:T(8,128)}, u32[]{:S(2)}, u32[]{:S(2)}) collective-permute-start(f32[256,1024]{1,0:T(8,128)S(1)} %copy-done), channel_id=1, source_target_pairs={{28,32},{60,64},{92,96},{124,128},{156,160},{188,192},{220,224},{2... | collective-permute-start | bytes 3145736 | tf_op jit(solution)/shard_map/ppermute | solution.py:293
  30.9 43.9 %collective-permute-start.1 = (f32[256,1024]{1,0:T(8,128)S(1)}, f32[256,1024]{1,0:T(8,128)}, u32[]{:S(2)}, u32[]{:S(2)}) collective-permute-start(f32[256,1024]{1,0:T(8,128)S(1)} %copy-done), channel_id=1, source_target_pairs={{0,4},{4,8},{8,12},{12,16},{16,20},{20,24},{24,28},{32,36},{36,40}... | collective-permute-start | bytes 3145736 | tf_op jit(solution)/shard_map/ppermute | solution.py:295
  33.2 11.0 %collective-permute-start.21 = (f32[1,128,256]{2,1,0:T(8,128)S(1)}, f32[1,128,256]{2,1,0:T(8,128)S(1)}, u32[]{:S(2)}, u32[]{:S(2)}) collective-permute-start(f32[1,128,256]{2,1,0:T(8,128)S(1)} %fusion.7), channel_id=1, source_target_pairs={{0,1},{1,0},{2,3},{3,2},{4,5},{5,4},{6,7},{7,6},{8,9},{9,8},{10,11... | collective-permute-start | bytes 393224 | tf_op jit(solution)/shard_map/ppermute | solution.py:223
  36.1 40.0 %all-to-all-start = ((f32[8,32,1024]{2,1,0:T(8,128)}), f32[8,32,1024]{2,1,0:T(8,128)S(1)}, u32[]{:S(2)}, u32[]{:S(2)}) async-start(f32[8,32,1024]{2,1,0:T(8,128)} %broadcast_in_dim.6), calls=%async_computation | async-start | bytes 2097152 | tf_op jit(solution)/shard_map/all_to_all | solution.py:271
  51.9 0.7 copy-start.1
  60.5 6.8 %collective-permute-start.26 = (f32[200,128]{1,0:T(8,128)S(1)}, f32[200,128]{1,0:T(8,128)S(1)}, u32[]{:S(2)}, u32[]{:S(2)}) collective-permute-start(f32[200,128]{1,0:T(8,128)S(1)} %factor_second.1), channel_id=1, source_target_pairs={{0,192},{1,193},{2,194},{3,195}} | collective-permute-start | bytes 307208 | tf_op jit(solution)/shard_map/ppermute | solution.py:282
  64.7 3.0 %collective-permute-start.24 = (f32[200,128]{1,0:T(8,128)S(1)}, f32[200,128]{1,0:T(8,128)S(1)}, u32[]{:S(2)}, u32[]{:S(2)}) collective-permute-start(f32[200,128]{1,0:T(8,128)S(1)} %factor_second.1), channel_id=1, source_target_pairs={{0,128},{1,129},{2,130},{3,131}} | collective-permute-start | bytes 307208 | tf_op jit(solution)/shard_map/ppermute | solution.py:282
  66.0 3.0 %collective-permute-start.25 = (f32[200,128]{1,0:T(8,128)S(1)}, f32[200,128]{1,0:T(8,128)S(1)}, u32[]{:S(2)}, u32[]{:S(2)}) collective-permute-start(f32[200,128]{1,0:T(8,128)S(1)} %factor_second.1), channel_id=1, source_target_pairs={{0,64},{1,65},{2,66},{3,67}} | collective-permute-start | bytes 307208 | tf_op jit(solution)/shard_map/ppermute | solution.py:282
  69.0 14.4 %collective-permute-start.29 = (f32[200,128]{1,0:T(8,128)S(1)}, f32[200,128]{1,0:T(8,128)}, u32[]{:S(2)}, u32[]{:S(2)}) collective-permute-start(f32[200,128]{1,0:T(8,128)S(1)} %add_select_fusion.4), channel_id=1, source_target_pairs={{0,32},{64,96},{128,160},{192,224},{1,33},{65,97},{129,161},{193,2... | collective-permute-start | bytes 307208 | tf_op jit(solution)/shard_map/ppermute | solution.py:282
  70.9 12.4 %collective-permute-start.27 = (f32[200,128]{1,0:T(8,128)S(1)}, f32[200,128]{1,0:T(8,128)}, u32[]{:S(2)}, u32[]{:S(2)}) collective-permute-start(f32[200,128]{1,0:T(8,128)S(1)} %add_select_fusion.4), channel_id=1, source_target_pairs={{0,16},{64,80},{128,144},{192,208},{1,17},{65,81},{129,145},{193,2... | collective-permute-start | bytes 307208 | tf_op jit(solution)/shard_map/ppermute | solution.py:282
  72.8 10.5 %collective-permute-start.28 = (f32[200,128]{1,0:T(8,128)S(1)}, f32[200,128]{1,0:T(8,128)}, u32[]{:S(2)}, u32[]{:S(2)}) collective-permute-start(f32[200,128]{1,0:T(8,128)S(1)} %add_select_fusion.4), channel_id=1, source_target_pairs={{0,48},{64,112},{128,176},{192,240},{1,49},{65,113},{129,177},{193... | collective-permute-start | bytes 307208 | tf_op jit(solution)/shard_map/ppermute | solution.py:282
  78.0 10.3 %collective-permute-start.16 = (f32[2,256,256]{2,1,0:T(8,128)S(1)}, f32[2,256,256]{2,1,0:T(8,128)S(1)}, u32[]{:S(2)}, u32[]{:S(2)}) collective-permute-start(f32[2,256,256]{2,1,0:T(8,128)S(1)} %cross.1), channel_id=1, source_target_pairs={{0,1},{1,0},{2,3},{3,2},{4,5},{5,4},{6,7},{7,6},{8,9},{9,8},{10,11... | collective-permute-start | bytes 1572872 | tf_op jit(solution)/shard_map/ppermute | solution.py:223
  83.2 5.3 %collective-permute-start.22 = (f32[1,2,64,256]{3,2,1,0:T(8,128)S(1)}, f32[1,2,64,256]{3,2,1,0:T(8,128)S(1)}, u32[]{:S(2)}, u32[]{:S(2)}) collective-permute-start(f32[1,2,64,256]{3,2,1,0:T(8,128)S(1)} %dynamic-slice_bitcast_fusion.1), channel_id=1, source_target_pairs={{0,1},{1,0},{2,3},{3,2},{4,5},{5,4},{6,7},{7,6},{8,9},{9,8},{10,11... | collective-permute-start | bytes 393224 | tf_op jit(solution)/shard_map/ppermute | solution.py:223
  84.4 13.7 %collective-permute-start.32 = (f32[200,128]{1,0:T(8,128)S(1)}, f32[200,128]{1,0:T(8,128)S(1)}, u32[]{:S(2)}, u32[]{:S(2)}) collective-permute-start(f32[200,128]{1,0:T(8,128)S(1)} %add_select_fusion.3), channel_id=1, source_target_pairs={{0,12},{16,28},{32,44},{48,60},{64,76},{80,92},{96,108},{112,124},... | collective-permute-start | bytes 307208 | tf_op jit(solution)/shard_map/ppermute | solution.py:282
  85.7 12.4 %collective-permute-start.30 = (f32[200,128]{1,0:T(8,128)S(1)}, f32[200,128]{1,0:T(8,128)S(1)}, u32[]{:S(2)}, u32[]{:S(2)}) collective-permute-start(f32[200,128]{1,0:T(8,128)S(1)} %add_select_fusion.3), channel_id=1, source_target_pairs={{0,8},{16,24},{32,40},{48,56},{64,72},{80,88},{96,104},{112,120},{... | collective-permute-start | bytes 307208 | tf_op jit(solution)/shard_map/ppermute | solution.py:282
  87.0 11.1 %collective-permute-start.31 = (f32[200,128]{1,0:T(8,128)S(1)}, f32[200,128]{1,0:T(8,128)S(1)}, u32[]{:S(2)}, u32[]{:S(2)}) collective-permute-start(f32[200,128]{1,0:T(8,128)S(1)} %add_select_fusion.3), channel_id=1, source_target_pairs={{0,4},{16,20},{32,36},{48,52},{64,68},{80,84},{96,100},{112,116},{... | collective-permute-start | bytes 307208 | tf_op jit(solution)/shard_map/ppermute | solution.py:282
  88.4 7.5 %collective-permute-start.17 = (f32[2,128,256]{2,1,0:T(8,128)S(1)}, f32[2,128,256]{2,1,0:T(8,128)S(1)}, u32[]{:S(2)}, u32[]{:S(2)}) collective-permute-start(f32[2,128,256]{2,1,0:T(8,128)S(1)} %dynamic-slice_bitcast_fusion), channel_id=1, source_target_pairs={{0,2},{2,0},{1,3},{3,1},{4,6},{6,4},{5,7},{7,5},{8,10},{10,8},{9,1... | collective-permute-start | bytes 786440 | tf_op jit(solution)/shard_map/ppermute | solution.py:223
  88.6 9.6 %collective-permute-start.23 = (f32[1,64,256]{2,1,0:T(8,128)S(1)}, f32[1,64,256]{2,1,0:T(8,128)S(1)}, u32[]{:S(2)}, u32[]{:S(2)}) collective-permute-start(f32[1,64,256]{2,1,0:T(8,128)S(1)} %dynamic-slice_bitcast_fusion.3), channel_id=1, source_target_pairs={{0,2},{2,0},{1,3},{3,1},{4,6},{6,4},{5,7},{7,5},{8,10},{10,8},{9,1... | collective-permute-start | bytes 196616 | tf_op jit(solution)/shard_map/ppermute | solution.py:223
  95.9 3.6 %collective-permute-start.18 = (f32[2,128,256]{2,1,0:T(8,128)S(1)}, f32[2,128,256]{2,1,0:T(8,128)S(1)}, u32[]{:S(2)}, u32[]{:S(2)}) collective-permute-start(f32[2,128,256]{2,1,0:T(8,128)S(1)} %fusion.8.own_ref), channel_id=1, source_target_pairs={{0,1},{1,0},{2,3},{3,2},{4,5},{5,4},{6,7},{7,6},{8,9},{9,8},{10,11... | collective-permute-start | bytes 786440 | tf_op jit(solution)/shard_map/ppermute | solution.py:223
  98.1 1.4 %collective-permute-start.33 = (f32[200,128]{1,0:T(8,128)S(1)}, f32[200,128]{1,0:T(8,128)S(1)}, u32[]{:S(2)}, u32[]{:S(2)}) collective-permute-start(f32[200,128]{1,0:T(8,128)S(1)} %add_select_fusion.2.mine_ref), channel_id=1, source_target_pairs={{0,1},{1,0},{2,3},{3,2},{4,5},{5,4},{6,7},{7,6},{8,9},{9,8},{10,11... | collective-permute-start | bytes 307208 | tf_op jit(solution)/shard_map/ppermute | solution.py:223

commit v6 on v5

--- a/solution.py
+++ b/solution.py
@@ -290,10 +290,10 @@
     at = jnp.stack(
         [lax.axis_index(PAR), lax.axis_index(BLK), lax.axis_index("core")]
     ).astype(jnp.int32)
-    wrapped = lax.ppermute(log_derivs, BLK, [(b, (b + 1) % 64) for b in range(7, 64, 8)])
+    wrapped = lax.ppermute(log_derivs, BLK, [(b, (b + 1) % 64) for b in range(3, 64, 4)])
     piece = scatter_lead(log_derivs)
-    near = lax.ppermute(log_derivs, BLK, [(b, b + 1) for b in range(64) if b % 8 != 7])
-    prev_rows = jnp.where(lax.axis_index(PLANE) == 0, wrapped, near)
+    near = lax.ppermute(log_derivs, BLK, [(b, b + 1) for b in range(64) if b % 4 != 3])
+    prev_rows = jnp.where(lax.axis_index("y") == 0, wrapped, near)
     self_part = outer_tile(log_derivs, log_derivs)[None]
     own, other = sum_halves(self_part)
     upper = lax.axis_index("core") == 0

time: 103 us -> 103 us (level)
  no operation moved by 1% of the time
where the time goes in v6:
time: 103 us; the launch traced here: 102 us
  starting transfers between devices  62.3 us (60%)
  Pallas kernels  19.9 us (19%)
  waiting for transfers between devices  10.5 us (10%)
  local copies, waits for them, and re-layouts  3.24 us (3%)
  other arithmetic  2.88 us (3%)
  matrix products  2.05 us (2%)
  between operations  1.13 us (1%)
    ppermute x9, starting transfers between devices, small_tree(): got = [lax.ppermute(value, BLK, route) for route in routes]  16.4 us
    ppermute x7, starting transfers between devices, scatter_lead(): lax.ppermute(rows[k * part:(k + 1) * part], BLK, [(0, k)])  13.8 us
    ppermute x9, starting transfers between devices, swapped(): return lax.ppermute(value, axis, [(0, 1), (1, 0)])  11.3 us
    ppermute x7, starting transfers between devices, along_z(): got = [lax.ppermute(piece, 'z', [(0, k)]) for k in STACK_ORDER]  9.07 us
    all_to_all x1, starting transfers between devices, over_plane(): lax.all_to_all(copies, PLANE, split_axis=0, concat_axis=0, tiled=True)  8.07 us
    pallas_call x1, Pallas kernels, factor_second(): pl.pallas_call(kernel, out_shape=f32(3 * n // 4 + 8, n // 2), in_specs=[S...  7.92 us
    pallas_call x1, Pallas kernels, factor_first(): pl.pallas_call(factor_first_kernel, out_shape=f32(2, n, n), in_specs=[VME...  7.59 us
    ppermute x9, waiting for transfers between devices, swapped(): return lax.ppermute(value, axis, [(0, 1), (1, 0)])  7.06 us
  transfers between devices with their start and end apart: 35, of which 5 were waited for; matrix products, arithmetic and copies ran while one was open for 6% of the time, Pallas kernels for 17%

profile of v6, /device:TPU:1, one launch (start us, length us, event | category | flops | bytes accessed | tf_op | source)
XLA Modules:
  0.0 102.0 jit_solution(2690886935562296189)
XLA Ops:
  0.6 1.4 %fusion.1 = (f32[32,1024]{1,0:T(8,128)S(1)}, f32[32,1024]{1,0:T(8,128)S(1)}, f32[32,1024]{1,0:T(8,128)S(1)}, f32[32,1024]{1,0:T(8,128)S(1)}, f32[32,1024]{1,0:T(...) fusion(f32[256,1024]{1,0:T(8,128)} %rows_ref.1), kind=kLoop, calls=%fused_computation.18 | loop fusion | bytes 1835008 | tf_op jit(solution)/shard_map/slice | solution.py:257
  2.0 5.5 %collective-permute-start.8 = (f32[32,1024]{1,0:T(8,128)S(1)}, f32[32,1024]{1,0:T(8,128)S(1)}, u32[]{:S(2)}, u32[]{:S(2)}) collective-permute-start(f32[32,1024]{1,0:T(8,128)S(1)} %get-tuple-element.13), channel_id=1, source_target_pairs={{0,16},{1,17},{2,18},{3,19}} | collective-permute-start | bytes 393224 | tf_op jit(solution)/shard_map/ppermute | solution.py:257
  7.5 1.3 %collective-permute-start.7 = (f32[32,1024]{1,0:T(8,128)S(1)}, f32[32,1024]{1,0:T(8,128)S(1)}, u32[]{:S(2)}, u32[]{:S(2)}) collective-permute-start(f32[32,1024]{1,0:T(8,128)S(1)} %get-tuple-element.14), channel_id=1, source_target_pairs={{0,12},{1,13},{2,14},{3,15}} | collective-permute-start | bytes 393224 | tf_op jit(solution)/shard_map/ppermute | solution.py:257
  8.8 1.3 %collective-permute-start.6 = (f32[32,1024]{1,0:T(8,128)S(1)}, f32[32,1024]{1,0:T(8,128)S(1)}, u32[]{:S(2)}, u32[]{:S(2)}) collective-permute-start(f32[32,1024]{1,0:T(8,128)S(1)} %get-tuple-element.15), channel_id=1, source_target_pairs={{0,4},{1,5},{2,6},{3,7}} | collective-permute-start | bytes 393224 | tf_op jit(solution)/shard_map/ppermute | solution.py:257
  10.1 1.9 %collective-permute-start.5 = (f32[32,1024]{1,0:T(8,128)S(1)}, f32[32,1024]{1,0:T(8,128)S(1)}, u32[]{:S(2)}, u32[]{:S(2)}) collective-permute-start(f32[32,1024]{1,0:T(8,128)S(1)} %get-tuple-element.16), channel_id=1, source_target_pairs={{0,28},{1,29},{2,30},{3,31}} | collective-permute-start | bytes 393224 | tf_op jit(solution)/shard_map/ppermute | solution.py:257
  12.0 1.3 %collective-permute-start.4 = (f32[32,1024]{1,0:T(8,128)S(1)}, f32[32,1024]{1,0:T(8,128)S(1)}, u32[]{:S(2)}, u32[]{:S(2)}) collective-permute-start(f32[32,1024]{1,0:T(8,128)S(1)} %get-tuple-element.17), channel_id=1, source_target_pairs={{0,20},{1,21},{2,22},{3,23}} | collective-permute-start | bytes 393224 | tf_op jit(solution)/shard_map/ppermute | solution.py:257
  13.3 0.0 collective-permute-done.8
  13.3 1.3 %collective-permute-start.2 = (f32[32,1024]{1,0:T(8,128)S(1)}, f32[32,1024]{1,0:T(8,128)S(1)}, u32[]{:S(2)}, u32[]{:S(2)}) collective-permute-start(f32[32,1024]{1,0:T(8,128)S(1)} %get-tuple-element.18), channel_id=1, source_target_pairs={{0,24},{1,25},{2,26},{3,27}} | collective-permute-start | bytes 393224 | tf_op jit(solution)/shard_map/ppermute | solution.py:257
  14.6 1.3 %collective-permute-start.3 = (f32[32,1024]{1,0:T(8,128)S(1)}, f32[32,1024]{1,0:T(8,128)S(1)}, u32[]{:S(2)}, u32[]{:S(2)}) collective-permute-start(f32[32,1024]{1,0:T(8,128)S(1)} %get-tuple-element.12), channel_id=1, source_target_pairs={{0,8},{1,9},{2,10},{3,11}} | collective-permute-start | bytes 393224 | tf_op jit(solution)/shard_map/ppermute | solution.py:257
  15.9 1.0 %convolution_bitcast_fusion = f32[1,256,256]{2,1,0:T(8,128)S(1)} fusion(f32[256,1024]{1,0:T(8,128)S(1)} %copy-done), kind=kOutput, calls=%fused_computation | convolution fusion | flops 805306368 | bytes 1310720 | tf_op jit(solution)/shard_map/dot_general | solution.py:24
  17.0 1.0 %collective-permute-start.19 = (f32[1,256,256]{2,1,0:T(8,128)S(1)}, f32[1,256,256]{2,1,0:T(8,128)S(1)}, u32[]{:S(2)}, u32[]{:S(2)}) collective-permute-start(f32[1,256,256]{2,1,0:T(8,128)S(1)} %convolution_bitcast_fusion), channel_id=1, source_target_pairs={{0,1},{1,0},{2,3},{3,2},{4,5},{5,4},{6,7},{7,6},{8,9},{9,8},{10,11... | collective-permute-start | bytes 786440 | tf_op jit(solution)/shard_map/ppermute | solution.py:223
  18.0 1.7 %collective-permute-done.2 = f32[32,1024]{1,0:T(8,128)S(1)} collective-permute-done((f32[32,1024]{1,0:T(8,128)S(1)}, f32[32,1024]{1,0:T(8,128)S(1)}, u32[]{:S(2)}, u32[]{:S(2)}) %collective-permute-start.2) | collective-permute-done | bytes 131104 | tf_op jit(solution)/shard_map/ppermute | solution.py:257
  19.8 0.0 collective-permute-done.3
  19.8 0.1 add_select_fusion.1
  19.8 1.3 %collective-permute-start.15 = (f32[32,1024]{1,0:T(8,128)S(1)}, f32[32,1024]{1,0:T(8,128)S(1)}, u32[]{:S(2)}, u32[]{:S(2)}) collective-permute-start(f32[32,1024]{1,0:T(8,128)S(1)} %add_select_fusion.1), channel_id=1, source_target_pairs={{0,224},{1,225},{2,226},{3,227},{4,228},{5,229},{6,230},{7,231},{8... | collective-permute-start | bytes 393224 | tf_op jit(solution)/shard_map/ppermute | solution.py:264
  21.1 1.3 %collective-permute-start.14 = (f32[32,1024]{1,0:T(8,128)S(1)}, f32[32,1024]{1,0:T(8,128)S(1)}, u32[]{:S(2)}, u32[]{:S(2)}) collective-permute-start(f32[32,1024]{1,0:T(8,128)S(1)} %add_select_fusion.1), channel_id=1, source_target_pairs={{0,32},{1,33},{2,34},{3,35},{4,36},{5,37},{6,38},{7,39},{8,40},{9,... | collective-permute-start | bytes 393224 | tf_op jit(solution)/shard_map/ppermute | solution.py:264
  22.4 0.0 collective-permute-done.19
  22.5 0.4 collective-permute-start.20
  22.9 0.1 pad_add_fusion.at_ref
  23.0 1.3 %collective-permute-start.13 = (f32[32,1024]{1,0:T(8,128)S(1)}, f32[32,1024]{1,0:T(8,128)S(1)}, u32[]{:S(2)}, u32[]{:S(2)}) collective-permute-start(f32[32,1024]{1,0:T(8,128)S(1)} %add_select_fusion.1), channel_id=1, source_target_pairs={{0,192},{1,193},{2,194},{3,195},{4,196},{5,197},{6,198},{7,199},{8... | collective-permute-start | bytes 393224 | tf_op jit(solution)/shard_map/ppermute | solution.py:264
  24.3 1.3 %collective-permute-start.12 = (f32[32,1024]{1,0:T(8,128)S(1)}, f32[32,1024]{1,0:T(8,128)S(1)}, u32[]{:S(2)}, u32[]{:S(2)}) collective-permute-start(f32[32,1024]{1,0:T(8,128)S(1)} %add_select_fusion.1), channel_id=1, source_target_pairs={{0,64},{1,65},{2,66},{3,67},{4,68},{5,69},{6,70},{7,71},{8,72},{9,... | collective-permute-start | bytes 393224 | tf_op jit(solution)/shard_map/ppermute | solution.py:264
  25.6 1.3 %collective-permute-start.11 = (f32[32,1024]{1,0:T(8,128)S(1)}, f32[32,1024]{1,0:T(8,128)S(1)}, u32[]{:S(2)}, u32[]{:S(2)}) collective-permute-start(f32[32,1024]{1,0:T(8,128)S(1)} %add_select_fusion.1), channel_id=1, source_target_pairs={{0,160},{1,161},{2,162},{3,163},{4,164},{5,165},{6,166},{7,167},{8... | collective-permute-start | bytes 393224 | tf_op jit(solution)/shard_map/ppermute | solution.py:264
  26.9 0.0 collective-permute-done.14
  26.9 1.3 %collective-permute-start.9 = (f32[32,1024]{1,0:T(8,128)S(1)}, f32[32,1024]{1,0:T(8,128)S(1)}, u32[]{:S(2)}, u32[]{:S(2)}) collective-permute-start(f32[32,1024]{1,0:T(8,128)S(1)} %add_select_fusion.1), channel_id=1, source_target_pairs={{0,128},{1,129},{2,130},{3,131},{4,132},{5,133},{6,134},{7,135},{8... | collective-permute-start | bytes 393224 | tf_op jit(solution)/shard_map/ppermute | solution.py:264
  28.2 1.3 %collective-permute-start.10 = (f32[32,1024]{1,0:T(8,128)S(1)}, f32[32,1024]{1,0:T(8,128)S(1)}, u32[]{:S(2)}, u32[]{:S(2)}) collective-permute-start(f32[32,1024]{1,0:T(8,128)S(1)} %add_select_fusion.1), channel_id=1, source_target_pairs={{0,96},{1,97},{2,98},{3,99},{4,100},{5,101},{6,102},{7,103},{8,104... | collective-permute-start | bytes 393224 | tf_op jit(solution)/shard_map/ppermute | solution.py:264
  29.6 1.3 %collective-permute-start = (f32[256,1024]{1,0:T(8,128)S(1)}, f32[256,1024]{1,0:T(8,128)}, u32[]{:S(2)}, u32[]{:S(2)}) collective-permute-start(f32[256,1024]{1,0:T(8,128)S(1)} %copy-done), channel_id=1, source_target_pairs={{12,16},{28,32},{44,48},{60,64},{76,80},{92,96},{108,112},{124,128... | collective-permute-start | bytes 3145736 | tf_op jit(solution)/shard_map/ppermute | solution.py:293
  30.9 0.0 collective-permute-done.12
  30.9 2.3 %collective-permute-start.1 = (f32[256,1024]{1,0:T(8,128)S(1)}, f32[256,1024]{1,0:T(8,128)}, u32[]{:S(2)}, u32[]{:S(2)}) collective-permute-start(f32[256,1024]{1,0:T(8,128)S(1)} %copy-done), channel_id=1, source_target_pairs={{0,4},{4,8},{8,12},{16,20},{20,24},{24,28},{32,36},{36,40},{40,44}... | collective-permute-start | bytes 3145736 | tf_op jit(solution)/shard_map/ppermute | solution.py:295
  33.2 0.0 collective-permute-done.11
  33.2 1.8 %collective-permute-start.21 = (f32[1,128,256]{2,1,0:T(8,128)S(1)}, f32[1,128,256]{2,1,0:T(8,128)S(1)}, u32[]{:S(2)}, u32[]{:S(2)}) collective-permute-start(f32[1,128,256]{2,1,0:T(8,128)S(1)} %fusion.7), channel_id=1, source_target_pairs={{0,1},{1,0},{2,3},{3,2},{4,5},{5,4},{6,7},{7,6},{8,9},{9,8},{10,11... | collective-permute-start | bytes 393224 | tf_op jit(solution)/shard_map/ppermute | solution.py:223
  35.0 0.0 collective-permute-done.9
  35.0 0.0 collective-permute-done.10
  35.0 0.1 add_select_fusion
  35.0 1.1 %broadcast_in_dim.6 = f32[8,32,1024]{2,1,0:T(8,128)} broadcast(f32[32,1024]{1,0:T(8,128)S(1)} %add_select_fusion), dimensions={1,2} | broadcast | bytes 1179648 | tf_op jit(solution)/shard_map/broadcast_in_dim | solution.py:270
  36.1 8.1 %all-to-all-start = ((f32[8,32,1024]{2,1,0:T(8,128)}), f32[8,32,1024]{2,1,0:T(8,128)S(1)}, u32[]{:S(2)}, u32[]{:S(2)}) async-start(f32[8,32,1024]{2,1,0:T(8,128)} %broadcast_in_dim.6), calls=%async_computation | async-start | bytes 2097152 | tf_op jit(solution)/shard_map/all_to_all | solution.py:271
  44.3 7.6 %factor_first.1.state_in_ref = f32[2,256,256]{2,1,0:T(8,128)S(1)} custom-call(f32[256,256]{1,0:T(8,128)S(1)} %pad_maximum_fusion.sum_ref.self_ref), custom_call_target="tpu_custom_call" | custom-call | flops 8000000000 | bytes 1048576 | tf_op jit(solution)/shard_map/factor_first/pallas_call | solution.py:118
  51.9 0.0 copy-start.1
  51.9 0.7 copy-done.1
  52.6 7.9 %factor_second.1 = f32[200,128]{1,0:T(8,128)S(1)} custom-call(s32[3]{0:T(128)S(1)} %pad_add_fusion.at_ref, f32[2,256,256]{2,1,0:T(8,128)S(1)} %factor_first.1.state_in_ref, f32[1,256]{1,0:T(1,128)S(1)} %bitcast.44), custom_call_target="tpu_custom_call" | custom-call | flops 8000000000 | bytes 1048576 | tf_op jit(solution)/shard_map/factor_second/pallas_call | solution.py:136
  60.5 4.2 %collective-permute-start.26 = (f32[200,128]{1,0:T(8,128)S(1)}, f32[200,128]{1,0:T(8,128)S(1)}, u32[]{:S(2)}, u32[]{:S(2)}) collective-permute-start(f32[200,128]{1,0:T(8,128)S(1)} %factor_second.1), channel_id=1, source_target_pairs={{0,192},{1,193},{2,194},{3,195}} | collective-permute-start | bytes 307208 | tf_op jit(solution)/shard_map/ppermute | solution.py:282
  64.7 1.3 %collective-permute-start.24 = (f32[200,128]{1,0:T(8,128)S(1)}, f32[200,128]{1,0:T(8,128)S(1)}, u32[]{:S(2)}, u32[]{:S(2)}) collective-permute-start(f32[200,128]{1,0:T(8,128)S(1)} %factor_second.1), channel_id=1, source_target_pairs={{0,128},{1,129},{2,130},{3,131}} | collective-permute-start | bytes 307208 | tf_op jit(solution)/shard_map/ppermute | solution.py:282
  66.0 1.3 %collective-permute-start.25 = (f32[200,128]{1,0:T(8,128)S(1)}, f32[200,128]{1,0:T(8,128)S(1)}, u32[]{:S(2)}, u32[]{:S(2)}) collective-permute-start(f32[200,128]{1,0:T(8,128)S(1)} %factor_second.1), channel_id=1, source_target_pairs={{0,64},{1,65},{2,66},{3,67}} | collective-permute-start | bytes 307208 | tf_op jit(solution)/shard_map/ppermute | solution.py:282
  67.3 0.3 collective-permute-done.24
  67.6 1.3 %collective-permute-done.25 = f32[200,128]{1,0:T(8,128)S(1)} collective-permute-done((f32[200,128]{1,0:T(8,128)S(1)}, f32[200,128]{1,0:T(8,128)S(1)}, u32[]{:S(2)}, u32[]{:S(2)}) %collective-permute-start.25) | collective-permute-done | bytes 102432 | tf_op jit(solution)/shard_map/ppermute | solution.py:282
  69.0 1.9 %collective-permute-start.29 = (f32[200,128]{1,0:T(8,128)S(1)}, f32[200,128]{1,0:T(8,128)}, u32[]{:S(2)}, u32[]{:S(2)}) collective-permute-start(f32[200,128]{1,0:T(8,128)S(1)} %add_select_fusion.4), channel_id=1, source_target_pairs={{0,32},{64,96},{128,160},{192,224},{1,33},{65,97},{129,161},{193,2... | collective-permute-start | bytes 307208 | tf_op jit(solution)/shard_map/ppermute | solution.py:282
  70.9 1.9 %collective-permute-start.27 = (f32[200,128]{1,0:T(8,128)S(1)}, f32[200,128]{1,0:T(8,128)}, u32[]{:S(2)}, u32[]{:S(2)}) collective-permute-start(f32[200,128]{1,0:T(8,128)S(1)} %add_select_fusion.4), channel_id=1, source_target_pairs={{0,16},{64,80},{128,144},{192,208},{1,17},{65,81},{129,145},{193,2... | collective-permute-start | bytes 307208 | tf_op jit(solution)/shard_map/ppermute | solution.py:282
  72.8 1.9 %collective-permute-start.28 = (f32[200,128]{1,0:T(8,128)S(1)}, f32[200,128]{1,0:T(8,128)}, u32[]{:S(2)}, u32[]{:S(2)}) collective-permute-start(f32[200,128]{1,0:T(8,128)S(1)} %add_select_fusion.4), channel_id=1, source_target_pairs={{0,48},{64,112},{128,176},{192,240},{1,49},{65,113},{129,177},{193... | collective-permute-start | bytes 307208 | tf_op jit(solution)/shard_map/ppermute | solution.py:282
  74.7 1.4 %broadcast_select_fusion.prev_ref = f32[256,1024]{1,0:T(8,128)S(1)} fusion(f32[256,1024]{1,0:T(8,128)} %collective-permute-done, f32[256,1024]{1,0:T(8,128)} %collective-permute-done.1, pred[]{:T(512)S(6)} %eq.22), kind=kLoop, calls=%fused_computation.1 | loop fusion | flops 262144 | bytes 3145729 | tf_op jit(solution)/shard_map/jit(_where)/select_n | solution.py:296
  76.1 1.9 %cross.1 = f32[2,256,256]{2,1,0:T(8,128)S(1)} custom-call(f32[256,1024]{1,0:T(8,128)S(1)} %copy-done, f32[256,1024]{1,0:T(8,128)S(1)} %broadcast_select_fusion.prev_ref, f32[256,1024]{1,0:T(8,128)S(1)} %bitcast.43), custom_call_target="tpu_custom_call" | custom-call | flops 1000000000 | bytes 1048576 | tf_op jit(solution)/shard_map/cross/pallas_call | solution.py:155
  78.0 4.1 %collective-permute-start.16 = (f32[2,256,256]{2,1,0:T(8,128)S(1)}, f32[2,256,256]{2,1,0:T(8,128)S(1)}, u32[]{:S(2)}, u32[]{:S(2)}) collective-permute-start(f32[2,256,256]{2,1,0:T(8,128)S(1)} %cross.1), channel_id=1, source_target_pairs={{0,1},{1,0},{2,3},{3,2},{4,5},{5,4},{6,7},{7,6},{8,9},{9,8},{10,11... | collective-permute-start | bytes 1572872 | tf_op jit(solution)/shard_map/ppermute | solution.py:223
  82.1 1.0 %fusion.2 = f32[256,256]{0,1:T(8,128)S(1)} fusion(f32[256,1024]{1,0:T(8,128)S(1)} %broadcast_select_fusion.prev_ref, f32[256,1024]{1,0:T(8,128)S(1)} %copy-done), kind=kOutput, calls=%fused_computation.19 | convolution fusion | flops 805306368 | bytes 2359296 | tf_op jit(solution)/shard_map/dot_general | solution.py:24
  83.2 0.1 collective-permute-start.22
  83.3 1.0 %add_select_fusion.3 = f32[200,128]{1,0:T(8,128)S(1)} fusion(f32[200,128]{1,0:T(8,128)S(1)} %add_select_fusion.4, f32[200,128]{1,0:T(8,128)} %collective-permute-done.29, f32[200,128]{1,0:T(8,128)} %collective-permute-done.27, f32[200,128]{1,0:T(8,128)} %collective-permute-done.28, pred[]{:T(512)S(6)} %and.14), kind=kLoop, calls=%fused_computation.12 | loop fusion | flops 76800 | bytes 512001 | tf_op jit(solution)/shard_map/jit(_where)/select_n | solution.py:283
  84.4 1.3 %collective-permute-start.32 = (f32[200,128]{1,0:T(8,128)S(1)}, f32[200,128]{1,0:T(8,128)S(1)}, u32[]{:S(2)}, u32[]{:S(2)}) collective-permute-start(f32[200,128]{1,0:T(8,128)S(1)} %add_select_fusion.3), channel_id=1, source_target_pairs={{0,12},{16,28},{32,44},{48,60},{64,76},{80,92},{96,108},{112,124},... | collective-permute-start | bytes 307208 | tf_op jit(solution)/shard_map/ppermute | solution.py:282
  85.7 1.3 %collective-permute-start.30 = (f32[200,128]{1,0:T(8,128)S(1)}, f32[200,128]{1,0:T(8,128)S(1)}, u32[]{:S(2)}, u32[]{:S(2)}) collective-permute-start(f32[200,128]{1,0:T(8,128)S(1)} %add_select_fusion.3), channel_id=1, source_target_pairs={{0,8},{16,24},{32,40},{48,56},{64,72},{80,88},{96,104},{112,120},{... | collective-permute-start | bytes 307208 | tf_op jit(solution)/shard_map/ppermute | solution.py:282
  87.0 1.3 %collective-permute-start.31 = (f32[200,128]{1,0:T(8,128)S(1)}, f32[200,128]{1,0:T(8,128)S(1)}, u32[]{:S(2)}, u32[]{:S(2)}) collective-permute-start(f32[200,128]{1,0:T(8,128)S(1)} %add_select_fusion.3), channel_id=1, source_target_pairs={{0,4},{16,20},{32,36},{48,52},{64,68},{80,84},{96,100},{112,116},{... | collective-permute-start | bytes 307208 | tf_op jit(solution)/shard_map/ppermute | solution.py:282
  88.3 0.1 add.121
  88.4 0.1 collective-permute-start.17
  88.6 1.5 %collective-permute-start.23 = (f32[1,64,256]{2,1,0:T(8,128)S(1)}, f32[1,64,256]{2,1,0:T(8,128)S(1)}, u32[]{:S(2)}, u32[]{:S(2)}) collective-permute-start(f32[1,64,256]{2,1,0:T(8,128)S(1)} %dynamic-slice_bitcast_fusion.3), channel_id=1, source_target_pairs={{0,2},{2,0},{1,3},{3,1},{4,6},{6,4},{5,7},{7,5},{8,10},{10,8},{9,1... | collective-permute-start | bytes 196616 | tf_op jit(solution)/shard_map/ppermute | solution.py:223
  90.1 5.8 %collective-permute-done.17 = f32[2,128,256]{2,1,0:T(8,128)S(1)} collective-permute-done((f32[2,128,256]{2,1,0:T(8,128)S(1)}, f32[2,128,256]{2,1,0:T(8,128)S(1)}, u32[]{:S(2)}, u32[]{:S(2)}) %collective-permute-start.17) | collective-permute-done | bytes 262176 | tf_op jit(solution)/shard_map/ppermute | solution.py:223
  95.9 2.1 %collective-permute-start.18 = (f32[2,128,256]{2,1,0:T(8,128)S(1)}, f32[2,128,256]{2,1,0:T(8,128)S(1)}, u32[]{:S(2)}, u32[]{:S(2)}) collective-permute-start(f32[2,128,256]{2,1,0:T(8,128)S(1)} %fusion.8.own_ref), channel_id=1, source_target_pairs={{0,1},{1,0},{2,3},{3,2},{4,5},{5,4},{6,7},{7,6},{8,9},{9,8},{10,11... | collective-permute-start | bytes 786440 | tf_op jit(solution)/shard_map/ppermute | solution.py:223
  98.1 0.1 collective-permute-start.33
  98.2 1.3 %collective-permute-done.33.twin_ref = f32[200,128]{1,0:T(8,128)S(1)} collective-permute-done((f32[200,128]{1,0:T(8,128)S(1)}, f32[200,128]{1,0:T(8,128)S(1)}, u32[]{:S(2)}, u32[]{:S(2)}) %collective-permute-start.33) | collective-permute-done | bytes 102432 | tf_op jit(solution)/shard_map/ppermute | solution.py:223
  99.5 2.5 %finish.1 = (f32[256,256]{1,0:T(8,128)}, f32[1,256]{1,0:T(1,128)}, f32[64,256]{1,0:T(8,128)}, f32[64,256]{1,0:T(8,128)}) custom-call(s32[3]{0:T(128)S(1)} %pad_add_fusion.at_ref, f32[2,128,256]{2,1,0:T(8,128)S(1)} %fusion.8.own_ref, f32[2,128,256]{2,1,0:T(8,128)S(1)} %collective-permute-done.18.other_ref, f32[256,256]{1,0:T(8,128)S(1)} %pad_maximum_fusion.sum_ref.self_ref, ...), custom_call_target="tpu_custom_call" | custom-call | flops 1000000000 | bytes 1048576 | tf_op jit(solution)/shard_map/finish/pallas_call | solution.py:206
  (37 shorter events, 0.4 us)
Async XLA Ops:
  0.6 15.3 %copy-start = (f32[256,1024]{1,0:T(8,128)S(1)}, f32[256,1024]{1,0:T(8,128)}, u32[]{:S(2)}) copy-start(f32[256,1024]{1,0:T(8,128)} %rows_ref.1) | copy-start | bytes 3145732
  2.0 11.3 %collective-permute-start.8 = (f32[32,1024]{1,0:T(8,128)S(1)}, f32[32,1024]{1,0:T(8,128)S(1)}, u32[]{:S(2)}, u32[]{:S(2)}) collective-permute-start(f32[32,1024]{1,0:T(8,128)S(1)} %get-tuple-element.13), channel_id=1, source_target_pairs={{0,16},{1,17},{2,18},{3,19}} | collective-permute-start | bytes 393224 | tf_op jit(solution)/shard_map/ppermute | solution.py:257
  7.5 7.1 %collective-permute-start.7 = (f32[32,1024]{1,0:T(8,128)S(1)}, f32[32,1024]{1,0:T(8,128)S(1)}, u32[]{:S(2)}, u32[]{:S(2)}) collective-permute-start(f32[32,1024]{1,0:T(8,128)S(1)} %get-tuple-element.14), channel_id=1, source_target_pairs={{0,12},{1,13},{2,14},{3,15}} | collective-permute-start | bytes 393224 | tf_op jit(solution)/shard_map/ppermute | solution.py:257
  8.8 8.2 %collective-permute-start.6 = (f32[32,1024]{1,0:T(8,128)S(1)}, f32[32,1024]{1,0:T(8,128)S(1)}, u32[]{:S(2)}, u32[]{:S(2)}) collective-permute-start(f32[32,1024]{1,0:T(8,128)S(1)} %get-tuple-element.15), channel_id=1, source_target_pairs={{0,4},{1,5},{2,6},{3,7}} | collective-permute-start | bytes 393224 | tf_op jit(solution)/shard_map/ppermute | solution.py:257
  10.1 7.9 %collective-permute-start.5 = (f32[32,1024]{1,0:T(8,128)S(1)}, f32[32,1024]{1,0:T(8,128)S(1)}, u32[]{:S(2)}, u32[]{:S(2)}) collective-permute-start(f32[32,1024]{1,0:T(8,128)S(1)} %get-tuple-element.16), channel_id=1, source_target_pairs={{0,28},{1,29},{2,30},{3,31}} | collective-permute-start | bytes 393224 | tf_op jit(solution)/shard_map/ppermute | solution.py:257
  12.0 6.0 %collective-permute-start.4 = (f32[32,1024]{1,0:T(8,128)S(1)}, f32[32,1024]{1,0:T(8,128)S(1)}, u32[]{:S(2)}, u32[]{:S(2)}) collective-permute-start(f32[32,1024]{1,0:T(8,128)S(1)} %get-tuple-element.17), channel_id=1, source_target_pairs={{0,20},{1,21},{2,22},{3,23}} | collective-permute-start | bytes 393224 | tf_op jit(solution)/shard_map/ppermute | solution.py:257
  13.3 6.5 %collective-permute-start.2 = (f32[32,1024]{1,0:T(8,128)S(1)}, f32[32,1024]{1,0:T(8,128)S(1)}, u32[]{:S(2)}, u32[]{:S(2)}) collective-permute-start(f32[32,1024]{1,0:T(8,128)S(1)} %get-tuple-element.18), channel_id=1, source_target_pairs={{0,24},{1,25},{2,26},{3,27}} | collective-permute-start | bytes 393224 | tf_op jit(solution)/shard_map/ppermute | solution.py:257
  14.6 5.1 %collective-permute-start.3 = (f32[32,1024]{1,0:T(8,128)S(1)}, f32[32,1024]{1,0:T(8,128)S(1)}, u32[]{:S(2)}, u32[]{:S(2)}) collective-permute-start(f32[32,1024]{1,0:T(8,128)S(1)} %get-tuple-element.12), channel_id=1, source_target_pairs={{0,8},{1,9},{2,10},{3,11}} | collective-permute-start | bytes 393224 | tf_op jit(solution)/shard_map/ppermute | solution.py:257
  17.0 5.5 %collective-permute-start.19 = (f32[1,256,256]{2,1,0:T(8,128)S(1)}, f32[1,256,256]{2,1,0:T(8,128)S(1)}, u32[]{:S(2)}, u32[]{:S(2)}) collective-permute-start(f32[1,256,256]{2,1,0:T(8,128)S(1)} %convolution_bitcast_fusion), channel_id=1, source_target_pairs={{0,1},{1,0},{2,3},{3,2},{4,5},{5,4},{6,7},{7,6},{8,9},{9,8},{10,11... | collective-permute-start | bytes 786440 | tf_op jit(solution)/shard_map/ppermute | solution.py:223
  19.8 5.8 %collective-permute-start.15 = (f32[32,1024]{1,0:T(8,128)S(1)}, f32[32,1024]{1,0:T(8,128)S(1)}, u32[]{:S(2)}, u32[]{:S(2)}) collective-permute-start(f32[32,1024]{1,0:T(8,128)S(1)} %add_select_fusion.1), channel_id=1, source_target_pairs={{0,224},{1,225},{2,226},{3,227},{4,228},{5,229},{6,230},{7,231},{8... | collective-permute-start | bytes 393224 | tf_op jit(solution)/shard_map/ppermute | solution.py:264
  21.1 5.8 %collective-permute-start.14 = (f32[32,1024]{1,0:T(8,128)S(1)}, f32[32,1024]{1,0:T(8,128)S(1)}, u32[]{:S(2)}, u32[]{:S(2)}) collective-permute-start(f32[32,1024]{1,0:T(8,128)S(1)} %add_select_fusion.1), channel_id=1, source_target_pairs={{0,32},{1,33},{2,34},{3,35},{4,36},{5,37},{6,38},{7,39},{8,40},{9,... | collective-permute-start | bytes 393224 | tf_op jit(solution)/shard_map/ppermute | solution.py:264
  22.5 5.7 %collective-permute-start.20 = (f32[1,128,256]{2,1,0:T(8,128)S(1)}, f32[1,128,256]{2,1,0:T(8,128)S(1)}, u32[]{:S(2)}, u32[]{:S(2)}) collective-permute-start(f32[1,128,256]{2,1,0:T(8,128)S(1)} %dynamic-slice_bitcast_fusion.2), channel_id=1, source_target_pairs={{0,2},{2,0},{1,3},{3,1},{4,6},{6,4},{5,7},{7,5},{8,10},{10,8},{9,1... | collective-permute-start | bytes 393224 | tf_op jit(solution)/shard_map/ppermute | solution.py:223
  23.0 6.6 %collective-permute-start.13 = (f32[32,1024]{1,0:T(8,128)S(1)}, f32[32,1024]{1,0:T(8,128)S(1)}, u32[]{:S(2)}, u32[]{:S(2)}) collective-permute-start(f32[32,1024]{1,0:T(8,128)S(1)} %add_select_fusion.1), channel_id=1, source_target_pairs={{0,192},{1,193},{2,194},{3,195},{4,196},{5,197},{6,198},{7,199},{8... | collective-permute-start | bytes 393224 | tf_op jit(solution)/shard_map/ppermute | solution.py:264
  24.3 6.6 %collective-permute-start.12 = (f32[32,1024]{1,0:T(8,128)S(1)}, f32[32,1024]{1,0:T(8,128)S(1)}, u32[]{:S(2)}, u32[]{:S(2)}) collective-permute-start(f32[32,1024]{1,0:T(8,128)S(1)} %add_select_fusion.1), channel_id=1, source_target_pairs={{0,64},{1,65},{2,66},{3,67},{4,68},{5,69},{6,70},{7,71},{8,72},{9,... | collective-permute-start | bytes 393224 | tf_op jit(solution)/shard_map/ppermute | solution.py:264
  25.6 7.6 %collective-permute-start.11 = (f32[32,1024]{1,0:T(8,128)S(1)}, f32[32,1024]{1,0:T(8,128)S(1)}, u32[]{:S(2)}, u32[]{:S(2)}) collective-permute-start(f32[32,1024]{1,0:T(8,128)S(1)} %add_select_fusion.1), channel_id=1, source_target_pairs={{0,160},{1,161},{2,162},{3,163},{4,164},{5,165},{6,166},{7,167},{8... | collective-permute-start | bytes 393224 | tf_op jit(solution)/shard_map/ppermute | solution.py:264
  26.9 8.1 %collective-permute-start.9 = (f32[32,1024]{1,0:T(8,128)S(1)}, f32[32,1024]{1,0:T(8,128)S(1)}, u32[]{:S(2)}, u32[]{:S(2)}) collective-permute-start(f32[32,1024]{1,0:T(8,128)S(1)} %add_select_fusion.1), channel_id=1, source_target_pairs={{0,128},{1,129},{2,130},{3,131},{4,132},{5,133},{6,134},{7,135},{8... | collective-permute-start | bytes 393224 | tf_op jit(solution)/shard_map/ppermute | solution.py:264
  28.2 6.7 %collective-permute-start.10 = (f32[32,1024]{1,0:T(8,128)S(1)}, f32[32,1024]{1,0:T(8,128)S(1)}, u32[]{:S(2)}, u32[]{:S(2)}) collective-permute-start(f32[32,1024]{1,0:T(8,128)S(1)} %add_select_fusion.1), channel_id=1, source_target_pairs={{0,96},{1,97},{2,98},{3,99},{4,100},{5,101},{6,102},{7,103},{8,104... | collective-permute-start | bytes 393224 | tf_op jit(solution)/shard_map/ppermute | solution.py:264
  29.6 45.2 %collective-permute-start = (f32[256,1024]{1,0:T(8,128)S(1)}, f32[256,1024]{1,0:T(8,128)}, u32[]{:S(2)}, u32[]{:S(2)}) collective-permute-start(f32[256,1024]{1,0:T(8,128)S(1)} %copy-done), channel_id=1, source_target_pairs={{12,16},{28,32},{44,48},{60,64},{76,80},{92,96},{108,112},{124,128... | collective-permute-start | bytes 3145736 | tf_op jit(solution)/shard_map/ppermute | solution.py:293
  30.9 43.9 %collective-permute-start.1 = (f32[256,1024]{1,0:T(8,128)S(1)}, f32[256,1024]{1,0:T(8,128)}, u32[]{:S(2)}, u32[]{:S(2)}) collective-permute-start(f32[256,1024]{1,0:T(8,128)S(1)} %copy-done), channel_id=1, source_target_pairs={{0,4},{4,8},{8,12},{16,20},{20,24},{24,28},{32,36},{36,40},{40,44}... | collective-permute-start | bytes 3145736 | tf_op jit(solution)/shard_map/ppermute | solution.py:295
  33.2 11.0 %collective-permute-start.21 = (f32[1,128,256]{2,1,0:T(8,128)S(1)}, f32[1,128,256]{2,1,0:T(8,128)S(1)}, u32[]{:S(2)}, u32[]{:S(2)}) collective-permute-start(f32[1,128,256]{2,1,0:T(8,128)S(1)} %fusion.7), channel_id=1, source_target_pairs={{0,1},{1,0},{2,3},{3,2},{4,5},{5,4},{6,7},{7,6},{8,9},{9,8},{10,11... | collective-permute-start | bytes 393224 | tf_op jit(solution)/shard_map/ppermute | solution.py:223
  36.1 40.0 %all-to-all-start = ((f32[8,32,1024]{2,1,0:T(8,128)}), f32[8,32,1024]{2,1,0:T(8,128)S(1)}, u32[]{:S(2)}, u32[]{:S(2)}) async-start(f32[8,32,1024]{2,1,0:T(8,128)} %broadcast_in_dim.6), calls=%async_computation | async-start | bytes 2097152 | tf_op jit(solution)/shard_map/all_to_all | solution.py:271
  51.9 0.7 copy-start.1
  60.5 6.8 %collective-permute-start.26 = (f32[200,128]{1,0:T(8,128)S(1)}, f32[200,128]{1,0:T(8,128)S(1)}, u32[]{:S(2)}, u32[]{:S(2)}) collective-permute-start(f32[200,128]{1,0:T(8,128)S(1)} %factor_second.1), channel_id=1, source_target_pairs={{0,192},{1,193},{2,194},{3,195}} | collective-permute-start | bytes 307208 | tf_op jit(solution)/shard_map/ppermute | solution.py:282
  64.7 3.0 %collective-permute-start.24 = (f32[200,128]{1,0:T(8,128)S(1)}, f32[200,128]{1,0:T(8,128)S(1)}, u32[]{:S(2)}, u32[]{:S(2)}) collective-permute-start(f32[200,128]{1,0:T(8,128)S(1)} %factor_second.1), channel_id=1, source_target_pairs={{0,128},{1,129},{2,130},{3,131}} | collective-permute-start | bytes 307208 | tf_op jit(solution)/shard_map/ppermute | solution.py:282
  66.0 3.0 %collective-permute-start.25 = (f32[200,128]{1,0:T(8,128)S(1)}, f32[200,128]{1,0:T(8,128)S(1)}, u32[]{:S(2)}, u32[]{:S(2)}) collective-permute-start(f32[200,128]{1,0:T(8,128)S(1)} %factor_second.1), channel_id=1, source_target_pairs={{0,64},{1,65},{2,66},{3,67}} | collective-permute-start | bytes 307208 | tf_op jit(solution)/shard_map/ppermute | solution.py:282
  69.0 14.4 %collective-permute-start.29 = (f32[200,128]{1,0:T(8,128)S(1)}, f32[200,128]{1,0:T(8,128)}, u32[]{:S(2)}, u32[]{:S(2)}) collective-permute-start(f32[200,128]{1,0:T(8,128)S(1)} %add_select_fusion.4), channel_id=1, source_target_pairs={{0,32},{64,96},{128,160},{192,224},{1,33},{65,97},{129,161},{193,2... | collective-permute-start | bytes 307208 | tf_op jit(solution)/shard_map/ppermute | solution.py:282
  70.9 12.4 %collective-permute-start.27 = (f32[200,128]{1,0:T(8,128)S(1)}, f32[200,128]{1,0:T(8,128)}, u32[]{:S(2)}, u32[]{:S(2)}) collective-permute-start(f32[200,128]{1,0:T(8,128)S(1)} %add_select_fusion.4), channel_id=1, source_target_pairs={{0,16},{64,80},{128,144},{192,208},{1,17},{65,81},{129,145},{193,2... | collective-permute-start | bytes 307208 | tf_op jit(solution)/shard_map/ppermute | solution.py:282
  72.8 10.5 %collective-permute-start.28 = (f32[200,128]{1,0:T(8,128)S(1)}, f32[200,128]{1,0:T(8,128)}, u32[]{:S(2)}, u32[]{:S(2)}) collective-permute-start(f32[200,128]{1,0:T(8,128)S(1)} %add_select_fusion.4), channel_id=1, source_target_pairs={{0,48},{64,112},{128,176},{192,240},{1,49},{65,113},{129,177},{193... | collective-permute-start | bytes 307208 | tf_op jit(solution)/shard_map/ppermute | solution.py:282
  78.0 10.3 %collective-permute-start.16 = (f32[2,256,256]{2,1,0:T(8,128)S(1)}, f32[2,256,256]{2,1,0:T(8,128)S(1)}, u32[]{:S(2)}, u32[]{:S(2)}) collective-permute-start(f32[2,256,256]{2,1,0:T(8,128)S(1)} %cross.1), channel_id=1, source_target_pairs={{0,1},{1,0},{2,3},{3,2},{4,5},{5,4},{6,7},{7,6},{8,9},{9,8},{10,11... | collective-permute-start | bytes 1572872 | tf_op jit(solution)/shard_map/ppermute | solution.py:223
  83.2 5.3 %collective-permute-start.22 = (f32[1,2,64,256]{3,2,1,0:T(8,128)S(1)}, f32[1,2,64,256]{3,2,1,0:T(8,128)S(1)}, u32[]{:S(2)}, u32[]{:S(2)}) collective-permute-start(f32[1,2,64,256]{3,2,1,0:T(8,128)S(1)} %dynamic-slice_bitcast_fusion.1), channel_id=1, source_target_pairs={{0,1},{1,0},{2,3},{3,2},{4,5},{5,4},{6,7},{7,6},{8,9},{9,8},{10,11... | collective-permute-start | bytes 393224 | tf_op jit(solution)/shard_map/ppermute | solution.py:223
  84.4 13.7 %collective-permute-start.32 = (f32[200,128]{1,0:T(8,128)S(1)}, f32[200,128]{1,0:T(8,128)S(1)}, u32[]{:S(2)}, u32[]{:S(2)}) collective-permute-start(f32[200,128]{1,0:T(8,128)S(1)} %add_select_fusion.3), channel_id=1, source_target_pairs={{0,12},{16,28},{32,44},{48,60},{64,76},{80,92},{96,108},{112,124},... | collective-permute-start | bytes 307208 | tf_op jit(solution)/shard_map/ppermute | solution.py:282
  85.7 12.4 %collective-permute-start.30 = (f32[200,128]{1,0:T(8,128)S(1)}, f32[200,128]{1,0:T(8,128)S(1)}, u32[]{:S(2)}, u32[]{:S(2)}) collective-permute-start(f32[200,128]{1,0:T(8,128)S(1)} %add_select_fusion.3), channel_id=1, source_target_pairs={{0,8},{16,24},{32,40},{48,56},{64,72},{80,88},{96,104},{112,120},{... | collective-permute-start | bytes 307208 | tf_op jit(solution)/shard_map/ppermute | solution.py:282
  87.0 11.1 %collective-permute-start.31 = (f32[200,128]{1,0:T(8,128)S(1)}, f32[200,128]{1,0:T(8,128)S(1)}, u32[]{:S(2)}, u32[]{:S(2)}) collective-permute-start(f32[200,128]{1,0:T(8,128)S(1)} %add_select_fusion.3), channel_id=1, source_target_pairs={{0,4},{16,20},{32,36},{48,52},{64,68},{80,84},{96,100},{112,116},{... | collective-permute-start | bytes 307208 | tf_op jit(solution)/shard_map/ppermute | solution.py:282
  88.4 7.5 %collective-permute-start.17 = (f32[2,128,256]{2,1,0:T(8,128)S(1)}, f32[2,128,256]{2,1,0:T(8,128)S(1)}, u32[]{:S(2)}, u32[]{:S(2)}) collective-permute-start(f32[2,128,256]{2,1,0:T(8,128)S(1)} %dynamic-slice_bitcast_fusion), channel_id=1, source_target_pairs={{0,2},{2,0},{1,3},{3,1},{4,6},{6,4},{5,7},{7,5},{8,10},{10,8},{9,1... | collective-permute-start | bytes 786440 | tf_op jit(solution)/shard_map/ppermute | solution.py:223
  88.6 9.6 %collective-permute-start.23 = (f32[1,64,256]{2,1,0:T(8,128)S(1)}, f32[1,64,256]{2,1,0:T(8,128)S(1)}, u32[]{:S(2)}, u32[]{:S(2)}) collective-permute-start(f32[1,64,256]{2,1,0:T(8,128)S(1)} %dynamic-slice_bitcast_fusion.3), channel_id=1, source_target_pairs={{0,2},{2,0},{1,3},{3,1},{4,6},{6,4},{5,7},{7,5},{8,10},{10,8},{9,1... | collective-permute-start | bytes 196616 | tf_op jit(solution)/shard_map/ppermute | solution.py:223
  95.9 3.6 %collective-permute-start.18 = (f32[2,128,256]{2,1,0:T(8,128)S(1)}, f32[2,128,256]{2,1,0:T(8,128)S(1)}, u32[]{:S(2)}, u32[]{:S(2)}) collective-permute-start(f32[2,128,256]{2,1,0:T(8,128)S(1)} %fusion.8.own_ref), channel_id=1, source_target_pairs={{0,1},{1,0},{2,3},{3,2},{4,5},{5,4},{6,7},{7,6},{8,9},{9,8},{10,11... | collective-permute-start | bytes 786440 | tf_op jit(solution)/shard_map/ppermute | solution.py:223
  98.1 1.4 %collective-permute-start.33 = (f32[200,128]{1,0:T(8,128)S(1)}, f32[200,128]{1,0:T(8,128)S(1)}, u32[]{:S(2)}, u32[]{:S(2)}) collective-permute-start(f32[200,128]{1,0:T(8,128)S(1)} %add_select_fusion.2.mine_ref), channel_id=1, source_target_pairs={{0,1},{1,0},{2,3},{3,2},{4,5},{5,4},{6,7},{7,6},{8,9},{9,8},{10,11... | collective-permute-start | bytes 307208 | tf_op jit(solution)/shard_map/ppermute | solution.py:223

commit v7 on v6

--- a/solution.py
+++ b/solution.py
@@ -18,6 +18,7 @@
 
 ridge_shift = 0.05
 CHUNK = 64
+HELPER = 8
 
 
 def dot(a, b, ca, cb):
@@ -77,31 +78,39 @@
             )
 
 
-def factor_first_kernel(sum_ref, state_ref):
-    n = sum_ref.shape[0]
-    tile_ref, inverse_ref = state_ref.at[0], state_ref.at[1]
-    tile_ref[...] = sum_ref[...] + ridge_shift * unit(n, n).astype(jnp.float32)
-    inverse_ref[...] = jnp.zeros((n, n), jnp.float32)
-    eliminate(tile_ref, inverse_ref, 0, n // CHUNK // 2)
-
-
-def factor_second_kernel(at_ref, state_ref, energy_ref, packed_ref):
-    n = state_ref.shape[-1]
-    share = n // 4
-    tile_ref, inverse_ref = state_ref.at[0], state_ref.at[1]
-    eliminate(tile_ref, inverse_ref, n // CHUNK // 2, n // CHUNK)
-    half = n // 2
-    start = pl.multiple_of(at_ref[2] * share, share)
-    packed_ref[:share, :] = inverse_ref[pl.ds(start, share), :half]
-    packed_ref[share:half, :] = inverse_ref[pl.ds(start + half, share), :half]
-    packed_ref[half : half + share, :] = inverse_ref[pl.ds(start + half, share), half:]
-    lead = outer_tile(jnp.broadcast_to(energy_ref[...], (8, n)), inverse_ref[...])
-    first = lax.broadcasted_iota(jnp.int32, (8, half), 0) == 0
-    packed_ref[half + share :, :] = jnp.where(first, lead[:, :half], lead[:, half:])
+def tile_kernel(rows_ref, energy_ref, out_ref):
+    n = rows_ref.shape[0]
+    out_ref[:n, :] = outer_tile(rows_ref[...], rows_ref[...])
+    out_ref[n:, :] = jnp.broadcast_to(energy_ref[...], (8, n))
+
+
+def factor_kernel(at_ref, chip_ref, twin_ref, packed_ref, tile_ref, inverse_ref):
+    n = tile_ref.shape[0]
+    share, half = n // 4, n // 2
+    core = at_ref[2]
+
+    @pl.when(at_ref[1] != HELPER)
+    def _():
+        packed_ref[...] = jnp.zeros(packed_ref.shape, jnp.float32)
+
+    @pl.when(at_ref[1] == HELPER)
+    def _():
+        tile_ref[...] = chip_ref[:n, :] + twin_ref[:n, :] + ridge_shift * unit(n, n).astype(jnp.float32)
+        inverse_ref[...] = jnp.zeros((n, n), jnp.float32)
+        eliminate(tile_ref, inverse_ref, 0, n // CHUNK)
+        start = pl.multiple_of(core * share, share)
+        packed_ref[:share, :] = inverse_ref[pl.ds(start, share), :half]
+        packed_ref[share:half, :] = inverse_ref[pl.ds(start + half, share), :half]
+        packed_ref[half : half + share, :] = inverse_ref[pl.ds(start + half, share), half:]
+        energy = 0.25 * (chip_ref[n:, :] + twin_ref[n:, :])
+        lead = outer_tile(energy, inverse_ref[...])
+        first = lax.broadcasted_iota(jnp.int32, (8, half), 0) == 0
+        packed_ref[half + share :, :] = jnp.where(first, lead[:, :half], lead[:, half:])
 
 
 VMEM = pl.BlockSpec(memory_space=pltpu.VMEM)
 SMEM = pl.BlockSpec(memory_space=pltpu.SMEM)
+ANY = pl.BlockSpec(memory_space=pl.ANY)
 GRANT = pltpu.CompilerParams(vmem_limit_bytes=16 * 2**20)
 
 
@@ -113,36 +122,31 @@
     return pl.CostEstimate(flops=flops, bytes_accessed=2**20, transcendentals=0)
 
 
-def factor_first(total):
-    n = total.shape[0]
-    return pl.pallas_call(
-        factor_first_kernel,
-        out_shape=f32(2, n, n),
-        in_specs=[VMEM],
+def self_tile(rows, energies):
+    n = rows.shape[0]
+    return pl.pallas_call(
+        tile_kernel,
+        out_shape=f32(n + 8, n),
+        in_specs=[VMEM] * 2,
         out_specs=VMEM,
-        name="factor_first",
-        compiler_params=GRANT,
-        cost_estimate=cost(8 * 10**9),
-    )(total)
-
-
-def factor_second(at, state, energies):
-    n = state.shape[-1]
-
-    def kernel(at_ref, state_in_ref, energy_ref, packed_ref, state_ref):
-        state_ref[...] = state_in_ref[...]
-        factor_second_kernel(at_ref, state_ref, energy_ref, packed_ref)
-
-    return pl.pallas_call(
-        kernel,
+        name="tile",
+        compiler_params=GRANT,
+        cost_estimate=cost(10**8),
+    )(rows, energies)
+
+
+def factor(at, chip, twin):
+    n = chip.shape[-1]
+    return pl.pallas_call(
+        factor_kernel,
         out_shape=f32(3 * n // 4 + 8, n // 2),
         in_specs=[SMEM] + [VMEM] * 2,
         out_specs=VMEM,
-        scratch_shapes=[pltpu.VMEM((2, n, n), jnp.float32)],
-        name="factor_second",
+        scratch_shapes=[pltpu.VMEM((n, n), jnp.float32)] * 2,
+        name="factor",
         compiler_params=GRANT,
         cost_estimate=cost(8 * 10**9),
-    )(at, state, energies)
+    )(at, chip, twin)
 
 
 def cross_kernel(rows_ref, prev_ref, lead_ref, out_ref):
@@ -163,8 +167,34 @@
     )(rows, prev_rows, lead_rows)
 
 
+def early_kernel(at_ref, rows_ref, prev_ref, keep_ref, send_ref, tile_ref):
+    share = tile_ref.shape[0] // 4
+    core = at_ref[2]
+    for number, right in ((0, rows_ref), (1, prev_ref)):
+        tile_ref[...] = outer_tile(rows_ref[...], right[...])
+        for xl in range(2):
+            mine = pl.multiple_of((2 * xl + core) * share, share)
+            other = pl.multiple_of((2 * xl + 1 - core) * share, share)
+            keep_ref[number, xl] = tile_ref[pl.ds(mine, share), :]
+            send_ref[number, xl] = tile_ref[pl.ds(other, share), :]
+
+
+def early_tiles(at, rows, prev_rows):
+    n = rows.shape[0]
+    return pl.pallas_call(
+        early_kernel,
+        out_shape=(f32(2, 2, n // 4, n),) * 2,
+        in_specs=[SMEM, VMEM, VMEM],
+        out_specs=(VMEM,) * 2,
+        scratch_shapes=[pltpu.VMEM((n, n), jnp.float32)],
+        name="early",
+        compiler_params=GRANT,
+        cost_estimate=cost(10**9),
+    )(at, rows, prev_rows)
+
+
 def finish_kernel(
-    at_ref, own_ref, other_ref, self_ref, cycle_ref, energy_ref, mine_ref, twin_ref,
+    at_ref, own_ref, other_ref, early_ref, energy_ref, mine_ref, twin_ref,
     panel_ref, energies_ref, diagonal_ref, neighbour_ref, sums_ref, inverse_ref, prev_ref,
 ):
     n = inverse_ref.shape[0]
@@ -191,22 +221,22 @@
         == lax.broadcasted_iota(jnp.int32, (share, n), 1)
     ).astype(jnp.float32)
     diagonal_ref[...] = (
-        self_ref[pl.ds(start, share), :] + ridge_shift * shifted - outer_tile(own, panel)
-    )
-    neighbour_ref[...] = cycle_ref[...] - outer_tile(own, prev_ref[...])
+        early_ref[0] + ridge_shift * shifted - outer_tile(own, panel)
+    )
+    neighbour_ref[...] = early_ref[1] - outer_tile(own, prev_ref[...])
     last = half + share
     lead = jnp.concatenate([mine_ref[last : last + 1, :], mine_ref[last + 1 : last + 2, :]], axis=1)
     remainder = energy_ref[...] - outer_tile(jnp.broadcast_to(lead, (8, n)), panel)[:1]
     energies_ref[...] = jnp.where(at_ref[1] == 0, lead, remainder)
 
 
-def finish(at, own, other, self_sum, cycle_rows, energies, parts):
-    n = self_sum.shape[-1]
+def finish(at, own, other, early, energies, parts):
+    n = early.shape[-1]
     share = n // 4
     return pl.pallas_call(
         finish_kernel,
         out_shape=(f32(n, n), f32(1, n), f32(share, n), f32(share, n)),
-        in_specs=[SMEM] + [VMEM] * 7,
+        in_specs=[SMEM] + [VMEM] * 6,
         out_specs=(VMEM,) * 4,
         scratch_shapes=[
             pltpu.VMEM((2, n, n), jnp.float32),
@@ -216,20 +246,26 @@
         name="finish",
         compiler_params=GRANT,
         cost_estimate=cost(10**9),
-    )(at, own, other, self_sum, cycle_rows, energies, *parts)
+    )(at, own, other, early, energies, *parts)
 
 
 def swapped(value, axis):
     return lax.ppermute(value, axis, [(0, 1), (1, 0)])
 
 
-def sum_scattered(partials):
-    k, n = partials.shape[0], partials.shape[-1]
-    quarters = partials.reshape(k, 2, 2, n // 4, n)
-    core, xl = lax.axis_index("core"), lax.axis_index("xl")
-    pick = lambda a, i, d: lax.dynamic_index_in_dim(a, i, d, keepdims=False)
-    halves = pick(quarters, core, 2) + swapped(pick(quarters, 1 - core, 2), "core")
-    return pick(halves, xl, 1) + swapped(pick(halves, 1 - xl, 1), "xl")
+def sum_scattered(keep, send):
+    xl = lax.axis_index("xl")
+    pick = lambda a, i: lax.dynamic_index_in_dim(a, i, 1, keepdims=False)
+    halves = keep + swapped(send, "core")
+    return pick(halves, xl) + swapped(pick(halves, 1 - xl), "xl")
+
+
+def lent(value, flip):
+    return lax.ppermute(value, ALL, [(p, 4 * HELPER + (p ^ flip)) for p in range(4)])
+
+
+def helper_swapped(value):
+    return lax.ppermute(value, ALL, [(4 * HELPER + p, 4 * HELPER + (p ^ 1)) for p in range(4)])
 
 
 def sum_halves(partials):
@@ -273,13 +309,20 @@
 
 def small_tree(value):
     z, xh, y = (lax.axis_index(a) for a in BLK)
+    ahead = (z + 7) % 8
+    at = lambda i: (i + HELPER) % 64
     rounds = (
-        ([[(0, 8 * k)] for k in (4, 2, 6)], z == 0),
-        ([[(8 * k, 8 * k + d) for k in range(0, 8, 2)] for d in (4, 12, 8)], (z % 2 == 0) & (xh == 0)),
+        ([[(0, 8 * k)] for k in (4, 2, 6)], ahead == 0),
+        (
+            [[(8 * k, 8 * k + d) for k in range(0, 8, 2)] for d in (4, 12, 8)],
+            (ahead % 2 == 0) & (xh == 0),
+        ),
         ([[(4 * k, 4 * k + d) for k in range(16)] for d in (2, 1, 3)], y == 0),
     )
     for routes, holds in rounds:
-        got = [lax.ppermute(value, BLK, route) for route in routes]
+        got = [
+            lax.ppermute(value, BLK, [(at(i), at(k)) for i, k in route]) for route in routes
+        ]
         value = jnp.where(holds, value, total(got))
     return value
 
@@ -288,29 +331,26 @@
     n = log_derivs.shape[0]
     energy_row = energies.reshape(1, n)
     at = jnp.stack(
-        [lax.axis_index(PAR), lax.axis_index(BLK), lax.axis_index("core")]
+        [lax.axis_index(a) for a in (PAR, BLK, "core", "y")]
     ).astype(jnp.int32)
     wrapped = lax.ppermute(log_derivs, BLK, [(b, (b + 1) % 64) for b in range(3, 64, 4)])
+    self_part = self_tile(log_derivs, energy_row)
+    chip = lent(self_part, 0) + lent(self_part, 2)
     piece = scatter_lead(log_derivs)
     near = lax.ppermute(log_derivs, BLK, [(b, b + 1) for b in range(64) if b % 4 != 3])
-    prev_rows = jnp.where(lax.axis_index("y") == 0, wrapped, near)
-    self_part = outer_tile(log_derivs, log_derivs)[None]
-    own, other = sum_halves(self_part)
-    upper = lax.axis_index("core") == 0
-    self_sum = jnp.concatenate(
-        [jnp.where(upper, own[0], other[0]), jnp.where(upper, other[0], own[0])]
-    )
+    twin = helper_swapped(chip)
     piece = along_z(piece)
-    state = factor_first(self_sum)
+    packed = factor(at, chip, twin)
     lead_rows = over_plane(piece).reshape(log_derivs.shape)
-    packed = factor_second(at, state, energy_row)
     packed = small_tree(packed)
     twin = swapped(packed, "core")
-    cycle_rows = sum_scattered(outer_tile(log_derivs, prev_rows)[None])[0]
+    prev_rows = jnp.where(lax.axis_index("y") == 0, wrapped, near)
+    keep, send = early_tiles(at, log_derivs, prev_rows)
+    early = sum_scattered(keep, send)
     partials = cross(log_derivs, prev_rows, lead_rows)
     own, other = sum_halves(partials)
     panel, energies_next, diagonal, neighbour = finish(
-        at, own, other, self_sum, cycle_rows, energy_row, (packed, twin)
+        at, own, other, early, energy_row, (packed, twin)
     )
     return panel, energies_next.reshape(n), diagonal, neighbour
 

time: 103 us -> 128 us (1.24)
  the two profiles are of different devices: /device:TPU:1 before, /device:TPU:96 now
where the time goes in v7:
time: 128 us; the launch traced here: 127 us
  starting transfers between devices  56.1 us (44%)
  waiting for transfers between devices  54.1 us (42%)
  Pallas kernels  9.79 us (8%)
  local copies, waits for them, and re-layouts  3.21 us (3%)
  other arithmetic  2.9 us (2%)
    all_to_all x1, starting transfers between devices, over_plane(): lax.all_to_all(copies, PLANE, split_axis=0, concat_axis=0, tiled=True)  23.8 us
    ppermute x9, waiting for transfers between devices, small_tree(): lax.ppermute(value, BLK, [(at(i), at(k)) for i, k in route])  23.5 us
    ppermute x7, waiting for transfers between devices, along_z(): got = [lax.ppermute(piece, 'z', [(0, k)]) for k in STACK_ORDER]  17.5 us
    ppermute x9, starting transfers between devices, small_tree(): lax.ppermute(value, BLK, [(at(i), at(k)) for i, k in route])  10.6 us
    all_to_all x1, waiting for transfers between devices, over_plane(): lax.all_to_all(copies, PLANE, split_axis=0, concat_axis=0, tiled=True)  8.45 us
    ppermute x7, starting transfers between devices, along_z(): got = [lax.ppermute(piece, 'z', [(0, k)]) for k in STACK_ORDER]  5.29 us
    ppermute x1, starting transfers between devices, on_device(): lax.ppermute(log_derivs, BLK, [(b, b + 1) for b in range(64) if b % 4 != 3])  4.79 us
    ppermute x7, starting transfers between devices, scatter_lead(): lax.ppermute(rows[k * part:(k + 1) * part], BLK, [(0, k)])  4.68 us
  transfers between devices with their start and end apart: 35, of which 5 were waited for; matrix products, arithmetic and copies ran while one was open for 3% of the time, Pallas kernels for 6%

profile of v7, /device:TPU:96, one launch (start us, length us, event | category | flops | bytes accessed | tf_op | source)
XLA Modules:
  0.0 127.3 jit_solution(7466512761600687064)
XLA Ops:
  0.6 1.4 %fusion = (f32[32,1024]{1,0:T(8,128)S(1)}, f32[32,1024]{1,0:T(8,128)S(1)}, f32[32,1024]{1,0:T(8,128)S(1)}, f32[32,1024]{1,0:T(8,128)S(1)}, f32[32,1024]{1,0:T(8,...) fusion(f32[256,1024]{1,0:T(8,128)} %rows_ref.5), kind=kLoop, calls=%fused_computation.10 | loop fusion | bytes 1835008 | tf_op jit(solution)/shard_map/slice | solution.py:293
  2.0 0.7 collective-permute-start.8
  2.7 0.7 collective-permute-start.7
  3.4 0.7 collective-permute-start.6
  4.1 0.7 collective-permute-start.5
  4.7 0.7 collective-permute-start.4
  5.4 0.0 collective-permute-done.8
  5.4 0.7 collective-permute-start.2
  6.1 0.7 collective-permute-start.3
  6.8 0.0 collective-permute-done.6
  6.8 0.0 collective-permute-done.4
  6.8 0.0 collective-permute-done.2
  6.9 0.1 add_select_fusion.1
  6.9 0.7 collective-permute-start.15
  7.6 0.7 collective-permute-start.14
  8.3 0.7 collective-permute-start.13
  9.0 0.7 collective-permute-start.12
  9.6 1.3 %collective-permute-start = (f32[256,1024]{1,0:T(8,128)S(1)}, f32[256,1024]{1,0:T(8,128)}, u32[]{:S(2)}, u32[]{:S(2)}) collective-permute-start(f32[256,1024]{1,0:T(8,128)S(1)} %copy-done), channel_id=1, source_target_pairs={{12,16},{28,32},{44,48},{60,64},{76,80},{92,96},{108,112},{124,128... | collective-permute-start | bytes 3145736 | tf_op jit(solution)/shard_map/ppermute | solution.py:336
  10.9 0.0 collective-permute-done.15
  11.0 4.8 %collective-permute-start.1 = (f32[256,1024]{1,0:T(8,128)S(1)}, f32[256,1024]{1,0:T(8,128)}, u32[]{:S(2)}, u32[]{:S(2)}) collective-permute-start(f32[256,1024]{1,0:T(8,128)S(1)} %copy-done), channel_id=1, source_target_pairs={{0,4},{4,8},{8,12},{16,20},{20,24},{24,28},{32,36},{36,40},{40,44}... | collective-permute-start | bytes 3145736 | tf_op jit(solution)/shard_map/ppermute | solution.py:340
  15.7 0.7 collective-permute-start.11
  16.4 0.0 collective-permute-done.13
  16.4 0.7 collective-permute-start.9
  17.1 1.3 %collective-permute-start.10 = (f32[32,1024]{1,0:T(8,128)S(1)}, f32[32,1024]{1,0:T(8,128)S(1)}, u32[]{:S(2)}, u32[]{:S(2)}) collective-permute-start(f32[32,1024]{1,0:T(8,128)S(1)} %add_select_fusion.1), channel_id=1, source_target_pairs={{0,96},{1,97},{2,98},{3,99},{4,100},{5,101},{6,102},{7,103},{8,104... | collective-permute-start | bytes 393224 | tf_op jit(solution)/shard_map/ppermute | solution.py:300
  18.4 0.0 collective-permute-done.11
  18.4 0.0 collective-permute-done.9
  18.4 17.5 %collective-permute-done.10 = f32[32,1024]{1,0:T(8,128)S(1)} collective-permute-done((f32[32,1024]{1,0:T(8,128)S(1)}, f32[32,1024]{1,0:T(8,128)S(1)}, u32[]{:S(2)}, u32[]{:S(2)}) %collective-permute-start.10) | collective-permute-done | bytes 131104 | tf_op jit(solution)/shard_map/ppermute | solution.py:300
  35.9 0.1 add_select_fusion
  36.0 1.1 broadcast_in_dim.3
  37.1 23.8 %all-to-all-start = ((f32[8,32,1024]{2,1,0:T(8,128)}), f32[8,32,1024]{2,1,0:T(8,128)S(1)}, u32[]{:S(2)}, u32[]{:S(2)}) async-start(f32[8,32,1024]{2,1,0:T(8,128)} %broadcast_in_dim.3), calls=%async_computation | async-start | bytes 2097152 | tf_op jit(solution)/shard_map/all_to_all | solution.py:307
  60.8 0.7 copy-done.1
  61.5 1.0 tile.1
  62.5 0.7 collective-permute-start.21
  63.2 0.7 collective-permute-start.22
  63.9 0.1 pad_add_fusion.at_ref
  64.0 0.0 collective-permute-done.21
  64.0 0.0 collective-permute-done.22
  64.1 1.4 %collective-permute-start.23 = (f32[264,256]{1,0:T(8,128)S(1)}, f32[264,256]{1,0:T(8,128)}, u32[]{:S(2)}, u32[]{:S(2)}) collective-permute-start(f32[264,256]{1,0:T(8,128)S(1)} %add.126.chip_ref), channel_id=1, source_target_pairs={{32,33},{33,32},{34,35},{35,34}} | collective-permute-start | bytes 811016 | tf_op jit(solution)/shard_map/ppermute | solution.py:268
  65.4 1.4 %broadcast_select_fusion.prev_ref = f32[256,1024]{1,0:T(8,128)S(1)} fusion(f32[256,1024]{1,0:T(8,128)} %collective-permute-done, f32[256,1024]{1,0:T(8,128)} %collective-permute-done.1, pred[]{:T(512)S(6)} %eq.22), kind=kLoop, calls=%fused_computation | loop fusion | flops 262144 | bytes 3145729 | tf_op jit(solution)/shard_map/jit(_where)/select_n | solution.py:347
  66.8 8.4 %all-to-all-done = f32[8,32,1024]{2,1,0:T(8,128)S(1)} async-done(((f32[8,32,1024]{2,1,0:T(8,128)}), f32[8,32,1024]{2,1,0:T(8,128)S(1)}, u32[]{:S(2)}, u32[]{:S(2)}) %all-to-all-start) | async-done | bytes 1048608 | tf_op jit(solution)/shard_map/all_to_all | solution.py:307
  75.3 2.7 %cross.1 = f32[2,256,256]{2,1,0:T(8,128)} custom-call(f32[256,1024]{1,0:T(8,128)S(1)} %copy-done, f32[256,1024]{1,0:T(8,128)S(1)} %broadcast_select_fusion.prev_ref, f32[256,1024]{1,0:T(8,128)S(1)} %bitcast.18), custom_call_target="tpu_custom_call" | custom-call | flops 1000000000 | bytes 1048576 | tf_op jit(solution)/shard_map/cross/pallas_call | solution.py:159
  77.9 1.0 factor.1
  78.9 0.7 collective-permute-start.26
  79.6 0.7 collective-permute-start.24
  80.3 1.3 %collective-permute-start.25 = (f32[200,128]{1,0:T(8,128)S(1)}, f32[200,128]{1,0:T(8,128)S(1)}, u32[]{:S(2)}, u32[]{:S(2)}) collective-permute-start(f32[200,128]{1,0:T(8,128)S(1)} %factor.1), channel_id=1, source_target_pairs={{32,96},{33,97},{34,98},{35,99}} | collective-permute-start | bytes 307208 | tf_op jit(solution)/shard_map/ppermute | solution.py:324
  81.6 0.0 collective-permute-done.26
  81.6 0.0 collective-permute-done.24
  81.6 23.5 %collective-permute-done.25 = f32[200,128]{1,0:T(8,128)S(1)} collective-permute-done((f32[200,128]{1,0:T(8,128)S(1)}, f32[200,128]{1,0:T(8,128)S(1)}, u32[]{:S(2)}, u32[]{:S(2)}) %collective-permute-start.25) | collective-permute-done | bytes 102432 | tf_op jit(solution)/shard_map/ppermute | solution.py:324
  105.2 1.3 %collective-permute-start.29 = (f32[200,128]{1,0:T(8,128)S(1)}, f32[200,128]{1,0:T(8,128)S(1)}, u32[]{:S(2)}, u32[]{:S(2)}) collective-permute-start(f32[200,128]{1,0:T(8,128)S(1)} %add_select_fusion.4), channel_id=1, source_target_pairs={{32,64},{96,128},{160,192},{224,0},{33,65},{97,129},{161,193},{225... | collective-permute-start | bytes 307208 | tf_op jit(solution)/shard_map/ppermute | solution.py:324
  106.5 1.3 %collective-permute-start.27 = (f32[200,128]{1,0:T(8,128)S(1)}, f32[200,128]{1,0:T(8,128)S(1)}, u32[]{:S(2)}, u32[]{:S(2)}) collective-permute-start(f32[200,128]{1,0:T(8,128)S(1)} %add_select_fusion.4), channel_id=1, source_target_pairs={{32,48},{96,112},{160,176},{224,240},{33,49},{97,113},{161,177},{2... | collective-permute-start | bytes 307208 | tf_op jit(solution)/shard_map/ppermute | solution.py:324
  107.8 1.5 %collective-permute-start.28 = (f32[200,128]{1,0:T(8,128)S(1)}, f32[200,128]{1,0:T(8,128)S(1)}, u32[]{:S(2)}, u32[]{:S(2)}) collective-permute-start(f32[200,128]{1,0:T(8,128)S(1)} %add_select_fusion.4), channel_id=1, source_target_pairs={{32,80},{96,144},{160,208},{224,16},{33,81},{97,145},{161,209},{22... | collective-permute-start | bytes 307208 | tf_op jit(solution)/shard_map/ppermute | solution.py:324
  109.2 2.6 %early.1 = (f32[2,2,64,256]{3,2,1,0:T(8,128)S(1)}, f32[2,2,64,256]{3,2,1,0:T(8,128)S(1)}) custom-call(s32[4]{0:T(128)S(1)} %pad_add_fusion.at_ref, f32[256,1024]{1,0:T(8,128)S(1)} %copy-done, f32[256,1024]{1,0:T(8,128)S(1)} %broadcast_select_fusion.prev_ref), custom_call_target="tpu_custom_call" | custom-call | flops 1000000000 | bytes 1048576 | tf_op jit(solution)/shard_map/early/pallas_call | solution.py:184
  111.8 0.1 collective-permute-start.19
  111.9 1.1 add.116
  113.1 0.2 collective-permute-start.17
  113.3 1.3 %collective-permute-start.32 = (f32[200,128]{1,0:T(8,128)S(1)}, f32[200,128]{1,0:T(8,128)S(1)}, u32[]{:S(2)}, u32[]{:S(2)}) collective-permute-start(f32[200,128]{1,0:T(8,128)S(1)} %add_select_fusion.3), channel_id=1, source_target_pairs={{32,44},{48,60},{64,76},{80,92},{96,108},{112,124},{128,140},{144,... | collective-permute-start | bytes 307208 | tf_op jit(solution)/shard_map/ppermute | solution.py:324
  114.6 1.3 %collective-permute-start.30 = (f32[200,128]{1,0:T(8,128)S(1)}, f32[200,128]{1,0:T(8,128)S(1)}, u32[]{:S(2)}, u32[]{:S(2)}) collective-permute-start(f32[200,128]{1,0:T(8,128)S(1)} %add_select_fusion.3), channel_id=1, source_target_pairs={{32,40},{48,56},{64,72},{80,88},{96,104},{112,120},{128,136},{144,... | collective-permute-start | bytes 307208 | tf_op jit(solution)/shard_map/ppermute | solution.py:324
  116.0 1.3 %collective-permute-start.31 = (f32[200,128]{1,0:T(8,128)S(1)}, f32[200,128]{1,0:T(8,128)S(1)}, u32[]{:S(2)}, u32[]{:S(2)}) collective-permute-start(f32[200,128]{1,0:T(8,128)S(1)} %add_select_fusion.3), channel_id=1, source_target_pairs={{32,36},{48,52},{64,68},{80,84},{96,100},{112,116},{128,132},{144,... | collective-permute-start | bytes 307208 | tf_op jit(solution)/shard_map/ppermute | solution.py:324
  117.3 2.0 %collective-permute-start.20 = (f32[2,64,256]{2,1,0:T(8,128)S(1)}, f32[2,64,256]{2,1,0:T(8,128)S(1)}, u32[]{:S(2)}, u32[]{:S(2)}) collective-permute-start(f32[2,64,256]{2,1,0:T(8,128)S(1)} %dynamic-slice_bitcast_fusion.1), channel_id=1, source_target_pairs={{0,2},{2,0},{1,3},{3,1},{4,6},{6,4},{5,7},{7,5},{8,10},{10,8},{9,1... | collective-permute-start | bytes 393224 | tf_op jit(solution)/shard_map/ppermute | solution.py:253
  119.3 3.0 %collective-permute-done.17 = f32[2,128,256]{2,1,0:T(8,128)S(1)} collective-permute-done((f32[2,128,256]{2,1,0:T(8,128)S(1)}, f32[2,128,256]{2,1,0:T(8,128)S(1)}, u32[]{:S(2)}, u32[]{:S(2)}) %collective-permute-start.17) | collective-permute-done | bytes 262176 | tf_op jit(solution)/shard_map/ppermute | solution.py:253
  122.4 0.1 collective-permute-start.18
  122.5 0.6 collective-permute-start.33
  123.1 1.6 %collective-permute-done.20 = f32[2,64,256]{2,1,0:T(8,128)S(1)} collective-permute-done((f32[2,64,256]{2,1,0:T(8,128)S(1)}, f32[2,64,256]{2,1,0:T(8,128)S(1)}, u32[]{:S(2)}, u32[]{:S(2)}) %collective-permute-start.20) | collective-permute-done | bytes 131104 | tf_op jit(solution)/shard_map/ppermute | solution.py:253
  124.7 2.5 %finish.1 = (f32[256,256]{1,0:T(8,128)}, f32[1,256]{1,0:T(1,128)}, f32[64,256]{1,0:T(8,128)}, f32[64,256]{1,0:T(8,128)}) custom-call(s32[4]{0:T(128)S(1)} %pad_add_fusion.at_ref, f32[2,128,256]{2,1,0:T(8,128)S(1)} %fusion.1.own_ref, f32[2,128,256]{2,1,0:T(8,128)S(1)} %collective-permute-done.18.other_ref, f32[2,64,256]{2,1,0:T(8,128)S(1)} %bitcast_add_fusion.early_ref, ...), custom_call_target="tpu_custom_call" | custom-call | flops 1000000000 | bytes 1048576 | tf_op jit(solution)/shard_map/finish/pallas_call | solution.py:236
  (31 shorter events, 0.3 us)
Async XLA Ops:
  0.6 6.2 %copy-start = (f32[256,1024]{1,0:T(8,128)S(1)}, f32[256,1024]{1,0:T(8,128)}, u32[]{:S(2)}) copy-start(f32[256,1024]{1,0:T(8,128)} %rows_ref.5) | copy-start | bytes 3145732
  2.0 3.4 %collective-permute-start.8 = (f32[32,1024]{1,0:T(8,128)S(1)}, f32[32,1024]{1,0:T(8,128)S(1)}, u32[]{:S(2)}, u32[]{:S(2)}) collective-permute-start(f32[32,1024]{1,0:T(8,128)S(1)} %get-tuple-element.17), channel_id=1, source_target_pairs={{0,16},{1,17},{2,18},{3,19}} | collective-permute-start | bytes 393224 | tf_op jit(solution)/shard_map/ppermute | solution.py:293
  2.7 3.4 %collective-permute-start.7 = (f32[32,1024]{1,0:T(8,128)S(1)}, f32[32,1024]{1,0:T(8,128)S(1)}, u32[]{:S(2)}, u32[]{:S(2)}) collective-permute-start(f32[32,1024]{1,0:T(8,128)S(1)} %get-tuple-element.18), channel_id=1, source_target_pairs={{0,12},{1,13},{2,14},{3,15}} | collective-permute-start | bytes 393224 | tf_op jit(solution)/shard_map/ppermute | solution.py:293
  3.4 3.4 %collective-permute-start.6 = (f32[32,1024]{1,0:T(8,128)S(1)}, f32[32,1024]{1,0:T(8,128)S(1)}, u32[]{:S(2)}, u32[]{:S(2)}) collective-permute-start(f32[32,1024]{1,0:T(8,128)S(1)} %get-tuple-element.19), channel_id=1, source_target_pairs={{0,4},{1,5},{2,6},{3,7}} | collective-permute-start | bytes 393224 | tf_op jit(solution)/shard_map/ppermute | solution.py:293
  4.1 2.8 %collective-permute-start.5 = (f32[32,1024]{1,0:T(8,128)S(1)}, f32[32,1024]{1,0:T(8,128)S(1)}, u32[]{:S(2)}, u32[]{:S(2)}) collective-permute-start(f32[32,1024]{1,0:T(8,128)S(1)} %get-tuple-element.20), channel_id=1, source_target_pairs={{0,28},{1,29},{2,30},{3,31}} | collective-permute-start | bytes 393224 | tf_op jit(solution)/shard_map/ppermute | solution.py:293
  4.7 2.1 %collective-permute-start.4 = (f32[32,1024]{1,0:T(8,128)S(1)}, f32[32,1024]{1,0:T(8,128)S(1)}, u32[]{:S(2)}, u32[]{:S(2)}) collective-permute-start(f32[32,1024]{1,0:T(8,128)S(1)} %get-tuple-element.21), channel_id=1, source_target_pairs={{0,20},{1,21},{2,22},{3,23}} | collective-permute-start | bytes 393224 | tf_op jit(solution)/shard_map/ppermute | solution.py:293
  5.4 1.4 %collective-permute-start.2 = (f32[32,1024]{1,0:T(8,128)S(1)}, f32[32,1024]{1,0:T(8,128)S(1)}, u32[]{:S(2)}, u32[]{:S(2)}) collective-permute-start(f32[32,1024]{1,0:T(8,128)S(1)} %get-tuple-element.22), channel_id=1, source_target_pairs={{0,24},{1,25},{2,26},{3,27}} | collective-permute-start | bytes 393224 | tf_op jit(solution)/shard_map/ppermute | solution.py:293
  6.1 0.7 collective-permute-start.3
  6.9 4.0 %collective-permute-start.15 = (f32[32,1024]{1,0:T(8,128)S(1)}, f32[32,1024]{1,0:T(8,128)S(1)}, u32[]{:S(2)}, u32[]{:S(2)}) collective-permute-start(f32[32,1024]{1,0:T(8,128)S(1)} %add_select_fusion.1), channel_id=1, source_target_pairs={{0,224},{1,225},{2,226},{3,227},{4,228},{5,229},{6,230},{7,231},{8... | collective-permute-start | bytes 393224 | tf_op jit(solution)/shard_map/ppermute | solution.py:300
  7.6 8.1 %collective-permute-start.14 = (f32[32,1024]{1,0:T(8,128)S(1)}, f32[32,1024]{1,0:T(8,128)S(1)}, u32[]{:S(2)}, u32[]{:S(2)}) collective-permute-start(f32[32,1024]{1,0:T(8,128)S(1)} %add_select_fusion.1), channel_id=1, source_target_pairs={{0,32},{1,33},{2,34},{3,35},{4,36},{5,37},{6,38},{7,39},{8,40},{9,... | collective-permute-start | bytes 393224 | tf_op jit(solution)/shard_map/ppermute | solution.py:300
  8.3 8.1 %collective-permute-start.13 = (f32[32,1024]{1,0:T(8,128)S(1)}, f32[32,1024]{1,0:T(8,128)S(1)}, u32[]{:S(2)}, u32[]{:S(2)}) collective-permute-start(f32[32,1024]{1,0:T(8,128)S(1)} %add_select_fusion.1), channel_id=1, source_target_pairs={{0,192},{1,193},{2,194},{3,195},{4,196},{5,197},{6,198},{7,199},{8... | collective-permute-start | bytes 393224 | tf_op jit(solution)/shard_map/ppermute | solution.py:300
  9.0 8.1 %collective-permute-start.12 = (f32[32,1024]{1,0:T(8,128)S(1)}, f32[32,1024]{1,0:T(8,128)S(1)}, u32[]{:S(2)}, u32[]{:S(2)}) collective-permute-start(f32[32,1024]{1,0:T(8,128)S(1)} %add_select_fusion.1), channel_id=1, source_target_pairs={{0,64},{1,65},{2,66},{3,67},{4,68},{5,69},{6,70},{7,71},{8,72},{9,... | collective-permute-start | bytes 393224 | tf_op jit(solution)/shard_map/ppermute | solution.py:300
  9.6 55.8 %collective-permute-start = (f32[256,1024]{1,0:T(8,128)S(1)}, f32[256,1024]{1,0:T(8,128)}, u32[]{:S(2)}, u32[]{:S(2)}) collective-permute-start(f32[256,1024]{1,0:T(8,128)S(1)} %copy-done), channel_id=1, source_target_pairs={{12,16},{28,32},{44,48},{60,64},{76,80},{92,96},{108,112},{124,128... | collective-permute-start | bytes 3145736 | tf_op jit(solution)/shard_map/ppermute | solution.py:336
  11.0 54.5 %collective-permute-start.1 = (f32[256,1024]{1,0:T(8,128)S(1)}, f32[256,1024]{1,0:T(8,128)}, u32[]{:S(2)}, u32[]{:S(2)}) collective-permute-start(f32[256,1024]{1,0:T(8,128)S(1)} %copy-done), channel_id=1, source_target_pairs={{0,4},{4,8},{8,12},{16,20},{20,24},{24,28},{32,36},{36,40},{40,44}... | collective-permute-start | bytes 3145736 | tf_op jit(solution)/shard_map/ppermute | solution.py:340
  15.7 2.7 %collective-permute-start.11 = (f32[32,1024]{1,0:T(8,128)S(1)}, f32[32,1024]{1,0:T(8,128)S(1)}, u32[]{:S(2)}, u32[]{:S(2)}) collective-permute-start(f32[32,1024]{1,0:T(8,128)S(1)} %add_select_fusion.1), channel_id=1, source_target_pairs={{0,160},{1,161},{2,162},{3,163},{4,164},{5,165},{6,166},{7,167},{8... | collective-permute-start | bytes 393224 | tf_op jit(solution)/shard_map/ppermute | solution.py:300
  16.4 2.0 %collective-permute-start.9 = (f32[32,1024]{1,0:T(8,128)S(1)}, f32[32,1024]{1,0:T(8,128)S(1)}, u32[]{:S(2)}, u32[]{:S(2)}) collective-permute-start(f32[32,1024]{1,0:T(8,128)S(1)} %add_select_fusion.1), channel_id=1, source_target_pairs={{0,128},{1,129},{2,130},{3,131},{4,132},{5,133},{6,134},{7,135},{8... | collective-permute-start | bytes 393224 | tf_op jit(solution)/shard_map/ppermute | solution.py:300
  17.1 18.8 %collective-permute-start.10 = (f32[32,1024]{1,0:T(8,128)S(1)}, f32[32,1024]{1,0:T(8,128)S(1)}, u32[]{:S(2)}, u32[]{:S(2)}) collective-permute-start(f32[32,1024]{1,0:T(8,128)S(1)} %add_select_fusion.1), channel_id=1, source_target_pairs={{0,96},{1,97},{2,98},{3,99},{4,100},{5,101},{6,102},{7,103},{8,104... | collective-permute-start | bytes 393224 | tf_op jit(solution)/shard_map/ppermute | solution.py:300
  37.1 38.2 %all-to-all-start = ((f32[8,32,1024]{2,1,0:T(8,128)}), f32[8,32,1024]{2,1,0:T(8,128)S(1)}, u32[]{:S(2)}, u32[]{:S(2)}) async-start(f32[8,32,1024]{2,1,0:T(8,128)} %broadcast_in_dim.3), calls=%async_computation | async-start | bytes 2097152 | tf_op jit(solution)/shard_map/all_to_all | solution.py:307
  60.8 0.7 copy-start.1
  62.5 1.5 %collective-permute-start.21 = (f32[264,256]{1,0:T(8,128)S(1)}, f32[264,256]{1,0:T(8,128)S(1)}, u32[]{:S(2)}, u32[]{:S(2)}) collective-permute-start(f32[264,256]{1,0:T(8,128)S(1)} %tile.1), channel_id=1, source_target_pairs={{0,32},{1,33},{2,34},{3,35}} | collective-permute-start | bytes 811016 | tf_op jit(solution)/shard_map/ppermute | solution.py:264
  63.2 0.8 collective-permute-start.22
  64.1 13.9 %collective-permute-start.23 = (f32[264,256]{1,0:T(8,128)S(1)}, f32[264,256]{1,0:T(8,128)}, u32[]{:S(2)}, u32[]{:S(2)}) collective-permute-start(f32[264,256]{1,0:T(8,128)S(1)} %add.126.chip_ref), channel_id=1, source_target_pairs={{32,33},{33,32},{34,35},{35,34}} | collective-permute-start | bytes 811016 | tf_op jit(solution)/shard_map/ppermute | solution.py:268
  77.9 34.0 %collective-permute-start.16 = (f32[2,256,256]{2,1,0:T(8,128)}, f32[2,256,256]{2,1,0:T(8,128)S(1)}, u32[]{:S(2)}, u32[]{:S(2)}) collective-permute-start(f32[2,256,256]{2,1,0:T(8,128)} %cross.1), channel_id=1, source_target_pairs={{0,1},{1,0},{2,3},{3,2},{4,5},{5,4},{6,7},{7,6},{8,9},{9,8},{10,11... | collective-permute-start | bytes 1572872 | tf_op jit(solution)/shard_map/ppermute | solution.py:253
  78.9 2.7 %collective-permute-start.26 = (f32[200,128]{1,0:T(8,128)S(1)}, f32[200,128]{1,0:T(8,128)S(1)}, u32[]{:S(2)}, u32[]{:S(2)}) collective-permute-start(f32[200,128]{1,0:T(8,128)S(1)} %factor.1), channel_id=1, source_target_pairs={{32,224},{33,225},{34,226},{35,227}} | collective-permute-start | bytes 307208 | tf_op jit(solution)/shard_map/ppermute | solution.py:324
  79.6 2.0 %collective-permute-start.24 = (f32[200,128]{1,0:T(8,128)S(1)}, f32[200,128]{1,0:T(8,128)S(1)}, u32[]{:S(2)}, u32[]{:S(2)}) collective-permute-start(f32[200,128]{1,0:T(8,128)S(1)} %factor.1), channel_id=1, source_target_pairs={{32,160},{33,161},{34,162},{35,163}} | collective-permute-start | bytes 307208 | tf_op jit(solution)/shard_map/ppermute | solution.py:324
  80.3 24.8 %collective-permute-start.25 = (f32[200,128]{1,0:T(8,128)S(1)}, f32[200,128]{1,0:T(8,128)S(1)}, u32[]{:S(2)}, u32[]{:S(2)}) collective-permute-start(f32[200,128]{1,0:T(8,128)S(1)} %factor.1), channel_id=1, source_target_pairs={{32,96},{33,97},{34,98},{35,99}} | collective-permute-start | bytes 307208 | tf_op jit(solution)/shard_map/ppermute | solution.py:324
  105.2 8.1 %collective-permute-start.29 = (f32[200,128]{1,0:T(8,128)S(1)}, f32[200,128]{1,0:T(8,128)S(1)}, u32[]{:S(2)}, u32[]{:S(2)}) collective-permute-start(f32[200,128]{1,0:T(8,128)S(1)} %add_select_fusion.4), channel_id=1, source_target_pairs={{32,64},{96,128},{160,192},{224,0},{33,65},{97,129},{161,193},{225... | collective-permute-start | bytes 307208 | tf_op jit(solution)/shard_map/ppermute | solution.py:324
  106.5 6.8 %collective-permute-start.27 = (f32[200,128]{1,0:T(8,128)S(1)}, f32[200,128]{1,0:T(8,128)S(1)}, u32[]{:S(2)}, u32[]{:S(2)}) collective-permute-start(f32[200,128]{1,0:T(8,128)S(1)} %add_select_fusion.4), channel_id=1, source_target_pairs={{32,48},{96,112},{160,176},{224,240},{33,49},{97,113},{161,177},{2... | collective-permute-start | bytes 307208 | tf_op jit(solution)/shard_map/ppermute | solution.py:324
  107.8 5.5 %collective-permute-start.28 = (f32[200,128]{1,0:T(8,128)S(1)}, f32[200,128]{1,0:T(8,128)S(1)}, u32[]{:S(2)}, u32[]{:S(2)}) collective-permute-start(f32[200,128]{1,0:T(8,128)S(1)} %add_select_fusion.4), channel_id=1, source_target_pairs={{32,80},{96,144},{160,208},{224,16},{33,81},{97,145},{161,209},{22... | collective-permute-start | bytes 307208 | tf_op jit(solution)/shard_map/ppermute | solution.py:324
  111.8 5.4 %collective-permute-start.19 = (f32[2,2,64,256]{3,2,1,0:T(8,128)S(1)}, f32[2,2,64,256]{3,2,1,0:T(8,128)S(1)}, u32[]{:S(2)}, u32[]{:S(2)}) collective-permute-start(f32[2,2,64,256]{3,2,1,0:T(8,128)S(1)} %get-tuple-element.11), channel_id=1, source_target_pairs={{0,1},{1,0},{2,3},{3,2},{4,5},{5,4},{6,7},{7,6},{8,9},{9,8},{10,11... | collective-permute-start | bytes 786440 | tf_op jit(solution)/shard_map/ppermute | solution.py:253
  113.1 9.3 %collective-permute-start.17 = (f32[2,128,256]{2,1,0:T(8,128)S(1)}, f32[2,128,256]{2,1,0:T(8,128)S(1)}, u32[]{:S(2)}, u32[]{:S(2)}) collective-permute-start(f32[2,128,256]{2,1,0:T(8,128)S(1)} %dynamic-slice_bitcast_fusion), channel_id=1, source_target_pairs={{0,2},{2,0},{1,3},{3,1},{4,6},{6,4},{5,7},{7,5},{8,10},{10,8},{9,1... | collective-permute-start | bytes 786440 | tf_op jit(solution)/shard_map/ppermute | solution.py:253
  113.3 9.1 %collective-permute-start.32 = (f32[200,128]{1,0:T(8,128)S(1)}, f32[200,128]{1,0:T(8,128)S(1)}, u32[]{:S(2)}, u32[]{:S(2)}) collective-permute-start(f32[200,128]{1,0:T(8,128)S(1)} %add_select_fusion.3), channel_id=1, source_target_pairs={{32,44},{48,60},{64,76},{80,92},{96,108},{112,124},{128,140},{144,... | collective-permute-start | bytes 307208 | tf_op jit(solution)/shard_map/ppermute | solution.py:324
  114.6 7.8 %collective-permute-start.30 = (f32[200,128]{1,0:T(8,128)S(1)}, f32[200,128]{1,0:T(8,128)S(1)}, u32[]{:S(2)}, u32[]{:S(2)}) collective-permute-start(f32[200,128]{1,0:T(8,128)S(1)} %add_select_fusion.3), channel_id=1, source_target_pairs={{32,40},{48,56},{64,72},{80,88},{96,104},{112,120},{128,136},{144,... | collective-permute-start | bytes 307208 | tf_op jit(solution)/shard_map/ppermute | solution.py:324
  116.0 6.5 %collective-permute-start.31 = (f32[200,128]{1,0:T(8,128)S(1)}, f32[200,128]{1,0:T(8,128)S(1)}, u32[]{:S(2)}, u32[]{:S(2)}) collective-permute-start(f32[200,128]{1,0:T(8,128)S(1)} %add_select_fusion.3), channel_id=1, source_target_pairs={{32,36},{48,52},{64,68},{80,84},{96,100},{112,116},{128,132},{144,... | collective-permute-start | bytes 307208 | tf_op jit(solution)/shard_map/ppermute | solution.py:324
  117.3 7.3 %collective-permute-start.20 = (f32[2,64,256]{2,1,0:T(8,128)S(1)}, f32[2,64,256]{2,1,0:T(8,128)S(1)}, u32[]{:S(2)}, u32[]{:S(2)}) collective-permute-start(f32[2,64,256]{2,1,0:T(8,128)S(1)} %dynamic-slice_bitcast_fusion.1), channel_id=1, source_target_pairs={{0,2},{2,0},{1,3},{3,1},{4,6},{6,4},{5,7},{7,5},{8,10},{10,8},{9,1... | collective-permute-start | bytes 393224 | tf_op jit(solution)/shard_map/ppermute | solution.py:253
  122.4 2.3 %collective-permute-start.18 = (f32[2,128,256]{2,1,0:T(8,128)S(1)}, f32[2,128,256]{2,1,0:T(8,128)S(1)}, u32[]{:S(2)}, u32[]{:S(2)}) collective-permute-start(f32[2,128,256]{2,1,0:T(8,128)S(1)} %fusion.1.own_ref), channel_id=1, source_target_pairs={{0,1},{1,0},{2,3},{3,2},{4,5},{5,4},{6,7},{7,6},{8,9},{9,8},{10,11... | collective-permute-start | bytes 786440 | tf_op jit(solution)/shard_map/ppermute | solution.py:253
  122.5 2.1 %collective-permute-start.33 = (f32[200,128]{1,0:T(8,128)S(1)}, f32[200,128]{1,0:T(8,128)S(1)}, u32[]{:S(2)}, u32[]{:S(2)}) collective-permute-start(f32[200,128]{1,0:T(8,128)S(1)} %add_select_fusion.2.mine_ref), channel_id=1, source_target_pairs={{0,1},{1,0},{2,3},{3,2},{4,5},{5,4},{6,7},{7,6},{8,9},{9,8},{10,11... | collective-permute-start | bytes 307208 | tf_op jit(solution)/shard_map/ppermute | solution.py:253

commit v8 on v7

--- a/solution.py
+++ b/solution.py
@@ -40,24 +40,44 @@
 def triangle_inverse(tile):
     n = tile.shape[0]
     held = jnp.concatenate([tile, unit(n, n).astype(jnp.float32)], axis=1)
-    rows = lax.broadcasted_iota(jnp.int32, held.shape, 0)
-    for j in range(0, n, 2):
+    rows = lax.broadcasted_iota(jnp.int32, (8, 2 * n), 0)
+    for j in range(0, n, 4):
         low = (j // 8) * 8
-        part, at = held[low:, :], rows[low:]
-        first = jnp.broadcast_to(part[:, j : j + 1], part.shape)
-        second = jnp.broadcast_to(part[:, j + 1 : j + 2], part.shape)
-        row_a, row_b = held[j : j + 1, :], held[j + 1 : j + 2, :]
         k = j - low
-        a, b, c = first[k : k + 1], first[k + 1 : k + 2], second[k + 1 : k + 2]
-        over_a = 1.0 / a
-        over_det = 1.0 / (a * c - b * b)
-        t = b * over_a
-        row_b = row_b - t * row_a
-        update = first * over_a * row_a + (second - first * t) * (a * over_det) * row_b
-        update = jnp.where(at > j + 1, update, 0.0)
-        update = jnp.where(at == j + 1, jnp.broadcast_to(t * row_a, part.shape), update)
-        part = part - update
-        held = jnp.concatenate([held[:low], part], axis=0) if low else part
+        part = held[low:, :]
+        column = [jnp.broadcast_to(part[:, j + m : j + m + 1], part.shape) for m in range(4)]
+        row = [held[j + m : j + m + 1, :] for m in range(4)]
+        entry = lambda i, m: column[m][k + i : k + i + 1]
+        over_0 = 1.0 / entry(0, 0)
+        t = entry(1, 0) * over_0
+        over_1 = entry(0, 0) * (
+            1.0 / (entry(0, 0) * entry(1, 1) - entry(1, 0) * entry(1, 0))
+        )
+        row_1 = row[1] - t * row[0]
+        rest_2, rest_3 = entry(2, 1) - t * entry(2, 0), entry(3, 1) - t * entry(3, 0)
+        g20, g30 = entry(2, 0) * over_0, entry(3, 0) * over_0
+        g21, g31 = rest_2 * over_1, rest_3 * over_1
+        row_2 = row[2] - g20 * row[0] - g21 * row_1
+        row_3 = row[3] - g30 * row[0] - g31 * row_1
+        b22 = entry(2, 2) - g20 * entry(2, 0) - g21 * rest_2
+        b32 = entry(3, 2) - g30 * entry(2, 0) - g31 * rest_2
+        b33 = entry(3, 3) - g30 * entry(3, 0) - g31 * rest_3
+        over_2 = 1.0 / b22
+        s = b32 * over_2
+        over_3 = b22 * (1.0 / (b22 * b33 - b32 * b32))
+        row_3 = row_3 - s * row_2
+        f0 = column[0] * over_0
+        f1 = (column[1] - column[0] * t) * over_1
+        left_2 = column[2] - f0 * entry(2, 0) - f1 * rest_2
+        left_3 = column[3] - f0 * entry(3, 0) - f1 * rest_3
+        f2 = left_2 * over_2
+        f3 = (left_3 - left_2 * s) * over_3
+        new = part - (f0 * row[0] + f1 * row_1 + f2 * row_2 + f3 * row_3)
+        head = jnp.where(rows > k + 3, new[:8], part[:8])
+        for m, value in ((1, row_1), (2, row_2), (3, row_3)):
+            head = jnp.where(rows == k + m, jnp.broadcast_to(value, head.shape), head)
+        pieces = ([held[:low]] if low else []) + [head] + ([new[8:]] if low + 8 < n else [])
+        held = jnp.concatenate(pieces, axis=0) if len(pieces) > 1 else head
     pivots = jnp.sum(jnp.where(unit(n, 2 * n), held, 0.0), axis=1, keepdims=True)
     return held[:, n:] * (1.0 / jnp.sqrt(pivots))
 

time: 128 us -> 124 us (0.969)
  waiting for transfers between devices: 54.1 us -> 50.3 us
    ppermute x9, waiting for transfers between devices: 23.5 us -> 19.8 us  [small_tree(): lax.ppermute(value, BLK, [(at(i), at(k)) for i, k in route])]
where the time goes in v8:
time: 124 us
  starting transfers between devices  56.1 us (45%)
  waiting for transfers between devices  50.3 us (41%)
  Pallas kernels  9.79 us (8%)
  local copies, waits for them, and re-layouts  3.21 us (3%)
  other arithmetic  2.9 us (2%)
    all_to_all x1, starting transfers between devices, over_plane(): lax.all_to_all(copies, PLANE, split_axis=0, concat_axis=0, tiled=True)  23.8 us
    ppermute x9, waiting for transfers between devices, small_tree(): lax.ppermute(value, BLK, [(at(i), at(k)) for i, k in route])  19.8 us
    ppermute x7, waiting for transfers between devices, along_z(): got = [lax.ppermute(piece, 'z', [(0, k)]) for k in STACK_ORDER]  17.5 us
    ppermute x9, starting transfers between devices, small_tree(): lax.ppermute(value, BLK, [(at(i), at(k)) for i, k in route])  10.6 us
    all_to_all x1, waiting for transfers between devices, over_plane(): lax.all_to_all(copies, PLANE, split_axis=0, concat_axis=0, tiled=True)  8.45 us
    ppermute x7, starting transfers between devices, along_z(): got = [lax.ppermute(piece, 'z', [(0, k)]) for k in STACK_ORDER]  5.29 us
    ppermute x1, starting transfers between devices, on_device(): lax.ppermute(log_derivs, BLK, [(b, b + 1) for b in range(64) if b % 4 != 3])  4.79 us
    ppermute x7, starting transfers between devices, scatter_lead(): lax.ppermute(rows[k * part:(k + 1) * part], BLK, [(0, k)])  4.68 us
  transfers between devices with their start and end apart: 35, of which 5 were waited for; matrix products, arithmetic and copies ran while one was open for 3% of the time, Pallas kernels for 6%

profile of v8, /device:TPU:96, one launch (start us, length us, event | category | flops | bytes accessed | tf_op | source)
XLA Modules:
  0.0 123.5 jit_solution(17618650137994918103)
XLA Ops:
  0.6 1.4 %fusion = (f32[32,1024]{1,0:T(8,128)S(1)}, f32[32,1024]{1,0:T(8,128)S(1)}, f32[32,1024]{1,0:T(8,128)S(1)}, f32[32,1024]{1,0:T(8,128)S(1)}, f32[32,1024]{1,0:T(8,...) fusion(f32[256,1024]{1,0:T(8,128)} %rows_ref.5), kind=kLoop, calls=%fused_computation.10 | loop fusion | bytes 1835008 | tf_op jit(solution)/shard_map/slice | solution.py:313
  2.0 0.7 collective-permute-start.8
  2.7 0.7 collective-permute-start.7
  3.4 0.7 collective-permute-start.6
  4.1 0.7 collective-permute-start.5
  4.7 0.7 collective-permute-start.4
  5.4 0.0 collective-permute-done.8
  5.4 0.7 collective-permute-start.2
  6.1 0.7 collective-permute-start.3
  6.8 0.0 collective-permute-done.6
  6.8 0.0 collective-permute-done.4
  6.8 0.0 collective-permute-done.2
  6.9 0.1 add_select_fusion.1
  6.9 0.7 collective-permute-start.15
  7.6 0.7 collective-permute-start.14
  8.3 0.7 collective-permute-start.13
  9.0 0.7 collective-permute-start.12
  9.6 1.3 %collective-permute-start = (f32[256,1024]{1,0:T(8,128)S(1)}, f32[256,1024]{1,0:T(8,128)}, u32[]{:S(2)}, u32[]{:S(2)}) collective-permute-start(f32[256,1024]{1,0:T(8,128)S(1)} %copy-done), channel_id=1, source_target_pairs={{12,16},{28,32},{44,48},{60,64},{76,80},{92,96},{108,112},{124,128... | collective-permute-start | bytes 3145736 | tf_op jit(solution)/shard_map/ppermute | solution.py:356
  10.9 0.0 collective-permute-done.15
  11.0 4.8 %collective-permute-start.1 = (f32[256,1024]{1,0:T(8,128)S(1)}, f32[256,1024]{1,0:T(8,128)}, u32[]{:S(2)}, u32[]{:S(2)}) collective-permute-start(f32[256,1024]{1,0:T(8,128)S(1)} %copy-done), channel_id=1, source_target_pairs={{0,4},{4,8},{8,12},{16,20},{20,24},{24,28},{32,36},{36,40},{40,44}... | collective-permute-start | bytes 3145736 | tf_op jit(solution)/shard_map/ppermute | solution.py:360
  15.7 0.7 collective-permute-start.11
  16.4 0.0 collective-permute-done.13
  16.4 0.7 collective-permute-start.9
  17.1 1.3 %collective-permute-start.10 = (f32[32,1024]{1,0:T(8,128)S(1)}, f32[32,1024]{1,0:T(8,128)S(1)}, u32[]{:S(2)}, u32[]{:S(2)}) collective-permute-start(f32[32,1024]{1,0:T(8,128)S(1)} %add_select_fusion.1), channel_id=1, source_target_pairs={{0,96},{1,97},{2,98},{3,99},{4,100},{5,101},{6,102},{7,103},{8,104... | collective-permute-start | bytes 393224 | tf_op jit(solution)/shard_map/ppermute | solution.py:320
  18.4 0.0 collective-permute-done.11
  18.4 0.0 collective-permute-done.9
  18.4 17.5 %collective-permute-done.10 = f32[32,1024]{1,0:T(8,128)S(1)} collective-permute-done((f32[32,1024]{1,0:T(8,128)S(1)}, f32[32,1024]{1,0:T(8,128)S(1)}, u32[]{:S(2)}, u32[]{:S(2)}) %collective-permute-start.10) | collective-permute-done | bytes 131104 | tf_op jit(solution)/shard_map/ppermute | solution.py:320
  35.9 0.1 add_select_fusion
  36.0 1.1 broadcast_in_dim.3
  37.1 23.8 %all-to-all-start = ((f32[8,32,1024]{2,1,0:T(8,128)}), f32[8,32,1024]{2,1,0:T(8,128)S(1)}, u32[]{:S(2)}, u32[]{:S(2)}) async-start(f32[8,32,1024]{2,1,0:T(8,128)} %broadcast_in_dim.3), calls=%async_computation | async-start | bytes 2097152 | tf_op jit(solution)/shard_map/all_to_all | solution.py:327
  60.8 0.7 copy-done.1
  61.5 1.0 tile.1
  62.5 0.7 collective-permute-start.21
  63.2 0.7 collective-permute-start.22
  63.9 0.1 pad_add_fusion.at_ref
  64.0 0.0 collective-permute-done.21
  64.0 0.0 collective-permute-done.22
  64.1 1.4 %collective-permute-start.23 = (f32[264,256]{1,0:T(8,128)S(1)}, f32[264,256]{1,0:T(8,128)}, u32[]{:S(2)}, u32[]{:S(2)}) collective-permute-start(f32[264,256]{1,0:T(8,128)S(1)} %add.126.chip_ref), channel_id=1, source_target_pairs={{32,33},{33,32},{34,35},{35,34}} | collective-permute-start | bytes 811016 | tf_op jit(solution)/shard_map/ppermute | solution.py:288
  65.4 1.4 %broadcast_select_fusion.prev_ref = f32[256,1024]{1,0:T(8,128)S(1)} fusion(f32[256,1024]{1,0:T(8,128)} %collective-permute-done, f32[256,1024]{1,0:T(8,128)} %collective-permute-done.1, pred[]{:T(512)S(6)} %eq.22), kind=kLoop, calls=%fused_computation | loop fusion | flops 262144 | bytes 3145729 | tf_op jit(solution)/shard_map/jit(_where)/select_n | solution.py:367
  66.8 8.4 %all-to-all-done = f32[8,32,1024]{2,1,0:T(8,128)S(1)} async-done(((f32[8,32,1024]{2,1,0:T(8,128)}), f32[8,32,1024]{2,1,0:T(8,128)S(1)}, u32[]{:S(2)}, u32[]{:S(2)}) %all-to-all-start) | async-done | bytes 1048608 | tf_op jit(solution)/shard_map/all_to_all | solution.py:327
  75.3 2.7 %cross.1 = f32[2,256,256]{2,1,0:T(8,128)} custom-call(f32[256,1024]{1,0:T(8,128)S(1)} %copy-done, f32[256,1024]{1,0:T(8,128)S(1)} %broadcast_select_fusion.prev_ref, f32[256,1024]{1,0:T(8,128)S(1)} %bitcast.18), custom_call_target="tpu_custom_call" | custom-call | flops 1000000000 | bytes 1048576 | tf_op jit(solution)/shard_map/cross/pallas_call | solution.py:179
  77.9 1.0 factor.1
  78.9 0.7 collective-permute-start.26
  79.6 0.7 collective-permute-start.24
  80.3 1.3 %collective-permute-start.25 = (f32[200,128]{1,0:T(8,128)S(1)}, f32[200,128]{1,0:T(8,128)S(1)}, u32[]{:S(2)}, u32[]{:S(2)}) collective-permute-start(f32[200,128]{1,0:T(8,128)S(1)} %factor.1), channel_id=1, source_target_pairs={{32,96},{33,97},{34,98},{35,99}} | collective-permute-start | bytes 307208 | tf_op jit(solution)/shard_map/ppermute | solution.py:344
  81.6 0.0 collective-permute-done.26
  81.6 0.0 collective-permute-done.24
  81.6 19.8 %collective-permute-done.25 = f32[200,128]{1,0:T(8,128)S(1)} collective-permute-done((f32[200,128]{1,0:T(8,128)S(1)}, f32[200,128]{1,0:T(8,128)S(1)}, u32[]{:S(2)}, u32[]{:S(2)}) %collective-permute-start.25) | collective-permute-done | bytes 102432 | tf_op jit(solution)/shard_map/ppermute | solution.py:344
  101.4 1.3 %collective-permute-start.29 = (f32[200,128]{1,0:T(8,128)S(1)}, f32[200,128]{1,0:T(8,128)S(1)}, u32[]{:S(2)}, u32[]{:S(2)}) collective-permute-start(f32[200,128]{1,0:T(8,128)S(1)} %add_select_fusion.4), channel_id=1, source_target_pairs={{32,64},{96,128},{160,192},{224,0},{33,65},{97,129},{161,193},{225... | collective-permute-start | bytes 307208 | tf_op jit(solution)/shard_map/ppermute | solution.py:344
  102.7 1.3 %collective-permute-start.27 = (f32[200,128]{1,0:T(8,128)S(1)}, f32[200,128]{1,0:T(8,128)S(1)}, u32[]{:S(2)}, u32[]{:S(2)}) collective-permute-start(f32[200,128]{1,0:T(8,128)S(1)} %add_select_fusion.4), channel_id=1, source_target_pairs={{32,48},{96,112},{160,176},{224,240},{33,49},{97,113},{161,177},{2... | collective-permute-start | bytes 307208 | tf_op jit(solution)/shard_map/ppermute | solution.py:344
  104.0 1.5 %collective-permute-start.28 = (f32[200,128]{1,0:T(8,128)S(1)}, f32[200,128]{1,0:T(8,128)S(1)}, u32[]{:S(2)}, u32[]{:S(2)}) collective-permute-start(f32[200,128]{1,0:T(8,128)S(1)} %add_select_fusion.4), channel_id=1, source_target_pairs={{32,80},{96,144},{160,208},{224,16},{33,81},{97,145},{161,209},{22... | collective-permute-start | bytes 307208 | tf_op jit(solution)/shard_map/ppermute | solution.py:344
  105.5 2.6 %early.1 = (f32[2,2,64,256]{3,2,1,0:T(8,128)S(1)}, f32[2,2,64,256]{3,2,1,0:T(8,128)S(1)}) custom-call(s32[4]{0:T(128)S(1)} %pad_add_fusion.at_ref, f32[256,1024]{1,0:T(8,128)S(1)} %copy-done, f32[256,1024]{1,0:T(8,128)S(1)} %broadcast_select_fusion.prev_ref), custom_call_target="tpu_custom_call" | custom-call | flops 1000000000 | bytes 1048576 | tf_op jit(solution)/shard_map/early/pallas_call | solution.py:204
  108.1 0.1 collective-permute-start.19
  108.2 1.1 add.116
  109.3 0.2 collective-permute-start.17
  109.6 1.3 %collective-permute-start.32 = (f32[200,128]{1,0:T(8,128)S(1)}, f32[200,128]{1,0:T(8,128)S(1)}, u32[]{:S(2)}, u32[]{:S(2)}) collective-permute-start(f32[200,128]{1,0:T(8,128)S(1)} %add_select_fusion.3), channel_id=1, source_target_pairs={{32,44},{48,60},{64,76},{80,92},{96,108},{112,124},{128,140},{144,... | collective-permute-start | bytes 307208 | tf_op jit(solution)/shard_map/ppermute | solution.py:344
  110.9 1.3 %collective-permute-start.30 = (f32[200,128]{1,0:T(8,128)S(1)}, f32[200,128]{1,0:T(8,128)S(1)}, u32[]{:S(2)}, u32[]{:S(2)}) collective-permute-start(f32[200,128]{1,0:T(8,128)S(1)} %add_select_fusion.3), channel_id=1, source_target_pairs={{32,40},{48,56},{64,72},{80,88},{96,104},{112,120},{128,136},{144,... | collective-permute-start | bytes 307208 | tf_op jit(solution)/shard_map/ppermute | solution.py:344
  112.2 1.3 %collective-permute-start.31 = (f32[200,128]{1,0:T(8,128)S(1)}, f32[200,128]{1,0:T(8,128)S(1)}, u32[]{:S(2)}, u32[]{:S(2)}) collective-permute-start(f32[200,128]{1,0:T(8,128)S(1)} %add_select_fusion.3), channel_id=1, source_target_pairs={{32,36},{48,52},{64,68},{80,84},{96,100},{112,116},{128,132},{144,... | collective-permute-start | bytes 307208 | tf_op jit(solution)/shard_map/ppermute | solution.py:344
  113.6 2.0 %collective-permute-start.20 = (f32[2,64,256]{2,1,0:T(8,128)S(1)}, f32[2,64,256]{2,1,0:T(8,128)S(1)}, u32[]{:S(2)}, u32[]{:S(2)}) collective-permute-start(f32[2,64,256]{2,1,0:T(8,128)S(1)} %dynamic-slice_bitcast_fusion.1), channel_id=1, source_target_pairs={{0,2},{2,0},{1,3},{3,1},{4,6},{6,4},{5,7},{7,5},{8,10},{10,8},{9,1... | collective-permute-start | bytes 393224 | tf_op jit(solution)/shard_map/ppermute | solution.py:273
  115.6 3.0 %collective-permute-done.17 = f32[2,128,256]{2,1,0:T(8,128)S(1)} collective-permute-done((f32[2,128,256]{2,1,0:T(8,128)S(1)}, f32[2,128,256]{2,1,0:T(8,128)S(1)}, u32[]{:S(2)}, u32[]{:S(2)}) %collective-permute-start.17) | collective-permute-done | bytes 262176 | tf_op jit(solution)/shard_map/ppermute | solution.py:273
  118.6 0.1 collective-permute-start.18
  118.8 0.6 collective-permute-start.33
  119.4 1.6 %collective-permute-done.20 = f32[2,64,256]{2,1,0:T(8,128)S(1)} collective-permute-done((f32[2,64,256]{2,1,0:T(8,128)S(1)}, f32[2,64,256]{2,1,0:T(8,128)S(1)}, u32[]{:S(2)}, u32[]{:S(2)}) %collective-permute-start.20) | collective-permute-done | bytes 131104 | tf_op jit(solution)/shard_map/ppermute | solution.py:273
  121.0 2.5 %finish.1 = (f32[256,256]{1,0:T(8,128)}, f32[1,256]{1,0:T(1,128)}, f32[64,256]{1,0:T(8,128)}, f32[64,256]{1,0:T(8,128)}) custom-call(s32[4]{0:T(128)S(1)} %pad_add_fusion.at_ref, f32[2,128,256]{2,1,0:T(8,128)S(1)} %fusion.1.own_ref, f32[2,128,256]{2,1,0:T(8,128)S(1)} %collective-permute-done.18.other_ref, f32[2,64,256]{2,1,0:T(8,128)S(1)} %bitcast_add_fusion.early_ref, ...), custom_call_target="tpu_custom_call" | custom-call | flops 1000000000 | bytes 1048576 | tf_op jit(solution)/shard_map/finish/pallas_call | solution.py:256
  (31 shorter events, 0.3 us)
Async XLA Ops:
  0.6 6.2 %copy-start = (f32[256,1024]{1,0:T(8,128)S(1)}, f32[256,1024]{1,0:T(8,128)}, u32[]{:S(2)}) copy-start(f32[256,1024]{1,0:T(8,128)} %rows_ref.5) | copy-start | bytes 3145732
  2.0 3.4 %collective-permute-start.8 = (f32[32,1024]{1,0:T(8,128)S(1)}, f32[32,1024]{1,0:T(8,128)S(1)}, u32[]{:S(2)}, u32[]{:S(2)}) collective-permute-start(f32[32,1024]{1,0:T(8,128)S(1)} %get-tuple-element.17), channel_id=1, source_target_pairs={{0,16},{1,17},{2,18},{3,19}} | collective-permute-start | bytes 393224 | tf_op jit(solution)/shard_map/ppermute | solution.py:313
  2.7 3.4 %collective-permute-start.7 = (f32[32,1024]{1,0:T(8,128)S(1)}, f32[32,1024]{1,0:T(8,128)S(1)}, u32[]{:S(2)}, u32[]{:S(2)}) collective-permute-start(f32[32,1024]{1,0:T(8,128)S(1)} %get-tuple-element.18), channel_id=1, source_target_pairs={{0,12},{1,13},{2,14},{3,15}} | collective-permute-start | bytes 393224 | tf_op jit(solution)/shard_map/ppermute | solution.py:313
  3.4 3.4 %collective-permute-start.6 = (f32[32,1024]{1,0:T(8,128)S(1)}, f32[32,1024]{1,0:T(8,128)S(1)}, u32[]{:S(2)}, u32[]{:S(2)}) collective-permute-start(f32[32,1024]{1,0:T(8,128)S(1)} %get-tuple-element.19), channel_id=1, source_target_pairs={{0,4},{1,5},{2,6},{3,7}} | collective-permute-start | bytes 393224 | tf_op jit(solution)/shard_map/ppermute | solution.py:313
  4.1 2.8 %collective-permute-start.5 = (f32[32,1024]{1,0:T(8,128)S(1)}, f32[32,1024]{1,0:T(8,128)S(1)}, u32[]{:S(2)}, u32[]{:S(2)}) collective-permute-start(f32[32,1024]{1,0:T(8,128)S(1)} %get-tuple-element.20), channel_id=1, source_target_pairs={{0,28},{1,29},{2,30},{3,31}} | collective-permute-start | bytes 393224 | tf_op jit(solution)/shard_map/ppermute | solution.py:313
  4.7 2.1 %collective-permute-start.4 = (f32[32,1024]{1,0:T(8,128)S(1)}, f32[32,1024]{1,0:T(8,128)S(1)}, u32[]{:S(2)}, u32[]{:S(2)}) collective-permute-start(f32[32,1024]{1,0:T(8,128)S(1)} %get-tuple-element.21), channel_id=1, source_target_pairs={{0,20},{1,21},{2,22},{3,23}} | collective-permute-start | bytes 393224 | tf_op jit(solution)/shard_map/ppermute | solution.py:313
  5.4 1.4 %collective-permute-start.2 = (f32[32,1024]{1,0:T(8,128)S(1)}, f32[32,1024]{1,0:T(8,128)S(1)}, u32[]{:S(2)}, u32[]{:S(2)}) collective-permute-start(f32[32,1024]{1,0:T(8,128)S(1)} %get-tuple-element.22), channel_id=1, source_target_pairs={{0,24},{1,25},{2,26},{3,27}} | collective-permute-start | bytes 393224 | tf_op jit(solution)/shard_map/ppermute | solution.py:313
  6.1 0.7 collective-permute-start.3
  6.9 4.0 %collective-permute-start.15 = (f32[32,1024]{1,0:T(8,128)S(1)}, f32[32,1024]{1,0:T(8,128)S(1)}, u32[]{:S(2)}, u32[]{:S(2)}) collective-permute-start(f32[32,1024]{1,0:T(8,128)S(1)} %add_select_fusion.1), channel_id=1, source_target_pairs={{0,224},{1,225},{2,226},{3,227},{4,228},{5,229},{6,230},{7,231},{8... | collective-permute-start | bytes 393224 | tf_op jit(solution)/shard_map/ppermute | solution.py:320
  7.6 8.1 %collective-permute-start.14 = (f32[32,1024]{1,0:T(8,128)S(1)}, f32[32,1024]{1,0:T(8,128)S(1)}, u32[]{:S(2)}, u32[]{:S(2)}) collective-permute-start(f32[32,1024]{1,0:T(8,128)S(1)} %add_select_fusion.1), channel_id=1, source_target_pairs={{0,32},{1,33},{2,34},{3,35},{4,36},{5,37},{6,38},{7,39},{8,40},{9,... | collective-permute-start | bytes 393224 | tf_op jit(solution)/shard_map/ppermute | solution.py:320
  8.3 8.1 %collective-permute-start.13 = (f32[32,1024]{1,0:T(8,128)S(1)}, f32[32,1024]{1,0:T(8,128)S(1)}, u32[]{:S(2)}, u32[]{:S(2)}) collective-permute-start(f32[32,1024]{1,0:T(8,128)S(1)} %add_select_fusion.1), channel_id=1, source_target_pairs={{0,192},{1,193},{2,194},{3,195},{4,196},{5,197},{6,198},{7,199},{8... | collective-permute-start | bytes 393224 | tf_op jit(solution)/shard_map/ppermute | solution.py:320
  9.0 8.1 %collective-permute-start.12 = (f32[32,1024]{1,0:T(8,128)S(1)}, f32[32,1024]{1,0:T(8,128)S(1)}, u32[]{:S(2)}, u32[]{:S(2)}) collective-permute-start(f32[32,1024]{1,0:T(8,128)S(1)} %add_select_fusion.1), channel_id=1, source_target_pairs={{0,64},{1,65},{2,66},{3,67},{4,68},{5,69},{6,70},{7,71},{8,72},{9,... | collective-permute-start | bytes 393224 | tf_op jit(solution)/shard_map/ppermute | solution.py:320
  9.6 55.8 %collective-permute-start = (f32[256,1024]{1,0:T(8,128)S(1)}, f32[256,1024]{1,0:T(8,128)}, u32[]{:S(2)}, u32[]{:S(2)}) collective-permute-start(f32[256,1024]{1,0:T(8,128)S(1)} %copy-done), channel_id=1, source_target_pairs={{12,16},{28,32},{44,48},{60,64},{76,80},{92,96},{108,112},{124,128... | collective-permute-start | bytes 3145736 | tf_op jit(solution)/shard_map/ppermute | solution.py:356
  11.0 54.5 %collective-permute-start.1 = (f32[256,1024]{1,0:T(8,128)S(1)}, f32[256,1024]{1,0:T(8,128)}, u32[]{:S(2)}, u32[]{:S(2)}) collective-permute-start(f32[256,1024]{1,0:T(8,128)S(1)} %copy-done), channel_id=1, source_target_pairs={{0,4},{4,8},{8,12},{16,20},{20,24},{24,28},{32,36},{36,40},{40,44}... | collective-permute-start | bytes 3145736 | tf_op jit(solution)/shard_map/ppermute | solution.py:360
  15.7 2.7 %collective-permute-start.11 = (f32[32,1024]{1,0:T(8,128)S(1)}, f32[32,1024]{1,0:T(8,128)S(1)}, u32[]{:S(2)}, u32[]{:S(2)}) collective-permute-start(f32[32,1024]{1,0:T(8,128)S(1)} %add_select_fusion.1), channel_id=1, source_target_pairs={{0,160},{1,161},{2,162},{3,163},{4,164},{5,165},{6,166},{7,167},{8... | collective-permute-start | bytes 393224 | tf_op jit(solution)/shard_map/ppermute | solution.py:320
  16.4 2.0 %collective-permute-start.9 = (f32[32,1024]{1,0:T(8,128)S(1)}, f32[32,1024]{1,0:T(8,128)S(1)}, u32[]{:S(2)}, u32[]{:S(2)}) collective-permute-start(f32[32,1024]{1,0:T(8,128)S(1)} %add_select_fusion.1), channel_id=1, source_target_pairs={{0,128},{1,129},{2,130},{3,131},{4,132},{5,133},{6,134},{7,135},{8... | collective-permute-start | bytes 393224 | tf_op jit(solution)/shard_map/ppermute | solution.py:320
  17.1 18.8 %collective-permute-start.10 = (f32[32,1024]{1,0:T(8,128)S(1)}, f32[32,1024]{1,0:T(8,128)S(1)}, u32[]{:S(2)}, u32[]{:S(2)}) collective-permute-start(f32[32,1024]{1,0:T(8,128)S(1)} %add_select_fusion.1), channel_id=1, source_target_pairs={{0,96},{1,97},{2,98},{3,99},{4,100},{5,101},{6,102},{7,103},{8,104... | collective-permute-start | bytes 393224 | tf_op jit(solution)/shard_map/ppermute | solution.py:320
  37.1 38.2 %all-to-all-start = ((f32[8,32,1024]{2,1,0:T(8,128)}), f32[8,32,1024]{2,1,0:T(8,128)S(1)}, u32[]{:S(2)}, u32[]{:S(2)}) async-start(f32[8,32,1024]{2,1,0:T(8,128)} %broadcast_in_dim.3), calls=%async_computation | async-start | bytes 2097152 | tf_op jit(solution)/shard_map/all_to_all | solution.py:327
  60.8 0.7 copy-start.1
  62.5 1.5 %collective-permute-start.21 = (f32[264,256]{1,0:T(8,128)S(1)}, f32[264,256]{1,0:T(8,128)S(1)}, u32[]{:S(2)}, u32[]{:S(2)}) collective-permute-start(f32[264,256]{1,0:T(8,128)S(1)} %tile.1), channel_id=1, source_target_pairs={{0,32},{1,33},{2,34},{3,35}} | collective-permute-start | bytes 811016 | tf_op jit(solution)/shard_map/ppermute | solution.py:284
  63.2 0.8 collective-permute-start.22
  64.1 13.9 %collective-permute-start.23 = (f32[264,256]{1,0:T(8,128)S(1)}, f32[264,256]{1,0:T(8,128)}, u32[]{:S(2)}, u32[]{:S(2)}) collective-permute-start(f32[264,256]{1,0:T(8,128)S(1)} %add.126.chip_ref), channel_id=1, source_target_pairs={{32,33},{33,32},{34,35},{35,34}} | collective-permute-start | bytes 811016 | tf_op jit(solution)/shard_map/ppermute | solution.py:288
  77.9 30.2 %collective-permute-start.16 = (f32[2,256,256]{2,1,0:T(8,128)}, f32[2,256,256]{2,1,0:T(8,128)S(1)}, u32[]{:S(2)}, u32[]{:S(2)}) collective-permute-start(f32[2,256,256]{2,1,0:T(8,128)} %cross.1), channel_id=1, source_target_pairs={{0,1},{1,0},{2,3},{3,2},{4,5},{5,4},{6,7},{7,6},{8,9},{9,8},{10,11... | collective-permute-start | bytes 1572872 | tf_op jit(solution)/shard_map/ppermute | solution.py:273
  78.9 2.7 %collective-permute-start.26 = (f32[200,128]{1,0:T(8,128)S(1)}, f32[200,128]{1,0:T(8,128)S(1)}, u32[]{:S(2)}, u32[]{:S(2)}) collective-permute-start(f32[200,128]{1,0:T(8,128)S(1)} %factor.1), channel_id=1, source_target_pairs={{32,224},{33,225},{34,226},{35,227}} | collective-permute-start | bytes 307208 | tf_op jit(solution)/shard_map/ppermute | solution.py:344
  79.6 2.0 %collective-permute-start.24 = (f32[200,128]{1,0:T(8,128)S(1)}, f32[200,128]{1,0:T(8,128)S(1)}, u32[]{:S(2)}, u32[]{:S(2)}) collective-permute-start(f32[200,128]{1,0:T(8,128)S(1)} %factor.1), channel_id=1, source_target_pairs={{32,160},{33,161},{34,162},{35,163}} | collective-permute-start | bytes 307208 | tf_op jit(solution)/shard_map/ppermute | solution.py:344
  80.3 21.1 %collective-permute-start.25 = (f32[200,128]{1,0:T(8,128)S(1)}, f32[200,128]{1,0:T(8,128)S(1)}, u32[]{:S(2)}, u32[]{:S(2)}) collective-permute-start(f32[200,128]{1,0:T(8,128)S(1)} %factor.1), channel_id=1, source_target_pairs={{32,96},{33,97},{34,98},{35,99}} | collective-permute-start | bytes 307208 | tf_op jit(solution)/shard_map/ppermute | solution.py:344
  101.4 8.1 %collective-permute-start.29 = (f32[200,128]{1,0:T(8,128)S(1)}, f32[200,128]{1,0:T(8,128)S(1)}, u32[]{:S(2)}, u32[]{:S(2)}) collective-permute-start(f32[200,128]{1,0:T(8,128)S(1)} %add_select_fusion.4), channel_id=1, source_target_pairs={{32,64},{96,128},{160,192},{224,0},{33,65},{97,129},{161,193},{225... | collective-permute-start | bytes 307208 | tf_op jit(solution)/shard_map/ppermute | solution.py:344
  102.7 6.8 %collective-permute-start.27 = (f32[200,128]{1,0:T(8,128)S(1)}, f32[200,128]{1,0:T(8,128)S(1)}, u32[]{:S(2)}, u32[]{:S(2)}) collective-permute-start(f32[200,128]{1,0:T(8,128)S(1)} %add_select_fusion.4), channel_id=1, source_target_pairs={{32,48},{96,112},{160,176},{224,240},{33,49},{97,113},{161,177},{2... | collective-permute-start | bytes 307208 | tf_op jit(solution)/shard_map/ppermute | solution.py:344
  104.0 5.5 %collective-permute-start.28 = (f32[200,128]{1,0:T(8,128)S(1)}, f32[200,128]{1,0:T(8,128)S(1)}, u32[]{:S(2)}, u32[]{:S(2)}) collective-permute-start(f32[200,128]{1,0:T(8,128)S(1)} %add_select_fusion.4), channel_id=1, source_target_pairs={{32,80},{96,144},{160,208},{224,16},{33,81},{97,145},{161,209},{22... | collective-permute-start | bytes 307208 | tf_op jit(solution)/shard_map/ppermute | solution.py:344
  108.1 5.4 %collective-permute-start.19 = (f32[2,2,64,256]{3,2,1,0:T(8,128)S(1)}, f32[2,2,64,256]{3,2,1,0:T(8,128)S(1)}, u32[]{:S(2)}, u32[]{:S(2)}) collective-permute-start(f32[2,2,64,256]{3,2,1,0:T(8,128)S(1)} %get-tuple-element.11), channel_id=1, source_target_pairs={{0,1},{1,0},{2,3},{3,2},{4,5},{5,4},{6,7},{7,6},{8,9},{9,8},{10,11... | collective-permute-start | bytes 786440 | tf_op jit(solution)/shard_map/ppermute | solution.py:273
  109.3 9.3 %collective-permute-start.17 = (f32[2,128,256]{2,1,0:T(8,128)S(1)}, f32[2,128,256]{2,1,0:T(8,128)S(1)}, u32[]{:S(2)}, u32[]{:S(2)}) collective-permute-start(f32[2,128,256]{2,1,0:T(8,128)S(1)} %dynamic-slice_bitcast_fusion), channel_id=1, source_target_pairs={{0,2},{2,0},{1,3},{3,1},{4,6},{6,4},{5,7},{7,5},{8,10},{10,8},{9,1... | collective-permute-start | bytes 786440 | tf_op jit(solution)/shard_map/ppermute | solution.py:273
  109.6 9.1 %collective-permute-start.32 = (f32[200,128]{1,0:T(8,128)S(1)}, f32[200,128]{1,0:T(8,128)S(1)}, u32[]{:S(2)}, u32[]{:S(2)}) collective-permute-start(f32[200,128]{1,0:T(8,128)S(1)} %add_select_fusion.3), channel_id=1, source_target_pairs={{32,44},{48,60},{64,76},{80,92},{96,108},{112,124},{128,140},{144,... | collective-permute-start | bytes 307208 | tf_op jit(solution)/shard_map/ppermute | solution.py:344
  110.9 7.8 %collective-permute-start.30 = (f32[200,128]{1,0:T(8,128)S(1)}, f32[200,128]{1,0:T(8,128)S(1)}, u32[]{:S(2)}, u32[]{:S(2)}) collective-permute-start(f32[200,128]{1,0:T(8,128)S(1)} %add_select_fusion.3), channel_id=1, source_target_pairs={{32,40},{48,56},{64,72},{80,88},{96,104},{112,120},{128,136},{144,... | collective-permute-start | bytes 307208 | tf_op jit(solution)/shard_map/ppermute | solution.py:344
  112.2 6.5 %collective-permute-start.31 = (f32[200,128]{1,0:T(8,128)S(1)}, f32[200,128]{1,0:T(8,128)S(1)}, u32[]{:S(2)}, u32[]{:S(2)}) collective-permute-start(f32[200,128]{1,0:T(8,128)S(1)} %add_select_fusion.3), channel_id=1, source_target_pairs={{32,36},{48,52},{64,68},{80,84},{96,100},{112,116},{128,132},{144,... | collective-permute-start | bytes 307208 | tf_op jit(solution)/shard_map/ppermute | solution.py:344
  113.6 7.3 %collective-permute-start.20 = (f32[2,64,256]{2,1,0:T(8,128)S(1)}, f32[2,64,256]{2,1,0:T(8,128)S(1)}, u32[]{:S(2)}, u32[]{:S(2)}) collective-permute-start(f32[2,64,256]{2,1,0:T(8,128)S(1)} %dynamic-slice_bitcast_fusion.1), channel_id=1, source_target_pairs={{0,2},{2,0},{1,3},{3,1},{4,6},{6,4},{5,7},{7,5},{8,10},{10,8},{9,1... | collective-permute-start | bytes 393224 | tf_op jit(solution)/shard_map/ppermute | solution.py:273
  118.6 2.3 %collective-permute-start.18 = (f32[2,128,256]{2,1,0:T(8,128)S(1)}, f32[2,128,256]{2,1,0:T(8,128)S(1)}, u32[]{:S(2)}, u32[]{:S(2)}) collective-permute-start(f32[2,128,256]{2,1,0:T(8,128)S(1)} %fusion.1.own_ref), channel_id=1, source_target_pairs={{0,1},{1,0},{2,3},{3,2},{4,5},{5,4},{6,7},{7,6},{8,9},{9,8},{10,11... | collective-permute-start | bytes 786440 | tf_op jit(solution)/shard_map/ppermute | solution.py:273
  118.8 2.1 %collective-permute-start.33 = (f32[200,128]{1,0:T(8,128)S(1)}, f32[200,128]{1,0:T(8,128)S(1)}, u32[]{:S(2)}, u32[]{:S(2)}) collective-permute-start(f32[200,128]{1,0:T(8,128)S(1)} %add_select_fusion.2.mine_ref), channel_id=1, source_target_pairs={{0,1},{1,0},{2,3},{3,2},{4,5},{5,4},{6,7},{7,6},{8,9},{9,8},{10,11... | collective-permute-start | bytes 307208 | tf_op jit(solution)/shard_map/ppermute | solution.py:273
